TPU v7x, 32 devices: a whole 2x2x4 slice. The times are simulated.
32 devices in a mesh: ens: 8 (over z, y), space: 4 (over x, core).
Axes of the slice: x: 2, y: 2, z: 4, core: 2. Of those that a mesh axis runs over, the one named last changes fastest.
Arguments:
- grid_hidden: bfloat16 [8, 512, 1024], P('ens', 'space'), may hold values from -600 to 600
- latent: bfloat16 [8, 512, 1024], P('ens', 'space'), may hold values from -6 to 6
- tile_neighbor_index: int32 [4, 128], P('space'), may hold values from 0 to 511, as said below
- target: float32 [100, 512], P(None, 'space'), may hold values from -6 to 6
- w_query: bfloat16 [1024, 1024], replicated, may hold values from -0.1875 to 0.1875
- w_key: bfloat16 [1024, 1024], replicated, may hold values from -0.1875 to 0.1875
- w_value: bfloat16 [1024, 1024], replicated, may hold values from -0.1875 to 0.1875
- w_mix: bfloat16 [1024, 1024], replicated, may hold values from -0.1875 to 0.1875
- readout_weight: bfloat16 [100, 1024], replicated, may hold values from -0.1875 to 0.1875
Outputs:
- fair_ranked_score_loss: float32 [], replicated
- grad_out: float32 [100, 1024], replicated
- grad_query: float32 [1024, 1024], P('ens', 'space')
- grad_key: float32 [1024, 1024], P('ens', 'space')
- grad_value: float32 [1024, 1024], P('ens', 'space')
- grad_mix: float32 [1024, 1024], P('ens', 'space')
Inputs may be any that keep to these rules, and one draw needn't show every extreme that they name: `tile_neighbor_index`: row t holds 128 distinct latent node indices, all among the nodes of space shard s = t and of the two shards beside it, counted cyclically; shard s holds nodes s * 128 to (s + 1) * 128 - 1.
All inputs are finite; a program needn't handle non-finite values.
Results may differ from a plain program's by a relative error of at most 0.025.
Values may be sent and summed in bfloat16 or wider, within the bound.
No kernel may reach another device: no remote copies, remote signals or barrier semaphores. Data moves between devices by JAX's collectives and lax.ppermute only.
A program may use at most 128 MiB of HBM per device.

v0:
```python
import jax
import jax.numpy as jnp
from jax import lax
from jax.sharding import PartitionSpec as P

HEADS = 16


EPS = 1e-06
SMOOTH = 0.01


def with_halo(value, sides, width):
    for axis, dim in sides:
        size, length = (lax.axis_size(axis), value.shape[dim])
        up = [(i, (i + 1) % size) for i in range(size)]
        down = [(j, i) for i, j in up]
        last = lax.slice_in_dim(value, length - width, length, axis=dim)
        leading = lax.slice_in_dim(value, 0, width, axis=dim)
        before = lax.ppermute(last, axis, up)
        after = lax.ppermute(leading, axis, down)
        value = jnp.concatenate([before, value, after], axis=dim)
    return value


def by_heads(values_in):
    return values_in.reshape(
        values_in.shape[0], values_in.shape[1], HEADS, values_in.shape[2] // HEADS
    )


def rows_times(blocks, matrix):
    flat_rows = blocks.reshape(-1, blocks.shape[-1])
    product = jnp.dot(flat_rows, matrix, preferred_element_type=jnp.float32)
    return product.reshape(blocks.shape[:-1] + (matrix.shape[1],))


def contract_rows(left_side, right_side):
    return lax.dot_general(
        left_side, right_side, (((0,), (0,)), ((), ())), preferred_element_type=jnp.float32
    )


def contracted_columns(left_side, right_side):
    return lax.dot_general(
        left_side, right_side, (((1,), (1,)), ((), ())), preferred_element_type=jnp.float32
    )


def decoder_forward(grid_point_rows, latent_node_rows, weight_params):
    w_query, w_key, w_value, w_mix, readout_weight = weight_params
    features = grid_point_rows.shape[-1]
    factor = (features // HEADS) ** (-0.5)
    queries = rows_times(grid_point_rows, w_query).astype(jnp.bfloat16)
    keyset = rows_times(latent_node_rows, w_key).astype(jnp.bfloat16)
    valueset = rows_times(latent_node_rows, w_value).astype(jnp.bfloat16)
    scores = (
        jnp.einsum(
            "tqhd,tkhd->thqk",
            by_heads(queries),
            by_heads(keyset),
            preferred_element_type=jnp.float32,
        )
        * factor
    )
    highest = jnp.max(scores, axis=-1, keepdims=True)
    raised = jnp.exp(scores - highest)
    softmaxed = raised / jnp.sum(raised, axis=-1, keepdims=True)
    softmaxed_b = softmaxed.astype(jnp.bfloat16)
    attended = jnp.einsum(
        "thqk,tkhd->tqhd", softmaxed_b, by_heads(valueset), preferred_element_type=jnp.float32
    )
    attended = attended.reshape(grid_point_rows.shape).astype(jnp.bfloat16)
    hidden = grid_point_rows.astype(jnp.float32) + rows_times(attended, w_mix)
    inverse = lax.rsqrt(jnp.mean(hidden * hidden, axis=-1, keepdims=True) + EPS)
    normed = hidden * inverse
    normed_backward = normed.astype(jnp.bfloat16).reshape(-1, features)
    member_prediction = contracted_columns(readout_weight, normed_backward)
    saved_activations = (
        grid_point_rows,
        latent_node_rows,
        queries,
        keyset,
        valueset,
        softmaxed,
        softmaxed_b,
        attended,
        inverse,
        normed,
        normed_backward,
    )
    return (member_prediction, saved_activations)


def backward(saved_activations, loss_slopes, weight_params):
    w_query, w_key, w_value, w_mix, readout_weight = weight_params
    (
        grid_point_rows,
        latent_node_rows,
        queries,
        keyset,
        valueset,
        softmaxed,
        softmaxed_b,
        attended,
        inverse,
        normed,
        normed_backward,
    ) = saved_activations
    features = grid_point_rows.shape[-1]
    factor = (features // HEADS) ** (-0.5)
    slopes_b = loss_slopes.astype(jnp.bfloat16)
    grad_out = jnp.dot(slopes_b, normed_backward, preferred_element_type=jnp.float32)
    d_normed = contract_rows(slopes_b, readout_weight)
    normed_rows = normed.reshape(-1, features)
    d_hidden = inverse.reshape(-1, 1) * (
        d_normed - normed_rows * jnp.mean(d_normed * normed_rows, axis=-1, keepdims=True)
    )
    d_hidden_b = d_hidden.astype(jnp.bfloat16)
    grad_mix = contract_rows(attended.reshape(-1, features), d_hidden_b)
    d_attended = (
        contracted_columns(d_hidden_b, w_mix).astype(jnp.bfloat16).reshape(grid_point_rows.shape)
    )
    d_probs = jnp.einsum(
        "tqhd,tkhd->thqk",
        by_heads(d_attended),
        by_heads(valueset),
        preferred_element_type=jnp.float32,
    )
    d_values = jnp.einsum(
        "thqk,tqhd->tkhd", softmaxed_b, by_heads(d_attended), preferred_element_type=jnp.float32
    )
    d_values = d_values.reshape(latent_node_rows.shape).astype(jnp.bfloat16)
    d_scores = softmaxed * (d_probs - jnp.sum(d_probs * softmaxed, axis=-1, keepdims=True)) * factor
    d_scores_b = d_scores.astype(jnp.bfloat16)
    d_queries = jnp.einsum(
        "thqk,tkhd->tqhd", d_scores_b, by_heads(keyset), preferred_element_type=jnp.float32
    )
    d_queries = d_queries.reshape(grid_point_rows.shape).astype(jnp.bfloat16)
    d_keys = jnp.einsum(
        "thqk,tqhd->tkhd", d_scores_b, by_heads(queries), preferred_element_type=jnp.float32
    )
    d_keys = d_keys.reshape(latent_node_rows.shape).astype(jnp.bfloat16)
    grid_flat = grid_point_rows.reshape(-1, features)
    node_flat = latent_node_rows.reshape(-1, features)
    grad_query = contract_rows(grid_flat, d_queries.reshape(-1, features))
    grad_key = contract_rows(node_flat, d_keys.reshape(-1, features))
    grad_value = contract_rows(node_flat, d_values.reshape(-1, features))
    return (grad_out, grad_query, grad_key, grad_value, grad_mix)


def member_ranked_score(member_own_field, members_all, truth_rows, loss_scale_weight):
    members_count = members_all.shape[0]
    to_truth = member_own_field - truth_rows[None]
    skill_term = jnp.sqrt(to_truth * to_truth + SMOOTH)

    def add_member(running, other_member):
        apart_by = member_own_field - other_member[None]
        spread = jnp.sqrt(apart_by * apart_by + SMOOTH)
        return ((running[0] + spread, running[1] + apart_by / spread), None)

    zero_field = jnp.zeros(member_own_field.shape, jnp.float32)
    (spread_sum, slope_sum), _ = lax.scan(add_member, (zero_field, zero_field), members_all)
    pair_weight = 1.0 / (members_count * (members_count - 1))
    loss_part = loss_scale_weight * (
        jnp.sum(skill_term) / members_count
        - 0.5 * pair_weight * jnp.sum(spread_sum - jnp.sqrt(jnp.float32(SMOOTH)))
    )
    loss_slopes = loss_scale_weight * (
        to_truth / skill_term / members_count - pair_weight * slope_sum
    )
    return (loss_part, loss_slopes)


def body(
    grid_hidden, latent, tile_neighbor_index, target, w_query, w_key, w_value, w_mix, readout_weight
):
    node_count = latent.shape[1]
    features = latent.shape[2]
    shards = lax.axis_size("space")
    shard_index = lax.axis_index("space")
    weight_params = (w_query, w_key, w_value, w_mix, readout_weight)
    rimmed = with_halo(latent, (("space", 1),), node_count)
    positions = jnp.mod(tile_neighbor_index - (shard_index - 1) * node_count, node_count * shards)
    latent_node_rows = jnp.take(rimmed[0], positions, axis=0)
    grid_point_rows = grid_hidden[0].reshape(-1, 128, features)
    member_prediction, saved_activations = decoder_forward(
        grid_point_rows, latent_node_rows, weight_params
    )
    member_own_field = member_prediction[None]
    loss_scale_weight = (target.shape[0] * target.shape[1] * shards) ** (-0.5)
    members_count = lax.axis_size("ens")
    slice_width = target.shape[1] // members_count
    spread_out = lax.all_to_all(member_own_field, "ens", split_axis=2, concat_axis=0, tiled=True)
    truth_rows = lax.dynamic_slice_in_dim(
        target, lax.axis_index("ens") * slice_width, slice_width, 1
    )
    loss_part, member_slopes = member_ranked_score(
        spread_out, spread_out, truth_rows, loss_scale_weight
    )
    loss_slopes = lax.all_to_all(
        member_slopes.astype(jnp.bfloat16), "ens", split_axis=0, concat_axis=2, tiled=True
    ).astype(member_slopes.dtype)
    grad_out, grad_query, grad_key, grad_value, grad_mix = backward(
        saved_activations, loss_slopes[0], weight_params
    )
    fair_ranked_score_loss, grad_out = lax.psum((loss_part, grad_out), ("ens", "space"))
    gradients = (grad_query, grad_key, grad_value, grad_mix)
    gradients = (
        lax.psum_scatter(
            gradients[0].astype(jnp.bfloat16), "ens", scatter_dimension=0, tiled=True
        ).astype(jnp.float32),
        lax.psum_scatter(
            gradients[1].astype(jnp.bfloat16), "ens", scatter_dimension=0, tiled=True
        ).astype(jnp.float32),
        lax.psum_scatter(
            gradients[2].astype(jnp.bfloat16), "ens", scatter_dimension=0, tiled=True
        ).astype(jnp.float32),
        lax.psum_scatter(
            gradients[3].astype(jnp.bfloat16), "ens", scatter_dimension=0, tiled=True
        ).astype(jnp.float32),
    )
    gradients = (
        lax.psum_scatter(
            gradients[0].astype(jnp.bfloat16), "space", scatter_dimension=1, tiled=True
        ).astype(jnp.float32),
        lax.psum_scatter(
            gradients[1].astype(jnp.bfloat16), "space", scatter_dimension=1, tiled=True
        ).astype(jnp.float32),
        lax.psum_scatter(
            gradients[2].astype(jnp.bfloat16), "space", scatter_dimension=1, tiled=True
        ).astype(jnp.float32),
        lax.psum_scatter(
            gradients[3].astype(jnp.bfloat16), "space", scatter_dimension=1, tiled=True
        ).astype(jnp.float32),
    )
    return (
        fair_ranked_score_loss,
        grad_out,
        gradients[0],
        gradients[1],
        gradients[2],
        gradients[3],
    )


def solution(mesh):
    in_specs = (
        P("ens", "space", None),
        P("ens", "space", None),
        P("space", None),
        P(None, "space"),
        P(),
        P(),
        P(),
        P(),
        P(),
    )
    out_specs = (
        P(),
        P(),
        P("ens", "space"),
        P("ens", "space"),
        P("ens", "space"),
        P("ens", "space"),
    )
    return jax.shard_map(body, mesh=mesh, in_specs=in_specs, out_specs=out_specs, check_vma=False)
```

profile of v0, /device:TPU:0, one launch (start us, length us, event | category | flops | bytes accessed | tf_op | source)
XLA Modules:
  0.0 478.6 jit_solution(7946606421447477873)
XLA Ops:
  8.6 2.0 collective-permute-start.1
  10.6 2.1 convolution_convert_fusion.9
  19.4 2.2 convolution_convert_fusion.8
  21.8 2.2 convolution_convert_fusion.10
  30.8 5.8 %all-to-all-start = ((f32[1,100,128]{1,0,2:T(1,128)}), f32[1,100,128]{1,0,2:T(1,128)S(1)}, u32[]{:S(2)}, u32[]{:S(2)}) async-start(f32[1,100,128]{1,0,2:T(1,128)} %copy.45), calls=%async_computation | async-start | bytes 131072 | tf_op jit(solution)/shard_map/all_to_all | solution.py:194
  37.7 6.0 %all-to-all-done = f32[1,100,128]{1,0,2:T(1,128)S(1)} async-done(((f32[1,100,128]{1,0,2:T(1,128)}), f32[1,100,128]{1,0,2:T(1,128)S(1)}, u32[]{:S(2)}, u32[]{:S(2)}) %all-to-all-start) | async-done | bytes 51232 | tf_op jit(solution)/shard_map/all_to_all | solution.py:194
  45.0 9.0 %all_to_all.33 = bf16[8,100,16]{1,2,0:T(8,128)(2,1)S(1)} all-to-all(bf16[8,100,16]{1,2,0:T(8,128)(2,1)S(1)} %get-tuple-element.76), channel_id=1, replica_groups=mesh['ens'=8,'space'=4] {'ens'}, dimensions={0} | all-to-all | bytes 51200 | tf_op jit(solution)/shard_map/all_to_all | solution.py:201
  55.5 2.0 convolution_convert_fusion
  58.6 2.3 fusion.42
  60.9 2.8 convolution_convert_fusion.5
  63.8 2.0 convert_bitcast_fusion
  65.8 4.0 copy.56
  70.7 3.4 convolution_convert_fusion.4
  74.1 3.1 convolution_convert_fusion.2
  77.3 2.4 convolution_convert_fusion.3
  79.8 3.1 convolution_convert_fusion.1
  82.9 41.5 %reduce-scatter.21.cloned.1.call-done = bf16[128,1024]{1,0:T(8,128)(2,1)} async-done(((bf16[1024,1024]{1,0:T(8,128)(2,1)}), bf16[128,1024]{1,0:T(8,128)(2,1)}) %reduce-scatter.21.cloned.1.call-update) | async-done | bytes 262160 | tf_op jit(solution)/shard_map/reduce_scatter | solution.py:219
  124.5 70.9 %reduce-scatter.25.cloned.1.call-done = bf16[128,1024]{1,0:T(8,128)(2,1)} async-done(((bf16[1024,1024]{1,0:T(8,128)(2,1)}), bf16[128,1024]{1,0:T(8,128)(2,1)}) %reduce-scatter.25.cloned.1.call-update) | async-done | bytes 262160
  197.3 69.1 %reduce-scatter.13.cloned.1.call-done = bf16[128,1024]{1,0:T(8,128)(2,1)} async-done(((bf16[1024,1024]{1,0:T(8,128)(2,1)}), bf16[128,1024]{1,0:T(8,128)(2,1)}) %reduce-scatter.13.cloned.1.call-update) | async-done | bytes 262160 | tf_op jit(solution)/shard_map/reduce_scatter | solution.py:213
  266.5 70.7 %reduce-scatter.17.cloned.1.call-done = bf16[128,1024]{1,0:T(8,128)(2,1)} async-done(((bf16[1024,1024]{1,0:T(8,128)(2,1)}), bf16[128,1024]{1,0:T(8,128)(2,1)}) %reduce-scatter.17.cloned.1.call-update) | async-done | bytes 262160 | tf_op jit(solution)/shard_map/reduce_scatter | solution.py:216
  340.3 39.6 %psum.14 = f32[]{:T(128)} all-reduce(f32[]{:T(128)S(6)} %mul.80), channel_id=1, replica_groups=mesh['ens'=8,'space'=4] {'ens','space'}, use_global_device_ids=true, to_apply=%region_7.8 | all-reduce | flops 1 | bytes 8 | tf_op jit(solution)/shard_map/psum | solution.py:207
  383.0 20.9 %reduce-scatter.15.cloned.1.call-done = bf16[128,256]{1,0:T(8,128)(2,1)} async-done(((bf16[128,1024]{1,0:T(8,128)(2,1)}), bf16[128,256]{1,0:T(8,128)(2,1)}) %reduce-scatter.15.cloned.1.call-update) | async-done | bytes 65552 | tf_op jit(solution)/shard_map/reduce_scatter | solution.py:227
  405.3 21.0 %reduce-scatter.19.cloned.1.call-done = bf16[128,256]{1,0:T(8,128)(2,1)} async-done(((bf16[128,1024]{1,0:T(8,128)(2,1)}), bf16[128,256]{1,0:T(8,128)(2,1)}) %reduce-scatter.19.cloned.1.call-update) | async-done | bytes 65552 | tf_op jit(solution)/shard_map/reduce_scatter | solution.py:230
  427.9 41.5 %all-reduce.2.cloned.1.call-done = f32[100,1024]{1,0:T(8,128)} async-done(((f32[100,1024]{1,0:T(8,128)}), f32[100,1024]{1,0:T(8,128)}) %all-reduce.2.cloned.1.call-update) | async-done | bytes 409616 | tf_op jit(solution)/shard_map/psum | solution.py:207
  (99 shorter events, 32.1 us)
Async XLA Ops:
  8.0 19.5 %copy-start = (bf16[1024,1024]{1,0:T(8,128)(2,1)S(1)}, bf16[1024,1024]{1,0:T(8,128)(2,1)}, u32[]{:S(2)}) copy-start(bf16[1024,1024]{1,0:T(8,128)(2,1)} %param.18) | copy-start | bytes 6291460
  8.0 9.5 %copy-start.11 = (bf16[1,128,1024]{2,1,0:T(8,128)(2,1)S(1)}, bf16[1,128,1024]{2,1,0:T(8,128)(2,1)}, u32[]{:S(2)}) copy-start(bf16[1,128,1024]{2,1,0:T(8,128)(2,1)} %param.12) | copy-start | bytes 786436
  8.0 5.5 %copy-start.13 = (s32[1,128]{1,0:T(1,128)S(1)}, s32[1,128]{1,0:T(1,128)}, u32[]{:S(2)}) copy-start(s32[1,128]{1,0:T(1,128)} %param.13) | copy-start | bytes 1540
  8.0 6.9 %collective-permute-start = (bf16[1,128,1024]{2,1,0:T(8,128)(2,1)}, bf16[1,128,1024]{2,1,0:T(8,128)(2,1)S(1)}, u32[]{:S(2)}, u32[]{:S(2)}) collective-permute-start(bf16[1,128,1024]{2,1,0:T(8,128)(2,1)} %param.12), channel_id=1, source_target_pairs={{0,1},{1,2},{2,3},{3,0},{4,5},{5,6},{6,7},{7,4},{8,9},{9,10},{10,1... | collective-permute-start | bytes 786440 | tf_op jit(solution)/shard_map/ppermute | solution.py:20
  8.6 8.9 %collective-permute-start.1 = (bf16[1,128,1024]{2,1,0:T(8,128)(2,1)}, bf16[1,128,1024]{2,1,0:T(8,128)(2,1)}, u32[]{:S(2)}, u32[]{:S(2)}) collective-permute-start(bf16[1,128,1024]{2,1,0:T(8,128)(2,1)} %param.12), channel_id=1, source_target_pairs={{1,0},{2,1},{3,2},{0,3},{5,4},{6,5},{7,6},{4,7},{9,8},{10,9},{11,1... | collective-permute-start | bytes 786440 | tf_op jit(solution)/shard_map/ppermute | solution.py:21
  19.4 4.6 copy-start.1
  21.6 2.6 copy-start.8
  21.8 3.9 copy-start.10
  24.2 3.2 copy-start.4
  25.7 1.7 copy-start.3
  30.8 12.8 %all-to-all-start = ((f32[1,100,128]{1,0,2:T(1,128)}), f32[1,100,128]{1,0,2:T(1,128)S(1)}, u32[]{:S(2)}, u32[]{:S(2)}) async-start(f32[1,100,128]{1,0,2:T(1,128)} %copy.45), calls=%async_computation | async-start | bytes 131072 | tf_op jit(solution)/shard_map/all_to_all | solution.py:194
  36.7 87.8 %reduce-scatter.21.cloned.1.call-start = ((), (), s32[]{:S(2)}) async-start(), calls=%async_computation.16 | async-start | bytes 2359296 | tf_op jit(solution)/shard_map/reduce_scatter | solution.py:219
  54.1 1.3 copy-start.6
  57.6 137.8 %reduce-scatter.25.cloned.1.call-start = ((), (), s32[]{:S(2)}) async-start(), calls=%async_computation.18 | async-start | bytes 2359296
  69.8 1.0 copy-start.9
  69.8 4.4 copy-start.2
  69.8 196.6 %reduce-scatter.13.cloned.1.call-start = ((), (), s32[]{:S(2)}) async-start(), calls=%async_computation.12 | async-start | bytes 2359296 | tf_op jit(solution)/shard_map/reduce_scatter | solution.py:213
  77.3 259.9 %reduce-scatter.17.cloned.1.call-start = ((), (), s32[]{:S(2)}) async-start(), calls=%async_computation.14 | async-start | bytes 2359296 | tf_op jit(solution)/shard_map/reduce_scatter | solution.py:216
  82.9 254.4 %copy-start.7 = (bf16[8,100,16]{1,2,0:T(8,128)(2,1)S(1)}, bf16[8,100,16]{1,2,0:T(8,128)(2,1)}, u32[]{:S(2)}) copy-start(bf16[8,100,16]{1,2,0:T(8,128)(2,1)} %copy-done.6) | copy-start | bytes 76804
  82.9 297.0 %reduce-scatter.23.cloned.1.call-start = ((), (), s32[]{:S(2)}) async-start(), calls=%async_computation.17 | async-start | bytes 327680 | tf_op jit(solution)/shard_map/reduce_scatter | solution.py:233
  124.5 256.9 %reduce-scatter.11.cloned.1.call-start = ((), (), s32[]{:S(2)}) async-start(), calls=%async_computation.11 | async-start | bytes 327680 | tf_op jit(solution)/shard_map/reduce_scatter | solution.py:224
  197.2 206.6 %reduce-scatter.15.cloned.1.call-start = ((), (), s32[]{:S(2)}) async-start(), calls=%async_computation.13 | async-start | bytes 327680 | tf_op jit(solution)/shard_map/reduce_scatter | solution.py:227
  266.4 159.9 %reduce-scatter.19.cloned.1.call-start = ((), (), s32[]{:S(2)}) async-start(), calls=%async_computation.15 | async-start | bytes 327680 | tf_op jit(solution)/shard_map/reduce_scatter | solution.py:230
  337.2 132.1 %all-reduce.2.cloned.1.call-start = ((), (), s32[]{:S(2)}) async-start(), calls=%async_computation.10 | async-start | bytes 851968 | tf_op jit(solution)/shard_map/psum | solution.py:207
  (2 other events, 1.6 us)
Sparse Core Ops, SparseCore 0:
  57.7 66.7 reduce-scatter.20
  128.0 67.3 reduce-scatter.24
  199.0 67.3 reduce-scatter.12
  269.8 67.3 reduce-scatter.16
  339.5 19.0 reduce-scatter.22
  360.9 20.3 reduce-scatter.10
  383.8 19.9 reduce-scatter.14
  406.3 20.0 reduce-scatter.18
Sparse Core Ops, SparseCore 1:
  343.6 125.7 all-reduce.1
where the time goes:
time: 480 us; the launch traced here: 479 us
  waiting for transfers between devices  345 us (72%)
  blocking collectives  48.7 us (10%)
  matrix products  35.5 us (7%)
  between operations  17.1 us (4%)
  local copies, waits for them, and re-layouts  15.9 us (3%)
  starting transfers between devices  8.72 us (2%)
  other arithmetic  7.48 us (2%)
    unnamed x10, waiting for transfers between devices  71 us
    reduce_scatter x1, waiting for transfers between devices, body(): lax.psum_scatter(gradients[2].astype(jnp.bfloat16), 'ens', scatter_dimens...  70.7 us
    reduce_scatter x1, waiting for transfers between devices, body(): lax.psum_scatter(gradients[1].astype(jnp.bfloat16), 'ens', scatter_dimens...  69.1 us
    reduce_scatter x1, waiting for transfers between devices, body(): lax.psum_scatter(gradients[3].astype(jnp.bfloat16), 'ens', scatter_dimens...  41.5 us
    psum x1, waiting for transfers between devices, body(): lax.psum((loss_part, grad_out), ('ens', 'space'))  41.5 us
    psum x1, blocking collectives, body(): lax.psum((loss_part, grad_out), ('ens', 'space'))  39.6 us
    reduce_scatter x1, waiting for transfers between devices, body(): lax.psum_scatter(gradients[2].astype(jnp.bfloat16), 'space', scatter_dime...  21 us
    reduce_scatter x1, waiting for transfers between devices, body(): lax.psum_scatter(gradients[1].astype(jnp.bfloat16), 'space', scatter_dime...  20.9 us
  transfers between devices with their start and end apart: 12, of which 10 were waited for; matrix products, arithmetic and copies ran while one was open for 8% of the time, Pallas kernels for 0%

commit v1 on v0

v1 whole, which is shorter than its diff:
```python
import jax
import jax.numpy as jnp
from jax import lax
from jax.sharding import PartitionSpec as P

HEADS = 16
EPS = 1e-06
SMOOTH = 0.01


def swap(value, axis, bit):
    size = lax.axis_size(axis)
    return lax.ppermute(value, axis, [(i, i ^ bit) for i in range(size)])


def gather_shards(value, axis):
    size = lax.axis_size(axis)
    parts, slots = value[None], [0]
    bit = size // 2
    while bit:
        parts = jnp.concatenate([parts, swap(parts, axis, bit)], axis=0)
        slots = slots + [s ^ bit for s in slots]
        bit //= 2
    return parts, slots


def in_shard_order(parts, slots, axis):
    place = [0] * len(slots)
    for position, slot in enumerate(slots):
        place[slot] = position
    order = jnp.asarray(place, jnp.int32)[lax.axis_index(axis) ^ jnp.arange(len(slots))]
    return jnp.take(parts, order, axis=0)


def by_heads(values_in):
    return values_in.reshape(values_in.shape[0], HEADS, values_in.shape[1] // HEADS)


def dot32(left, right, dims):
    return lax.dot_general(left, right, (dims, ((), ())), preferred_element_type=jnp.float32)


def rows_times(rows, matrix):
    return dot32(rows, matrix, ((1,), (0,)))


def split16(value):
    high = lax.reduce_precision(value, 8, 7)
    return high.astype(jnp.bfloat16), (value - high).astype(jnp.bfloat16)


def forward(grid_rows, node_rows, weights):
    w_query, w_key, w_value, w_mix, readout_weight = weights
    features = grid_rows.shape[-1]
    factor = (features // HEADS) ** (-0.5)
    queries = rows_times(grid_rows, w_query).astype(jnp.bfloat16)
    keyset = rows_times(node_rows, w_key).astype(jnp.bfloat16)
    valueset = rows_times(node_rows, w_value).astype(jnp.bfloat16)
    scores = factor * jnp.einsum(
        "qhd,khd->hqk", by_heads(queries), by_heads(keyset), preferred_element_type=jnp.float32
    )
    raised = jnp.exp(scores - jnp.max(scores, axis=-1, keepdims=True))
    softmaxed = raised / jnp.sum(raised, axis=-1, keepdims=True)
    attended = jnp.einsum(
        "hqk,khd->qhd",
        softmaxed.astype(jnp.bfloat16),
        by_heads(valueset),
        preferred_element_type=jnp.float32,
    )
    attended = attended.reshape(grid_rows.shape).astype(jnp.bfloat16)
    hidden = grid_rows.astype(jnp.float32) + rows_times(attended, w_mix)
    inverse = lax.rsqrt(jnp.mean(hidden * hidden, axis=-1, keepdims=True) + EPS)
    normed = hidden * inverse
    normed_b = normed.astype(jnp.bfloat16)
    forecast = dot32(readout_weight, normed_b, ((1,), (1,)))
    return forecast, (queries, keyset, valueset, softmaxed, attended, inverse, normed, normed_b)


def backward(saved, slopes_b, weights):
    w_query, w_key, w_value, w_mix, readout_weight = weights
    queries, keyset, valueset, softmaxed, attended, inverse, normed, normed_b = saved
    features = queries.shape[-1]
    factor = (features // HEADS) ** (-0.5)
    softmaxed_b = softmaxed.astype(jnp.bfloat16)
    d_normed = dot32(slopes_b, readout_weight, ((0,), (0,)))
    d_hidden = inverse * (d_normed - normed * jnp.mean(d_normed * normed, axis=-1, keepdims=True))
    d_hidden = d_hidden.astype(jnp.bfloat16)
    d_attended = dot32(d_hidden, w_mix, ((1,), (1,))).astype(jnp.bfloat16)
    d_heads = by_heads(d_attended)
    d_probs = jnp.einsum(
        "qhd,khd->hqk", d_heads, by_heads(valueset), preferred_element_type=jnp.float32
    )
    d_values = jnp.einsum(
        "hqk,qhd->khd", softmaxed_b, d_heads, preferred_element_type=jnp.float32
    )
    d_scores = softmaxed * (d_probs - jnp.sum(d_probs * softmaxed, axis=-1, keepdims=True)) * factor
    d_scores = d_scores.astype(jnp.bfloat16)
    d_queries = jnp.einsum(
        "hqk,khd->qhd", d_scores, by_heads(keyset), preferred_element_type=jnp.float32
    )
    d_keys = jnp.einsum(
        "hqk,qhd->khd", d_scores, by_heads(queries), preferred_element_type=jnp.float32
    )
    flat = lambda v: v.reshape(queries.shape).astype(jnp.bfloat16)
    return d_hidden, flat(d_queries), flat(d_keys), flat(d_values)


def ranked_score(fields, truth, weight):
    members = fields.shape[0]
    pair_weight = 1.0 / (members * (members - 1))
    to_truth = fields - truth[None]
    skill = jnp.sqrt(to_truth * to_truth + SMOOTH)
    apart = fields[:, None] - fields[None, :]
    spread = jnp.sqrt(apart * apart + SMOOTH)
    loss = weight * (
        jnp.sum(skill) / members
        - 0.5 * pair_weight * jnp.sum(jnp.sum(spread, axis=1) - jnp.sqrt(jnp.float32(SMOOTH)))
    )
    slopes = weight * (to_truth / skill / members - pair_weight * jnp.sum(apart / spread, axis=1))
    return loss, slopes


def rows_of(flat, width):
    short = -flat.shape[0] % (16 * width)
    return jnp.pad(flat, (0, short)).reshape(-1, width)


def body(
    grid_hidden, latent, tile_neighbor_index, target, w_query, w_key, w_value, w_mix, readout_weight
):
    nodes, features = latent.shape[1:]
    points = grid_hidden.shape[1]
    channels = target.shape[0]
    shards, members = lax.axis_size("space"), lax.axis_size("ens")
    shard, member = lax.axis_index("space"), lax.axis_index("ens")
    weights = (w_query, w_key, w_value, w_mix, readout_weight)
    weight = (channels * points * shards) ** (-0.5)
    width, depth = features // shards, features // members
    bf16 = jnp.bfloat16

    latents, latent_slots = gather_shards(latent[0], "space")
    latents = in_shard_order(latents, latent_slots, "space").reshape(-1, features)
    index = tile_neighbor_index.reshape(-1)
    node_rows = jnp.take(latents, index, axis=0)
    grid_rows = grid_hidden[0]
    forecast, saved = forward(grid_rows, node_rows, weights)
    attended, normed_b = saved[4], saved[7]

    tags = jnp.concatenate([index // 128, index % 128]).astype(bf16)
    extra = jnp.concatenate([grid_rows, attended, rows_of(tags, features)], axis=0)

    high, low = split16(forecast)
    slices = jnp.transpose(normed_b.reshape(points, members, depth), (1, 0, 2))
    fields = jnp.concatenate([high.reshape(-1), low.reshape(-1)])
    packed = jnp.concatenate(
        [
            jnp.broadcast_to(fields, (members,) + fields.shape).reshape(members, -1, 128),
            slices.reshape(members, -1, 128),
        ],
        axis=1,
    )
    extras, slots = gather_shards(extra, "space")
    packed = lax.all_to_all(packed, "ens", split_axis=0, concat_axis=0, tiled=True)
    size = channels * points // 128
    fields = (packed[:, :size].astype(jnp.float32) + packed[:, size : 2 * size]).reshape(
        members, channels, points
    )
    loss, slopes = ranked_score(fields, target, weight)
    slopes_b = slopes.astype(bf16)
    grad_out = jnp.einsum(
        "mcp,mpf->cf",
        slopes_b,
        packed[:, 2 * size :].reshape(members, points, depth),
        preferred_element_type=jnp.float32,
    )
    own_slopes = lax.dynamic_index_in_dim(slopes_b, member, 0, keepdims=False)
    d_hidden, d_queries, d_keys, d_values = backward(saved, own_slopes, weights)

    high = lax.reduce_precision(loss, 8, 7)
    low = lax.reduce_precision(loss - high, 8, 7)
    rest = loss - high - low
    small = jnp.concatenate([grad_out.astype(bf16).reshape(-1), jnp.stack([high, low, rest]).astype(bf16)])
    small = rows_of(small, width)
    blocks = jnp.concatenate([d_queries, d_keys, d_values, d_hidden], axis=0)
    blocks = jnp.transpose(blocks.reshape(-1, shards, width), (1, 0, 2))
    blocks = jnp.concatenate(
        [blocks, jnp.broadcast_to(small, (shards,) + small.shape)], axis=1
    )
    blocks = lax.all_to_all(blocks, "space", split_axis=0, concat_axis=0, tiled=True)
    small = blocks[:, 4 * points :].astype(jnp.float32).reshape(shards, -1)
    small = jnp.sum(small[:, : channels * depth + 3], axis=0)
    fair_ranked_score_loss = jnp.sum(small[-3:])
    d_all = blocks[:, : 4 * points].reshape(shards, 4, points, width)

    extras = in_shard_order(extras, slots, "space")
    tags = extras[:, 2 * points :].reshape(shards, -1)[:, : 2 * points].astype(jnp.int32)
    index = (tags[:, :points] * 128 + tags[:, points:]).reshape(-1)
    all_nodes = jnp.take(latents, index, axis=0)
    all_grid = extras[:, :points].reshape(-1, features)
    all_attended = extras[:, points : 2 * points].reshape(-1, features)
    pick = lambda i: d_all[:, i].reshape(-1, width)
    gradients = [
        dot32(rows, pick(i), ((0,), (0,))).astype(bf16).reshape(members, depth, width)
        for i, rows in enumerate((all_grid, all_nodes, all_nodes, all_attended))
    ]
    tail = rows_of(small[:-3].astype(bf16), width)
    gradients.append(jnp.broadcast_to(tail, (members,) + tail.shape))
    gradients = jnp.concatenate(gradients, axis=1)
    gradients = lax.all_to_all(gradients, "ens", split_axis=0, concat_axis=0, tiled=True)
    grad_out = gradients[:, 4 * depth :].reshape(members, -1)[:, : channels * depth]
    grad_out = jnp.transpose(grad_out.reshape(members, channels, depth), (1, 0, 2))
    grad_out = grad_out.reshape(channels, features).astype(jnp.float32)
    sums = jnp.sum(gradients[:, : 4 * depth].astype(jnp.float32), axis=0)
    grads = [sums[i * depth : (i + 1) * depth] for i in range(4)]
    return (fair_ranked_score_loss, grad_out, grads[0], grads[1], grads[2], grads[3])


def solution(mesh):
    in_specs = (
        P("ens", "space", None),
        P("ens", "space", None),
        P("space", None),
        P(None, "space"),
        P(),
        P(),
        P(),
        P(),
        P(),
    )
    out_specs = (
        P(),
        P(),
        P("ens", "space"),
        P("ens", "space"),
        P("ens", "space"),
        P("ens", "space"),
    )
    return jax.shard_map(body, mesh=mesh, in_specs=in_specs, out_specs=out_specs, check_vma=False)
```

time: 480 us -> 199 us (0.41)
  waiting for transfers between devices: 345 us -> 70.1 us
  blocking collectives: 48.7 us -> 0 us
  local copies, waits for them, and re-layouts: 15.9 us -> 39.2 us
  other arithmetic: 7.48 us -> 28.4 us
  starting transfers between devices: 8.72 us -> 20.9 us
  between operations: 17.1 us -> 6.03 us
    reduce_scatter x7 -> x0, waiting for transfers between devices: 223 us -> none  [the longest x1 70.7 us: body(): lax.psum_scatter(gradients[2].astype(jnp.bfloat16), 'ens', scatter_dimens...]
    unnamed x10 -> x0, waiting for transfers between devices: 71 us -> none
    all_to_all x1 -> x3, waiting for transfers between devices: 6 us -> 54 us  [the longest x1 54 us: body(): lax.all_to_all(gradients, 'ens', split_axis=0, concat_axis=0, tiled=True)]
    psum x1 -> x0, waiting for transfers between devices: 41.5 us -> none  [body(): lax.psum((loss_part, grad_out), ('ens', 'space'))]
    psum x1 -> x0, blocking collectives: 39.6 us -> none  [body(): lax.psum((loss_part, grad_out), ('ens', 'space'))]
    ppermute x2 -> x4, waiting for transfers between devices: 3.2 us -> 16.1 us  [swap(): return lax.ppermute(value, axis, [(i, i ^ bit) for i in range(size)])]
    convert_element_type x4 -> x8, local copies, waits for them, and re-layouts: 1.37 us -> 12.8 us  [the longest x3 5.36 us: backward(): flat = lambda v: v.reshape(queries.shape).astype(jnp.bfloat16)]
    all_to_all x1 -> x3, starting transfers between devices: 5.83 us -> 16.3 us  [the longest x1 6.07 us: body(): lax.all_to_all(packed, 'ens', split_axis=0, concat_axis=0, tiled=True)]
  transfers between devices with their start and end apart: 12 -> 7, of which waited for: 10 -> 4; matrix products, arithmetic and copies ran while one was open for 8% -> 31% of each run, Pallas kernels for 0% -> 0%
where the time goes in v1:
time: 199 us; the launch traced here: 198 us
  waiting for transfers between devices  70.1 us (35%)
  local copies, waits for them, and re-layouts  39.2 us (20%)
  matrix products  33 us (17%)
  other arithmetic  28.4 us (14%)
  starting transfers between devices  20.9 us (11%)
  between operations  6.03 us (3%)
    all_to_all x1, waiting for transfers between devices, body(): lax.all_to_all(gradients, 'ens', split_axis=0, concat_axis=0, tiled=True)  54 us
    ppermute x4, waiting for transfers between devices, swap(): return lax.ppermute(value, axis, [(i, i ^ bit) for i in range(size)])  16.1 us
    dot_general x11, matrix products, dot32(): lax.dot_general(left, right, (dims, ((), ())), preferred_element_type=jnp...  14.7 us
    unnamed x48, local copies, waits for them, and re-layouts  9.61 us
    concatenate x4, other arithmetic, gather_shards(): parts = jnp.concatenate([parts, swap(parts, axis, bit)], axis=0)  6.61 us
    all_to_all x1, starting transfers between devices, body(): lax.all_to_all(packed, 'ens', split_axis=0, concat_axis=0, tiled=True)  6.07 us
    all_to_all x1, starting transfers between devices, body(): lax.all_to_all(gradients, 'ens', split_axis=0, concat_axis=0, tiled=True)  5.71 us
    convert_element_type x3, local copies, waits for them, and re-layouts, backward(): flat = lambda v: v.reshape(queries.shape).astype(jnp.bfloat16)  5.36 us
  transfers between devices with their start and end apart: 7, of which 4 were waited for; matrix products, arithmetic and copies ran while one was open for 31% of the time, Pallas kernels for 0%

profile of v1, /device:TPU:0, one launch (start us, length us, event | category | flops | bytes accessed | tf_op | source)
XLA Modules:
  0.0 197.5 jit_solution(11293377243267120338)
XLA Ops:
  0.7 3.0 %collective-permute-start = (bf16[1,128,1024]{2,1,0:T(8,128)(2,1)}, bf16[1,128,1024]{2,1,0:T(8,128)(2,1)S(1)}, u32[]{:S(2)}, u32[]{:S(2)}) collective-permute-start(bf16[1,128,1024]{2,1,0:T(8,128)(2,1)} %param.12), channel_id=1, source_target_pairs={{0,2},{1,3},{2,0},{3,1},{4,6},{5,7},{6,4},{7,5},{8,10},{9,11},{10,... | collective-permute-start | bytes 786440 | tf_op jit(solution)/shard_map/ppermute | solution.py:13
  5.0 2.1 %convolution_convert_fusion.10 = bf16[128,1024]{1,0:T(8,128)(2,1)S(1)} fusion(bf16[1024,1024]{1,0:T(8,128)(2,1)} %param.15, bf16[1,128,1024]{2,1,0:T(8,128)(2,1)} %param.11), kind=kOutput, calls=%fused_computation.34 | convolution fusion | flops 268566528 | bytes 2621440 | tf_op jit(solution)/shard_map/dot_general | solution.py:40
  17.2 2.9 %convolution_convert_fusion.9 = bf16[128,1024]{1,0:T(8,128)(2,1)} fusion(bf16[1024,1024]{1,0:T(8,128)(2,1)} %param.17, bf16[128,1024]{1,0:T(8,128)(2,1)S(1)} %gather_fusion.2, pred[128]{0:T(512)(128)(4,1)S(1)} %compare_and_fusion.2), kind=kOutput, calls=%fused_computation.33 | convolution fusion | flops 268697600 | bytes 2621568 | tf_op jit(solution)/shard_map/dot_general | solution.py:40
  24.3 2.4 %fusion.53 = (f32[16,128]{1,0:T(8,128)S(1)}, f32[16,128,128]{1,2,0:T(8,128)}) fusion(bf16[128,16,64]{0,2,1:T(8,128)(2,1)} %bitcast.170, bf16[128,16,64]{0,2,1:T(8,128)(2,1)S(1)} %bitcast.174), kind=kOutput, calls=%fused_computation.142 | convolution fusion | flops 34340992 | bytes 1581056 | tf_op jit(solution)/shard_map/sub | solution.py:62
  26.8 2.6 %convolution_convert_fusion.8 = bf16[16,64,128]{2,1,0:T(8,128)(2,1)} fusion(bf16[128,16,64]{0,2,1:T(8,128)(2,1)} %bitcast.155, f32[16,128]{1,0:T(8,128)S(1)} %get-tuple-element.26, bf16[128,16,64]{0,2,1:T(8,128)(2,1)} %bitcast.171, bf16[128,16,64]{0,2,1:T(8,128)(2,1)} %bitcast.175), kind=kOutput, calls=%fused_computation.32 | convolution fusion | flops 68290688 | bytes 1056768 | tf_op jit(solution)/shard_map/hqk,khd->qhd/dot_general | solution.py:64
  33.0 6.1 %all-to-all-start = ((bf16[8,328,128]{2,1,0:T(8,128)(2,1)}), bf16[8,328,128]{2,1,0:T(8,128)(2,1)}, u32[]{:S(2)}, u32[]{:S(2)}) async-start(bf16[8,328,128]{2,1,0:T(8,128)(2,1)} %pad_maximum_fusion.5), calls=%async_computation | async-start | bytes 1343488 | tf_op jit(solution)/shard_map/all_to_all | solution.py:163
  44.2 13.2 %collective-permute-done.2 = bf16[1,272,1024]{2,1,0:T(8,128)(2,1)} collective-permute-done((bf16[1,272,1024]{2,1,0:T(8,128)(2,1)}, bf16[1,272,1024]{2,1,0:T(8,128)(2,1)}, u32[]{:S(2)}, u32[]{:S(2)}) %collective-permute-start.2) | collective-permute-done | bytes 557088 | tf_op jit(solution)/shard_map/ppermute | solution.py:13
  57.4 2.3 %pad_maximum_fusion.2 = bf16[2,272,1024]{2,1,0:T(8,128)(2,1)} fusion(bf16[1,272,1024]{2,1,0:T(8,128)(2,1)} %collective-permute-done.2, bf16[1,272,1024]{2,1,0:T(8,128)(2,1)} %maximum_bitcast_fusion), kind=kLoop, calls=%fused_computation.41 | loop fusion | flops 557056 | bytes 2228224 | tf_op jit(solution)/shard_map/concatenate | solution.py:21
  61.0 4.1 %fusion.4 = (f32[8,100,128]{2,1,0:T(8,128)S(1)}, f32[8,100,128]{2,1,0:T(8,128)}) fusion(f32[8,100,128]{2,0,1:T(8,128)S(1)} %copy.82, f32[8,100,128]{2,1,0:T(8,128)S(1)} %convert_add_fusion), kind=kLoop, calls=%fused_computation.12 | loop fusion | flops 4710400 | bytes 1638400 | tf_op jit(solution)/shard_map/reduce_sum | solution.py:117
  66.5 2.2 %fusion.20 = (f32[]{:T(128)}, bf16[8,100,128]{2,1,0:T(8,128)(2,1)S(1)}) fusion(f32[100,128]{1,0:T(8,128)S(1)} %copy-done.16, bf16[8,328,128]{2,1,0:T(8,128)(2,1)} %all-to-all-done, f32[8,100,128]{2,1,0:T(8,128)} %get-tuple-element.7), kind=kLoop, calls=%fused_computation.62 | loop fusion | flops 1331199 | bytes 1075204 | tf_op jit(solution)/shard_map/reduce_sum | solution.py:116
  78.9 2.6 %convolution_convert_fusion.4 = bf16[16,64,128]{2,1,0:T(8,128)(2,1)} fusion(bf16[128,16,64]{0,2,1:T(8,128)(2,1)} %bitcast.157, f32[16,128]{1,0:T(8,128)S(1)} %get-tuple-element.26, bf16[128,16,64]{0,2,1:T(8,128)(2,1)} %bitcast.172, bf16[128,16,64]{0,2,1:T(8,128)(2,1)} %bitcast.176), kind=kOutput, calls=%fused_computation.28 | convolution fusion | flops 68290688 | bytes 1056768 | tf_op jit(solution)/shard_map/hqk,qhd->khd/dot_general | solution.py:93
  84.7 2.4 %fusion.54 = f32[16,128,128]{1,2,0:T(8,128)} fusion(bf16[128,16,64]{0,2,1:T(8,128)(2,1)} %bitcast.158, bf16[128,16,64]{0,2,1:T(8,128)(2,1)} %bitcast.156), kind=kOutput, calls=%fused_computation.143 | convolution fusion | flops 33554432 | bytes 1572864 | tf_op jit(solution)/shard_map/qhd,khd->hqk/dot_general | solution.py:90
  87.1 3.5 %convolution_convert_fusion.5 = bf16[16,64,128]{2,1,0:T(8,128)(2,1)} fusion(bf16[128,16,64]{0,2,1:T(8,128)(2,1)} %bitcast.173, f32[16,128,128]{1,2,0:T(8,128)} %fusion.54, f32[16,128,128]{1,2,0:T(8,128)} %get-tuple-element.27, f32[16,128]{1,0:T(8,128)S(1)} %get-tuple-element.26), kind=kOutput, calls=%fused_computation.29 | convolution fusion | flops 35522688 | bytes 2629632 | tf_op jit(solution)/shard_map/hqk,qhd->khd/dot_general | solution.py:101
  92.4 3.5 %convolution_convert_fusion.6 = bf16[16,64,128]{2,1,0:T(8,128)(2,1)} fusion(bf16[128,16,64]{0,2,1:T(8,128)(2,1)} %bitcast.177, f32[16,128,128]{1,2,0:T(8,128)} %fusion.54, f32[16,128,128]{1,2,0:T(8,128)} %get-tuple-element.27, f32[16,128]{1,0:T(8,128)S(1)} %get-tuple-element.26), kind=kOutput, calls=%fused_computation.30 | convolution fusion | flops 35522688 | bytes 2629632 | tf_op jit(solution)/shard_map/hqk,khd->qhd/dot_general | solution.py:98
  100.1 4.5 %all-to-all-start.1 = ((bf16[4,576,256]{2,1,0:T(8,128)(2,1)}), bf16[4,576,256]{2,1,0:T(8,128)(2,1)}, u32[]{:S(2)}, u32[]{:S(2)}) async-start(bf16[4,576,256]{2,1,0:T(8,128)(2,1)} %pad_maximum_fusion.1), calls=%async_computation.1 | async-start | bytes 2359296 | tf_op jit(solution)/shard_map/all_to_all | solution.py:189
  104.6 3.2 %pad_maximum_fusion = bf16[4,272,1024]{2,1,0:T(8,128)(2,1)} fusion(bf16[2,272,1024]{2,1,0:T(8,128)(2,1)} %collective-permute-done.3, bf16[1,272,1024]{2,1,0:T(8,128)(2,1)} %collective-permute-done.2, bf16[1,272,1024]{2,1,0:T(8,128)(2,1)} %maximum_bitcast_fusion), kind=kLoop, calls=%fused_computation.14 | loop fusion | flops 2228224 | bytes 4456448 | tf_op jit(solution)/shard_map/concatenate | solution.py:21
  107.8 3.7 %gather_fusion.3 = bf16[4,272,1024]{2,1,0:T(8,128)(2,1)} fusion(bf16[4,272,1024]{2,1,0:T(8,128)(2,1)} %pad_maximum_fusion, s32[1024]{0:T(1024)S(1)} %pad_clamp_fusion.2), kind=kCustom, calls=%fused_computation.3 | custom fusion | bytes 4456464 | tf_op jit(solution)/shard_map/jit(_take)/gather | solution.py:32
  111.4 1.9 broadcast_select_fusion
  114.9 2.8 %gather_fusion.4 = bf16[512,1024]{1,0:T(8,128)(2,1)} fusion(bf16[512,1024]{1,0:T(8,128)(2,1)S(1)} %bitcast_select_fusion, s32[1024]{0:T(1024)S(1)} %pad_clamp_fusion), kind=kCustom, calls=%fused_computation.4 | custom fusion | bytes 2099200 | tf_op jit(solution)/shard_map/jit(_take)/gather | solution.py:198
  117.7 3.0 %fusion.50 = (bf16[4,128,1024]{2,1,0:T(8,128)(2,1)}, bf16[4,128,1024]{2,1,0:T(8,128)(2,1)}) fusion(bf16[4,272,1024]{2,1,0:T(8,128)(2,1)} %copy-done.3), kind=kLoop, calls=%fused_computation.139 | loop fusion | bytes 4194304 | tf_op jit(solution)/shard_map/slice | solution.py:200
  124.1 2.0 convolution_convert_fusion.1
  132.4 5.7 %all-to-all-start.2 = ((bf16[8,576,256]{2,1,0:T(8,128)(2,1)}), bf16[8,576,256]{2,1,0:T(8,128)(2,1)}, u32[]{:S(2)}, u32[]{:S(2)}) async-start(bf16[8,576,256]{2,1,0:T(8,128)(2,1)} %broadcast_dynamic-update-slice_fusion), calls=%async_computation.2 | async-start | bytes 4718592 | tf_op jit(solution)/shard_map/all_to_all | solution.py:209
  138.7 54.0 %all-to-all-done.2 = bf16[8,576,256]{2,1,0:T(8,128)(2,1)} async-done(((bf16[8,576,256]{2,1,0:T(8,128)(2,1)}), bf16[8,576,256]{2,1,0:T(8,128)(2,1)}, u32[]{:S(2)}, u32[]{:S(2)}) %all-to-all-start.2) | async-done | bytes 2359328 | tf_op jit(solution)/shard_map/all_to_all | solution.py:209
  193.9 1.9 convert_reduce_fusion
  (122 shorter events, 55.9 us)
Async XLA Ops:
  0.6 28.7 %copy-start = (bf16[1024,1024]{1,0:T(8,128)(2,1)S(1)}, bf16[1024,1024]{1,0:T(8,128)(2,1)}, u32[]{:S(2)}) copy-start(bf16[1024,1024]{1,0:T(8,128)(2,1)} %param.18) | copy-start | bytes 6291460
  0.6 7.4 %copy-start.1 = (s32[4]{0:T(128)S(1)}, s32[4]{0:T(128)}, u32[]{:S(2)}) copy-start(s32[4]{0:T(128)} %constant.132.clone) | copy-start | bytes 52
  0.7 9.6 %copy-start.9 = (bf16[1,128,1024]{2,1,0:T(8,128)(2,1)S(1)}, bf16[1,128,1024]{2,1,0:T(8,128)(2,1)}, u32[]{:S(2)}) copy-start(bf16[1,128,1024]{2,1,0:T(8,128)(2,1)} %param.12) | copy-start | bytes 786436
  0.7 9.5 %collective-permute-start = (bf16[1,128,1024]{2,1,0:T(8,128)(2,1)}, bf16[1,128,1024]{2,1,0:T(8,128)(2,1)S(1)}, u32[]{:S(2)}, u32[]{:S(2)}) collective-permute-start(bf16[1,128,1024]{2,1,0:T(8,128)(2,1)} %param.12), channel_id=1, source_target_pairs={{0,2},{1,3},{2,0},{3,1},{4,6},{5,7},{6,4},{7,5},{8,10},{9,11},{10,... | collective-permute-start | bytes 786440 | tf_op jit(solution)/shard_map/ppermute | solution.py:13
  10.3 2.0 %collective-permute-start.1 = (bf16[2,128,1024]{2,1,0:T(8,128)(2,1)S(1)}, bf16[2,128,1024]{2,1,0:T(8,128)(2,1)S(1)}, u32[]{:S(2)}, u32[]{:S(2)}) collective-permute-start(bf16[2,128,1024]{2,1,0:T(8,128)(2,1)S(1)} %pad_maximum_fusion.6), channel_id=1, source_target_pairs={{0,1},{1,0},{2,3},{3,2},{4,5},{5,4},{6,7},{7,6},{8,9},{9,8},{10,11... | collective-permute-start | bytes 1572872 | tf_op jit(solution)/shard_map/ppermute | solution.py:13
  17.2 3.0 %copy-start.5 = (bf16[1024,1024]{1,0:T(8,128)(2,1)S(1)}, bf16[1024,1024]{1,0:T(8,128)(2,1)}, u32[]{:S(2)}) copy-start(bf16[1024,1024]{1,0:T(8,128)(2,1)} %param.16) | copy-start | bytes 6291460
  22.4 4.3 %copy-start.13 = (bf16[128,1024]{0,1:T(8,128)(2,1)}, bf16[128,1024]{0,1:T(8,128)(2,1)S(1)}, u32[]{:S(2)}) copy-start(bf16[128,1024]{0,1:T(8,128)(2,1)S(1)} %copy.77) | copy-start | bytes 786436
  26.8 2.6 %copy-start.4 = (bf16[1,128,1024]{2,1,0:T(8,128)(2,1)S(1)}, bf16[1,128,1024]{2,1,0:T(8,128)(2,1)}, u32[]{:S(2)}) copy-start(bf16[1,128,1024]{2,1,0:T(8,128)(2,1)} %param.11) | copy-start | bytes 786436
  29.3 2.4 %copy-start.12 = (bf16[100,1024]{1,0:T(8,128)(2,1)S(1)}, bf16[100,1024]{1,0:T(8,128)(2,1)}, u32[]{:S(2)}) copy-start(bf16[100,1024]{1,0:T(8,128)(2,1)} %param.19) | copy-start | bytes 614404
  30.9 0.8 copy-start.2
  31.7 7.4 %copy-start.17 = (s32[1,128]{1,0:T(1,128)S(1)}, s32[1,128]{1,0:T(1,128)}, u32[]{:S(2)}) copy-start(s32[1,128]{1,0:T(1,128)} %param.13) | copy-start | bytes 1540
  33.0 26.8 %all-to-all-start = ((bf16[8,328,128]{2,1,0:T(8,128)(2,1)}), bf16[8,328,128]{2,1,0:T(8,128)(2,1)}, u32[]{:S(2)}, u32[]{:S(2)}) async-start(bf16[8,328,128]{2,1,0:T(8,128)(2,1)} %pad_maximum_fusion.5), calls=%async_computation | async-start | bytes 1343488 | tf_op jit(solution)/shard_map/all_to_all | solution.py:163
  42.7 14.7 %collective-permute-start.2 = (bf16[1,272,1024]{2,1,0:T(8,128)(2,1)}, bf16[1,272,1024]{2,1,0:T(8,128)(2,1)}, u32[]{:S(2)}, u32[]{:S(2)}) collective-permute-start(bf16[1,272,1024]{2,1,0:T(8,128)(2,1)} %maximum_bitcast_fusion), channel_id=1, source_target_pairs={{0,2},{1,3},{2,0},{3,1},{4,6},{5,7},{6,4},{7,5},{8,10},{9,11},{10,... | collective-permute-start | bytes 1671176 | tf_op jit(solution)/shard_map/ppermute | solution.py:13
  59.8 6.7 %copy-start.16 = (f32[100,128]{1,0:T(8,128)S(1)}, f32[100,128]{1,0:T(8,128)}, u32[]{:S(2)}) copy-start(f32[100,128]{1,0:T(8,128)} %param.14) | copy-start | bytes 153604
  59.8 44.8 %collective-permute-start.3 = (bf16[2,272,1024]{2,1,0:T(8,128)(2,1)}, bf16[2,272,1024]{2,1,0:T(8,128)(2,1)}, u32[]{:S(2)}, u32[]{:S(2)}) collective-permute-start(bf16[2,272,1024]{2,1,0:T(8,128)(2,1)} %pad_maximum_fusion.2), channel_id=1, source_target_pairs={{0,1},{1,0},{2,3},{3,2},{4,5},{5,4},{6,7},{7,6},{8,9},{9,8},{10,11... | collective-permute-start | bytes 3342344 | tf_op jit(solution)/shard_map/ppermute | solution.py:13
  68.6 5.8 %copy-start.11 = (bf16[8,100,128]{2,1,0:T(8,128)(2,1)}, bf16[8,100,128]{2,1,0:T(8,128)(2,1)S(1)}, u32[]{:S(2)}) copy-start(bf16[8,100,128]{2,1,0:T(8,128)(2,1)S(1)} %get-tuple-element.17) | copy-start | bytes 614404
  100.1 20.6 %all-to-all-start.1 = ((bf16[4,576,256]{2,1,0:T(8,128)(2,1)}), bf16[4,576,256]{2,1,0:T(8,128)(2,1)}, u32[]{:S(2)}, u32[]{:S(2)}) async-start(bf16[4,576,256]{2,1,0:T(8,128)(2,1)} %pad_maximum_fusion.1), calls=%async_computation.1 | async-start | bytes 2359296 | tf_op jit(solution)/shard_map/all_to_all | solution.py:189
  113.3 1.4 copy-start.3
  124.1 2.0 %copy-start.6 = (bf16[512,1024]{1,0:T(8,128)(2,1)S(1)}, bf16[512,1024]{1,0:T(8,128)(2,1)}, u32[]{:S(2)}) copy-start(bf16[512,1024]{1,0:T(8,128)(2,1)} %gather_fusion.4) | copy-start | bytes 3145732
  124.1 2.0 %copy-start.15 = (bf16[4,1,128,256]{3,2,1,0:T(8,128)(2,1)S(1)}, bf16[4,1,128,256]{3,2,1,0:T(8,128)(2,1)}, u32[]{:S(2)}) copy-start(bf16[4,1,128,256]{3,2,1,0:T(8,128)(2,1)} %get-tuple-element.14) | copy-start | bytes 786436
  126.1 1.2 copy-start.8
  126.1 1.3 copy-start.14
  126.8 1.9 copy-start.7
  132.4 60.3 %all-to-all-start.2 = ((bf16[8,576,256]{2,1,0:T(8,128)(2,1)}), bf16[8,576,256]{2,1,0:T(8,128)(2,1)}, u32[]{:S(2)}, u32[]{:S(2)}) async-start(bf16[8,576,256]{2,1,0:T(8,128)(2,1)} %broadcast_dynamic-update-slice_fusion), calls=%async_computation.2 | async-start | bytes 4718592 | tf_op jit(solution)/shard_map/all_to_all | solution.py:209
  (1 other events, 0.7 us)

commit v2 on v1

v2 whole, which is shorter than its diff:
```python
import functools

import jax
import jax.numpy as jnp
from jax import lax
from jax.experimental import pallas as pl
from jax.experimental.pallas import tpu as pltpu
from jax.sharding import PartitionSpec as P

HEADS = 16
EPS = 1e-06
SMOOTH = 0.01
LANES = 128
MISC = 8
BF16, F32 = jnp.bfloat16, jnp.float32
VMEM = pl.BlockSpec(memory_space=pltpu.VMEM)
SMEM = pl.BlockSpec(memory_space=pltpu.SMEM)
ANY = pl.BlockSpec(memory_space=pl.ANY)


def dot32(left, right, contract=(1, 0)):
    dims = (((contract[0],), (contract[1],)), ((), ()))
    return lax.dot_general(left, right, dims, preferred_element_type=F32)


def swap(value, axis, bits):
    size = lax.axis_size(axis)
    return lax.ppermute(value, axis, [(i, i ^ bits) for i in range(size)])


def gather_slots(value, axis):
    parts = [value]
    for k in range(1, lax.axis_size(axis)):
        parts.append(swap(parts[k - 1], axis, 1) if k % 2 else swap(value, axis, k))
    return parts


def halves(pair):
    lane = lax.broadcasted_iota(jnp.int32, pair.shape, 1)
    zero = jnp.zeros_like(pair)
    first = lane < pair.shape[1] // 2
    return jnp.concatenate([jnp.where(first, pair, zero), jnp.where(first, zero, pair)], axis=0)


def joined(blocks):
    rows = blocks.shape[0] // 2
    lane = lax.broadcasted_iota(jnp.int32, (rows, blocks.shape[1]), 1)
    return jnp.where(lane < blocks.shape[1] // 2, blocks[:rows], blocks[rows:])


def query_kernel(rows_ref, w_hbm, out_ref, w_ref, sem):
    chunks = w_ref.shape[0]
    step = w_ref.shape[2]
    copies = [
        pltpu.make_async_copy(w_hbm.at[:, pl.ds(c * step, step)], w_ref.at[c], sem.at[c])
        for c in range(chunks)
    ]
    for copy in copies:
        copy.start()
    for c, copy in enumerate(copies):
        copy.wait()
        out_ref[:, c * step : (c + 1) * step] = dot32(rows_ref[...], w_ref[c]).astype(BF16)


def project_queries(rows, weight):
    features = weight.shape[0]
    step = min(512, features)
    return pl.pallas_call(
        query_kernel,
        out_shape=jax.ShapeDtypeStruct(rows.shape, BF16),
        in_specs=[VMEM, ANY],
        out_specs=VMEM,
        scratch_shapes=[
            pltpu.VMEM((features // step, features, step), BF16),
            pltpu.SemaphoreType.DMA((features // step,)),
        ],
        cost_estimate=pl.CostEstimate(
            flops=2 * rows.size * features, bytes_accessed=2 * weight.size, transcendentals=0
        ),
        name="project_queries",
    )(rows, weight)


def forward_kernel(shards, members, *refs):
    position_ref, grid_ref, query_ref, readout_ref = refs[:4]
    latent_refs = refs[4 : 4 + shards]
    weights_hbm = refs[4 + shards : 7 + shards]
    (
        key_ref,
        value_ref,
        soft_ref,
        attended_ref,
        normed_ref,
        inverse_ref,
        packed_ref,
        *w_refs,
        sem,
    ) = refs[7 + shards :]
    copies = [pltpu.make_async_copy(s, d, sem.at[i]) for i, (s, d) in enumerate(zip(weights_hbm, w_refs))]
    for copy in copies:
        copy.start()
    points, features = grid_ref.shape
    latents = jnp.concatenate([ref[...] for ref in latent_refs], axis=0)
    node = lax.broadcasted_iota(jnp.int32, (points, latents.shape[0]), 1)
    chosen = jnp.where(node == position_ref[...], 1.0, 0.0).astype(BF16)
    nodes = dot32(chosen, latents).astype(BF16)
    copies[0].wait()
    key_ref[...] = dot32(nodes, w_refs[0][...]).astype(BF16)
    copies[1].wait()
    value_ref[...] = dot32(nodes, w_refs[1][...]).astype(BF16)
    factor = (features // HEADS) ** (-0.5)
    for pair in range(features // LANES):
        at = slice(pair * LANES, (pair + 1) * LANES)
        scores = dot32(query_ref[:, at], halves(key_ref[:, at]), (1, 1)) * factor
        soft = []
        for head in range(2):
            block = scores[:, head * LANES : (head + 1) * LANES]
            raised = jnp.exp(block - jnp.max(block, axis=-1, keepdims=True))
            soft.append(raised / jnp.sum(raised, axis=-1, keepdims=True))
        soft = jnp.concatenate(soft, axis=1)
        soft_ref[pair] = soft
        attended_ref[:, at] = dot32(soft.astype(BF16), halves(value_ref[:, at])).astype(BF16)
    copies[2].wait()
    hidden = grid_ref[...].astype(F32) + dot32(attended_ref[...], w_refs[2][...])
    inverse = lax.rsqrt(jnp.mean(hidden * hidden, axis=-1, keepdims=True) + EPS)
    normed = hidden * inverse
    normed_ref[...] = normed
    inverse_ref[...] = inverse
    normed_b = normed.astype(BF16)
    forecast = dot32(readout_ref[...], normed_b, (1, 1))
    high = forecast.astype(BF16)
    low = (forecast - high.astype(F32)).astype(BF16)
    channels = readout_ref.shape[0]
    depth = features // members
    pieces = LANES // depth
    part = points // pieces
    for m in range(members):
        packed_ref[m, :channels] = high
        packed_ref[m, channels : 2 * channels] = low
        for p in range(pieces):
            packed_ref[m, 2 * channels :, p * depth : (p + 1) * depth] = normed_b[
                p * part : (p + 1) * part, m * depth : (m + 1) * depth
            ]


def forward(position, grid_rows, queries, readout, latents, weights, members):
    points, features = grid_rows.shape
    channels = readout.shape[0]
    depth = features // members
    rows = 2 * channels + points * depth // LANES
    shape = jax.ShapeDtypeStruct
    return pl.pallas_call(
        functools.partial(forward_kernel, len(latents), members),
        out_shape=(
            shape((points, features), BF16),
            shape((points, features), BF16),
            shape((features // LANES, points, 2 * LANES), F32),
            shape((points, features), BF16),
            shape((points, features), F32),
            shape((points, 1), F32),
            shape((members, rows, LANES), BF16),
        ),
        in_specs=[VMEM] * (4 + len(latents)) + [ANY] * 3,
        out_specs=(VMEM,) * 7,
        scratch_shapes=[pltpu.VMEM((features, features), BF16)] * 3
        + [pltpu.SemaphoreType.DMA((3,))],
        cost_estimate=pl.CostEstimate(
            flops=8 * points * features * features,
            bytes_accessed=6 * features * features,
            transcendentals=points * LANES * HEADS,
        ),
        name="decoder_forward",
    )(position, grid_rows, queries, readout, *latents, *weights)


def backward_kernel(
    shards,
    channels_used,
    member_ref,
    packed_ref,
    target_ref,
    index_ref,
    query_ref,
    key_ref,
    value_ref,
    soft_ref,
    normed_ref,
    inverse_ref,
    readout_ref,
    w_hbm,
    out_ref,
    w_ref,
    slope_ref,
    d_attended_ref,
    small_ref,
    sem,
):
    copy = pltpu.make_async_copy(w_hbm, w_ref, sem)
    copy.start()
    members = packed_ref.shape[0]
    points, features = normed_ref.shape
    channels = readout_ref.shape[0]
    width, depth = features // shards, features // members
    weight = (channels_used * points * shards) ** (-0.5)
    pair_weight = 1.0 / (members * (members - 1))
    chunk = 16

    def crps(c, loss):
        at = pl.ds(pl.multiple_of(c * chunk, chunk), chunk)
        low_at = pl.ds(pl.multiple_of(c * chunk + channels, chunk), chunk)
        fields = [
            packed_ref[m, at].astype(F32) + packed_ref[m, low_at].astype(F32)
            for m in range(members)
        ]
        truth = target_ref[at]
        skill = jnp.zeros_like(truth)
        slopes = []
        for m in range(members):
            apart = fields[m] - truth
            square = apart * apart + SMOOTH
            root = lax.rsqrt(square)
            skill = skill + square * root
            slopes.append(apart * root * (weight / members))
        spread = jnp.zeros_like(truth)
        for m in range(members):
            for k in range(m):
                apart = fields[m] - fields[k]
                square = apart * apart + SMOOTH
                root = lax.rsqrt(square)
                spread = spread + square * root
                ratio = apart * root * (weight * pair_weight)
                slopes[m] = slopes[m] - ratio
                slopes[k] = slopes[k] + ratio
        for m in range(members):
            slope_ref[m, at] = slopes[m].astype(BF16)
        channel = c * chunk + lax.broadcasted_iota(jnp.int32, truth.shape, 0)
        term = skill * (1.0 / members) - spread * pair_weight
        return loss + jnp.where(channel < channels_used, term, 0.0)

    loss = lax.fori_loop(0, channels // chunk, crps, jnp.zeros((chunk, points), F32))
    loss = weight * jnp.sum(jnp.sum(loss, axis=0, keepdims=True), axis=1, keepdims=True)

    pieces = LANES // depth
    part = points // pieces
    total = jnp.zeros((channels, depth), F32)
    for m in range(members):
        tail = packed_ref[m, 2 * channels :]
        for p in range(pieces):
            total = total + dot32(
                slope_ref[m][:, p * part : (p + 1) * part], tail[:, p * depth : (p + 1) * depth]
            )
    rows = small_ref.shape[0] - MISC
    for p in range(channels // rows):
        small_ref[:rows, p * depth : (p + 1) * depth] = total[p * rows : (p + 1) * rows]
    first = loss.astype(BF16).astype(F32)
    second = (loss - first).astype(BF16).astype(F32)
    for i, value in enumerate((first, second, loss - first - second)):
        small_ref[rows + i : rows + i + 1] = jnp.broadcast_to(value, (1, width))
    small_ref[rows + 3 : rows + MISC] = jnp.zeros((MISC - 3, width), F32)
    small_ref[rows + 3 : rows + 3 + index_ref.shape[0]] = index_ref[...]
    small = small_ref[...].astype(BF16)
    for s in range(shards):
        out_ref[s, 4 * points :] = small

    def put(kind, column, value):
        step = min(width, value.shape[1])
        for c in range(0, value.shape[1], step):
            shard, lane = divmod(column + c, width)
            out_ref[shard, kind * points : (kind + 1) * points, lane : lane + step] = value[
                :, c : c + step
            ]

    own = slope_ref[member_ref[0]]
    normed = normed_ref[...]
    d_normed = dot32(own, readout_ref[...], (0, 0))
    mean = jnp.mean(d_normed * normed, axis=-1, keepdims=True)
    d_hidden = (inverse_ref[...] * (d_normed - normed * mean)).astype(BF16)
    put(3, 0, d_hidden)
    copy.wait()
    d_attended_ref[...] = dot32(d_hidden, w_ref[...], (1, 1)).astype(BF16)
    factor = (features // HEADS) ** (-0.5)
    for pair in range(features // LANES):
        at = slice(pair * LANES, (pair + 1) * LANES)
        soft = soft_ref[pair]
        d_out = d_attended_ref[:, at]
        d_probs = dot32(d_out, halves(value_ref[:, at]), (1, 1))
        put(2, pair * LANES, joined(dot32(soft.astype(BF16), d_out, (0, 0))).astype(BF16))
        product = d_probs * soft
        d_scores = []
        for head in range(2):
            block = slice(head * LANES, (head + 1) * LANES)
            summed = jnp.sum(product[:, block], axis=-1, keepdims=True)
            d_scores.append(soft[:, block] * (d_probs[:, block] - summed) * factor)
        d_scores = jnp.concatenate(d_scores, axis=1).astype(BF16)
        put(0, pair * LANES, dot32(d_scores, halves(key_ref[:, at])).astype(BF16))
        put(1, pair * LANES, joined(dot32(d_scores, query_ref[:, at], (0, 0))).astype(BF16))


def backward(member, packed, target, index, saved, readout, w_mix, shards, channels_used):
    members = packed.shape[0]
    features = w_mix.shape[0]
    points = saved[0].shape[0]
    channels = readout.shape[0]
    width, depth = features // shards, features // members
    small = channels * depth // width + MISC
    small = small + -small % 16
    return pl.pallas_call(
        functools.partial(backward_kernel, shards, channels_used),
        out_shape=jax.ShapeDtypeStruct((shards, 4 * points + small, width), BF16),
        in_specs=[SMEM] + [VMEM] * 10 + [ANY],
        out_specs=VMEM,
        scratch_shapes=[
            pltpu.VMEM((features, features), BF16),
            pltpu.VMEM((members, channels, points), BF16),
            pltpu.VMEM((points, features), BF16),
            pltpu.VMEM((channels * depth // width + MISC, width), F32)
            if small == channels * depth // width + MISC
            else pltpu.VMEM((small, width), F32),
            pltpu.SemaphoreType.DMA,
        ],
        cost_estimate=pl.CostEstimate(
            flops=4 * points * features * features,
            bytes_accessed=4 * features * features,
            transcendentals=0,
        ),
        name="decoder_backward",
    )(member, packed, target, index, *saved, readout, w_mix)


def gradient_kernel(shards, members, nodes, channels, shard_ref, blocks_ref, *refs):
    latent_refs, grid_refs, attended_refs = (refs[i * shards : (i + 1) * shards] for i in range(3))
    out_ref, loss_ref = refs[3 * shards :]
    points, features = grid_refs[0].shape
    width, depth = features // shards, features // members
    shard = shard_ref[0]
    rows = channels * depth // width
    start = 4 * points
    small = jnp.zeros((blocks_ref.shape[1] - start, width), F32)
    for s in range(shards):
        small = small + blocks_ref[s, start:].astype(F32)
    loss_ref[...] = jnp.sum(small[rows : rows + 3, :1], axis=0, keepdims=True)
    small = small.astype(BF16)
    for m in range(members):
        out_ref[m, 4 * depth :] = small

    def slots(kind):
        at = slice(kind * points, (kind + 1) * points)
        return jnp.concatenate([blocks_ref[shard ^ k, at] for k in range(shards)], axis=0)

    def put(kind, lefts, right):
        left = jnp.concatenate([ref[...] for ref in lefts], axis=0)
        total = dot32(left, right, (0, 0)).astype(BF16)
        for m in range(members):
            out_ref[m, kind * depth : (kind + 1) * depth] = total[m * depth : (m + 1) * depth]

    put(3, attended_refs, slots(3))
    chosen = []
    for k in range(shards):
        index = blocks_ref[shard ^ k, start + rows : start + rows + MISC].astype(jnp.int32)
        if width >= 2 * points:
            owner, offset = index[3:4, :points], index[3:4, points : 2 * points]
        else:
            lines = points // width
            owner, offset = (
                jnp.concatenate([index[3 + b + i : 4 + b + i] for i in range(lines)], axis=1)
                for b in (0, lines)
            )
        position = (owner ^ shard) * nodes + offset
        node = lax.broadcasted_iota(jnp.int32, (nodes * shards, points), 0)
        chosen.append(jnp.where(node == position, 1.0, 0.0).astype(BF16))
    chosen = jnp.concatenate(chosen, axis=1)
    put(1, latent_refs, dot32(chosen, slots(1)).astype(BF16))
    put(2, latent_refs, dot32(chosen, slots(2)).astype(BF16))
    put(0, grid_refs, slots(0))


def gradients(shard, blocks, latents, grids, attendeds, members, channels):
    shards, rows, width = blocks.shape
    points, features = grids[0].shape
    depth = features // members
    return pl.pallas_call(
        functools.partial(gradient_kernel, shards, members, latents[0].shape[0], channels),
        out_shape=(
            jax.ShapeDtypeStruct((members, 4 * depth + rows - 4 * points, width), BF16),
            jax.ShapeDtypeStruct((1, 1), F32),
        ),
        in_specs=[SMEM] + [VMEM] * (1 + 3 * shards),
        out_specs=(VMEM, VMEM),
        cost_estimate=pl.CostEstimate(
            flops=8 * points * shards * features * width,
            bytes_accessed=8 * points * shards * features,
            transcendentals=0,
        ),
        name="weight_gradients",
    )(shard, blocks, *latents, *grids, *attendeds)


def sum_kernel(channels, blocks_ref, out_ref, *grad_refs):
    members, _, width = blocks_ref.shape
    depth = grad_refs[0].shape[0]
    for i, ref in enumerate(grad_refs):
        at = slice(i * depth, (i + 1) * depth)
        total = blocks_ref[0, at].astype(F32)
        for m in range(1, members):
            total = total + blocks_ref[m, at].astype(F32)
        ref[...] = total
    rows = channels * depth // width
    for m in range(members):
        small = blocks_ref[m, 4 * depth :].astype(F32)
        for p in range(width // depth):
            last = min((p + 1) * rows, out_ref.shape[0])
            out_ref[p * rows : last, m * depth : (m + 1) * depth] = small[
                : last - p * rows, p * depth : (p + 1) * depth
            ]


def sum_members(blocks, channels, channels_used, depth):
    members, _, width = blocks.shape
    shape = jax.ShapeDtypeStruct
    return pl.pallas_call(
        functools.partial(sum_kernel, channels),
        out_shape=(shape((channels_used, depth * members), F32),) + (shape((depth, width), F32),) * 4,
        in_specs=[VMEM],
        out_specs=(VMEM,) * 5,
        name="sum_members",
    )(blocks)


def body(
    grid_hidden, latent, tile_neighbor_index, target, w_query, w_key, w_value, w_mix, readout_weight
):
    nodes, features = latent.shape[1:]
    points = grid_hidden.shape[1]
    channels_used = target.shape[0]
    shards, members = lax.axis_size("space"), lax.axis_size("ens")
    shard, member = lax.axis_index("space"), lax.axis_index("ens")
    width, depth = features // shards, features // members

    latents = gather_slots(latent[0], "space")
    grid_rows = grid_hidden[0]
    queries = project_queries(grid_rows, w_query)
    spare = ((0, -channels_used % 16), (0, 0))
    readout = jnp.pad(readout_weight, spare)
    truth = jnp.pad(target, spare)
    channels = readout.shape[0]
    index = tile_neighbor_index.reshape(-1)
    owner, offset = index // nodes, index % nodes
    tags = jnp.concatenate([owner, offset]).astype(F32).reshape(-1, width)
    position = ((owner ^ shard) * nodes + offset)[:, None]
    *saved, packed = forward(
        position, grid_rows, queries, readout, latents, (w_key, w_value, w_mix), members
    )
    keyset, valueset, soft, attended, normed, inverse = saved
    packed = lax.all_to_all(packed, "ens", split_axis=0, concat_axis=0, tiled=True)
    grids = gather_slots(grid_rows, "space")
    attendeds = gather_slots(attended, "space")
    saved = (queries, keyset, valueset, soft, normed, inverse)
    blocks = backward(
        member[None], packed, truth, tags, saved, readout, w_mix, shards, channels_used
    )
    blocks = lax.all_to_all(blocks, "space", split_axis=0, concat_axis=0, tiled=True)
    blocks, loss = gradients(shard[None], blocks, latents, grids, attendeds, members, channels)
    blocks = lax.all_to_all(blocks, "ens", split_axis=0, concat_axis=0, tiled=True)
    grad_out, *grads = sum_members(blocks, channels, channels_used, depth)
    return (loss.reshape(()), grad_out, *grads)


def solution(mesh):
    in_specs = (
        P("ens", "space", None),
        P("ens", "space", None),
        P("space", None),
        P(None, "space"),
        P(),
        P(),
        P(),
        P(),
        P(),
    )
    out_specs = (
        P(),
        P(),
        P("ens", "space"),
        P("ens", "space"),
        P("ens", "space"),
        P("ens", "space"),
    )
    return jax.shard_map(body, mesh=mesh, in_specs=in_specs, out_specs=out_specs, check_vma=False)
```

time: 199 us -> 159 us (0.80)
  blocking collectives: 0 us -> 58.8 us
  matrix products: 33 us -> 0 us
  local copies, waits for them, and re-layouts: 39.2 us -> 6.36 us
  other arithmetic: 28.4 us -> 1.28 us
  Pallas kernels: 0 us -> 25.3 us
  waiting for transfers between devices: 70.1 us -> 50.6 us
  starting transfers between devices: 20.9 us -> 15.4 us
  between operations: 6.03 us -> 0.81 us
    all_to_all x0 -> x1, blocking collectives: none -> 58.8 us  [body(): lax.all_to_all(blocks, 'ens', split_axis=0, concat_axis=0, tiled=True)]
    all_to_all x1 -> x0, waiting for transfers between devices: 54 us -> none  [body(): lax.all_to_all(gradients, 'ens', split_axis=0, concat_axis=0, tiled=True)]
    dot_general x17 -> x0, matrix products: 30.5 us -> none  [the longest x11 14.7 us: dot32(): lax.dot_general(left, right, (dims, ((), ())), preferred_element_type=jnp...]
    pallas_call x0 -> x5, Pallas kernels: none -> 25.3 us  [the longest x1 7.18 us: backward(): pl.pallas_call(functools.partial(backward_kernel, shards, channels_used),...]
    all_to_all x1, waiting for transfers between devices: 0.01 us -> 18.2 us  [body(): lax.all_to_all(packed, 'ens', split_axis=0, concat_axis=0, tiled=True)]
    ppermute x4 -> x9, waiting for transfers between devices: 16.1 us -> 32.4 us  [swap(): return lax.ppermute(value, axis, [(i, i ^ bits) for i in range(size)])]
    convert_element_type x8 -> x0, local copies, waits for them, and re-layouts: 12.8 us -> none  [the longest x3 5.36 us: backward(): flat = lambda v: v.reshape(queries.shape).astype(jnp.bfloat16)]
    concatenate x9 -> x0, other arithmetic: 9.83 us -> none  [the longest x4 6.61 us: gather_shards(): parts = jnp.concatenate([parts, swap(parts, axis, bit)], axis=0)]
  transfers between devices with their start and end apart: 7 -> 11, of which waited for: 4 -> 5; matrix products, arithmetic and copies ran while one was open for 31% -> 3% of each run, Pallas kernels for 0% -> 2%
where the time goes in v2:
time: 159 us
  blocking collectives  58.8 us (37%)
  waiting for transfers between devices  50.6 us (32%)
  Pallas kernels  25.3 us (16%)
  starting transfers between devices  15.4 us (10%)
  local copies, waits for them, and re-layouts  6.36 us (4%)
    all_to_all x1, blocking collectives, body(): lax.all_to_all(blocks, 'ens', split_axis=0, concat_axis=0, tiled=True)  58.8 us
    ppermute x9, waiting for transfers between devices, swap(): return lax.ppermute(value, axis, [(i, i ^ bits) for i in range(size)])  32.4 us
    all_to_all x1, waiting for transfers between devices, body(): lax.all_to_all(packed, 'ens', split_axis=0, concat_axis=0, tiled=True)  18.2 us
    pallas_call x1, Pallas kernels, backward(): pl.pallas_call(functools.partial(backward_kernel, shards, channels_used),...  7.18 us
    pallas_call x1, Pallas kernels, forward(): pl.pallas_call(functools.partial(forward_kernel, len(latents), members),...  6.65 us
    all_to_all x1, starting transfers between devices, body(): lax.all_to_all(packed, 'ens', split_axis=0, concat_axis=0, tiled=True)  6.09 us
    ppermute x9, starting transfers between devices, swap(): return lax.ppermute(value, axis, [(i, i ^ bits) for i in range(size)])  5.64 us
    pallas_call x1, Pallas kernels, gradients(): pl.pallas_call(functools.partial(gradient_kernel, shards, members, latent...  5.2 us
  transfers between devices with their start and end apart: 11, of which 5 were waited for; matrix products, arithmetic and copies ran while one was open for 3% of the time, Pallas kernels for 2%

profile of v2, /device:TPU:0, one launch (start us, length us, event | category | flops | bytes accessed | tf_op | source)
XLA Modules:
  0.0 158.5 jit_solution(7740841449862561339)
XLA Ops:
  0.6 3.0 %collective-permute-start.1 = (bf16[128,1024]{1,0:T(8,128)(2,1)}, bf16[128,1024]{1,0:T(8,128)(2,1)S(1)}, u32[]{:S(2)}, u32[]{:S(2)}) collective-permute-start(bf16[128,1024]{1,0:T(8,128)(2,1)} %bitcast.11), channel_id=1, source_target_pairs={{0,2},{1,3},{2,0},{3,1},{4,6},{5,7},{6,4},{7,5},{8,10},{9,11},{10,... | collective-permute-start | bytes 786440 | tf_op jit(solution)/shard_map/ppermute | solution.py:28
  3.7 6.5 %collective-permute-done.1.refs_6_.refs_2_ = bf16[128,1024]{1,0:T(8,128)(2,1)S(1)} collective-permute-done((bf16[128,1024]{1,0:T(8,128)(2,1)}, bf16[128,1024]{1,0:T(8,128)(2,1)S(1)}, u32[]{:S(2)}, u32[]{:S(2)}) %collective-permute-start.1) | collective-permute-done | bytes 262176 | tf_op jit(solution)/shard_map/ppermute | solution.py:28
  10.2 0.8 copy.15
  10.9 1.6 %pad.8.refs_3_.readout_ref = bf16[112,1024]{1,0:T(8,128)(2,1)} pad(bf16[100,1024]{1,0:T(8,128)(2,1)} %param.17, bf16[]{:T(256)} %constant.43.clone.1), padding=0_12x0_0 | pad | bytes 434178 | tf_op jit(solution)/shard_map/jit(_pad)/pad | solution.py:443
  12.6 3.5 %project_queries.1.refs_2_.query_ref = bf16[128,1024]{1,0:T(8,128)(2,1)} custom-call(bf16[128,1024]{1,0:T(8,128)(2,1)} %bitcast.6, bf16[1024,1024]{1,0:T(8,128)(2,1)} %w_hbm.2), custom_call_target="tpu_custom_call" | custom-call | flops 268435456 | bytes 2097152 | tf_op jit(solution)/shard_map/project_queries/pallas_call | solution.py:68
  16.1 0.7 fusion.2.refs_0_
  16.9 0.7 copy-done.4
  17.5 0.7 copy-done.5
  18.2 6.6 %decoder_forward.1 = (bf16[128,1024]{1,0:T(8,128)(2,1)}, bf16[128,1024]{1,0:T(8,128)(2,1)}, f32[8,128,256]{2,1,0:T(8,128)}, bf16[128,1024]{1,0:T(8,128)(2,1)}, f...) custom-call(s32[128,1]{1,0:T(8,128)} %fusion.2.refs_0_, bf16[128,1024]{1,0:T(8,128)(2,1)} %bitcast.7, ...), custom_call_target="tpu_custom_call" | custom-call | flops 1073741824 | bytes 6291456 | tf_op jit(solution)/shard_map/decoder_forward/pallas_call | solution.py:152
  24.9 6.1 %all-to-all-start = ((bf16[8,352,128]{2,1,0:T(8,128)(2,1)}), bf16[8,352,128]{2,1,0:T(8,128)(2,1)S(1)}, u32[]{:S(2)}, u32[]{:S(2)}) async-start(bf16[8,352,128]{2,1,0:T(8,128)(2,1)} %get-tuple-element.20), calls=%async_computation | async-start | bytes 1441792 | tf_op jit(solution)/shard_map/all_to_all | solution.py:454
  31.0 0.6 pad.9.target_ref
  31.6 0.6 add_convert_fusion.index_ref
  32.2 18.2 %all-to-all-done.packed_ref = bf16[8,352,128]{2,1,0:T(8,128)(2,1)S(1)} async-done(((bf16[8,352,128]{2,1,0:T(8,128)(2,1)}), bf16[8,352,128]{2,1,0:T(8,128)(2,1)S(1)}, u32[]{:S(2)}, u32[]{:S(2)}) %all-to-all-start) | async-done | bytes 720928 | tf_op jit(solution)/shard_map/all_to_all | solution.py:454
  50.4 0.9 copy-done.1
  51.3 7.2 %decoder_backward.1 = bf16[4,576,256]{2,1,0:T(8,128)(2,1)} custom-call(s32[1]{0:T(128)} %bitcast.1.member_ref, bf16[8,352,128]{2,1,0:T(8,128)(2,1)} %copy-done.1, f32[112,128]{1,0:T(8,128)} %pad.9.target_ref, f32[1,256]{1,0:T(1,128)} %add_convert_fusion.index_ref, bf16[128,1024]{1,0:T(8,128)(2,1)} %project_queries.1.refs_2_.query_ref, ...), custom_call_target="tpu_custom_call" | custom-call | flops 536870912 | bytes 4194304 | tf_op jit(solution)/shard_map/decoder_backward/pallas_call | solution.py:307
  58.5 3.7 %all-to-all-start.1 = ((bf16[4,576,256]{2,1,0:T(8,128)(2,1)}), bf16[4,576,256]{2,1,0:T(8,128)(2,1)S(1)}, u32[]{:S(2)}, u32[]{:S(2)}) async-start(bf16[4,576,256]{2,1,0:T(8,128)(2,1)} %decoder_backward.1), calls=%async_computation.1 | async-start | bytes 2359296 | tf_op jit(solution)/shard_map/all_to_all | solution.py:461
  62.2 2.0 %collective-permute-start.4 = (bf16[128,1024]{1,0:T(8,128)(2,1)S(1)}, bf16[128,1024]{1,0:T(8,128)(2,1)S(1)}, u32[]{:S(2)}, u32[]{:S(2)}) collective-permute-start(bf16[128,1024]{1,0:T(8,128)(2,1)S(1)} %bitcast.9), channel_id=1, source_target_pairs={{0,2},{1,3},{2,0},{3,1},{4,6},{5,7},{6,4},{7,5},{8,10},{9,11},{10,... | collective-permute-start | bytes 786440 | tf_op jit(solution)/shard_map/ppermute | solution.py:28
  64.3 19.9 %collective-permute-done.4.refs_6_ = bf16[128,1024]{1,0:T(8,128)(2,1)S(1)} collective-permute-done((bf16[128,1024]{1,0:T(8,128)(2,1)S(1)}, bf16[128,1024]{1,0:T(8,128)(2,1)S(1)}, u32[]{:S(2)}, u32[]{:S(2)}) %collective-permute-start.4) | collective-permute-done | bytes 262176 | tf_op jit(solution)/shard_map/ppermute | solution.py:28
  84.7 4.5 %collective-permute-done.7.refs_10_ = bf16[128,1024]{1,0:T(8,128)(2,1)S(1)} collective-permute-done((bf16[128,1024]{1,0:T(8,128)(2,1)S(1)}, bf16[128,1024]{1,0:T(8,128)(2,1)S(1)}, u32[]{:S(2)}, u32[]{:S(2)}) %collective-permute-start.7) | collective-permute-done | bytes 262176 | tf_op jit(solution)/shard_map/ppermute | solution.py:28
  89.3 1.5 collective-permute-done.8.refs_11_
  90.8 0.6 copy-done.12
  91.8 5.2 %weight_gradients.1 = (bf16[8,576,256]{2,1,0:T(8,128)(2,1)}, f32[1,1]{1,0:T(1,128)}) custom-call(s32[1]{0:T(128)} %bitcast.shard_ref, bf16[4,576,256]{2,1,0:T(8,128)(2,1)} %copy-done, bf16[128,1024]{1,0:T(8,128)(2,1)} %bitcast.14, bf16[128,1024]{1,0:T(8,128)(2,1)} %copy-done.4, bf16[128,1024]{1,0:T(8,128)(2,1)} %copy-done.3, bf16[128,1024]{1,0:T(8,128)(2,1)} %copy-done.5, ...), custom_call_target="tpu_custom_call" | custom-call | flops 1073741824 | bytes 4194304 | tf_op jit(solution)/shard_map/weight_gradients/pallas_call | solution.py:381
  97.0 58.8 %all_to_all.15.blocks_ref = bf16[8,576,256]{2,1,0:T(8,128)(2,1)} all-to-all(bf16[8,576,256]{2,1,0:T(8,128)(2,1)} %get-tuple-element.28), channel_id=1, replica_groups=mesh['ens'=8,'space'=4] {'ens'}, dimensions={0} | all-to-all | bytes 4718592 | tf_op jit(solution)/shard_map/all_to_all | solution.py:463
  155.8 2.7 %sum_members.1 = (f32[100,1024]{1,0:T(8,128)}, f32[128,256]{1,0:T(8,128)}, f32[128,256]{1,0:T(8,128)}, f32[128,256]{1,0:T(8,128)}, f32[128,256]{1,0:T(8,128)}) custom-call(bf16[8,576,256]{2,1,0:T(8,128)(2,1)} %all_to_all.15.blocks_ref), custom_call_target="tpu_custom_call" | custom-call | tf_op jit(solution)/shard_map/sum_members/pallas_call | solution.py:420
  (40 shorter events, 1.1 us)
Async XLA Ops:
  0.6 9.6 %collective-permute-start.1 = (bf16[128,1024]{1,0:T(8,128)(2,1)}, bf16[128,1024]{1,0:T(8,128)(2,1)S(1)}, u32[]{:S(2)}, u32[]{:S(2)}) collective-permute-start(bf16[128,1024]{1,0:T(8,128)(2,1)} %bitcast.11), channel_id=1, source_target_pairs={{0,2},{1,3},{2,0},{3,1},{4,6},{5,7},{6,4},{7,5},{8,10},{9,11},{10,... | collective-permute-start | bytes 786440 | tf_op jit(solution)/shard_map/ppermute | solution.py:28
  3.7 13.2 %collective-permute-start = (bf16[128,1024]{1,0:T(8,128)(2,1)}, bf16[128,1024]{1,0:T(8,128)(2,1)S(1)}, u32[]{:S(2)}, u32[]{:S(2)}) collective-permute-start(bf16[128,1024]{1,0:T(8,128)(2,1)} %bitcast.12), channel_id=1, source_target_pairs={{0,1},{1,0},{2,3},{3,2},{4,5},{5,4},{6,7},{7,6},{8,9},{9,8},{10,11... | collective-permute-start | bytes 786440 | tf_op jit(solution)/shard_map/ppermute | solution.py:28
  10.2 6.7 %copy-start.3 = (bf16[128,1024]{1,0:T(8,128)(2,1)}, bf16[128,1024]{1,0:T(8,128)(2,1)S(1)}, u32[]{:S(2)}) copy-start(bf16[128,1024]{1,0:T(8,128)(2,1)S(1)} %collective-permute-done.1.refs_6_.refs_2_) | copy-start | bytes 786436
  10.2 6.7 %collective-permute-start.2 = (bf16[128,1024]{1,0:T(8,128)(2,1)S(1)}, bf16[128,1024]{1,0:T(8,128)(2,1)S(1)}, u32[]{:S(2)}, u32[]{:S(2)}) collective-permute-start(bf16[128,1024]{1,0:T(8,128)(2,1)S(1)} %collective-permute-done.1.refs_6_.refs_2_), channel_id=1, source_target_pairs={{0,1},{1,0},{2,3},{3,2},{4,5},{5,4},{6,7},{7,6},{8,9},{9,8},{10,11... | collective-permute-start | bytes 786440 | tf_op jit(solution)/shard_map/ppermute | solution.py:28
  16.8 14.2 %copy-start.13 = (f32[100,128]{1,0:T(8,128)S(1)}, f32[100,128]{1,0:T(8,128)}, u32[]{:S(2)}) copy-start(f32[100,128]{1,0:T(8,128)} %param.12) | copy-start | bytes 153604
  16.8 14.8 %copy-start.14 = (s32[1,128]{1,0:T(1,128)S(1)}, s32[1,128]{1,0:T(1,128)}, u32[]{:S(2)}) copy-start(s32[1,128]{1,0:T(1,128)} %param.11) | copy-start | bytes 1540
  17.5 0.7 copy-start.5
  24.9 25.5 %all-to-all-start = ((bf16[8,352,128]{2,1,0:T(8,128)(2,1)}), bf16[8,352,128]{2,1,0:T(8,128)(2,1)S(1)}, u32[]{:S(2)}, u32[]{:S(2)}) async-start(bf16[8,352,128]{2,1,0:T(8,128)(2,1)} %get-tuple-element.20), calls=%async_computation | async-start | bytes 1441792 | tf_op jit(solution)/shard_map/all_to_all | solution.py:454
  50.4 0.9 copy-start.1
  58.5 3.7 %copy-start.2 = (bf16[1,128,1024]{2,1,0:T(8,128)(2,1)S(1)}, bf16[1,128,1024]{2,1,0:T(8,128)(2,1)}, u32[]{:S(2)}) copy-start(bf16[1,128,1024]{2,1,0:T(8,128)(2,1)} %param.9) | copy-start | bytes 786436
  58.5 5.7 %copy-start.6 = (bf16[128,1024]{1,0:T(8,128)(2,1)S(1)}, bf16[128,1024]{1,0:T(8,128)(2,1)}, u32[]{:S(2)}) copy-start(bf16[128,1024]{1,0:T(8,128)(2,1)} %get-tuple-element.26.refs_8_) | copy-start | bytes 786436
  58.5 32.3 %all-to-all-start.1 = ((bf16[4,576,256]{2,1,0:T(8,128)(2,1)}), bf16[4,576,256]{2,1,0:T(8,128)(2,1)S(1)}, u32[]{:S(2)}, u32[]{:S(2)}) async-start(bf16[4,576,256]{2,1,0:T(8,128)(2,1)} %decoder_backward.1), calls=%async_computation.1 | async-start | bytes 2359296 | tf_op jit(solution)/shard_map/all_to_all | solution.py:461
  62.2 22.0 %collective-permute-start.4 = (bf16[128,1024]{1,0:T(8,128)(2,1)S(1)}, bf16[128,1024]{1,0:T(8,128)(2,1)S(1)}, u32[]{:S(2)}, u32[]{:S(2)}) collective-permute-start(bf16[128,1024]{1,0:T(8,128)(2,1)S(1)} %bitcast.9), channel_id=1, source_target_pairs={{0,2},{1,3},{2,0},{3,1},{4,6},{5,7},{6,4},{7,5},{8,10},{9,11},{10,... | collective-permute-start | bytes 786440 | tf_op jit(solution)/shard_map/ppermute | solution.py:28
  64.2 25.0 %collective-permute-start.7 = (bf16[128,1024]{1,0:T(8,128)(2,1)S(1)}, bf16[128,1024]{1,0:T(8,128)(2,1)S(1)}, u32[]{:S(2)}, u32[]{:S(2)}) collective-permute-start(bf16[128,1024]{1,0:T(8,128)(2,1)S(1)} %copy-done.6), channel_id=1, source_target_pairs={{0,2},{1,3},{2,0},{3,1},{4,6},{5,7},{6,4},{7,5},{8,10},{9,11},{10,... | collective-permute-start | bytes 786440 | tf_op jit(solution)/shard_map/ppermute | solution.py:28
  64.3 24.9 %collective-permute-start.3 = (bf16[128,1024]{1,0:T(8,128)(2,1)S(1)}, bf16[128,1024]{1,0:T(8,128)(2,1)S(1)}, u32[]{:S(2)}, u32[]{:S(2)}) collective-permute-start(bf16[128,1024]{1,0:T(8,128)(2,1)S(1)} %bitcast.10), channel_id=1, source_target_pairs={{0,1},{1,0},{2,3},{3,2},{4,5},{5,4},{6,7},{7,6},{8,9},{9,8},{10,11... | collective-permute-start | bytes 786440 | tf_op jit(solution)/shard_map/ppermute | solution.py:28
  84.1 6.6 %copy-start.7 = (bf16[128,1024]{1,0:T(8,128)(2,1)}, bf16[128,1024]{1,0:T(8,128)(2,1)S(1)}, u32[]{:S(2)}) copy-start(bf16[128,1024]{1,0:T(8,128)(2,1)S(1)} %collective-permute-done.4.refs_6_) | copy-start | bytes 786436
  84.1 5.1 %collective-permute-start.5 = (bf16[128,1024]{1,0:T(8,128)(2,1)S(1)}, bf16[128,1024]{1,0:T(8,128)(2,1)S(1)}, u32[]{:S(2)}, u32[]{:S(2)}) collective-permute-start(bf16[128,1024]{1,0:T(8,128)(2,1)S(1)} %collective-permute-done.4.refs_6_), channel_id=1, source_target_pairs={{0,1},{1,0},{2,3},{3,2},{4,5},{5,4},{6,7},{7,6},{8,9},{9,8},{10,11... | collective-permute-start | bytes 786440 | tf_op jit(solution)/shard_map/ppermute | solution.py:28
  84.2 5.1 %collective-permute-start.6 = (bf16[128,1024]{1,0:T(8,128)(2,1)S(1)}, bf16[128,1024]{1,0:T(8,128)(2,1)S(1)}, u32[]{:S(2)}, u32[]{:S(2)}) collective-permute-start(bf16[128,1024]{1,0:T(8,128)(2,1)S(1)} %copy-done.6), channel_id=1, source_target_pairs={{0,1},{1,0},{2,3},{3,2},{4,5},{5,4},{6,7},{7,6},{8,9},{9,8},{10,11... | collective-permute-start | bytes 786440 | tf_op jit(solution)/shard_map/ppermute | solution.py:28
  89.2 1.6 copy-start.8
  89.2 1.5 collective-permute-start.8
  89.2 1.6 copy-start.9
  89.2 1.5 copy-start.10
  89.2 1.5 copy-start.11
  90.7 1.1 copy-start
  (2 other events, 1.4 us)

commit v3 on v2

--- a/solution.py
+++ b/solution.py
@@ -6,6 +6,7 @@
 from jax.experimental import pallas as pl
 from jax.experimental.pallas import tpu as pltpu
 from jax.sharding import PartitionSpec as P
+
 
 HEADS = 16
 EPS = 1e-06
@@ -175,6 +176,7 @@
 
 def backward_kernel(
     shards,
+    blocks,
     channels_used,
     member_ref,
     packed_ref,
@@ -200,7 +202,7 @@
     members = packed_ref.shape[0]
     points, features = normed_ref.shape
     channels = readout_ref.shape[0]
-    width, depth = features // shards, features // members
+    width, depth = features // blocks, features // members
     weight = (channels_used * points * shards) ** (-0.5)
     pair_weight = 1.0 / (members * (members - 1))
     chunk = 16
@@ -249,24 +251,25 @@
             total = total + dot32(
                 slope_ref[m][:, p * part : (p + 1) * part], tail[:, p * depth : (p + 1) * depth]
             )
-    rows = small_ref.shape[0] - MISC
-    for p in range(channels // rows):
+    rows = channels * depth // width
+    for p in range(width // depth):
         small_ref[:rows, p * depth : (p + 1) * depth] = total[p * rows : (p + 1) * rows]
     first = loss.astype(BF16).astype(F32)
     second = (loss - first).astype(BF16).astype(F32)
     for i, value in enumerate((first, second, loss - first - second)):
         small_ref[rows + i : rows + i + 1] = jnp.broadcast_to(value, (1, width))
-    small_ref[rows + 3 : rows + MISC] = jnp.zeros((MISC - 3, width), F32)
+    spare = small_ref.shape[0] - rows - 3
+    small_ref[rows + 3 :] = jnp.zeros((spare, width), F32)
     small_ref[rows + 3 : rows + 3 + index_ref.shape[0]] = index_ref[...]
     small = small_ref[...].astype(BF16)
-    for s in range(shards):
-        out_ref[s, 4 * points :] = small
+    for b in range(blocks):
+        out_ref[b, 4 * points :] = small
 
     def put(kind, column, value):
         step = min(width, value.shape[1])
         for c in range(0, value.shape[1], step):
-            shard, lane = divmod(column + c, width)
-            out_ref[shard, kind * points : (kind + 1) * points, lane : lane + step] = value[
+            block, lane = divmod(column + c, width)
+            out_ref[block, kind * points : (kind + 1) * points, lane : lane + step] = value[
                 :, c : c + step
             ]
 
@@ -296,26 +299,28 @@
         put(1, pair * LANES, joined(dot32(d_scores, query_ref[:, at], (0, 0))).astype(BF16))
 
 
-def backward(member, packed, target, index, saved, readout, w_mix, shards, channels_used):
+def small_rows(channels, depth, width):
+    rows = channels * depth // width + MISC
+    return rows + -rows % 16
+
+
+def backward(member, packed, target, index, saved, readout, w_mix, shards, blocks, channels_used):
     members = packed.shape[0]
     features = w_mix.shape[0]
     points = saved[0].shape[0]
     channels = readout.shape[0]
-    width, depth = features // shards, features // members
-    small = channels * depth // width + MISC
-    small = small + -small % 16
+    width, depth = features // blocks, features // members
+    small = small_rows(channels, depth, width)
     return pl.pallas_call(
-        functools.partial(backward_kernel, shards, channels_used),
-        out_shape=jax.ShapeDtypeStruct((shards, 4 * points + small, width), BF16),
+        functools.partial(backward_kernel, shards, blocks, channels_used),
+        out_shape=jax.ShapeDtypeStruct((blocks, 4 * points + small, width), BF16),
         in_specs=[SMEM] + [VMEM] * 10 + [ANY],
         out_specs=VMEM,
         scratch_shapes=[
             pltpu.VMEM((features, features), BF16),
             pltpu.VMEM((members, channels, points), BF16),
             pltpu.VMEM((points, features), BF16),
-            pltpu.VMEM((channels * depth // width + MISC, width), F32)
-            if small == channels * depth // width + MISC
-            else pltpu.VMEM((small, width), F32),
+            pltpu.VMEM((small, width), F32),
             pltpu.SemaphoreType.DMA,
         ],
         cost_estimate=pl.CostEstimate(
@@ -327,40 +332,59 @@
     )(member, packed, target, index, *saved, readout, w_mix)
 
 
-def gradient_kernel(shards, members, nodes, channels, shard_ref, blocks_ref, *refs):
-    latent_refs, grid_refs, attended_refs = (refs[i * shards : (i + 1) * shards] for i in range(3))
+def gradient_kernel(shards, pair, members, nodes, channels, place_ref, blocks_ref, *refs):
+    latent_refs, early_refs, late_refs = (refs[i * shards : (i + 1) * shards] for i in range(3))
     out_ref, loss_ref = refs[3 * shards :]
-    points, features = grid_refs[0].shape
-    width, depth = features // shards, features // members
-    shard = shard_ref[0]
+    width = blocks_ref.shape[2]
+    features = late_refs[0].shape[1]
+    points = late_refs[0].shape[0] // pair
+    depth = features // members
+    lanes = pair * depth
+    shard, half = place_ref[0], place_ref[1]
     rows = channels * depth // width
     start = 4 * points
-    small = jnp.zeros((blocks_ref.shape[1] - start, width), F32)
-    for s in range(shards):
-        small = small + blocks_ref[s, start:].astype(F32)
-    loss_ref[...] = jnp.sum(small[rows : rows + 3, :1], axis=0, keepdims=True)
-    small = small.astype(BF16)
-    for m in range(members):
-        out_ref[m, 4 * depth :] = small
-
-    def slots(kind):
+    loss = jnp.zeros((1, 1), F32)
+    for t in range(pair):
+        total = jnp.zeros((blocks_ref.shape[1] - start, width), F32)
+        for s in range(shards):
+            total = total + blocks_ref[s * pair + t, start:].astype(F32)
+        if t == 0:
+            loss = jnp.sum(total[rows : rows + 3, :1], axis=0, keepdims=True)
+        total = total.astype(BF16)
+        for z in range(members // pair):
+            for p in range(width // depth):
+                out_ref[z, 4 * width + p * rows : 4 * width + (p + 1) * rows, t * depth : (t + 1) * depth] = (
+                    total[:rows, p * depth : (p + 1) * depth]
+                )
+    loss_ref[...] = loss
+
+    def slots(kind, t):
         at = slice(kind * points, (kind + 1) * points)
-        return jnp.concatenate([blocks_ref[shard ^ k, at] for k in range(shards)], axis=0)
-
-    def put(kind, lefts, right):
-        left = jnp.concatenate([ref[...] for ref in lefts], axis=0)
-        total = dot32(left, right, (0, 0)).astype(BF16)
-        for m in range(members):
-            out_ref[m, kind * depth : (kind + 1) * depth] = total[m * depth : (m + 1) * depth]
-
-    put(3, attended_refs, slots(3))
+        return [blocks_ref[(shard ^ k) * pair + (half ^ t), at] for k in range(shards)]
+
+    def put(kind, total):
+        total = total.astype(BF16)
+        at = slice(kind * width, kind * width + total.shape[0])
+        for z in range(members // pair):
+            out_ref[z, at] = total[:, z * lanes : (z + 1) * lanes]
+
+    def rows_of(ref_list, part):
+        at = slice(part * points, (part + 1) * points)
+        return [ref[at] for ref in ref_list]
+
+    def product(kind, parts):
+        left = jnp.concatenate([v for t in range(pair) for v in slots(kind, t)], axis=0)
+        right = jnp.concatenate([v for part in parts for v in part], axis=0)
+        put(kind, dot32(left, right, (0, 0)))
+
+    product(3, [rows_of(late_refs, t) for t in range(pair)])
     chosen = []
     for k in range(shards):
-        index = blocks_ref[shard ^ k, start + rows : start + rows + MISC].astype(jnp.int32)
+        index = blocks_ref[(shard ^ k) * pair, start + rows : start + rows + MISC].astype(jnp.int32)
+        lines = max(points // width, 1)
         if width >= 2 * points:
             owner, offset = index[3:4, :points], index[3:4, points : 2 * points]
         else:
-            lines = points // width
             owner, offset = (
                 jnp.concatenate([index[3 + b + i : 4 + b + i] for i in range(lines)], axis=1)
                 for b in (0, lines)
@@ -369,75 +393,137 @@
         node = lax.broadcasted_iota(jnp.int32, (nodes * shards, points), 0)
         chosen.append(jnp.where(node == position, 1.0, 0.0).astype(BF16))
     chosen = jnp.concatenate(chosen, axis=1)
-    put(1, latent_refs, dot32(chosen, slots(1)).astype(BF16))
-    put(2, latent_refs, dot32(chosen, slots(2)).astype(BF16))
-    put(0, grid_refs, slots(0))
-
-
-def gradients(shard, blocks, latents, grids, attendeds, members, channels):
-    shards, rows, width = blocks.shape
-    points, features = grids[0].shape
+    sums = []
+    for t in range(pair):
+        both = [jnp.concatenate(slots(kind, t), axis=0) for kind in (1, 2)]
+        sums.append(dot32(chosen, jnp.concatenate(both, axis=1)).astype(BF16))
+    others = [[ref[...] for ref in latent_refs]]
+    if pair > 1:
+        others.append([ref[points : points + nodes] for ref in early_refs])
+    put(
+        1,
+        dot32(
+            jnp.concatenate(sums, axis=0),
+            jnp.concatenate([v for part in others for v in part], axis=0),
+            (0, 0),
+        ),
+    )
+    grids = [rows_of(early_refs, 0)]
+    if pair > 1:
+        grids.append([ref[points + nodes :] for ref in early_refs])
+    product(0, grids)
+
+
+def gradients(place, blocks, latents, early, late, members, pair, channels):
+    count, _, width = blocks.shape
+    shards = count // pair
+    features = late[0].shape[1]
+    points = late[0].shape[0] // pair
     depth = features // members
+    rows = 4 * width + channels
     return pl.pallas_call(
-        functools.partial(gradient_kernel, shards, members, latents[0].shape[0], channels),
+        functools.partial(
+            gradient_kernel, shards, pair, members, latents[0].shape[0], channels
+        ),
         out_shape=(
-            jax.ShapeDtypeStruct((members, 4 * depth + rows - 4 * points, width), BF16),
+            jax.ShapeDtypeStruct((members // pair, rows, pair * depth), BF16),
             jax.ShapeDtypeStruct((1, 1), F32),
         ),
         in_specs=[SMEM] + [VMEM] * (1 + 3 * shards),
         out_specs=(VMEM, VMEM),
         cost_estimate=pl.CostEstimate(
-            flops=8 * points * shards * features * width,
-            bytes_accessed=8 * points * shards * features,
+            flops=8 * points * count * features * width,
+            bytes_accessed=8 * points * count * features,
             transcendentals=0,
         ),
         name="weight_gradients",
-    )(shard, blocks, *latents, *grids, *attendeds)
-
-
-def sum_kernel(channels, blocks_ref, out_ref, *grad_refs):
-    members, _, width = blocks_ref.shape
-    depth = grad_refs[0].shape[0]
-    for i, ref in enumerate(grad_refs):
-        at = slice(i * depth, (i + 1) * depth)
+    )(place, blocks, *latents, *early, *late)
+
+
+def sum_kernel(pair, half_ref, blocks_ref, out_ref, *refs):
+    count, _, lanes = blocks_ref.shape
+    depth = lanes // pair
+    used = out_ref.shape[0]
+    width = refs[0].shape[1]
+    for z in range(count):
+        out_ref[:, z * lanes : (z + 1) * lanes] = blocks_ref[z, 4 * width : 4 * width + used].astype(F32)
+    for i in range(4):
+        at = slice(i * width, (i + 1) * width)
         total = blocks_ref[0, at].astype(F32)
-        for m in range(1, members):
-            total = total + blocks_ref[m, at].astype(F32)
-        ref[...] = total
-    rows = channels * depth // width
-    for m in range(members):
-        small = blocks_ref[m, 4 * depth :].astype(F32)
-        for p in range(width // depth):
-            last = min((p + 1) * rows, out_ref.shape[0])
-            out_ref[p * rows : last, m * depth : (m + 1) * depth] = small[
-                : last - p * rows, p * depth : (p + 1) * depth
-            ]
-
-
-def sum_members(blocks, channels, channels_used, depth):
-    members, _, width = blocks.shape
+        for z in range(1, count):
+            total = total + blocks_ref[z, at].astype(F32)
+        if pair == 1:
+            refs[i][...] = total.T
+        else:
+            first, second = total[:, :depth], total[:, depth:]
+            own = jnp.where(half_ref[0] == 0, first, second)
+            other = jnp.where(half_ref[0] == 0, second, first)
+            refs[i][...] = own.T
+            refs[4][i * depth : (i + 1) * depth] = other.T.astype(BF16)
+
+
+def sum_groups(half, blocks, pair, channels_used):
+    count, rows, lanes = blocks.shape
+    depth = lanes // pair
+    width = (rows - (channels_used + -channels_used % 16)) // 4
     shape = jax.ShapeDtypeStruct
+    outs = (shape((channels_used, lanes * count), F32),) + (shape((depth, width), F32),) * 4
+    if pair > 1:
+        outs = outs + (shape((4 * depth, width), BF16),)
     return pl.pallas_call(
-        functools.partial(sum_kernel, channels),
-        out_shape=(shape((channels_used, depth * members), F32),) + (shape((depth, width), F32),) * 4,
-        in_specs=[VMEM],
-        out_specs=(VMEM,) * 5,
-        name="sum_members",
-    )(blocks)
+        functools.partial(sum_kernel, pair),
+        out_shape=outs,
+        in_specs=[SMEM, VMEM],
+        out_specs=(VMEM,) * len(outs),
+        name="sum_groups",
+    )(half, blocks)
+
+
+def join_kernel(half_ref, other_ref, *refs):
+    keep_refs, out_refs = refs[:4], refs[4:]
+    depth, width = keep_refs[0].shape
+    first = half_ref[0] == 0
+    for i in range(4):
+        own = keep_refs[i][...]
+        other = other_ref[i * depth : (i + 1) * depth].astype(F32)
+        out_refs[i][:, :width] = jnp.where(first, own, other)
+        out_refs[i][:, width:] = jnp.where(first, other, own)
+
+
+def join_columns(half, other, keeps):
+    depth, width = keeps[0].shape
+    return pl.pallas_call(
+        join_kernel,
+        out_shape=(jax.ShapeDtypeStruct((depth, 2 * width), F32),) * 4,
+        in_specs=[SMEM] + [VMEM] * 5,
+        out_specs=(VMEM,) * 4,
+        name="join_columns",
+    )(half, other, *keeps)
 
 
 def body(
     grid_hidden, latent, tile_neighbor_index, target, w_query, w_key, w_value, w_mix, readout_weight
 ):
     nodes, features = latent.shape[1:]
-    points = grid_hidden.shape[1]
     channels_used = target.shape[0]
     shards, members = lax.axis_size("space"), lax.axis_size("ens")
     shard, member = lax.axis_index("space"), lax.axis_index("ens")
-    width, depth = features // shards, features // members
-
-    latents = gather_slots(latent[0], "space")
-    grid_rows = grid_hidden[0]
+    pair = 2 if members % 2 == 0 and shards <= 8 else 1
+    half = member % pair
+    count = shards * pair
+    width = features // count
+    groups = [
+        [(g + y) * shards + s for s in range(shards) for y in range(pair)]
+        for g in range(0, members, pair)
+    ]
+    lines = [list(range(y, members, pair)) for y in range(pair)]
+
+    own_latent, grid_rows = latent[0], grid_hidden[0]
+    latents = gather_slots(own_latent, "space")
+    early = grid_rows
+    if pair > 1:
+        partner = swap(jnp.concatenate([own_latent, grid_rows]), "ens", 1)
+        early = jnp.concatenate([grid_rows, partner])
     queries = project_queries(grid_rows, w_query)
     spare = ((0, -channels_used % 16), (0, 0))
     readout = jnp.pad(readout_weight, spare)
@@ -452,16 +538,34 @@
     )
     keyset, valueset, soft, attended, normed, inverse = saved
     packed = lax.all_to_all(packed, "ens", split_axis=0, concat_axis=0, tiled=True)
-    grids = gather_slots(grid_rows, "space")
-    attendeds = gather_slots(attended, "space")
+    late = attended
+    if pair > 1:
+        partner = swap(attended, "ens", 1)
+        late = jnp.concatenate([attended, partner])
+    early = gather_slots(early, "space")
+    late = gather_slots(late, "space")
+    packed, early, late = lax.optimization_barrier((packed, early, late))
     saved = (queries, keyset, valueset, soft, normed, inverse)
     blocks = backward(
-        member[None], packed, truth, tags, saved, readout, w_mix, shards, channels_used
-    )
-    blocks = lax.all_to_all(blocks, "space", split_axis=0, concat_axis=0, tiled=True)
-    blocks, loss = gradients(shard[None], blocks, latents, grids, attendeds, members, channels)
-    blocks = lax.all_to_all(blocks, "ens", split_axis=0, concat_axis=0, tiled=True)
-    grad_out, *grads = sum_members(blocks, channels, channels_used, depth)
+        member[None], packed, truth, tags, saved, readout, w_mix, shards, count, channels_used
+    )
+    blocks = lax.all_to_all(
+        blocks,
+        ("ens", "space"),
+        split_axis=0,
+        concat_axis=0,
+        axis_index_groups=groups,
+        tiled=True,
+    )
+    place = jnp.stack([shard, half])
+    blocks, loss = gradients(place, blocks, latents, early, late, members, pair, channels)
+    blocks = lax.all_to_all(
+        blocks, "ens", split_axis=0, concat_axis=0, axis_index_groups=lines, tiled=True
+    )
+    grad_out, *grads = sum_groups(half[None], blocks, pair, channels_used)
+    if pair > 1:
+        *keeps, other = grads
+        grads = join_columns(half[None], swap(other, "ens", 1), keeps)
     return (loss.reshape(()), grad_out, *grads)
 
 
@@ -485,4 +589,5 @@
         P("ens", "space"),
         P("ens", "space"),
     )
+
     return jax.shard_map(body, mesh=mesh, in_specs=in_specs, out_specs=out_specs, check_vma=False)

time: 159 us -> 138 us (0.87)
  blocking collectives: 58.8 us -> 35.5 us
  waiting for transfers between devices: 50.6 us -> 45.3 us
  starting transfers between devices: 15.4 us -> 18.6 us
  other arithmetic: 1.28 us -> 3.97 us
  Pallas kernels: 25.3 us -> 27.5 us
    all_to_all x1, blocking collectives: 58.8 us -> 35.5 us  [body(): lax.all_to_all(blocks, 'ens', split_axis=0, concat_axis=0, axis_index_gro...]
    all_to_all x1, waiting for transfers between devices: 0.01 us -> 16.7 us  [body(): lax.all_to_all(blocks, ('ens', 'space'), split_axis=0, concat_axis=0, axi...]
    all_to_all x1, waiting for transfers between devices: 18.2 us -> 3.59 us  [body(): lax.all_to_all(packed, 'ens', split_axis=0, concat_axis=0, tiled=True)]
    ppermute x9 -> x12, waiting for transfers between devices: 32.4 us -> 25.1 us  [swap(): return lax.ppermute(value, axis, [(i, i ^ bits) for i in range(size)])]
    ppermute x9 -> x12, starting transfers between devices: 5.64 us -> 10.1 us  [swap(): return lax.ppermute(value, axis, [(i, i ^ bits) for i in range(size)])]
    pallas_call x3 -> x4, Pallas kernels: 15.1 us -> 17.3 us  [the longest x1 7.24 us: backward(): pl.pallas_call(functools.partial(backward_kernel, shards, blocks, channel...]
    concatenate x0 -> x2, other arithmetic: none -> 2.11 us  [the longest x1 1.11 us: body(): partner = swap(jnp.concatenate([own_latent, grid_rows]), 'ens', 1)]
    unnamed x30 -> x29, local copies, waits for them, and re-layouts: 3.33 us -> 4.04 us
  transfers between devices with their start and end apart: 11 -> 14, of which waited for: 5 -> 7; matrix products, arithmetic and copies ran while one was open for 3% -> 4% of each run, Pallas kernels for 2% -> 7%
where the time goes in v3:
time: 138 us
  waiting for transfers between devices  45.3 us (33%)
  blocking collectives  35.5 us (26%)
  Pallas kernels  27.5 us (20%)
  starting transfers between devices  18.6 us (13%)
  local copies, waits for them, and re-layouts  6.25 us (5%)
  other arithmetic  3.97 us (3%)
    all_to_all x1, blocking collectives, body(): lax.all_to_all(blocks, 'ens', split_axis=0, concat_axis=0, axis_index_gro...  35.5 us
    ppermute x12, waiting for transfers between devices, swap(): return lax.ppermute(value, axis, [(i, i ^ bits) for i in range(size)])  25.1 us
    all_to_all x1, waiting for transfers between devices, body(): lax.all_to_all(blocks, ('ens', 'space'), split_axis=0, concat_axis=0, axi...  16.7 us
    ppermute x12, starting transfers between devices, swap(): return lax.ppermute(value, axis, [(i, i ^ bits) for i in range(size)])  10.1 us
    pallas_call x1, Pallas kernels, backward(): pl.pallas_call(functools.partial(backward_kernel, shards, blocks, channel...  7.24 us
    pallas_call x1, Pallas kernels, forward(): pl.pallas_call(functools.partial(forward_kernel, len(latents), members),...  6.67 us
    pallas_call x1, Pallas kernels, gradients(): pl.pallas_call(functools.partial(gradient_kernel, shards, pair, members,...  5.92 us
    all_to_all x1, starting transfers between devices, body(): lax.all_to_all(packed, 'ens', split_axis=0, concat_axis=0, tiled=True)  4.88 us
  transfers between devices with their start and end apart: 14, of which 7 were waited for; matrix products, arithmetic and copies ran while one was open for 4% of the time, Pallas kernels for 7%

profile of v3, /device:TPU:0, one launch (start us, length us, event | category | flops | bytes accessed | tf_op | source)
XLA Modules:
  0.0 137.9 jit_solution(5006839238920934176)
XLA Ops:
  0.6 1.1 pad_maximum_fusion.1
  1.8 3.1 %collective-permute-start.3 = (bf16[256,1024]{1,0:T(8,128)(2,1)S(1)}, bf16[256,1024]{1,0:T(8,128)(2,1)S(1)}, u32[]{:S(2)}, u32[]{:S(2)}) collective-permute-start(bf16[256,1024]{1,0:T(8,128)(2,1)S(1)} %pad_maximum_fusion.1), channel_id=1, source_target_pairs={{0,4},{4,0},{8,12},{12,8},{16,20},{20,16},{24,28},{28,24},{1,5},{5... | collective-permute-start | bytes 1572872 | tf_op jit(solution)/shard_map/ppermute | solution.py:29
  4.8 1.5 %collective-permute-start.1 = (bf16[128,1024]{1,0:T(8,128)(2,1)}, bf16[128,1024]{1,0:T(8,128)(2,1)S(1)}, u32[]{:S(2)}, u32[]{:S(2)}) collective-permute-start(bf16[128,1024]{1,0:T(8,128)(2,1)} %bitcast.29), channel_id=1, source_target_pairs={{0,2},{1,3},{2,0},{3,1},{4,6},{5,7},{6,4},{7,5},{8,10},{9,11},{10,... | collective-permute-start | bytes 786440 | tf_op jit(solution)/shard_map/ppermute | solution.py:29
  7.1 5.7 %collective-permute-done.1.refs_6_.refs_2_ = bf16[128,1024]{1,0:T(8,128)(2,1)S(1)} collective-permute-done((bf16[128,1024]{1,0:T(8,128)(2,1)}, bf16[128,1024]{1,0:T(8,128)(2,1)S(1)}, u32[]{:S(2)}, u32[]{:S(2)}) %collective-permute-start.1) | collective-permute-done | bytes 262176 | tf_op jit(solution)/shard_map/ppermute | solution.py:29
  12.8 3.9 %collective-permute-done.3 = bf16[256,1024]{1,0:T(8,128)(2,1)S(1)} collective-permute-done((bf16[256,1024]{1,0:T(8,128)(2,1)S(1)}, bf16[256,1024]{1,0:T(8,128)(2,1)S(1)}, u32[]{:S(2)}, u32[]{:S(2)}) %collective-permute-start.3) | collective-permute-done | bytes 524320 | tf_op jit(solution)/shard_map/ppermute | solution.py:29
  16.7 1.0 pad_maximum_fusion.refs_4_
  17.7 1.8 %collective-permute-start.5 = (bf16[384,1024]{1,0:T(8,128)(2,1)S(1)}, bf16[384,1024]{1,0:T(8,128)(2,1)}, u32[]{:S(2)}, u32[]{:S(2)}) collective-permute-start(bf16[384,1024]{1,0:T(8,128)(2,1)S(1)} %pad_maximum_fusion.refs_4_), channel_id=1, source_target_pairs={{0,2},{1,3},{2,0},{3,1},{4,6},{5,7},{6,4},{7,5},{8,10},{9,11},{10,... | collective-permute-start | bytes 2359304 | tf_op jit(solution)/shard_map/ppermute | solution.py:29
  21.0 3.5 %project_queries.1.refs_2_.query_ref = bf16[128,1024]{1,0:T(8,128)(2,1)} custom-call(bf16[128,1024]{1,0:T(8,128)(2,1)} %bitcast.26, bf16[1024,1024]{1,0:T(8,128)(2,1)} %w_hbm.2), custom_call_target="tpu_custom_call" | custom-call | flops 268435456 | bytes 2097152 | tf_op jit(solution)/shard_map/project_queries/pallas_call | solution.py:69
  25.9 6.7 %decoder_forward.1 = (bf16[128,1024]{1,0:T(8,128)(2,1)}, bf16[128,1024]{1,0:T(8,128)(2,1)}, f32[8,128,256]{2,1,0:T(8,128)}, bf16[128,1024]{1,0:T(8,128)(2,1)}, f...) custom-call(s32[128,1]{1,0:T(8,128)} %fusion.2.refs_0_, bf16[128,1024]{1,0:T(8,128)(2,1)} %bitcast.27, ...), custom_call_target="tpu_custom_call" | custom-call | flops 1073741824 | bytes 6291456 | tf_op jit(solution)/shard_map/decoder_forward/pallas_call | solution.py:153
  32.7 1.6 %collective-permute-start.7 = (bf16[128,1024]{1,0:T(8,128)(2,1)}, bf16[128,1024]{1,0:T(8,128)(2,1)S(1)}, u32[]{:S(2)}, u32[]{:S(2)}) collective-permute-start(bf16[128,1024]{1,0:T(8,128)(2,1)} %get-tuple-element.35), channel_id=1, source_target_pairs={{0,4},{4,0},{8,12},{12,8},{16,20},{20,16},{24,28},{28,24},{1,5},{5... | collective-permute-start | bytes 786440 | tf_op jit(solution)/shard_map/ppermute | solution.py:29
  34.2 4.9 %all-to-all-start = ((bf16[8,352,128]{2,1,0:T(8,128)(2,1)}), bf16[8,352,128]{2,1,0:T(8,128)(2,1)S(1)}, u32[]{:S(2)}, u32[]{:S(2)}) async-start(bf16[8,352,128]{2,1,0:T(8,128)(2,1)} %get-tuple-element.34), calls=%async_computation | async-start | bytes 1441792 | tf_op jit(solution)/shard_map/all_to_all | solution.py:540
  39.2 1.7 %collective-permute-done.7 = bf16[128,1024]{1,0:T(8,128)(2,1)S(1)} collective-permute-done((bf16[128,1024]{1,0:T(8,128)(2,1)}, bf16[128,1024]{1,0:T(8,128)(2,1)S(1)}, u32[]{:S(2)}, u32[]{:S(2)}) %collective-permute-start.7) | collective-permute-done | bytes 262176 | tf_op jit(solution)/shard_map/ppermute | solution.py:29
  42.1 9.6 %collective-permute-done.9.refs_10_ = bf16[256,1024]{1,0:T(8,128)(2,1)S(1)} collective-permute-done((bf16[256,1024]{1,0:T(8,128)(2,1)S(1)}, bf16[256,1024]{1,0:T(8,128)(2,1)S(1)}, u32[]{:S(2)}, u32[]{:S(2)}) %collective-permute-start.9) | collective-permute-done | bytes 524320 | tf_op jit(solution)/shard_map/ppermute | solution.py:29
  52.9 3.6 %all-to-all-done.packed_ref = bf16[8,352,128]{2,1,0:T(8,128)(2,1)S(1)} async-done(((bf16[8,352,128]{2,1,0:T(8,128)(2,1)}), bf16[8,352,128]{2,1,0:T(8,128)(2,1)S(1)}, u32[]{:S(2)}, u32[]{:S(2)}) %all-to-all-start) | async-done | bytes 720928 | tf_op jit(solution)/shard_map/all_to_all | solution.py:540
  57.4 7.2 %decoder_backward.1 = bf16[8,640,128]{2,1,0:T(8,128)(2,1)} custom-call(s32[1]{0:T(128)} %bitcast.2.member_ref, bf16[8,352,128]{2,1,0:T(8,128)(2,1)} %copy-done.2, f32[112,128]{1,0:T(8,128)} %pad.9.target_ref, f32[2,128]{1,0:T(2,128)} %fusion.7.index_ref, bf16[128,1024]{1,0:T(8,128)(2,1)} %project_queries.1.refs_2_.query_ref, ...), custom_call_target="tpu_custom_call" | custom-call | flops 536870912 | bytes 4194304 | tf_op jit(solution)/shard_map/decoder_backward/pallas_call | solution.py:314
  64.6 3.6 %all-to-all-start.1 = ((bf16[8,640,128]{2,1,0:T(8,128)(2,1)}), bf16[8,640,128]{2,1,0:T(8,128)(2,1)S(1)}, u32[]{:S(2)}, u32[]{:S(2)}) async-start(bf16[8,640,128]{2,1,0:T(8,128)(2,1)} %decoder_backward.1), calls=%async_computation.1 | async-start | bytes 2621440 | tf_op jit(solution)/shard_map/all_to_all | solution.py:552
  68.8 16.7 %all-to-all-done.1.blocks_ref = bf16[8,640,128]{2,1,0:T(8,128)(2,1)S(1)} async-done(((bf16[8,640,128]{2,1,0:T(8,128)(2,1)}), bf16[8,640,128]{2,1,0:T(8,128)(2,1)S(1)}, u32[]{:S(2)}, u32[]{:S(2)}) %all-to-all-start.1) | async-done | bytes 1310752 | tf_op jit(solution)/shard_map/all_to_all | solution.py:552
  85.5 1.1 copy-done
  86.6 5.9 %weight_gradients.1 = (bf16[4,624,256]{2,1,0:T(8,128)(2,1)}, f32[1,1]{1,0:T(1,128)}) custom-call(s32[2]{0:T(128)} %pad_add_fusion.place_ref, bf16[8,640,128]{2,1,0:T(8,128)(2,1)} %copy-done, bf16[128,1024]{1,0:T(8,128)(2,1)} %bitcast.32, bf16[128,1024]{1,0:T(8,128)(2,1)} %copy-done.5, bf16[128,1024]{1,0:T(8,128)(2,1)} %copy-done.4, ...), custom_call_target="tpu_custom_call" | custom-call | flops 1073741824 | bytes 8388608 | tf_op jit(solution)/shard_map/weight_gradients/pallas_call | solution.py:424
  92.5 35.5 %all_to_all.15.blocks_ref = bf16[4,624,256]{2,1,0:T(8,128)(2,1)} all-to-all(bf16[4,624,256]{2,1,0:T(8,128)(2,1)} %get-tuple-element.51), channel_id=1, replica_groups={{0,8,16,24},{4,12,20,28},{1,9,17,25},{5,13,21,29},{2,10,18,26},{6,14,22..., dimensions={0} | all-to-all | bytes 2555904 | tf_op jit(solution)/shard_map/all_to_all | solution.py:562
  127.9 2.3 %sum_groups.1 = (f32[100,1024]{1,0:T(8,128)}, f32[128,128]{1,0:T(8,128)}, f32[128,128]{1,0:T(8,128)}, f32[128,128]{1,0:T(8,128)}, f32[128,128]{1,0:T(8,128)}, /*index=5*/bf16[512,128]{1,0:T(8,128)(2,1)}) custom-call(s32[1]{0:T(128)} %bitcast.1.half_ref, bf16[4,624,256]{2,1,0:T(8,128)(2,1)} %all_to_all.15.blocks_ref), custom_call_target="tpu_custom_call" | custom-call | tf_op jit(solution)/shard_map/sum_groups/pallas_call | solution.py:473
  130.3 1.0 collective-permute-start.11
  131.3 4.2 %collective-permute-done.11.other_ref = bf16[512,128]{1,0:T(8,128)(2,1)S(1)} collective-permute-done((bf16[512,128]{1,0:T(8,128)(2,1)}, bf16[512,128]{1,0:T(8,128)(2,1)S(1)}, u32[]{:S(2)}, u32[]{:S(2)}) %collective-permute-start.11) | collective-permute-done | bytes 131104 | tf_op jit(solution)/shard_map/ppermute | solution.py:29
  136.1 1.8 %join_columns.1 = (f32[128,256]{1,0:T(8,128)}, f32[128,256]{1,0:T(8,128)}, f32[128,256]{1,0:T(8,128)}, f32[128,256]{1,0:T(8,128)}) custom-call(s32[1]{0:T(128)} %bitcast.1.half_ref, bf16[512,128]{1,0:T(8,128)(2,1)} %copy-done.11, f32[128,128]{1,0:T(8,128)} %get-tuple-element.54.refs_0_, f32[128,128]{1,0:T(8,128)} %get-tuple-element.55.refs_1_, ...), custom_call_target="tpu_custom_call" | custom-call | tf_op jit(solution)/shard_map/join_columns/pallas_call | solution.py:495
  (50 shorter events, 8.3 us)
Async XLA Ops:
  0.6 19.6 %copy-start.10 = (bf16[100,1024]{1,0:T(8,128)(2,1)S(1)}, bf16[100,1024]{1,0:T(8,128)(2,1)}, u32[]{:S(2)}) copy-start(bf16[100,1024]{1,0:T(8,128)(2,1)} %param.17) | copy-start | bytes 614404
  1.8 15.0 %collective-permute-start.3 = (bf16[256,1024]{1,0:T(8,128)(2,1)S(1)}, bf16[256,1024]{1,0:T(8,128)(2,1)S(1)}, u32[]{:S(2)}, u32[]{:S(2)}) collective-permute-start(bf16[256,1024]{1,0:T(8,128)(2,1)S(1)} %pad_maximum_fusion.1), channel_id=1, source_target_pairs={{0,4},{4,0},{8,12},{12,8},{16,20},{20,16},{24,28},{28,24},{1,5},{5... | collective-permute-start | bytes 1572872 | tf_op jit(solution)/shard_map/ppermute | solution.py:29
  4.8 8.0 %collective-permute-start.1 = (bf16[128,1024]{1,0:T(8,128)(2,1)}, bf16[128,1024]{1,0:T(8,128)(2,1)S(1)}, u32[]{:S(2)}, u32[]{:S(2)}) collective-permute-start(bf16[128,1024]{1,0:T(8,128)(2,1)} %bitcast.29), channel_id=1, source_target_pairs={{0,2},{1,3},{2,0},{3,1},{4,6},{5,7},{6,4},{7,5},{8,10},{9,11},{10,... | collective-permute-start | bytes 786440 | tf_op jit(solution)/shard_map/ppermute | solution.py:29
  6.3 18.2 %collective-permute-start = (bf16[128,1024]{1,0:T(8,128)(2,1)}, bf16[128,1024]{1,0:T(8,128)(2,1)S(1)}, u32[]{:S(2)}, u32[]{:S(2)}) collective-permute-start(bf16[128,1024]{1,0:T(8,128)(2,1)} %bitcast.30), channel_id=1, source_target_pairs={{0,1},{1,0},{2,3},{3,2},{4,5},{5,4},{6,7},{7,6},{8,9},{9,8},{10,11... | collective-permute-start | bytes 786440 | tf_op jit(solution)/shard_map/ppermute | solution.py:29
  12.8 11.7 %copy-start.4 = (bf16[128,1024]{1,0:T(8,128)(2,1)}, bf16[128,1024]{1,0:T(8,128)(2,1)S(1)}, u32[]{:S(2)}) copy-start(bf16[128,1024]{1,0:T(8,128)(2,1)S(1)} %collective-permute-done.1.refs_6_.refs_2_) | copy-start | bytes 786436
  12.8 11.7 %collective-permute-start.2 = (bf16[128,1024]{1,0:T(8,128)(2,1)S(1)}, bf16[128,1024]{1,0:T(8,128)(2,1)S(1)}, u32[]{:S(2)}, u32[]{:S(2)}) collective-permute-start(bf16[128,1024]{1,0:T(8,128)(2,1)S(1)} %collective-permute-done.1.refs_6_.refs_2_), channel_id=1, source_target_pairs={{0,1},{1,0},{2,3},{3,2},{4,5},{5,4},{6,7},{7,6},{8,9},{9,8},{10,11... | collective-permute-start | bytes 786440 | tf_op jit(solution)/shard_map/ppermute | solution.py:29
  17.7 23.7 %copy-start.1 = (bf16[384,1024]{1,0:T(8,128)(2,1)}, bf16[384,1024]{1,0:T(8,128)(2,1)S(1)}, u32[]{:S(2)}) copy-start(bf16[384,1024]{1,0:T(8,128)(2,1)S(1)} %pad_maximum_fusion.refs_4_) | copy-start | bytes 2359300
  17.7 23.7 %collective-permute-start.5 = (bf16[384,1024]{1,0:T(8,128)(2,1)S(1)}, bf16[384,1024]{1,0:T(8,128)(2,1)}, u32[]{:S(2)}, u32[]{:S(2)}) collective-permute-start(bf16[384,1024]{1,0:T(8,128)(2,1)S(1)} %pad_maximum_fusion.refs_4_), channel_id=1, source_target_pairs={{0,2},{1,3},{2,0},{3,1},{4,6},{5,7},{6,4},{7,5},{8,10},{9,11},{10,... | collective-permute-start | bytes 2359304 | tf_op jit(solution)/shard_map/ppermute | solution.py:29
  32.6 6.5 %copy-start.9 = (bf16[128,1024]{1,0:T(8,128)(2,1)S(1)}, bf16[128,1024]{1,0:T(8,128)(2,1)}, u32[]{:S(2)}) copy-start(bf16[128,1024]{1,0:T(8,128)(2,1)} %get-tuple-element.35) | copy-start | bytes 786436
  32.6 19.0 %copy-start.12 = (f32[100,128]{1,0:T(8,128)S(1)}, f32[100,128]{1,0:T(8,128)}, u32[]{:S(2)}) copy-start(f32[100,128]{1,0:T(8,128)} %param.12) | copy-start | bytes 153604
  32.6 19.7 %copy-start.13 = (s32[1,128]{1,0:T(1,128)S(1)}, s32[1,128]{1,0:T(1,128)}, u32[]{:S(2)}) copy-start(s32[1,128]{1,0:T(1,128)} %param.11) | copy-start | bytes 1540
  32.7 8.2 %collective-permute-start.7 = (bf16[128,1024]{1,0:T(8,128)(2,1)}, bf16[128,1024]{1,0:T(8,128)(2,1)S(1)}, u32[]{:S(2)}, u32[]{:S(2)}) collective-permute-start(bf16[128,1024]{1,0:T(8,128)(2,1)} %get-tuple-element.35), channel_id=1, source_target_pairs={{0,4},{4,0},{8,12},{12,8},{16,20},{20,16},{24,28},{28,24},{1,5},{5... | collective-permute-start | bytes 786440 | tf_op jit(solution)/shard_map/ppermute | solution.py:29
  34.2 22.3 %all-to-all-start = ((bf16[8,352,128]{2,1,0:T(8,128)(2,1)}), bf16[8,352,128]{2,1,0:T(8,128)(2,1)S(1)}, u32[]{:S(2)}, u32[]{:S(2)}) async-start(bf16[8,352,128]{2,1,0:T(8,128)(2,1)} %get-tuple-element.34), calls=%async_computation | async-start | bytes 1441792 | tf_op jit(solution)/shard_map/all_to_all | solution.py:540
  40.8 23.8 %copy-start.3 = (bf16[256,1024]{1,0:T(8,128)(2,1)}, bf16[256,1024]{1,0:T(8,128)(2,1)S(1)}, u32[]{:S(2)}) copy-start(bf16[256,1024]{1,0:T(8,128)(2,1)S(1)} %constant_dynamic-update-slice_fusion.refs_8_) | copy-start | bytes 1572868
  40.9 10.8 %collective-permute-start.9 = (bf16[256,1024]{1,0:T(8,128)(2,1)S(1)}, bf16[256,1024]{1,0:T(8,128)(2,1)S(1)}, u32[]{:S(2)}, u32[]{:S(2)}) collective-permute-start(bf16[256,1024]{1,0:T(8,128)(2,1)S(1)} %constant_dynamic-update-slice_fusion.refs_8_), channel_id=1, source_target_pairs={{0,2},{1,3},{2,0},{3,1},{4,6},{5,7},{6,4},{7,5},{8,10},{9,11},{10,... | collective-permute-start | bytes 1572872 | tf_op jit(solution)/shard_map/ppermute | solution.py:29
  41.5 11.4 %collective-permute-start.4 = (bf16[384,1024]{1,0:T(8,128)(2,1)S(1)}, bf16[384,1024]{1,0:T(8,128)(2,1)S(1)}, u32[]{:S(2)}, u32[]{:S(2)}) collective-permute-start(bf16[384,1024]{1,0:T(8,128)(2,1)S(1)} %pad_maximum_fusion.refs_4_), channel_id=1, source_target_pairs={{0,1},{1,0},{2,3},{3,2},{4,5},{5,4},{6,7},{7,6},{8,9},{9,8},{10,11... | collective-permute-start | bytes 2359304 | tf_op jit(solution)/shard_map/ppermute | solution.py:29
  41.5 15.0 %collective-permute-start.6 = (bf16[384,1024]{1,0:T(8,128)(2,1)}, bf16[384,1024]{1,0:T(8,128)(2,1)}, u32[]{:S(2)}, u32[]{:S(2)}) collective-permute-start(bf16[384,1024]{1,0:T(8,128)(2,1)} %collective-permute-done.5.refs_6_), channel_id=1, source_target_pairs={{0,1},{1,0},{2,3},{3,2},{4,5},{5,4},{6,7},{7,6},{8,9},{9,8},{10,11... | collective-permute-start | bytes 2359304 | tf_op jit(solution)/shard_map/ppermute | solution.py:29
  42.0 10.9 %collective-permute-start.8 = (bf16[256,1024]{1,0:T(8,128)(2,1)S(1)}, bf16[256,1024]{1,0:T(8,128)(2,1)}, u32[]{:S(2)}, u32[]{:S(2)}) collective-permute-start(bf16[256,1024]{1,0:T(8,128)(2,1)S(1)} %constant_dynamic-update-slice_fusion.refs_8_), channel_id=1, source_target_pairs={{0,1},{1,0},{2,3},{3,2},{4,5},{5,4},{6,7},{7,6},{8,9},{9,8},{10,11... | collective-permute-start | bytes 1572872 | tf_op jit(solution)/shard_map/ppermute | solution.py:29
  51.6 13.0 %copy-start.8 = (bf16[256,1024]{1,0:T(8,128)(2,1)}, bf16[256,1024]{1,0:T(8,128)(2,1)S(1)}, u32[]{:S(2)}) copy-start(bf16[256,1024]{1,0:T(8,128)(2,1)S(1)} %collective-permute-done.9.refs_10_) | copy-start | bytes 1572868
  51.6 4.9 %collective-permute-start.10 = (bf16[256,1024]{1,0:T(8,128)(2,1)S(1)}, bf16[256,1024]{1,0:T(8,128)(2,1)}, u32[]{:S(2)}, u32[]{:S(2)}) collective-permute-start(bf16[256,1024]{1,0:T(8,128)(2,1)S(1)} %collective-permute-done.9.refs_10_), channel_id=1, source_target_pairs={{0,1},{1,0},{2,3},{3,2},{4,5},{5,4},{6,7},{7,6},{8,9},{9,8},{10,11... | collective-permute-start | bytes 1572872 | tf_op jit(solution)/shard_map/ppermute | solution.py:29
  52.9 11.7 %copy-start.7 = (bf16[384,1024]{1,0:T(8,128)(2,1)}, bf16[384,1024]{1,0:T(8,128)(2,1)S(1)}, u32[]{:S(2)}) copy-start(bf16[384,1024]{1,0:T(8,128)(2,1)S(1)} %collective-permute-done.4.refs_5_) | copy-start | bytes 2359300
  64.6 20.8 %all-to-all-start.1 = ((bf16[8,640,128]{2,1,0:T(8,128)(2,1)}), bf16[8,640,128]{2,1,0:T(8,128)(2,1)S(1)}, u32[]{:S(2)}, u32[]{:S(2)}) async-start(bf16[8,640,128]{2,1,0:T(8,128)(2,1)} %decoder_backward.1), calls=%async_computation.1 | async-start | bytes 2621440 | tf_op jit(solution)/shard_map/all_to_all | solution.py:552
  85.5 1.1 copy-start
  130.3 5.2 %collective-permute-start.11 = (bf16[512,128]{1,0:T(8,128)(2,1)}, bf16[512,128]{1,0:T(8,128)(2,1)S(1)}, u32[]{:S(2)}, u32[]{:S(2)}) collective-permute-start(bf16[512,128]{1,0:T(8,128)(2,1)} %get-tuple-element.53), channel_id=1, source_target_pairs={{0,4},{4,0},{8,12},{12,8},{16,20},{20,16},{24,28},{28,24},{1,5},{5... | collective-permute-start | bytes 393224 | tf_op jit(solution)/shard_map/ppermute | solution.py:29
  (4 other events, 2.9 us)

commit v4 on v3

--- a/solution.py
+++ b/solution.py
@@ -49,7 +49,7 @@
     return jnp.where(lane < blocks.shape[1] // 2, blocks[:rows], blocks[rows:])
 
 
-def query_kernel(rows_ref, w_hbm, out_ref, w_ref, sem):
+def query_kernel(latent_ref, rows_ref, w_hbm, out_ref, both_ref, w_ref, sem):
     chunks = w_ref.shape[0]
     step = w_ref.shape[2]
     copies = [
@@ -58,19 +58,25 @@
     ]
     for copy in copies:
         copy.start()
+    nodes = latent_ref.shape[0]
+    both_ref[:nodes] = latent_ref[...]
+    both_ref[nodes:] = rows_ref[...]
     for c, copy in enumerate(copies):
         copy.wait()
         out_ref[:, c * step : (c + 1) * step] = dot32(rows_ref[...], w_ref[c]).astype(BF16)
 
 
-def project_queries(rows, weight):
+def project_queries(latent, rows, weight):
     features = weight.shape[0]
-    step = min(512, features)
+    step = min(256, features)
     return pl.pallas_call(
         query_kernel,
-        out_shape=jax.ShapeDtypeStruct(rows.shape, BF16),
-        in_specs=[VMEM, ANY],
-        out_specs=VMEM,
+        out_shape=(
+            jax.ShapeDtypeStruct(rows.shape, BF16),
+            jax.ShapeDtypeStruct((latent.shape[0] + rows.shape[0], features), BF16),
+        ),
+        in_specs=[VMEM, VMEM, ANY],
+        out_specs=(VMEM, VMEM),
         scratch_shapes=[
             pltpu.VMEM((features // step, features, step), BF16),
             pltpu.SemaphoreType.DMA((features // step,)),
@@ -79,13 +85,13 @@
             flops=2 * rows.size * features, bytes_accessed=2 * weight.size, transcendentals=0
         ),
         name="project_queries",
-    )(rows, weight)
+    )(latent, rows, weight)
 
 
 def forward_kernel(shards, members, *refs):
-    position_ref, grid_ref, query_ref, readout_ref = refs[:4]
-    latent_refs = refs[4 : 4 + shards]
-    weights_hbm = refs[4 + shards : 7 + shards]
+    shard_ref, index_ref, grid_ref, query_ref, readout_ref = refs[:5]
+    latent_refs = refs[5 : 5 + shards]
+    weights_hbm = refs[5 + shards : 8 + shards]
     (
         key_ref,
         value_ref,
@@ -96,15 +102,18 @@
         packed_ref,
         *w_refs,
         sem,
-    ) = refs[7 + shards :]
+    ) = refs[8 + shards :]
     copies = [pltpu.make_async_copy(s, d, sem.at[i]) for i, (s, d) in enumerate(zip(weights_hbm, w_refs))]
     for copy in copies:
         copy.start()
     points, features = grid_ref.shape
     latents = jnp.concatenate([ref[...] for ref in latent_refs], axis=0)
-    node = lax.broadcasted_iota(jnp.int32, (points, latents.shape[0]), 1)
-    chosen = jnp.where(node == position_ref[...], 1.0, 0.0).astype(BF16)
-    nodes = dot32(chosen, latents).astype(BF16)
+    each = latent_refs[0].shape[0]
+    index = index_ref[...]
+    position = ((index // each) ^ shard_ref[0]) * each + index % each
+    node = lax.broadcasted_iota(jnp.int32, (latents.shape[0], points), 0)
+    chosen = jnp.where(node == position, 1.0, 0.0).astype(BF16)
+    nodes = dot32(chosen, latents, (0, 0)).astype(BF16)
     copies[0].wait()
     key_ref[...] = dot32(nodes, w_refs[0][...]).astype(BF16)
     copies[1].wait()
@@ -131,22 +140,27 @@
     forecast = dot32(readout_ref[...], normed_b, (1, 1))
     high = forecast.astype(BF16)
     low = (forecast - high.astype(F32)).astype(BF16)
-    channels = readout_ref.shape[0]
     depth = features // members
     pieces = LANES // depth
     part = points // pieces
+    channels = (packed_ref.shape[1] - part) // 2
+    spare = jnp.zeros((channels - readout_ref.shape[0], points), BF16)
+    fields = jnp.concatenate([high, spare, low, spare], axis=0)
     for m in range(members):
-        packed_ref[m, :channels] = high
-        packed_ref[m, channels : 2 * channels] = low
+        packed_ref[m, : 2 * channels] = fields
         for p in range(pieces):
             packed_ref[m, 2 * channels :, p * depth : (p + 1) * depth] = normed_b[
                 p * part : (p + 1) * part, m * depth : (m + 1) * depth
             ]
 
 
-def forward(position, grid_rows, queries, readout, latents, weights, members):
+def padded(channels):
+    return channels + -channels % 16
+
+
+def forward(shard, index, grid_rows, queries, readout, latents, weights, members):
     points, features = grid_rows.shape
-    channels = readout.shape[0]
+    channels = padded(readout.shape[0])
     depth = features // members
     rows = 2 * channels + points * depth // LANES
     shape = jax.ShapeDtypeStruct
@@ -161,7 +175,7 @@
             shape((points, 1), F32),
             shape((members, rows, LANES), BF16),
         ),
-        in_specs=[VMEM] * (4 + len(latents)) + [ANY] * 3,
+        in_specs=[SMEM] + [VMEM] * (4 + len(latents)) + [ANY] * 3,
         out_specs=(VMEM,) * 7,
         scratch_shapes=[pltpu.VMEM((features, features), BF16)] * 3
         + [pltpu.SemaphoreType.DMA((3,))],
@@ -171,13 +185,13 @@
             transcendentals=points * LANES * HEADS,
         ),
         name="decoder_forward",
-    )(position, grid_rows, queries, readout, *latents, *weights)
+    )(shard, index, grid_rows, queries, readout, *latents, *weights)
 
 
 def backward_kernel(
     shards,
     blocks,
-    channels_used,
+    nodes,
     member_ref,
     packed_ref,
     target_ref,
@@ -195,13 +209,20 @@
     slope_ref,
     d_attended_ref,
     small_ref,
+    truth_ref,
+    weight_ref,
     sem,
 ):
     copy = pltpu.make_async_copy(w_hbm, w_ref, sem)
     copy.start()
     members = packed_ref.shape[0]
     points, features = normed_ref.shape
-    channels = readout_ref.shape[0]
+    channels_used = readout_ref.shape[0]
+    channels = truth_ref.shape[0]
+    for full, used in ((truth_ref, target_ref), (weight_ref, readout_ref)):
+        full[:channels_used] = used[...]
+        spare = (channels - channels_used, used.shape[1])
+        full[channels_used:] = jnp.zeros(spare, used.dtype)
     width, depth = features // blocks, features // members
     weight = (channels_used * points * shards) ** (-0.5)
     pair_weight = 1.0 / (members * (members - 1))
@@ -214,7 +235,7 @@
             packed_ref[m, at].astype(F32) + packed_ref[m, low_at].astype(F32)
             for m in range(members)
         ]
-        truth = target_ref[at]
+        truth = truth_ref[at]
         skill = jnp.zeros_like(truth)
         slopes = []
         for m in range(members):
@@ -260,7 +281,13 @@
         small_ref[rows + i : rows + i + 1] = jnp.broadcast_to(value, (1, width))
     spare = small_ref.shape[0] - rows - 3
     small_ref[rows + 3 :] = jnp.zeros((spare, width), F32)
-    small_ref[rows + 3 : rows + 3 + index_ref.shape[0]] = index_ref[...]
+    index = index_ref[...]
+    line = rows + 3
+    for tag in (index // nodes, index % nodes):
+        step = min(points, width)
+        for c in range(0, points, step):
+            small_ref[line : line + 1, :step] = tag[:, c : c + step].astype(F32)
+            line = line + 1
     small = small_ref[...].astype(BF16)
     for b in range(blocks):
         out_ref[b, 4 * points :] = small
@@ -275,7 +302,7 @@
 
     own = slope_ref[member_ref[0]]
     normed = normed_ref[...]
-    d_normed = dot32(own, readout_ref[...], (0, 0))
+    d_normed = dot32(own, weight_ref[...], (0, 0))
     mean = jnp.mean(d_normed * normed, axis=-1, keepdims=True)
     d_hidden = (inverse_ref[...] * (d_normed - normed * mean)).astype(BF16)
     put(3, 0, d_hidden)
@@ -304,15 +331,15 @@
     return rows + -rows % 16
 
 
-def backward(member, packed, target, index, saved, readout, w_mix, shards, blocks, channels_used):
+def backward(member, packed, target, index, saved, readout, w_mix, shards, blocks, nodes):
     members = packed.shape[0]
     features = w_mix.shape[0]
     points = saved[0].shape[0]
-    channels = readout.shape[0]
+    channels = padded(readout.shape[0])
     width, depth = features // blocks, features // members
     small = small_rows(channels, depth, width)
     return pl.pallas_call(
-        functools.partial(backward_kernel, shards, blocks, channels_used),
+        functools.partial(backward_kernel, shards, blocks, nodes),
         out_shape=jax.ShapeDtypeStruct((blocks, 4 * points + small, width), BF16),
         in_specs=[SMEM] + [VMEM] * 10 + [ANY],
         out_specs=VMEM,
@@ -321,6 +348,8 @@
             pltpu.VMEM((members, channels, points), BF16),
             pltpu.VMEM((points, features), BF16),
             pltpu.VMEM((small, width), F32),
+            pltpu.VMEM((channels, points), F32),
+            pltpu.VMEM((channels, features), BF16),
             pltpu.SemaphoreType.DMA,
         ],
         cost_estimate=pl.CostEstimate(
@@ -339,24 +368,24 @@
     features = late_refs[0].shape[1]
     points = late_refs[0].shape[0] // pair
     depth = features // members
-    lanes = pair * depth
     shard, half = place_ref[0], place_ref[1]
     rows = channels * depth // width
     start = 4 * points
-    loss = jnp.zeros((1, 1), F32)
+    parts = []
     for t in range(pair):
         total = jnp.zeros((blocks_ref.shape[1] - start, width), F32)
         for s in range(shards):
             total = total + blocks_ref[s * pair + t, start:].astype(F32)
         if t == 0:
             loss = jnp.sum(total[rows : rows + 3, :1], axis=0, keepdims=True)
-        total = total.astype(BF16)
-        for z in range(members // pair):
-            for p in range(width // depth):
-                out_ref[z, 4 * width + p * rows : 4 * width + (p + 1) * rows, t * depth : (t + 1) * depth] = (
-                    total[:rows, p * depth : (p + 1) * depth]
-                )
+        parts.append(total[:rows])
     loss_ref[...] = loss
+    small = parts[0]
+    if pair > 1:
+        small = jnp.where(half == 0, parts[0], parts[1])
+    small = small.astype(BF16)
+    for m in range(members):
+        out_ref[m, 4 * width :] = small
 
     def slots(kind, t):
         at = slice(kind * points, (kind + 1) * points)
@@ -365,8 +394,8 @@
     def put(kind, total):
         total = total.astype(BF16)
         at = slice(kind * width, kind * width + total.shape[0])
-        for z in range(members // pair):
-            out_ref[z, at] = total[:, z * lanes : (z + 1) * lanes]
+        for m in range(members):
+            out_ref[m, at] = total[:, m * depth : (m + 1) * depth]
 
     def rows_of(ref_list, part):
         at = slice(part * points, (part + 1) * points)
@@ -382,13 +411,10 @@
     for k in range(shards):
         index = blocks_ref[(shard ^ k) * pair, start + rows : start + rows + MISC].astype(jnp.int32)
         lines = max(points // width, 1)
-        if width >= 2 * points:
-            owner, offset = index[3:4, :points], index[3:4, points : 2 * points]
-        else:
-            owner, offset = (
-                jnp.concatenate([index[3 + b + i : 4 + b + i] for i in range(lines)], axis=1)
-                for b in (0, lines)
-            )
+        owner, offset = (
+            jnp.concatenate([index[3 + b + i : 4 + b + i] for i in range(lines)], axis=1)
+            for b in (0, lines)
+        )
         position = (owner ^ shard) * nodes + offset
         node = lax.broadcasted_iota(jnp.int32, (nodes * shards, points), 0)
         chosen.append(jnp.where(node == position, 1.0, 0.0).astype(BF16))
@@ -426,7 +452,7 @@
             gradient_kernel, shards, pair, members, latents[0].shape[0], channels
         ),
         out_shape=(
-            jax.ShapeDtypeStruct((members // pair, rows, pair * depth), BF16),
+            jax.ShapeDtypeStruct((members, rows, depth), BF16),
             jax.ShapeDtypeStruct((1, 1), F32),
         ),
         in_specs=[SMEM] + [VMEM] * (1 + 3 * shards),
@@ -440,101 +466,66 @@
     )(place, blocks, *latents, *early, *late)
 
 
-def sum_kernel(pair, half_ref, blocks_ref, out_ref, *refs):
-    count, _, lanes = blocks_ref.shape
-    depth = lanes // pair
+def sum_kernel(pair, blocks_ref, out_ref, *refs):
+    members, _, depth = blocks_ref.shape
     used = out_ref.shape[0]
-    width = refs[0].shape[1]
-    for z in range(count):
-        out_ref[:, z * lanes : (z + 1) * lanes] = blocks_ref[z, 4 * width : 4 * width + used].astype(F32)
+    width = refs[0].shape[1] // pair
+    for m in range(members):
+        out_ref[:, m * depth : (m + 1) * depth] = blocks_ref[m, 4 * width : 4 * width + used].astype(F32)
     for i in range(4):
         at = slice(i * width, (i + 1) * width)
-        total = blocks_ref[0, at].astype(F32)
-        for z in range(1, count):
-            total = total + blocks_ref[z, at].astype(F32)
-        if pair == 1:
-            refs[i][...] = total.T
-        else:
-            first, second = total[:, :depth], total[:, depth:]
-            own = jnp.where(half_ref[0] == 0, first, second)
-            other = jnp.where(half_ref[0] == 0, second, first)
-            refs[i][...] = own.T
-            refs[4][i * depth : (i + 1) * depth] = other.T.astype(BF16)
-
-
-def sum_groups(half, blocks, pair, channels_used):
-    count, rows, lanes = blocks.shape
-    depth = lanes // pair
-    width = (rows - (channels_used + -channels_used % 16)) // 4
+        for y in range(pair):
+            total = blocks_ref[y, at].astype(F32)
+            for m in range(y + pair, members, pair):
+                total = total + blocks_ref[m, at].astype(F32)
+            refs[i][:, y * width : (y + 1) * width] = total.T
+
+
+def sum_groups(blocks, pair, channels_used):
+    members, rows, depth = blocks.shape
+    width = (rows - padded(channels_used)) // 4
     shape = jax.ShapeDtypeStruct
-    outs = (shape((channels_used, lanes * count), F32),) + (shape((depth, width), F32),) * 4
-    if pair > 1:
-        outs = outs + (shape((4 * depth, width), BF16),)
     return pl.pallas_call(
         functools.partial(sum_kernel, pair),
-        out_shape=outs,
-        in_specs=[SMEM, VMEM],
-        out_specs=(VMEM,) * len(outs),
+        out_shape=(shape((channels_used, depth * members), F32),)
+        + (shape((depth, pair * width), F32),) * 4,
+        in_specs=[VMEM],
+        out_specs=(VMEM,) * 5,
         name="sum_groups",
-    )(half, blocks)
-
-
-def join_kernel(half_ref, other_ref, *refs):
-    keep_refs, out_refs = refs[:4], refs[4:]
-    depth, width = keep_refs[0].shape
-    first = half_ref[0] == 0
-    for i in range(4):
-        own = keep_refs[i][...]
-        other = other_ref[i * depth : (i + 1) * depth].astype(F32)
-        out_refs[i][:, :width] = jnp.where(first, own, other)
-        out_refs[i][:, width:] = jnp.where(first, other, own)
-
-
-def join_columns(half, other, keeps):
-    depth, width = keeps[0].shape
-    return pl.pallas_call(
-        join_kernel,
-        out_shape=(jax.ShapeDtypeStruct((depth, 2 * width), F32),) * 4,
-        in_specs=[SMEM] + [VMEM] * 5,
-        out_specs=(VMEM,) * 4,
-        name="join_columns",
-    )(half, other, *keeps)
+    )(blocks)
 
 
 def body(
     grid_hidden, latent, tile_neighbor_index, target, w_query, w_key, w_value, w_mix, readout_weight
 ):
-    nodes, features = latent.shape[1:]
+    nodes, _ = latent.shape[1:]
     channels_used = target.shape[0]
     shards, members = lax.axis_size("space"), lax.axis_size("ens")
     shard, member = lax.axis_index("space"), lax.axis_index("ens")
     pair = 2 if members % 2 == 0 and shards <= 8 else 1
     half = member % pair
     count = shards * pair
-    width = features // count
     groups = [
         [(g + y) * shards + s for s in range(shards) for y in range(pair)]
         for g in range(0, members, pair)
     ]
-    lines = [list(range(y, members, pair)) for y in range(pair)]
 
     own_latent, grid_rows = latent[0], grid_hidden[0]
     latents = gather_slots(own_latent, "space")
+    queries, both = project_queries(own_latent, grid_rows, w_query)
     early = grid_rows
     if pair > 1:
-        partner = swap(jnp.concatenate([own_latent, grid_rows]), "ens", 1)
+        partner = swap(both, "ens", 1)
         early = jnp.concatenate([grid_rows, partner])
-    queries = project_queries(grid_rows, w_query)
-    spare = ((0, -channels_used % 16), (0, 0))
-    readout = jnp.pad(readout_weight, spare)
-    truth = jnp.pad(target, spare)
-    channels = readout.shape[0]
-    index = tile_neighbor_index.reshape(-1)
-    owner, offset = index // nodes, index % nodes
-    tags = jnp.concatenate([owner, offset]).astype(F32).reshape(-1, width)
-    position = ((owner ^ shard) * nodes + offset)[:, None]
     *saved, packed = forward(
-        position, grid_rows, queries, readout, latents, (w_key, w_value, w_mix), members
+        shard[None],
+        tile_neighbor_index,
+        grid_rows,
+        queries,
+        readout_weight,
+        latents,
+        (w_key, w_value, w_mix),
+        members,
     )
     keyset, valueset, soft, attended, normed, inverse = saved
     packed = lax.all_to_all(packed, "ens", split_axis=0, concat_axis=0, tiled=True)
@@ -544,10 +535,18 @@
         late = jnp.concatenate([attended, partner])
     early = gather_slots(early, "space")
     late = gather_slots(late, "space")
-    packed, early, late = lax.optimization_barrier((packed, early, late))
     saved = (queries, keyset, valueset, soft, normed, inverse)
     blocks = backward(
-        member[None], packed, truth, tags, saved, readout, w_mix, shards, count, channels_used
+        member[None],
+        packed,
+        target,
+        tile_neighbor_index,
+        saved,
+        readout_weight,
+        w_mix,
+        shards,
+        count,
+        nodes,
     )
     blocks = lax.all_to_all(
         blocks,
@@ -558,14 +557,10 @@
         tiled=True,
     )
     place = jnp.stack([shard, half])
+    channels = padded(channels_used)
     blocks, loss = gradients(place, blocks, latents, early, late, members, pair, channels)
-    blocks = lax.all_to_all(
-        blocks, "ens", split_axis=0, concat_axis=0, axis_index_groups=lines, tiled=True
-    )
-    grad_out, *grads = sum_groups(half[None], blocks, pair, channels_used)
-    if pair > 1:
-        *keeps, other = grads
-        grads = join_columns(half[None], swap(other, "ens", 1), keeps)
+    blocks = lax.all_to_all(blocks, "ens", split_axis=0, concat_axis=0, tiled=True)
+    grad_out, *grads = sum_groups(blocks, pair, channels_used)
     return (loss.reshape(()), grad_out, *grads)
 
 

time: 138 us -> 142 us (1.029)
  waiting for transfers between devices: 45.3 us -> 54.2 us
  other arithmetic: 3.97 us -> 0.64 us
  local copies, waits for them, and re-layouts: 6.25 us -> 4.73 us
    ppermute x12 -> x11, waiting for transfers between devices: 25.1 us -> 54.2 us  [swap(): return lax.ppermute(value, axis, [(i, i ^ bits) for i in range(size)])]
    all_to_all x1, waiting for transfers between devices: 16.7 us -> 0.01 us  [body(): lax.all_to_all(blocks, ('ens', 'space'), split_axis=0, concat_axis=0, axi...]
    all_to_all x1, waiting for transfers between devices: 3.59 us -> 0.01 us  [body(): lax.all_to_all(packed, 'ens', split_axis=0, concat_axis=0, tiled=True)]
    pad x2 -> x0, local copies, waits for them, and re-layouts: 1.43 us -> none  [the longest x1 0.74 us: body(): readout = jnp.pad(readout_weight, spare)]
    pallas_call x4 -> x3, Pallas kernels: 14.9 us -> 13.6 us  [the longest x1 7.23 us: backward(): pl.pallas_call(functools.partial(backward_kernel, shards, blocks, nodes),...]
    ppermute x12 -> x11, starting transfers between devices: 10.1 us -> 9.41 us  [swap(): return lax.ppermute(value, axis, [(i, i ^ bits) for i in range(size)])]
    unnamed x29 -> x21, local copies, waits for them, and re-layouts: 4.04 us -> 3.77 us
  transfers between devices with their start and end apart: 14 -> 13, of which waited for: 7 -> 5; matrix products, arithmetic and copies ran while one was open for 4% -> 2% of each run, Pallas kernels for 7% -> 8%
where the time goes in v4:
time: 142 us
  waiting for transfers between devices  54.2 us (38%)
  blocking collectives  36.1 us (25%)
  Pallas kernels  26.2 us (18%)
  starting transfers between devices  19.2 us (14%)
  local copies, waits for them, and re-layouts  4.73 us (3%)
    ppermute x11, waiting for transfers between devices, swap(): return lax.ppermute(value, axis, [(i, i ^ bits) for i in range(size)])  54.2 us
    all_to_all x1, blocking collectives, body(): lax.all_to_all(blocks, 'ens', split_axis=0, concat_axis=0, tiled=True)  36.1 us
    ppermute x11, starting transfers between devices, swap(): return lax.ppermute(value, axis, [(i, i ^ bits) for i in range(size)])  9.41 us
    pallas_call x1, Pallas kernels, backward(): pl.pallas_call(functools.partial(backward_kernel, shards, blocks, nodes),...  7.23 us
    pallas_call x1, Pallas kernels, forward(): pl.pallas_call(functools.partial(forward_kernel, len(latents), members),...  6.69 us
    all_to_all x1, starting transfers between devices, body(): lax.all_to_all(packed, 'ens', split_axis=0, concat_axis=0, tiled=True)  6.23 us
    pallas_call x1, Pallas kernels, gradients(): pl.pallas_call(functools.partial(gradient_kernel, shards, pair, members,...  5.89 us
    pallas_call x1, Pallas kernels, project_queries(): pl.pallas_call(query_kernel, out_shape=(jax.ShapeDtypeStruct(rows.shape,...  4.05 us
  transfers between devices with their start and end apart: 13, of which 5 were waited for; matrix products, arithmetic and copies ran while one was open for 2% of the time, Pallas kernels for 8%

profile of v4, /device:TPU:0, one launch (start us, length us, event | category | flops | bytes accessed | tf_op | source)
XLA Modules:
  0.0 141.9 jit_solution(18070057848355786841)
XLA Ops:
  0.6 3.0 %collective-permute-start.1 = (bf16[128,1024]{1,0:T(8,128)(2,1)}, bf16[128,1024]{1,0:T(8,128)(2,1)S(1)}, u32[]{:S(2)}, u32[]{:S(2)}) collective-permute-start(bf16[128,1024]{1,0:T(8,128)(2,1)} %bitcast.6), channel_id=1, source_target_pairs={{0,2},{1,3},{2,0},{3,1},{4,6},{5,7},{6,4},{7,5},{8,10},{9,11},{10,... | collective-permute-start | bytes 786440 | tf_op jit(solution)/shard_map/ppermute | solution.py:29
  3.7 6.5 %collective-permute-done.1.refs_7_.refs_2_ = bf16[128,1024]{1,0:T(8,128)(2,1)S(1)} collective-permute-done((bf16[128,1024]{1,0:T(8,128)(2,1)}, bf16[128,1024]{1,0:T(8,128)(2,1)S(1)}, u32[]{:S(2)}, u32[]{:S(2)}) %collective-permute-start.1) | collective-permute-done | bytes 262176 | tf_op jit(solution)/shard_map/ppermute | solution.py:29
  10.2 4.0 %project_queries.1 = (bf16[128,1024]{1,0:T(8,128)(2,1)}, bf16[256,1024]{1,0:T(8,128)(2,1)}) custom-call(bf16[128,1024]{1,0:T(8,128)(2,1)} %bitcast.8, bf16[128,1024]{1,0:T(8,128)(2,1)} %bitcast.11, bf16[1024,1024]{1,0:T(8,128)(2,1)} %w_hbm.2), custom_call_target="tpu_custom_call" | custom-call | flops 268435456 | bytes 2097152 | tf_op jit(solution)/shard_map/project_queries/pallas_call | solution.py:72
  14.3 0.7 copy-done.6
  15.1 6.7 %decoder_forward.1 = (bf16[128,1024]{1,0:T(8,128)(2,1)}, bf16[128,1024]{1,0:T(8,128)(2,1)}, f32[8,128,256]{2,1,0:T(8,128)}, bf16[128,1024]{1,0:T(8,128)(2,1)}, f...) custom-call(s32[1]{0:T(128)} %bitcast.refs_0_, s32[1,128]{1,0:T(1,128)} %index_ref.1, ...), custom_call_target="tpu_custom_call" | custom-call | flops 1073741824 | bytes 6291456 | tf_op jit(solution)/shard_map/decoder_forward/pallas_call | solution.py:167
  21.8 6.2 %all-to-all-start = ((bf16[8,352,128]{2,1,0:T(8,128)(2,1)}), bf16[8,352,128]{2,1,0:T(8,128)(2,1)S(1)}, u32[]{:S(2)}, u32[]{:S(2)}) async-start(bf16[8,352,128]{2,1,0:T(8,128)(2,1)} %get-tuple-element.23), calls=%async_computation | async-start | bytes 1441792 | tf_op jit(solution)/shard_map/all_to_all | solution.py:531
  28.0 2.0 %collective-permute-start.3 = (bf16[256,1024]{1,0:T(8,128)(2,1)S(1)}, bf16[256,1024]{1,0:T(8,128)(2,1)S(1)}, u32[]{:S(2)}, u32[]{:S(2)}) collective-permute-start(bf16[256,1024]{1,0:T(8,128)(2,1)S(1)} %copy-done.9), channel_id=1, source_target_pairs={{0,4},{4,0},{8,12},{12,8},{16,20},{20,16},{24,28},{28,24},{1,5},{5... | collective-permute-start | bytes 1572872 | tf_op jit(solution)/shard_map/ppermute | solution.py:29
  30.1 19.9 %collective-permute-done.3 = bf16[256,1024]{1,0:T(8,128)(2,1)S(1)} collective-permute-done((bf16[256,1024]{1,0:T(8,128)(2,1)S(1)}, bf16[256,1024]{1,0:T(8,128)(2,1)S(1)}, u32[]{:S(2)}, u32[]{:S(2)}) %collective-permute-start.3) | collective-permute-done | bytes 524320 | tf_op jit(solution)/shard_map/ppermute | solution.py:29
  50.0 1.6 %collective-permute-start.5 = (bf16[384,1024]{1,0:T(8,128)(2,1)S(1)}, bf16[384,1024]{1,0:T(8,128)(2,1)S(1)}, u32[]{:S(2)}, u32[]{:S(2)}) collective-permute-start(bf16[384,1024]{1,0:T(8,128)(2,1)S(1)} %pad_maximum_fusion.refs_4_), channel_id=1, source_target_pairs={{0,2},{1,3},{2,0},{3,1},{4,6},{5,7},{6,4},{7,5},{8,10},{9,11},{10,... | collective-permute-start | bytes 2359304 | tf_op jit(solution)/shard_map/ppermute | solution.py:29
  51.8 1.0 constant_dynamic-update-slice_fusion.1
  52.9 0.9 copy-done.2
  53.7 7.2 %decoder_backward.1 = bf16[8,640,128]{2,1,0:T(8,128)(2,1)} custom-call(s32[1]{0:T(128)} %bitcast.2.member_ref, bf16[8,352,128]{2,1,0:T(8,128)(2,1)} %copy-done.2, f32[100,128]{1,0:T(8,128)} %target_ref.1, s32[1,128]{1,0:T(1,128)} %index_ref.1, bf16[128,1024]{1,0:T(8,128)(2,1)} %get-tuple-element.22.refs_3_.query_ref, ...), custom_call_target="tpu_custom_call" | custom-call | flops 536870912 | bytes 4194304 | tf_op jit(solution)/shard_map/decoder_backward/pallas_call | solution.py:341
  60.9 3.6 %all-to-all-start.1 = ((bf16[8,640,128]{2,1,0:T(8,128)(2,1)}), bf16[8,640,128]{2,1,0:T(8,128)(2,1)S(1)}, u32[]{:S(2)}, u32[]{:S(2)}) async-start(bf16[8,640,128]{2,1,0:T(8,128)(2,1)} %decoder_backward.1), calls=%async_computation.1 | async-start | bytes 2621440 | tf_op jit(solution)/shard_map/all_to_all | solution.py:551
  64.5 1.0 constant_dynamic-update-slice_fusion.refs_8_
  65.5 2.0 %collective-permute-start.9 = (bf16[256,1024]{1,0:T(8,128)(2,1)S(1)}, bf16[256,1024]{1,0:T(8,128)(2,1)}, u32[]{:S(2)}, u32[]{:S(2)}) collective-permute-start(bf16[256,1024]{1,0:T(8,128)(2,1)S(1)} %constant_dynamic-update-slice_fusion.refs_8_), channel_id=1, source_target_pairs={{0,2},{1,3},{2,0},{3,1},{4,6},{5,7},{6,4},{7,5},{8,10},{9,11},{10,... | collective-permute-start | bytes 1572872 | tf_op jit(solution)/shard_map/ppermute | solution.py:29
  67.5 2.3 %collective-permute-done.5.refs_6_ = bf16[384,1024]{1,0:T(8,128)(2,1)S(1)} collective-permute-done((bf16[384,1024]{1,0:T(8,128)(2,1)S(1)}, bf16[384,1024]{1,0:T(8,128)(2,1)S(1)}, u32[]{:S(2)}, u32[]{:S(2)}) %collective-permute-start.5) | collective-permute-done | bytes 786464 | tf_op jit(solution)/shard_map/ppermute | solution.py:29
  69.9 0.5 collective-permute-start.8
  70.4 23.9 %collective-permute-done.9.refs_10_ = bf16[256,1024]{1,0:T(8,128)(2,1)} collective-permute-done((bf16[256,1024]{1,0:T(8,128)(2,1)S(1)}, bf16[256,1024]{1,0:T(8,128)(2,1)}, u32[]{:S(2)}, u32[]{:S(2)}) %collective-permute-start.9) | collective-permute-done | bytes 524320 | tf_op jit(solution)/shard_map/ppermute | solution.py:29
  94.2 0.6 pad_add_fusion.place_ref
  94.8 1.7 %collective-permute-done.10.refs_11_ = bf16[256,1024]{1,0:T(8,128)(2,1)} collective-permute-done((bf16[256,1024]{1,0:T(8,128)(2,1)}, bf16[256,1024]{1,0:T(8,128)(2,1)}, u32[]{:S(2)}, u32[]{:S(2)}) %collective-permute-start.10) | collective-permute-done | bytes 524320 | tf_op jit(solution)/shard_map/ppermute | solution.py:29
  96.5 1.1 copy-done
  97.6 5.9 %weight_gradients.1 = (bf16[8,624,128]{2,1,0:T(8,128)(2,1)}, f32[1,1]{1,0:T(1,128)}) custom-call(s32[2]{0:T(128)} %pad_add_fusion.place_ref, bf16[8,640,128]{2,1,0:T(8,128)(2,1)} %copy-done, bf16[128,1024]{1,0:T(8,128)(2,1)} %bitcast.10, bf16[128,1024]{1,0:T(8,128)(2,1)} %copy-done.6, bf16[128,1024]{1,0:T(8,128)(2,1)} %copy-done.5, ...), custom_call_target="tpu_custom_call" | custom-call | flops 1073741824 | bytes 8388608 | tf_op jit(solution)/shard_map/weight_gradients/pallas_call | solution.py:450
  103.5 36.1 %all_to_all.15.blocks_ref = bf16[8,624,128]{2,1,0:T(8,128)(2,1)} all-to-all(bf16[8,624,128]{2,1,0:T(8,128)(2,1)} %get-tuple-element.32), channel_id=1, replica_groups=mesh['ens'=8,'space'=4] {'ens'}, dimensions={0} | all-to-all | bytes 2555904 | tf_op jit(solution)/shard_map/all_to_all | solution.py:562
  139.5 2.3 %sum_groups.1 = (f32[100,1024]{1,0:T(8,128)}, f32[128,256]{1,0:T(8,128)}, f32[128,256]{1,0:T(8,128)}, f32[128,256]{1,0:T(8,128)}, f32[128,256]{1,0:T(8,128)}) custom-call(bf16[8,624,128]{2,1,0:T(8,128)(2,1)} %all_to_all.15.blocks_ref), custom_call_target="tpu_custom_call" | custom-call | tf_op jit(solution)/shard_map/sum_groups/pallas_call | solution.py:488
  (32 shorter events, 0.5 us)
Async XLA Ops:
  0.6 9.6 %collective-permute-start.1 = (bf16[128,1024]{1,0:T(8,128)(2,1)}, bf16[128,1024]{1,0:T(8,128)(2,1)S(1)}, u32[]{:S(2)}, u32[]{:S(2)}) collective-permute-start(bf16[128,1024]{1,0:T(8,128)(2,1)} %bitcast.6), channel_id=1, source_target_pairs={{0,2},{1,3},{2,0},{3,1},{4,6},{5,7},{6,4},{7,5},{8,10},{9,11},{10,... | collective-permute-start | bytes 786440 | tf_op jit(solution)/shard_map/ppermute | solution.py:29
  3.7 10.6 %collective-permute-start = (bf16[128,1024]{1,0:T(8,128)(2,1)}, bf16[128,1024]{1,0:T(8,128)(2,1)S(1)}, u32[]{:S(2)}, u32[]{:S(2)}) collective-permute-start(bf16[128,1024]{1,0:T(8,128)(2,1)} %bitcast.7), channel_id=1, source_target_pairs={{0,1},{1,0},{2,3},{3,2},{4,5},{5,4},{6,7},{7,6},{8,9},{9,8},{10,11... | collective-permute-start | bytes 786440 | tf_op jit(solution)/shard_map/ppermute | solution.py:29
  10.2 4.1 %copy-start.5 = (bf16[128,1024]{1,0:T(8,128)(2,1)}, bf16[128,1024]{1,0:T(8,128)(2,1)S(1)}, u32[]{:S(2)}) copy-start(bf16[128,1024]{1,0:T(8,128)(2,1)S(1)} %collective-permute-done.1.refs_7_.refs_2_) | copy-start | bytes 786436
  10.2 4.1 %collective-permute-start.2 = (bf16[128,1024]{1,0:T(8,128)(2,1)S(1)}, bf16[128,1024]{1,0:T(8,128)(2,1)S(1)}, u32[]{:S(2)}, u32[]{:S(2)}) collective-permute-start(bf16[128,1024]{1,0:T(8,128)(2,1)S(1)} %collective-permute-done.1.refs_7_.refs_2_), channel_id=1, source_target_pairs={{0,1},{1,0},{2,3},{3,2},{4,5},{5,4},{6,7},{7,6},{8,9},{9,8},{10,11... | collective-permute-start | bytes 786440 | tf_op jit(solution)/shard_map/ppermute | solution.py:29
  14.3 0.8 copy-start.6
  14.3 0.8 copy-start.7
  15.1 12.9 %copy-start.9 = (bf16[256,1024]{1,0:T(8,128)(2,1)S(1)}, bf16[256,1024]{1,0:T(8,128)(2,1)}, u32[]{:S(2)}) copy-start(bf16[256,1024]{1,0:T(8,128)(2,1)} %get-tuple-element.29) | copy-start | bytes 1572868
  21.8 28.1 %copy-start.3 = (bf16[1,128,1024]{2,1,0:T(8,128)(2,1)S(1)}, bf16[1,128,1024]{2,1,0:T(8,128)(2,1)}, u32[]{:S(2)}) copy-start(bf16[1,128,1024]{2,1,0:T(8,128)(2,1)} %param.9) | copy-start | bytes 786436
  21.8 31.0 %all-to-all-start = ((bf16[8,352,128]{2,1,0:T(8,128)(2,1)}), bf16[8,352,128]{2,1,0:T(8,128)(2,1)S(1)}, u32[]{:S(2)}, u32[]{:S(2)}) async-start(bf16[8,352,128]{2,1,0:T(8,128)(2,1)} %get-tuple-element.23), calls=%async_computation | async-start | bytes 1441792 | tf_op jit(solution)/shard_map/all_to_all | solution.py:531
  28.0 21.9 %collective-permute-start.3 = (bf16[256,1024]{1,0:T(8,128)(2,1)S(1)}, bf16[256,1024]{1,0:T(8,128)(2,1)S(1)}, u32[]{:S(2)}, u32[]{:S(2)}) collective-permute-start(bf16[256,1024]{1,0:T(8,128)(2,1)S(1)} %copy-done.9), channel_id=1, source_target_pairs={{0,4},{4,0},{8,12},{12,8},{16,20},{20,16},{24,28},{28,24},{1,5},{5... | collective-permute-start | bytes 1572872 | tf_op jit(solution)/shard_map/ppermute | solution.py:29
  50.0 17.6 %copy-start.1 = (bf16[384,1024]{1,0:T(8,128)(2,1)}, bf16[384,1024]{1,0:T(8,128)(2,1)S(1)}, u32[]{:S(2)}) copy-start(bf16[384,1024]{1,0:T(8,128)(2,1)S(1)} %pad_maximum_fusion.refs_4_) | copy-start | bytes 2359300
  50.0 19.9 %collective-permute-start.5 = (bf16[384,1024]{1,0:T(8,128)(2,1)S(1)}, bf16[384,1024]{1,0:T(8,128)(2,1)S(1)}, u32[]{:S(2)}, u32[]{:S(2)}) collective-permute-start(bf16[384,1024]{1,0:T(8,128)(2,1)S(1)} %pad_maximum_fusion.refs_4_), channel_id=1, source_target_pairs={{0,2},{1,3},{2,0},{3,1},{4,6},{5,7},{6,4},{7,5},{8,10},{9,11},{10,... | collective-permute-start | bytes 2359304 | tf_op jit(solution)/shard_map/ppermute | solution.py:29
  51.5 13.0 %collective-permute-start.7 = (bf16[128,1024]{1,0:T(8,128)(2,1)}, bf16[128,1024]{1,0:T(8,128)(2,1)}, u32[]{:S(2)}, u32[]{:S(2)}) collective-permute-start(bf16[128,1024]{1,0:T(8,128)(2,1)} %get-tuple-element.30), channel_id=1, source_target_pairs={{0,4},{4,0},{8,12},{12,8},{16,20},{20,16},{24,28},{28,24},{1,5},{5... | collective-permute-start | bytes 786440 | tf_op jit(solution)/shard_map/ppermute | solution.py:29
  52.8 0.9 copy-start.2
  60.9 35.5 %all-to-all-start.1 = ((bf16[8,640,128]{2,1,0:T(8,128)(2,1)}), bf16[8,640,128]{2,1,0:T(8,128)(2,1)S(1)}, u32[]{:S(2)}, u32[]{:S(2)}) async-start(bf16[8,640,128]{2,1,0:T(8,128)(2,1)} %decoder_backward.1), calls=%async_computation.1 | async-start | bytes 2621440 | tf_op jit(solution)/shard_map/all_to_all | solution.py:551
  65.5 31.0 %copy-start.4 = (bf16[256,1024]{1,0:T(8,128)(2,1)}, bf16[256,1024]{1,0:T(8,128)(2,1)S(1)}, u32[]{:S(2)}) copy-start(bf16[256,1024]{1,0:T(8,128)(2,1)S(1)} %constant_dynamic-update-slice_fusion.refs_8_) | copy-start | bytes 1572868
  65.5 28.7 %collective-permute-start.9 = (bf16[256,1024]{1,0:T(8,128)(2,1)S(1)}, bf16[256,1024]{1,0:T(8,128)(2,1)}, u32[]{:S(2)}, u32[]{:S(2)}) collective-permute-start(bf16[256,1024]{1,0:T(8,128)(2,1)S(1)} %constant_dynamic-update-slice_fusion.refs_8_), channel_id=1, source_target_pairs={{0,2},{1,3},{2,0},{3,1},{4,6},{5,7},{6,4},{7,5},{8,10},{9,11},{10,... | collective-permute-start | bytes 1572872 | tf_op jit(solution)/shard_map/ppermute | solution.py:29
  67.5 27.3 %collective-permute-start.4 = (bf16[384,1024]{1,0:T(8,128)(2,1)S(1)}, bf16[384,1024]{1,0:T(8,128)(2,1)}, u32[]{:S(2)}, u32[]{:S(2)}) collective-permute-start(bf16[384,1024]{1,0:T(8,128)(2,1)S(1)} %pad_maximum_fusion.refs_4_), channel_id=1, source_target_pairs={{0,1},{1,0},{2,3},{3,2},{4,5},{5,4},{6,7},{7,6},{8,9},{9,8},{10,11... | collective-permute-start | bytes 2359304 | tf_op jit(solution)/shard_map/ppermute | solution.py:29
  69.9 26.6 %copy-start.8 = (bf16[384,1024]{1,0:T(8,128)(2,1)}, bf16[384,1024]{1,0:T(8,128)(2,1)S(1)}, u32[]{:S(2)}) copy-start(bf16[384,1024]{1,0:T(8,128)(2,1)S(1)} %collective-permute-done.5.refs_6_) | copy-start | bytes 2359300
  69.9 26.6 %collective-permute-start.6 = (bf16[384,1024]{1,0:T(8,128)(2,1)S(1)}, bf16[384,1024]{1,0:T(8,128)(2,1)}, u32[]{:S(2)}, u32[]{:S(2)}) collective-permute-start(bf16[384,1024]{1,0:T(8,128)(2,1)S(1)} %collective-permute-done.5.refs_6_), channel_id=1, source_target_pairs={{0,1},{1,0},{2,3},{3,2},{4,5},{5,4},{6,7},{7,6},{8,9},{9,8},{10,11... | collective-permute-start | bytes 2359304 | tf_op jit(solution)/shard_map/ppermute | solution.py:29
  69.9 25.0 %collective-permute-start.8 = (bf16[256,1024]{1,0:T(8,128)(2,1)S(1)}, bf16[256,1024]{1,0:T(8,128)(2,1)}, u32[]{:S(2)}, u32[]{:S(2)}) collective-permute-start(bf16[256,1024]{1,0:T(8,128)(2,1)S(1)} %constant_dynamic-update-slice_fusion.refs_8_), channel_id=1, source_target_pairs={{0,1},{1,0},{2,3},{3,2},{4,5},{5,4},{6,7},{7,6},{8,9},{9,8},{10,11... | collective-permute-start | bytes 1572872 | tf_op jit(solution)/shard_map/ppermute | solution.py:29
  94.2 2.3 %collective-permute-start.10 = (bf16[256,1024]{1,0:T(8,128)(2,1)}, bf16[256,1024]{1,0:T(8,128)(2,1)}, u32[]{:S(2)}, u32[]{:S(2)}) collective-permute-start(bf16[256,1024]{1,0:T(8,128)(2,1)} %collective-permute-done.9.refs_10_), channel_id=1, source_target_pairs={{0,1},{1,0},{2,3},{3,2},{4,5},{5,4},{6,7},{7,6},{8,9},{9,8},{10,11... | collective-permute-start | bytes 1572872 | tf_op jit(solution)/shard_map/ppermute | solution.py:29
  96.5 1.1 copy-start

commit v5 on v4

--- a/solution.py
+++ b/solution.py
@@ -140,18 +140,11 @@
     forecast = dot32(readout_ref[...], normed_b, (1, 1))
     high = forecast.astype(BF16)
     low = (forecast - high.astype(F32)).astype(BF16)
-    depth = features // members
-    pieces = LANES // depth
-    part = points // pieces
-    channels = (packed_ref.shape[1] - part) // 2
+    channels = packed_ref.shape[1] // 2
     spare = jnp.zeros((channels - readout_ref.shape[0], points), BF16)
     fields = jnp.concatenate([high, spare, low, spare], axis=0)
     for m in range(members):
-        packed_ref[m, : 2 * channels] = fields
-        for p in range(pieces):
-            packed_ref[m, 2 * channels :, p * depth : (p + 1) * depth] = normed_b[
-                p * part : (p + 1) * part, m * depth : (m + 1) * depth
-            ]
+        packed_ref[m] = fields
 
 
 def padded(channels):
@@ -161,8 +154,6 @@
 def forward(shard, index, grid_rows, queries, readout, latents, weights, members):
     points, features = grid_rows.shape
     channels = padded(readout.shape[0])
-    depth = features // members
-    rows = 2 * channels + points * depth // LANES
     shape = jax.ShapeDtypeStruct
     return pl.pallas_call(
         functools.partial(forward_kernel, len(latents), members),
@@ -173,7 +164,7 @@
             shape((points, features), BF16),
             shape((points, features), F32),
             shape((points, 1), F32),
-            shape((members, rows, LANES), BF16),
+            shape((members, 2 * channels, points), BF16),
         ),
         in_specs=[SMEM] + [VMEM] * (4 + len(latents)) + [ANY] * 3,
         out_specs=(VMEM,) * 7,
@@ -192,7 +183,7 @@
     shards,
     blocks,
     nodes,
-    member_ref,
+    place_ref,
     packed_ref,
     target_ref,
     index_ref,
@@ -205,6 +196,7 @@
     readout_ref,
     w_hbm,
     out_ref,
+    outer_ref,
     w_ref,
     slope_ref,
     d_attended_ref,
@@ -223,7 +215,7 @@
         full[:channels_used] = used[...]
         spare = (channels - channels_used, used.shape[1])
         full[channels_used:] = jnp.zeros(spare, used.dtype)
-    width, depth = features // blocks, features // members
+    width = features // blocks
     weight = (channels_used * points * shards) ** (-0.5)
     pair_weight = 1.0 / (members * (members - 1))
     chunk = 16
@@ -263,26 +255,13 @@
     loss = lax.fori_loop(0, channels // chunk, crps, jnp.zeros((chunk, points), F32))
     loss = weight * jnp.sum(jnp.sum(loss, axis=0, keepdims=True), axis=1, keepdims=True)
 
-    pieces = LANES // depth
-    part = points // pieces
-    total = jnp.zeros((channels, depth), F32)
-    for m in range(members):
-        tail = packed_ref[m, 2 * channels :]
-        for p in range(pieces):
-            total = total + dot32(
-                slope_ref[m][:, p * part : (p + 1) * part], tail[:, p * depth : (p + 1) * depth]
-            )
-    rows = channels * depth // width
-    for p in range(width // depth):
-        small_ref[:rows, p * depth : (p + 1) * depth] = total[p * rows : (p + 1) * rows]
     first = loss.astype(BF16).astype(F32)
     second = (loss - first).astype(BF16).astype(F32)
     for i, value in enumerate((first, second, loss - first - second)):
-        small_ref[rows + i : rows + i + 1] = jnp.broadcast_to(value, (1, width))
-    spare = small_ref.shape[0] - rows - 3
-    small_ref[rows + 3 :] = jnp.zeros((spare, width), F32)
+        small_ref[i : i + 1] = jnp.broadcast_to(value, (1, width))
+    small_ref[3:] = jnp.zeros((small_ref.shape[0] - 3, width), F32)
     index = index_ref[...]
-    line = rows + 3
+    line = 3
     for tag in (index // nodes, index % nodes):
         step = min(points, width)
         for c in range(0, points, step):
@@ -300,8 +279,16 @@
                 :, c : c + step
             ]
 
-    own = slope_ref[member_ref[0]]
+    own = slope_ref[place_ref[1]]
     normed = normed_ref[...]
+    outer = dot32(own, normed.astype(BF16))
+    columns = features // shards
+    parts = [outer[:, s * columns : (s + 1) * columns] for s in range(shards)]
+    for k in range(shards):
+        part = parts[0]
+        for s in range(1, shards):
+            part = jnp.where((place_ref[0] ^ k) == s, parts[s], part)
+        outer_ref[k] = part.astype(BF16)
     d_normed = dot32(own, weight_ref[...], (0, 0))
     mean = jnp.mean(d_normed * normed, axis=-1, keepdims=True)
     d_hidden = (inverse_ref[...] * (d_normed - normed * mean)).astype(BF16)
@@ -326,23 +313,21 @@
         put(1, pair * LANES, joined(dot32(d_scores, query_ref[:, at], (0, 0))).astype(BF16))
 
 
-def small_rows(channels, depth, width):
-    rows = channels * depth // width + MISC
-    return rows + -rows % 16
-
-
-def backward(member, packed, target, index, saved, readout, w_mix, shards, blocks, nodes):
+def backward(place, packed, target, index, saved, readout, w_mix, shards, blocks, nodes):
     members = packed.shape[0]
     features = w_mix.shape[0]
     points = saved[0].shape[0]
     channels = padded(readout.shape[0])
-    width, depth = features // blocks, features // members
-    small = small_rows(channels, depth, width)
+    width = features // blocks
+    small = 16
     return pl.pallas_call(
         functools.partial(backward_kernel, shards, blocks, nodes),
-        out_shape=jax.ShapeDtypeStruct((blocks, 4 * points + small, width), BF16),
+        out_shape=(
+            jax.ShapeDtypeStruct((blocks, 4 * points + small, width), BF16),
+            jax.ShapeDtypeStruct((shards, channels, features // shards), BF16),
+        ),
         in_specs=[SMEM] + [VMEM] * 10 + [ANY],
-        out_specs=VMEM,
+        out_specs=(VMEM, VMEM),
         scratch_shapes=[
             pltpu.VMEM((features, features), BF16),
             pltpu.VMEM((members, channels, points), BF16),
@@ -358,34 +343,24 @@
             transcendentals=0,
         ),
         name="decoder_backward",
-    )(member, packed, target, index, *saved, readout, w_mix)
-
-
-def gradient_kernel(shards, pair, members, nodes, channels, place_ref, blocks_ref, *refs):
-    latent_refs, early_refs, late_refs = (refs[i * shards : (i + 1) * shards] for i in range(3))
-    out_ref, loss_ref = refs[3 * shards :]
+    )(place, packed, target, index, *saved, readout, w_mix)
+
+
+def gradient_kernel(shards, pair, members, nodes, place_ref, blocks_ref, *refs):
+    latent_refs, early_refs, late_refs, grid_refs = (
+        refs[i * shards : (i + 1) * shards] for i in range(4)
+    )
+    out_ref, loss_ref = refs[4 * shards :]
     width = blocks_ref.shape[2]
     features = late_refs[0].shape[1]
     points = late_refs[0].shape[0] // pair
     depth = features // members
     shard, half = place_ref[0], place_ref[1]
-    rows = channels * depth // width
     start = 4 * points
-    parts = []
-    for t in range(pair):
-        total = jnp.zeros((blocks_ref.shape[1] - start, width), F32)
-        for s in range(shards):
-            total = total + blocks_ref[s * pair + t, start:].astype(F32)
-        if t == 0:
-            loss = jnp.sum(total[rows : rows + 3, :1], axis=0, keepdims=True)
-        parts.append(total[:rows])
-    loss_ref[...] = loss
-    small = parts[0]
-    if pair > 1:
-        small = jnp.where(half == 0, parts[0], parts[1])
-    small = small.astype(BF16)
-    for m in range(members):
-        out_ref[m, 4 * width :] = small
+    total = blocks_ref[0, start:].astype(F32)
+    for s in range(1, shards):
+        total = total + blocks_ref[s * pair, start:].astype(F32)
+    loss_ref[...] = jnp.sum(total[:3, :1], axis=0, keepdims=True)
 
     def slots(kind, t):
         at = slice(kind * points, (kind + 1) * points)
@@ -409,7 +384,7 @@
     product(3, [rows_of(late_refs, t) for t in range(pair)])
     chosen = []
     for k in range(shards):
-        index = blocks_ref[(shard ^ k) * pair, start + rows : start + rows + MISC].astype(jnp.int32)
+        index = blocks_ref[(shard ^ k) * pair, start : start + MISC].astype(jnp.int32)
         lines = max(points // width, 1)
         owner, offset = (
             jnp.concatenate([index[3 + b + i : 4 + b + i] for i in range(lines)], axis=1)
@@ -425,7 +400,7 @@
         sums.append(dot32(chosen, jnp.concatenate(both, axis=1)).astype(BF16))
     others = [[ref[...] for ref in latent_refs]]
     if pair > 1:
-        others.append([ref[points : points + nodes] for ref in early_refs])
+        others.append([ref[:nodes] for ref in early_refs])
     put(
         1,
         dot32(
@@ -434,28 +409,27 @@
             (0, 0),
         ),
     )
-    grids = [rows_of(early_refs, 0)]
+    grids = [[ref[...] for ref in grid_refs]]
     if pair > 1:
-        grids.append([ref[points + nodes :] for ref in early_refs])
+        grids.append([ref[nodes:] for ref in early_refs])
     product(0, grids)
 
 
-def gradients(place, blocks, latents, early, late, members, pair, channels):
+def gradients(place, blocks, latents, early, late, grids, members, pair):
     count, _, width = blocks.shape
     shards = count // pair
     features = late[0].shape[1]
     points = late[0].shape[0] // pair
     depth = features // members
-    rows = 4 * width + channels
     return pl.pallas_call(
         functools.partial(
-            gradient_kernel, shards, pair, members, latents[0].shape[0], channels
+            gradient_kernel, shards, pair, members, latents[0].shape[0]
         ),
         out_shape=(
-            jax.ShapeDtypeStruct((members, rows, depth), BF16),
+            jax.ShapeDtypeStruct((members, 4 * width, depth), BF16),
             jax.ShapeDtypeStruct((1, 1), F32),
         ),
-        in_specs=[SMEM] + [VMEM] * (1 + 3 * shards),
+        in_specs=[SMEM] + [VMEM] * (1 + 4 * shards),
         out_specs=(VMEM, VMEM),
         cost_estimate=pl.CostEstimate(
             flops=8 * points * count * features * width,
@@ -463,36 +437,68 @@
             transcendentals=0,
         ),
         name="weight_gradients",
-    )(place, blocks, *latents, *early, *late)
-
-
-def sum_kernel(pair, blocks_ref, out_ref, *refs):
-    members, _, depth = blocks_ref.shape
-    used = out_ref.shape[0]
-    width = refs[0].shape[1] // pair
-    for m in range(members):
-        out_ref[:, m * depth : (m + 1) * depth] = blocks_ref[m, 4 * width : 4 * width + used].astype(F32)
-    for i in range(4):
+    )(place, blocks, *latents, *early, *late, *grids)
+
+
+def sum_kernel(pair, blocks_ref, *refs):
+    members, rows, _ = blocks_ref.shape
+    width = rows // len(refs)
+    for i, ref in enumerate(refs):
         at = slice(i * width, (i + 1) * width)
         for y in range(pair):
             total = blocks_ref[y, at].astype(F32)
             for m in range(y + pair, members, pair):
                 total = total + blocks_ref[m, at].astype(F32)
-            refs[i][:, y * width : (y + 1) * width] = total.T
-
-
-def sum_groups(blocks, pair, channels_used):
-    members, rows, depth = blocks.shape
-    width = (rows - padded(channels_used)) // 4
-    shape = jax.ShapeDtypeStruct
+            ref[:, y * width : (y + 1) * width] = total.T
+
+
+def sum_groups(blocks, pair):
+    _, rows, depth = blocks.shape
     return pl.pallas_call(
         functools.partial(sum_kernel, pair),
-        out_shape=(shape((channels_used, depth * members), F32),)
-        + (shape((depth, pair * width), F32),) * 4,
+        out_shape=(jax.ShapeDtypeStruct((depth, pair * rows // 4), F32),) * 4,
         in_specs=[VMEM],
-        out_specs=(VMEM,) * 5,
+        out_specs=(VMEM,) * 4,
         name="sum_groups",
     )(blocks)
+
+
+def join_kernel(shard_ref, *refs):
+    *slot_refs, out_ref = refs
+    used, columns = out_ref.shape[0], slot_refs[0].shape[1]
+    values = [ref[...].astype(F32) for ref in slot_refs]
+    for s in range(len(values)):
+        value = values[0]
+        for k in range(1, len(values)):
+            value = jnp.where((shard_ref[0] ^ k) == s, values[k], value)
+        out_ref[:, s * columns : (s + 1) * columns] = value[:used]
+
+
+def join_columns(shard, parts, channels_used):
+    columns = parts[0].shape[1] * len(parts)
+    return pl.pallas_call(
+        join_kernel,
+        out_shape=jax.ShapeDtypeStruct((channels_used, columns), F32),
+        in_specs=[SMEM] + [VMEM] * len(parts),
+        out_specs=VMEM,
+        name="join_columns",
+    )(shard, *parts)
+
+
+def sum_outer(parts):
+    total = parts[0].astype(F32)
+    received = []
+    for k in range(1, parts.shape[0]):
+        received.append(swap(parts[k], "space", k))
+    for value in received:
+        total = total + value.astype(F32)
+    total = total.astype(BF16)
+    bit = 1
+    while bit < lax.axis_size("ens"):
+        other = swap(total, "ens", bit)
+        total = (total.astype(F32) + other.astype(F32)).astype(BF16)
+        bit = 2 * bit
+    return gather_slots(total, "space")
 
 
 def body(
@@ -512,11 +518,12 @@
 
     own_latent, grid_rows = latent[0], grid_hidden[0]
     latents = gather_slots(own_latent, "space")
+    grids = gather_slots(grid_rows, "space")
     queries, both = project_queries(own_latent, grid_rows, w_query)
-    early = grid_rows
+    early = latents
     if pair > 1:
-        partner = swap(both, "ens", 1)
-        early = jnp.concatenate([grid_rows, partner])
+        early = swap(both, "ens", 1)
+        early = gather_slots(early, "space")
     *saved, packed = forward(
         shard[None],
         tile_neighbor_index,
@@ -533,11 +540,10 @@
     if pair > 1:
         partner = swap(attended, "ens", 1)
         late = jnp.concatenate([attended, partner])
-    early = gather_slots(early, "space")
     late = gather_slots(late, "space")
     saved = (queries, keyset, valueset, soft, normed, inverse)
-    blocks = backward(
-        member[None],
+    blocks, outer = backward(
+        jnp.stack([shard, member]),
         packed,
         target,
         tile_neighbor_index,
@@ -557,10 +563,11 @@
         tiled=True,
     )
     place = jnp.stack([shard, half])
-    channels = padded(channels_used)
-    blocks, loss = gradients(place, blocks, latents, early, late, members, pair, channels)
+    outer = sum_outer(outer)
+    blocks, loss = gradients(place, blocks, latents, early, late, grids, members, pair)
     blocks = lax.all_to_all(blocks, "ens", split_axis=0, concat_axis=0, tiled=True)
-    grad_out, *grads = sum_groups(blocks, pair, channels_used)
+    grad_out = join_columns(shard[None], outer, channels_used)
+    grads = sum_groups(blocks, pair)
     return (loss.reshape(()), grad_out, *grads)
 
 

time: 142 us -> 130 us (0.915)
  blocking collectives: 36.1 us -> 0 us
  starting transfers between devices: 19.2 us -> 37.8 us
  waiting for transfers between devices: 54.2 us -> 56.2 us
    all_to_all x1 -> x0, blocking collectives: 36.1 us -> none  [body(): lax.all_to_all(blocks, 'ens', split_axis=0, concat_axis=0, tiled=True)]
    ppermute x11 -> x23, starting transfers between devices: 9.41 us -> 23.6 us  [swap(): return lax.ppermute(value, axis, [(i, i ^ bits) for i in range(size)])]
    all_to_all x0 -> x1, starting transfers between devices: none -> 5.59 us  [body(): lax.all_to_all(blocks, 'ens', split_axis=0, concat_axis=0, tiled=True)]
    unnamed x21 -> x37, local copies, waits for them, and re-layouts: 3.77 us -> 5.85 us
    ppermute x11 -> x23, waiting for transfers between devices: 54.2 us -> 56.2 us  [swap(): return lax.ppermute(value, axis, [(i, i ^ bits) for i in range(size)])]
    pallas_call x1 -> x2, Pallas kernels: 2.33 us -> 3.85 us  [the longest x1 2.12 us: sum_groups(): pl.pallas_call(functools.partial(sum_kernel, pair), out_shape=(jax.ShapeD...]
  transfers between devices with their start and end apart: 13 -> 26, of which waited for: 5 -> 11; matrix products, arithmetic and copies ran while one was open for 2% -> 2% of each run, Pallas kernels for 8% -> 15%
where the time goes in v5:
time: 130 us
  waiting for transfers between devices  56.2 us (43%)
  starting transfers between devices  37.8 us (29%)
  Pallas kernels  27.6 us (21%)
  local copies, waits for them, and re-layouts  5.89 us (5%)
    ppermute x23, waiting for transfers between devices, swap(): return lax.ppermute(value, axis, [(i, i ^ bits) for i in range(size)])  56.2 us
    ppermute x23, starting transfers between devices, swap(): return lax.ppermute(value, axis, [(i, i ^ bits) for i in range(size)])  23.6 us
    pallas_call x1, Pallas kernels, backward(): pl.pallas_call(functools.partial(backward_kernel, shards, blocks, nodes),...  7.34 us
    pallas_call x1, Pallas kernels, forward(): pl.pallas_call(functools.partial(forward_kernel, len(latents), members),...  6.58 us
    unnamed x37, local copies, waits for them, and re-layouts  5.85 us
    pallas_call x1, Pallas kernels, gradients(): pl.pallas_call(functools.partial(gradient_kernel, shards, pair, members,...  5.77 us
    all_to_all x1, starting transfers between devices, body(): lax.all_to_all(blocks, 'ens', split_axis=0, concat_axis=0, tiled=True)  5.59 us
    all_to_all x1, starting transfers between devices, body(): lax.all_to_all(packed, 'ens', split_axis=0, concat_axis=0, tiled=True)  4.89 us
  transfers between devices with their start and end apart: 26, of which 11 were waited for; matrix products, arithmetic and copies ran while one was open for 2% of the time, Pallas kernels for 15%

profile of v5, /device:TPU:0, one launch (start us, length us, event | category | flops | bytes accessed | tf_op | source)
XLA Modules:
  0.0 129.5 jit_solution(17643202966198840375)
XLA Ops:
  0.6 3.0 %collective-permute-start.1 = (bf16[128,1024]{1,0:T(8,128)(2,1)}, bf16[128,1024]{1,0:T(8,128)(2,1)S(1)}, u32[]{:S(2)}, u32[]{:S(2)}) collective-permute-start(bf16[128,1024]{1,0:T(8,128)(2,1)} %bitcast.20), channel_id=1, source_target_pairs={{0,2},{1,3},{2,0},{3,1},{4,6},{5,7},{6,4},{7,5},{8,10},{9,11},{10,... | collective-permute-start | bytes 786440 | tf_op jit(solution)/shard_map/ppermute | solution.py:29
  3.7 6.5 %collective-permute-done.1.refs_7_.refs_2_ = bf16[128,1024]{1,0:T(8,128)(2,1)S(1)} collective-permute-done((bf16[128,1024]{1,0:T(8,128)(2,1)}, bf16[128,1024]{1,0:T(8,128)(2,1)S(1)}, u32[]{:S(2)}, u32[]{:S(2)}) %collective-permute-start.1) | collective-permute-done | bytes 262176 | tf_op jit(solution)/shard_map/ppermute | solution.py:29
  10.2 4.0 %project_queries.1 = (bf16[128,1024]{1,0:T(8,128)(2,1)}, bf16[256,1024]{1,0:T(8,128)(2,1)}) custom-call(bf16[128,1024]{1,0:T(8,128)(2,1)} %bitcast.22, bf16[128,1024]{1,0:T(8,128)(2,1)} %bitcast.15, bf16[1024,1024]{1,0:T(8,128)(2,1)} %w_hbm.2), custom_call_target="tpu_custom_call" | custom-call | flops 268435456 | bytes 2097152 | tf_op jit(solution)/shard_map/project_queries/pallas_call | solution.py:72
  14.2 1.8 %collective-permute-start.3 = (bf16[256,1024]{1,0:T(8,128)(2,1)}, bf16[256,1024]{1,0:T(8,128)(2,1)S(1)}, u32[]{:S(2)}, u32[]{:S(2)}) collective-permute-start(bf16[256,1024]{1,0:T(8,128)(2,1)} %get-tuple-element.31), channel_id=1, source_target_pairs={{0,4},{4,0},{8,12},{12,8},{16,20},{20,16},{24,28},{28,24},{1,5},{5... | collective-permute-start | bytes 1572872 | tf_op jit(solution)/shard_map/ppermute | solution.py:29
  16.9 6.6 %decoder_forward.1 = (bf16[128,1024]{1,0:T(8,128)(2,1)}, bf16[128,1024]{1,0:T(8,128)(2,1)}, f32[8,128,256]{2,1,0:T(8,128)}, bf16[128,1024]{1,0:T(8,128)(2,1)}, f...) custom-call(s32[1]{0:T(128)} %bitcast.refs_0_.shard_ref, s32[1,128]{1,0:T(1,128)} %index_ref.1, ...), custom_call_target="tpu_custom_call" | custom-call | flops 1073741824 | bytes 6291456 | tf_op jit(solution)/shard_map/decoder_forward/pallas_call | solution.py:158
  23.4 4.9 %all-to-all-start = ((bf16[8,224,128]{2,1,0:T(8,128)(2,1)}), bf16[8,224,128]{2,1,0:T(8,128)(2,1)S(1)}, u32[]{:S(2)}, u32[]{:S(2)}) async-start(bf16[8,224,128]{2,1,0:T(8,128)(2,1)} %get-tuple-element.24), calls=%async_computation | async-start | bytes 917504 | tf_op jit(solution)/shard_map/all_to_all | solution.py:538
  28.3 2.0 %collective-permute-start.7 = (bf16[128,1024]{1,0:T(8,128)(2,1)}, bf16[128,1024]{1,0:T(8,128)(2,1)S(1)}, u32[]{:S(2)}, u32[]{:S(2)}) collective-permute-start(bf16[128,1024]{1,0:T(8,128)(2,1)} %get-tuple-element.32), channel_id=1, source_target_pairs={{0,4},{4,0},{8,12},{12,8},{16,20},{20,16},{24,28},{28,24},{1,5},{5... | collective-permute-start | bytes 786440 | tf_op jit(solution)/shard_map/ppermute | solution.py:29
  32.8 8.7 %collective-permute-done.7 = bf16[128,1024]{1,0:T(8,128)(2,1)S(1)} collective-permute-done((bf16[128,1024]{1,0:T(8,128)(2,1)}, bf16[128,1024]{1,0:T(8,128)(2,1)S(1)}, u32[]{:S(2)}, u32[]{:S(2)}) %collective-permute-start.7) | collective-permute-done | bytes 262176 | tf_op jit(solution)/shard_map/ppermute | solution.py:29
  41.5 1.6 %collective-permute-start.9 = (bf16[256,1024]{1,0:T(8,128)(2,1)S(1)}, bf16[256,1024]{1,0:T(8,128)(2,1)}, u32[]{:S(2)}, u32[]{:S(2)}) collective-permute-start(bf16[256,1024]{1,0:T(8,128)(2,1)S(1)} %constant_dynamic-update-slice_fusion.refs_8_), channel_id=1, source_target_pairs={{0,2},{1,3},{2,0},{3,1},{4,6},{5,7},{6,4},{7,5},{8,10},{9,11},{10,... | collective-permute-start | bytes 1572872 | tf_op jit(solution)/shard_map/ppermute | solution.py:29
  44.5 7.3 %decoder_backward.1 = (bf16[8,528,128]{2,1,0:T(8,128)(2,1)}, bf16[4,112,256]{2,1,0:T(8,128)(2,1)}) custom-call(s32[2]{0:T(128)} %pad_add_fusion.1.place_ref, bf16[8,224,128]{2,1,0:T(8,128)(2,1)} %copy-done.3, f32[100,128]{1,0:T(8,128)} %target_ref.1, s32[1,128]{1,0:T(1,128)} %index_ref.1, bf16[128,1024]{1,0:T(8,128)(2,1)} %get-tuple-element.23.refs_3_.query_ref, ...), custom_call_target="tpu_custom_call" | custom-call | flops 536870912 | bytes 4194304 | tf_op jit(solution)/shard_map/decoder_backward/pallas_call | solution.py:323
  51.8 3.7 %all-to-all-start.1 = ((bf16[8,528,128]{2,1,0:T(8,128)(2,1)}), bf16[8,528,128]{2,1,0:T(8,128)(2,1)S(1)}, u32[]{:S(2)}, u32[]{:S(2)}) async-start(bf16[8,528,128]{2,1,0:T(8,128)(2,1)} %get-tuple-element.30), calls=%async_computation.1 | async-start | bytes 2162688 | tf_op jit(solution)/shard_map/all_to_all | solution.py:557
  56.0 1.7 %collective-permute-start.12 = (bf16[128,1024]{1,0:T(8,128)(2,1)S(1)}, bf16[128,1024]{1,0:T(8,128)(2,1)S(1)}, u32[]{:S(2)}, u32[]{:S(2)}) collective-permute-start(bf16[128,1024]{1,0:T(8,128)(2,1)S(1)} %bitcast.19), channel_id=1, source_target_pairs={{0,2},{1,3},{2,0},{3,1},{4,6},{5,7},{6,4},{7,5},{8,10},{9,11},{10,... | collective-permute-start | bytes 786440 | tf_op jit(solution)/shard_map/ppermute | solution.py:29
  58.7 17.3 %collective-permute-done.12.refs_14_ = bf16[128,1024]{1,0:T(8,128)(2,1)S(1)} collective-permute-done((bf16[128,1024]{1,0:T(8,128)(2,1)S(1)}, bf16[128,1024]{1,0:T(8,128)(2,1)S(1)}, u32[]{:S(2)}, u32[]{:S(2)}) %collective-permute-start.12) | collective-permute-done | bytes 262176 | tf_op jit(solution)/shard_map/ppermute | solution.py:29
  79.3 5.8 %weight_gradients.1 = (bf16[8,512,128]{2,1,0:T(8,128)(2,1)}, f32[1,1]{1,0:T(1,128)}) custom-call(s32[2]{0:T(128)} %pad_add_fusion.place_ref, bf16[8,528,128]{2,1,0:T(8,128)(2,1)} %copy-done, bf16[128,1024]{1,0:T(8,128)(2,1)} %bitcast.24, bf16[128,1024]{1,0:T(8,128)(2,1)} %copy-done.6, bf16[128,1024]{1,0:T(8,128)(2,1)} %copy-done.5, ...), custom_call_target="tpu_custom_call" | custom-call | flops 1073741824 | bytes 8388608 | tf_op jit(solution)/shard_map/weight_gradients/pallas_call | solution.py:424
  85.0 5.6 %all-to-all-start.2 = ((bf16[8,512,128]{2,1,0:T(8,128)(2,1)}), bf16[8,512,128]{2,1,0:T(8,128)(2,1)S(1)}, u32[]{:S(2)}, u32[]{:S(2)}) async-start(bf16[8,512,128]{2,1,0:T(8,128)(2,1)} %get-tuple-element.35), calls=%async_computation.2 | async-start | bytes 2097152 | tf_op jit(solution)/shard_map/all_to_all | solution.py:568
  92.6 2.3 %collective-permute-done.16 = bf16[112,256]{1,0:T(8,128)(2,1)S(1)} collective-permute-done((bf16[112,256]{1,0:T(8,128)(2,1)S(1)}, bf16[112,256]{1,0:T(8,128)(2,1)S(1)}, u32[]{:S(2)}, u32[]{:S(2)}) %collective-permute-start.16) | collective-permute-done | bytes 57376 | tf_op jit(solution)/shard_map/ppermute | solution.py:29
  96.2 1.6 %collective-permute-start.17 = (bf16[112,256]{1,0:T(8,128)(2,1)S(1)}, bf16[112,256]{1,0:T(8,128)(2,1)S(1)}, u32[]{:S(2)}, u32[]{:S(2)}) collective-permute-start(bf16[112,256]{1,0:T(8,128)(2,1)S(1)} %fusion.2), channel_id=1, source_target_pairs={{0,4},{4,0},{8,12},{12,8},{16,20},{20,16},{24,28},{28,24},{1,5},{5... | collective-permute-start | bytes 172040 | tf_op jit(solution)/shard_map/ppermute | solution.py:29
  97.8 4.7 %collective-permute-done.17 = bf16[112,256]{1,0:T(8,128)(2,1)S(1)} collective-permute-done((bf16[112,256]{1,0:T(8,128)(2,1)S(1)}, bf16[112,256]{1,0:T(8,128)(2,1)S(1)}, u32[]{:S(2)}, u32[]{:S(2)}) %collective-permute-start.17) | collective-permute-done | bytes 57376 | tf_op jit(solution)/shard_map/ppermute | solution.py:29
  102.6 7.3 %collective-permute-done.18 = bf16[112,256]{1,0:T(8,128)(2,1)S(1)} collective-permute-done((bf16[112,256]{1,0:T(8,128)(2,1)S(1)}, bf16[112,256]{1,0:T(8,128)(2,1)S(1)}, u32[]{:S(2)}, u32[]{:S(2)}) %collective-permute-start.18) | collective-permute-done | bytes 57376 | tf_op jit(solution)/shard_map/ppermute | solution.py:29
  109.9 6.4 %collective-permute-start.19 = (bf16[112,256]{1,0:T(8,128)(2,1)S(1)}, bf16[112,256]{1,0:T(8,128)(2,1)S(1)}, u32[]{:S(2)}, u32[]{:S(2)}) collective-permute-start(bf16[112,256]{1,0:T(8,128)(2,1)S(1)} %add_convert_fusion.1), channel_id=1, source_target_pairs={{0,16},{4,20},{8,24},{12,28},{16,0},{20,4},{24,8},{28,12},{1,17},{... | collective-permute-start | bytes 172040 | tf_op jit(solution)/shard_map/ppermute | solution.py:29
  116.2 2.3 %collective-permute-done.19 = bf16[112,256]{1,0:T(8,128)(2,1)S(1)} collective-permute-done((bf16[112,256]{1,0:T(8,128)(2,1)S(1)}, bf16[112,256]{1,0:T(8,128)(2,1)S(1)}, u32[]{:S(2)}, u32[]{:S(2)}) %collective-permute-start.19) | collective-permute-done | bytes 57376 | tf_op jit(solution)/shard_map/ppermute | solution.py:29
  119.2 3.6 %collective-permute-done.21.refs_2_ = bf16[112,256]{1,0:T(8,128)(2,1)S(1)} collective-permute-done((bf16[112,256]{1,0:T(8,128)(2,1)S(1)}, bf16[112,256]{1,0:T(8,128)(2,1)S(1)}, u32[]{:S(2)}, u32[]{:S(2)}) %collective-permute-start.21) | collective-permute-done | bytes 57376 | tf_op jit(solution)/shard_map/ppermute | solution.py:29
  124.7 1.7 %join_columns.1 = f32[100,1024]{1,0:T(8,128)} custom-call(s32[1]{0:T(128)} %bitcast.refs_0_.shard_ref, bf16[112,256]{1,0:T(8,128)(2,1)} %copy-done.13, bf16[112,256]{1,0:T(8,128)(2,1)} %copy-done.16, bf16[112,256]{1,0:T(8,128)(2,1)} %copy-done.15, bf16[112,256]{1,0:T(8,128)(2,1)} %copy-done.17), custom_call_target="tpu_custom_call" | custom-call | tf_op jit(solution)/shard_map/join_columns/pallas_call | solution.py:479
  127.4 2.1 %sum_groups.1 = (f32[128,256]{1,0:T(8,128)}, f32[128,256]{1,0:T(8,128)}, f32[128,256]{1,0:T(8,128)}, f32[128,256]{1,0:T(8,128)}) custom-call(bf16[8,512,128]{2,1,0:T(8,128)(2,1)} %copy-done.1), custom_call_target="tpu_custom_call" | custom-call | tf_op jit(solution)/shard_map/sum_groups/pallas_call | solution.py:457
  (79 shorter events, 16.1 us)
Async XLA Ops:
  0.6 9.6 %collective-permute-start.1 = (bf16[128,1024]{1,0:T(8,128)(2,1)}, bf16[128,1024]{1,0:T(8,128)(2,1)S(1)}, u32[]{:S(2)}, u32[]{:S(2)}) collective-permute-start(bf16[128,1024]{1,0:T(8,128)(2,1)} %bitcast.20), channel_id=1, source_target_pairs={{0,2},{1,3},{2,0},{3,1},{4,6},{5,7},{6,4},{7,5},{8,10},{9,11},{10,... | collective-permute-start | bytes 786440 | tf_op jit(solution)/shard_map/ppermute | solution.py:29
  3.7 12.4 %collective-permute-start = (bf16[128,1024]{1,0:T(8,128)(2,1)}, bf16[128,1024]{1,0:T(8,128)(2,1)S(1)}, u32[]{:S(2)}, u32[]{:S(2)}) collective-permute-start(bf16[128,1024]{1,0:T(8,128)(2,1)} %bitcast.21), channel_id=1, source_target_pairs={{0,1},{1,0},{2,3},{3,2},{4,5},{5,4},{6,7},{7,6},{8,9},{9,8},{10,11... | collective-permute-start | bytes 786440 | tf_op jit(solution)/shard_map/ppermute | solution.py:29
  10.2 5.9 %collective-permute-start.2 = (bf16[128,1024]{1,0:T(8,128)(2,1)S(1)}, bf16[128,1024]{1,0:T(8,128)(2,1)S(1)}, u32[]{:S(2)}, u32[]{:S(2)}) collective-permute-start(bf16[128,1024]{1,0:T(8,128)(2,1)S(1)} %collective-permute-done.1.refs_7_.refs_2_), channel_id=1, source_target_pairs={{0,1},{1,0},{2,3},{3,2},{4,5},{5,4},{6,7},{7,6},{8,9},{9,8},{10,11... | collective-permute-start | bytes 786440 | tf_op jit(solution)/shard_map/ppermute | solution.py:29
  14.2 16.1 %collective-permute-start.3 = (bf16[256,1024]{1,0:T(8,128)(2,1)}, bf16[256,1024]{1,0:T(8,128)(2,1)S(1)}, u32[]{:S(2)}, u32[]{:S(2)}) collective-permute-start(bf16[256,1024]{1,0:T(8,128)(2,1)} %get-tuple-element.31), channel_id=1, source_target_pairs={{0,4},{4,0},{8,12},{12,8},{16,20},{20,16},{24,28},{28,24},{1,5},{5... | collective-permute-start | bytes 1572872 | tf_op jit(solution)/shard_map/ppermute | solution.py:29
  23.4 20.2 %all-to-all-start = ((bf16[8,224,128]{2,1,0:T(8,128)(2,1)}), bf16[8,224,128]{2,1,0:T(8,128)(2,1)S(1)}, u32[]{:S(2)}, u32[]{:S(2)}) async-start(bf16[8,224,128]{2,1,0:T(8,128)(2,1)} %get-tuple-element.24), calls=%async_computation | async-start | bytes 917504 | tf_op jit(solution)/shard_map/all_to_all | solution.py:538
  28.3 13.2 %collective-permute-start.7 = (bf16[128,1024]{1,0:T(8,128)(2,1)}, bf16[128,1024]{1,0:T(8,128)(2,1)S(1)}, u32[]{:S(2)}, u32[]{:S(2)}) collective-permute-start(bf16[128,1024]{1,0:T(8,128)(2,1)} %get-tuple-element.32), channel_id=1, source_target_pairs={{0,4},{4,0},{8,12},{12,8},{16,20},{20,16},{24,28},{28,24},{1,5},{5... | collective-permute-start | bytes 786440 | tf_op jit(solution)/shard_map/ppermute | solution.py:29
  30.4 27.8 %collective-permute-start.5 = (bf16[256,1024]{1,0:T(8,128)(2,1)S(1)}, bf16[256,1024]{1,0:T(8,128)(2,1)S(1)}, u32[]{:S(2)}, u32[]{:S(2)}) collective-permute-start(bf16[256,1024]{1,0:T(8,128)(2,1)S(1)} %collective-permute-done.3.refs_4_), channel_id=1, source_target_pairs={{0,2},{1,3},{2,0},{3,1},{4,6},{5,7},{6,4},{7,5},{8,10},{9,11},{10,... | collective-permute-start | bytes 1572872 | tf_op jit(solution)/shard_map/ppermute | solution.py:29
  41.5 16.7 %collective-permute-start.9 = (bf16[256,1024]{1,0:T(8,128)(2,1)S(1)}, bf16[256,1024]{1,0:T(8,128)(2,1)}, u32[]{:S(2)}, u32[]{:S(2)}) collective-permute-start(bf16[256,1024]{1,0:T(8,128)(2,1)S(1)} %constant_dynamic-update-slice_fusion.refs_8_), channel_id=1, source_target_pairs={{0,2},{1,3},{2,0},{3,1},{4,6},{5,7},{6,4},{7,5},{8,10},{9,11},{10,... | collective-permute-start | bytes 1572872 | tf_op jit(solution)/shard_map/ppermute | solution.py:29
  51.8 25.7 %all-to-all-start.1 = ((bf16[8,528,128]{2,1,0:T(8,128)(2,1)}), bf16[8,528,128]{2,1,0:T(8,128)(2,1)S(1)}, u32[]{:S(2)}, u32[]{:S(2)}) async-start(bf16[8,528,128]{2,1,0:T(8,128)(2,1)} %get-tuple-element.30), calls=%async_computation.1 | async-start | bytes 2162688 | tf_op jit(solution)/shard_map/all_to_all | solution.py:557
  55.6 2.2 %collective-permute-start.11 = (bf16[128,1024]{1,0:T(8,128)(2,1)S(1)}, bf16[128,1024]{1,0:T(8,128)(2,1)S(1)}, u32[]{:S(2)}, u32[]{:S(2)}) collective-permute-start(bf16[128,1024]{1,0:T(8,128)(2,1)S(1)} %bitcast.18), channel_id=1, source_target_pairs={{0,1},{1,0},{2,3},{3,2},{4,5},{5,4},{6,7},{7,6},{8,9},{9,8},{10,11... | collective-permute-start | bytes 786440 | tf_op jit(solution)/shard_map/ppermute | solution.py:29
  56.0 20.0 %collective-permute-start.12 = (bf16[128,1024]{1,0:T(8,128)(2,1)S(1)}, bf16[128,1024]{1,0:T(8,128)(2,1)S(1)}, u32[]{:S(2)}, u32[]{:S(2)}) collective-permute-start(bf16[128,1024]{1,0:T(8,128)(2,1)S(1)} %bitcast.19), channel_id=1, source_target_pairs={{0,2},{1,3},{2,0},{3,1},{4,6},{5,7},{6,4},{7,5},{8,10},{9,11},{10,... | collective-permute-start | bytes 786440 | tf_op jit(solution)/shard_map/ppermute | solution.py:29
  57.6 19.9 %collective-permute-start.4 = (bf16[256,1024]{1,0:T(8,128)(2,1)S(1)}, bf16[256,1024]{1,0:T(8,128)(2,1)}, u32[]{:S(2)}, u32[]{:S(2)}) collective-permute-start(bf16[256,1024]{1,0:T(8,128)(2,1)S(1)} %collective-permute-done.3.refs_4_), channel_id=1, source_target_pairs={{0,1},{1,0},{2,3},{3,2},{4,5},{5,4},{6,7},{7,6},{8,9},{9,8},{10,11... | collective-permute-start | bytes 1572872 | tf_op jit(solution)/shard_map/ppermute | solution.py:29
  57.7 19.8 %collective-permute-start.8 = (bf16[256,1024]{1,0:T(8,128)(2,1)S(1)}, bf16[256,1024]{1,0:T(8,128)(2,1)}, u32[]{:S(2)}, u32[]{:S(2)}) collective-permute-start(bf16[256,1024]{1,0:T(8,128)(2,1)S(1)} %constant_dynamic-update-slice_fusion.refs_8_), channel_id=1, source_target_pairs={{0,1},{1,0},{2,3},{3,2},{4,5},{5,4},{6,7},{7,6},{8,9},{9,8},{10,11... | collective-permute-start | bytes 1572872 | tf_op jit(solution)/shard_map/ppermute | solution.py:29
  58.1 19.4 %collective-permute-start.6 = (bf16[256,1024]{1,0:T(8,128)(2,1)S(1)}, bf16[256,1024]{1,0:T(8,128)(2,1)}, u32[]{:S(2)}, u32[]{:S(2)}) collective-permute-start(bf16[256,1024]{1,0:T(8,128)(2,1)S(1)} %collective-permute-done.5.refs_6_), channel_id=1, source_target_pairs={{0,1},{1,0},{2,3},{3,2},{4,5},{5,4},{6,7},{7,6},{8,9},{9,8},{10,11... | collective-permute-start | bytes 1572872 | tf_op jit(solution)/shard_map/ppermute | solution.py:29
  58.2 19.3 %collective-permute-start.10 = (bf16[256,1024]{1,0:T(8,128)(2,1)}, bf16[256,1024]{1,0:T(8,128)(2,1)}, u32[]{:S(2)}, u32[]{:S(2)}) collective-permute-start(bf16[256,1024]{1,0:T(8,128)(2,1)} %collective-permute-done.9.refs_10_), channel_id=1, source_target_pairs={{0,1},{1,0},{2,3},{3,2},{4,5},{5,4},{6,7},{7,6},{8,9},{9,8},{10,11... | collective-permute-start | bytes 1572872 | tf_op jit(solution)/shard_map/ppermute | solution.py:29
  85.0 41.4 %all-to-all-start.2 = ((bf16[8,512,128]{2,1,0:T(8,128)(2,1)}), bf16[8,512,128]{2,1,0:T(8,128)(2,1)S(1)}, u32[]{:S(2)}, u32[]{:S(2)}) async-start(bf16[8,512,128]{2,1,0:T(8,128)(2,1)} %get-tuple-element.35), calls=%async_computation.2 | async-start | bytes 2097152 | tf_op jit(solution)/shard_map/all_to_all | solution.py:568
  90.6 4.2 %collective-permute-start.16 = (bf16[112,256]{1,0:T(8,128)(2,1)S(1)}, bf16[112,256]{1,0:T(8,128)(2,1)S(1)}, u32[]{:S(2)}, u32[]{:S(2)}) collective-permute-start(bf16[112,256]{1,0:T(8,128)(2,1)S(1)} %get-tuple-element.41), channel_id=1, source_target_pairs={{0,3},{1,2},{2,1},{3,0},{4,7},{5,6},{6,5},{7,4},{8,11},{9,10},{10,... | collective-permute-start | bytes 172040 | tf_op jit(solution)/shard_map/ppermute | solution.py:29
  90.7 5.4 %collective-permute-start.15 = (bf16[112,256]{1,0:T(8,128)(2,1)S(1)}, bf16[112,256]{1,0:T(8,128)(2,1)S(1)}, u32[]{:S(2)}, u32[]{:S(2)}) collective-permute-start(bf16[112,256]{1,0:T(8,128)(2,1)S(1)} %get-tuple-element.42), channel_id=1, source_target_pairs={{0,2},{1,3},{2,0},{3,1},{4,6},{5,7},{6,4},{7,5},{8,10},{9,11},{10,... | collective-permute-start | bytes 172040 | tf_op jit(solution)/shard_map/ppermute | solution.py:29
  92.2 4.0 %collective-permute-start.14 = (bf16[112,256]{1,0:T(8,128)(2,1)S(1)}, bf16[112,256]{1,0:T(8,128)(2,1)S(1)}, u32[]{:S(2)}, u32[]{:S(2)}) collective-permute-start(bf16[112,256]{1,0:T(8,128)(2,1)S(1)} %get-tuple-element.40), channel_id=1, source_target_pairs={{0,1},{1,0},{2,3},{3,2},{4,5},{5,4},{6,7},{7,6},{8,9},{9,8},{10,11... | collective-permute-start | bytes 172040 | tf_op jit(solution)/shard_map/ppermute | solution.py:29
  96.2 6.3 %collective-permute-start.17 = (bf16[112,256]{1,0:T(8,128)(2,1)S(1)}, bf16[112,256]{1,0:T(8,128)(2,1)S(1)}, u32[]{:S(2)}, u32[]{:S(2)}) collective-permute-start(bf16[112,256]{1,0:T(8,128)(2,1)S(1)} %fusion.2), channel_id=1, source_target_pairs={{0,4},{4,0},{8,12},{12,8},{16,20},{20,16},{24,28},{28,24},{1,5},{5... | collective-permute-start | bytes 172040 | tf_op jit(solution)/shard_map/ppermute | solution.py:29
  102.5 7.3 %collective-permute-start.18 = (bf16[112,256]{1,0:T(8,128)(2,1)S(1)}, bf16[112,256]{1,0:T(8,128)(2,1)S(1)}, u32[]{:S(2)}, u32[]{:S(2)}) collective-permute-start(bf16[112,256]{1,0:T(8,128)(2,1)S(1)} %add_convert_fusion.2), channel_id=1, source_target_pairs={{0,8},{4,12},{8,0},{12,4},{16,24},{20,28},{24,16},{28,20},{1,9},{5... | collective-permute-start | bytes 172040 | tf_op jit(solution)/shard_map/ppermute | solution.py:29
  109.9 8.7 %collective-permute-start.19 = (bf16[112,256]{1,0:T(8,128)(2,1)S(1)}, bf16[112,256]{1,0:T(8,128)(2,1)S(1)}, u32[]{:S(2)}, u32[]{:S(2)}) collective-permute-start(bf16[112,256]{1,0:T(8,128)(2,1)S(1)} %add_convert_fusion.1), channel_id=1, source_target_pairs={{0,16},{4,20},{8,24},{12,28},{16,0},{20,4},{24,8},{28,12},{1,17},{... | collective-permute-start | bytes 172040 | tf_op jit(solution)/shard_map/ppermute | solution.py:29
  118.6 4.2 %collective-permute-start.21 = (bf16[112,256]{1,0:T(8,128)(2,1)S(1)}, bf16[112,256]{1,0:T(8,128)(2,1)S(1)}, u32[]{:S(2)}, u32[]{:S(2)}) collective-permute-start(bf16[112,256]{1,0:T(8,128)(2,1)S(1)} %add_convert_fusion.refs_0_), channel_id=1, source_target_pairs={{0,2},{1,3},{2,0},{3,1},{4,6},{5,7},{6,4},{7,5},{8,10},{9,11},{10,... | collective-permute-start | bytes 172040 | tf_op jit(solution)/shard_map/ppermute | solution.py:29
  119.2 3.6 %collective-permute-start.20 = (bf16[112,256]{1,0:T(8,128)(2,1)S(1)}, bf16[112,256]{1,0:T(8,128)(2,1)S(1)}, u32[]{:S(2)}, u32[]{:S(2)}) collective-permute-start(bf16[112,256]{1,0:T(8,128)(2,1)S(1)} %add_convert_fusion.refs_0_), channel_id=1, source_target_pairs={{0,1},{1,0},{2,3},{3,2},{4,5},{5,4},{6,7},{7,6},{8,9},{9,8},{10,11... | collective-permute-start | bytes 172040 | tf_op jit(solution)/shard_map/ppermute | solution.py:29
  (20 other events, 135.8 us)

commit v6 on v5

--- a/solution.py
+++ b/solution.py
@@ -347,13 +347,13 @@
 
 
 def gradient_kernel(shards, pair, members, nodes, place_ref, blocks_ref, *refs):
-    latent_refs, early_refs, late_refs, grid_refs = (
-        refs[i * shards : (i + 1) * shards] for i in range(4)
-    )
-    out_ref, loss_ref = refs[4 * shards :]
+    latent_refs, early_refs, late_refs, other_refs, grid_refs = (
+        refs[i * shards : (i + 1) * shards] for i in range(5)
+    )
+    out_ref, loss_ref = refs[5 * shards :]
     width = blocks_ref.shape[2]
     features = late_refs[0].shape[1]
-    points = late_refs[0].shape[0] // pair
+    points = late_refs[0].shape[0]
     depth = features // members
     shard, half = place_ref[0], place_ref[1]
     start = 4 * points
@@ -372,16 +372,12 @@
         for m in range(members):
             out_ref[m, at] = total[:, m * depth : (m + 1) * depth]
 
-    def rows_of(ref_list, part):
-        at = slice(part * points, (part + 1) * points)
-        return [ref[at] for ref in ref_list]
-
     def product(kind, parts):
         left = jnp.concatenate([v for t in range(pair) for v in slots(kind, t)], axis=0)
         right = jnp.concatenate([v for part in parts for v in part], axis=0)
         put(kind, dot32(left, right, (0, 0)))
 
-    product(3, [rows_of(late_refs, t) for t in range(pair)])
+    product(3, [[ref[...] for ref in part] for part in (late_refs, other_refs)[:pair]])
     chosen = []
     for k in range(shards):
         index = blocks_ref[(shard ^ k) * pair, start : start + MISC].astype(jnp.int32)
@@ -415,11 +411,11 @@
     product(0, grids)
 
 
-def gradients(place, blocks, latents, early, late, grids, members, pair):
+def gradients(place, blocks, latents, early, late, other, grids, members, pair):
     count, _, width = blocks.shape
     shards = count // pair
     features = late[0].shape[1]
-    points = late[0].shape[0] // pair
+    points = late[0].shape[0]
     depth = features // members
     return pl.pallas_call(
         functools.partial(
@@ -429,7 +425,7 @@
             jax.ShapeDtypeStruct((members, 4 * width, depth), BF16),
             jax.ShapeDtypeStruct((1, 1), F32),
         ),
-        in_specs=[SMEM] + [VMEM] * (1 + 4 * shards),
+        in_specs=[SMEM] + [VMEM] * (1 + 5 * shards),
         out_specs=(VMEM, VMEM),
         cost_estimate=pl.CostEstimate(
             flops=8 * points * count * features * width,
@@ -437,7 +433,7 @@
             transcendentals=0,
         ),
         name="weight_gradients",
-    )(place, blocks, *latents, *early, *late, *grids)
+    )(place, blocks, *latents, *early, *late, *other, *grids)
 
 
 def sum_kernel(pair, blocks_ref, *refs):
@@ -493,11 +489,10 @@
     for value in received:
         total = total + value.astype(F32)
     total = total.astype(BF16)
-    bit = 1
-    while bit < lax.axis_size("ens"):
+    size = lax.axis_size("ens")
+    for bit in [1 << i for i in range(1, size.bit_length() - 1)] + [1]:
         other = swap(total, "ens", bit)
         total = (total.astype(F32) + other.astype(F32)).astype(BF16)
-        bit = 2 * bit
     return gather_slots(total, "space")
 
 
@@ -536,11 +531,12 @@
     )
     keyset, valueset, soft, attended, normed, inverse = saved
     packed = lax.all_to_all(packed, "ens", split_axis=0, concat_axis=0, tiled=True)
-    late = attended
+    late = gather_slots(attended, "space")
+    other = late
     if pair > 1:
-        partner = swap(attended, "ens", 1)
-        late = jnp.concatenate([attended, partner])
-    late = gather_slots(late, "space")
+        other = []
+        for k, part in enumerate(late):
+            other.append(swap(other[k - 1], "space", 1) if k % 2 else swap(part, "ens", 1))
     saved = (queries, keyset, valueset, soft, normed, inverse)
     blocks, outer = backward(
         jnp.stack([shard, member]),
@@ -564,7 +560,9 @@
     )
     place = jnp.stack([shard, half])
     outer = sum_outer(outer)
-    blocks, loss = gradients(place, blocks, latents, early, late, grids, members, pair)
+    blocks, loss = gradients(
+        place, blocks, latents, early, late, other, grids, members, pair
+    )
     blocks = lax.all_to_all(blocks, "ens", split_axis=0, concat_axis=0, tiled=True)
     grad_out = join_columns(shard[None], outer, channels_used)
     grads = sum_groups(blocks, pair)

time: 130 us -> 149 us (1.15)
  waiting for transfers between devices: 56.2 us -> 73.5 us
  starting transfers between devices: 37.8 us -> 39.7 us
    ppermute x23 -> x26, waiting for transfers between devices: 56.2 us -> 73.5 us  [swap(): return lax.ppermute(value, axis, [(i, i ^ bits) for i in range(size)])]
    ppermute x23 -> x26, starting transfers between devices: 23.6 us -> 24.3 us  [swap(): return lax.ppermute(value, axis, [(i, i ^ bits) for i in range(size)])]
    unnamed x37 -> x46, local copies, waits for them, and re-layouts: 5.85 us -> 5.36 us
  transfers between devices with their start and end apart: 26 -> 29, of which waited for: 11 -> 12; matrix products, arithmetic and copies ran while one was open for 2% -> 1% of each run, Pallas kernels for 15% -> 9%
where the time goes in v6:
time: 149 us; the launch traced here: 148 us
  waiting for transfers between devices  73.5 us (49%)
  starting transfers between devices  39.7 us (27%)
  Pallas kernels  27.7 us (19%)
  local copies, waits for them, and re-layouts  5.37 us (4%)
    ppermute x26, waiting for transfers between devices, swap(): return lax.ppermute(value, axis, [(i, i ^ bits) for i in range(size)])  73.5 us
    ppermute x26, starting transfers between devices, swap(): return lax.ppermute(value, axis, [(i, i ^ bits) for i in range(size)])  24.3 us
    pallas_call x1, Pallas kernels, backward(): pl.pallas_call(functools.partial(backward_kernel, shards, blocks, nodes),...  7.38 us
    pallas_call x1, Pallas kernels, forward(): pl.pallas_call(functools.partial(forward_kernel, len(latents), members),...  6.62 us
    all_to_all x1, starting transfers between devices, body(): lax.all_to_all(packed, 'ens', split_axis=0, concat_axis=0, tiled=True)  6.09 us
    pallas_call x1, Pallas kernels, gradients(): pl.pallas_call(functools.partial(gradient_kernel, shards, pair, members,...  5.78 us
    all_to_all x1, starting transfers between devices, body(): lax.all_to_all(blocks, 'ens', split_axis=0, concat_axis=0, tiled=True)  5.59 us
    unnamed x46, local copies, waits for them, and re-layouts  5.36 us
  transfers between devices with their start and end apart: 29, of which 12 were waited for; matrix products, arithmetic and copies ran while one was open for 1% of the time, Pallas kernels for 9%

profile of v6, /device:TPU:0, one launch (start us, length us, event | category | flops | bytes accessed | tf_op | source)
XLA Modules:
  0.0 148.4 jit_solution(14576522020202736491)
XLA Ops:
  0.6 3.0 %collective-permute-start.1 = (bf16[128,1024]{1,0:T(8,128)(2,1)}, bf16[128,1024]{1,0:T(8,128)(2,1)S(1)}, u32[]{:S(2)}, u32[]{:S(2)}) collective-permute-start(bf16[128,1024]{1,0:T(8,128)(2,1)} %bitcast.20), channel_id=1, source_target_pairs={{0,2},{1,3},{2,0},{3,1},{4,6},{5,7},{6,4},{7,5},{8,10},{9,11},{10,... | collective-permute-start | bytes 786440 | tf_op jit(solution)/shard_map/ppermute | solution.py:29
  3.7 6.5 %collective-permute-done.1.refs_7_.refs_2_ = bf16[128,1024]{1,0:T(8,128)(2,1)S(1)} collective-permute-done((bf16[128,1024]{1,0:T(8,128)(2,1)}, bf16[128,1024]{1,0:T(8,128)(2,1)S(1)}, u32[]{:S(2)}, u32[]{:S(2)}) %collective-permute-start.1) | collective-permute-done | bytes 262176 | tf_op jit(solution)/shard_map/ppermute | solution.py:29
  10.2 4.0 %project_queries.1 = (bf16[128,1024]{1,0:T(8,128)(2,1)}, bf16[256,1024]{1,0:T(8,128)(2,1)}) custom-call(bf16[128,1024]{1,0:T(8,128)(2,1)} %bitcast.22, bf16[128,1024]{1,0:T(8,128)(2,1)} %bitcast.15, bf16[1024,1024]{1,0:T(8,128)(2,1)} %w_hbm.2), custom_call_target="tpu_custom_call" | custom-call | flops 268435456 | bytes 2097152 | tf_op jit(solution)/shard_map/project_queries/pallas_call | solution.py:72
  15.1 6.6 %decoder_forward.1 = (bf16[128,1024]{1,0:T(8,128)(2,1)}, bf16[128,1024]{1,0:T(8,128)(2,1)}, f32[8,128,256]{2,1,0:T(8,128)}, bf16[128,1024]{1,0:T(8,128)(2,1)}, f...) custom-call(s32[1]{0:T(128)} %bitcast.refs_0_.shard_ref, s32[1,128]{1,0:T(1,128)} %index_ref.1, ...), custom_call_target="tpu_custom_call" | custom-call | flops 1073741824 | bytes 6291456 | tf_op jit(solution)/shard_map/decoder_forward/pallas_call | solution.py:158
  21.7 6.1 %all-to-all-start = ((bf16[8,224,128]{2,1,0:T(8,128)(2,1)}), bf16[8,224,128]{2,1,0:T(8,128)(2,1)S(1)}, u32[]{:S(2)}, u32[]{:S(2)}) async-start(bf16[8,224,128]{2,1,0:T(8,128)(2,1)} %get-tuple-element.24), calls=%async_computation | async-start | bytes 917504 | tf_op jit(solution)/shard_map/all_to_all | solution.py:533
  27.8 2.0 %collective-permute-start.3 = (bf16[256,1024]{1,0:T(8,128)(2,1)S(1)}, bf16[256,1024]{1,0:T(8,128)(2,1)S(1)}, u32[]{:S(2)}, u32[]{:S(2)}) collective-permute-start(bf16[256,1024]{1,0:T(8,128)(2,1)S(1)} %copy-done.22), channel_id=1, source_target_pairs={{0,4},{4,0},{8,12},{12,8},{16,20},{20,16},{24,28},{28,24},{1,5},{5... | collective-permute-start | bytes 1572872 | tf_op jit(solution)/shard_map/ppermute | solution.py:29
  31.3 15.6 %collective-permute-done.3.refs_4_ = bf16[256,1024]{1,0:T(8,128)(2,1)S(1)} collective-permute-done((bf16[256,1024]{1,0:T(8,128)(2,1)S(1)}, bf16[256,1024]{1,0:T(8,128)(2,1)S(1)}, u32[]{:S(2)}, u32[]{:S(2)}) %collective-permute-start.3) | collective-permute-done | bytes 524320 | tf_op jit(solution)/shard_map/ppermute | solution.py:29
  49.7 7.4 %decoder_backward.1 = (bf16[8,528,128]{2,1,0:T(8,128)(2,1)}, bf16[4,112,256]{2,1,0:T(8,128)(2,1)}) custom-call(s32[2]{0:T(128)} %pad_add_fusion.1.place_ref, bf16[8,224,128]{2,1,0:T(8,128)(2,1)} %copy-done.3, f32[100,128]{1,0:T(8,128)} %target_ref.1, s32[1,128]{1,0:T(1,128)} %index_ref.1, bf16[128,1024]{1,0:T(8,128)(2,1)} %get-tuple-element.23.refs_3_.query_ref, ...), custom_call_target="tpu_custom_call" | custom-call | flops 536870912 | bytes 4194304 | tf_op jit(solution)/shard_map/decoder_backward/pallas_call | solution.py:323
  57.1 3.7 %all-to-all-start.1 = ((bf16[8,528,128]{2,1,0:T(8,128)(2,1)}), bf16[8,528,128]{2,1,0:T(8,128)(2,1)S(1)}, u32[]{:S(2)}, u32[]{:S(2)}) async-start(bf16[8,528,128]{2,1,0:T(8,128)(2,1)} %get-tuple-element.30), calls=%async_computation.1 | async-start | bytes 2162688 | tf_op jit(solution)/shard_map/all_to_all | solution.py:553
  61.4 1.9 %collective-permute-start.8 = (bf16[128,1024]{1,0:T(8,128)(2,1)S(1)}, bf16[128,1024]{1,0:T(8,128)(2,1)}, u32[]{:S(2)}, u32[]{:S(2)}) collective-permute-start(bf16[128,1024]{1,0:T(8,128)(2,1)S(1)} %copy-done.11), channel_id=1, source_target_pairs={{0,2},{1,3},{2,0},{3,1},{4,6},{5,7},{6,4},{7,5},{8,10},{9,11},{10,... | collective-permute-start | bytes 786440 | tf_op jit(solution)/shard_map/ppermute | solution.py:29
  63.3 1.5 %collective-permute-start.10 = (bf16[128,1024]{1,0:T(8,128)(2,1)S(1)}, bf16[128,1024]{1,0:T(8,128)(2,1)}, u32[]{:S(2)}, u32[]{:S(2)}) collective-permute-start(bf16[128,1024]{1,0:T(8,128)(2,1)S(1)} %copy-done.11), channel_id=1, source_target_pairs={{0,4},{4,0},{8,12},{12,8},{16,20},{20,16},{24,28},{28,24},{1,5},{5... | collective-permute-start | bytes 786440 | tf_op jit(solution)/shard_map/ppermute | solution.py:29
  65.1 16.3 %collective-permute-done.8.refs_10_ = bf16[128,1024]{1,0:T(8,128)(2,1)} collective-permute-done((bf16[128,1024]{1,0:T(8,128)(2,1)S(1)}, bf16[128,1024]{1,0:T(8,128)(2,1)}, u32[]{:S(2)}, u32[]{:S(2)}) %collective-permute-start.8) | collective-permute-done | bytes 262176 | tf_op jit(solution)/shard_map/ppermute | solution.py:29
  84.1 5.3 %collective-permute-done.12.refs_14_ = bf16[128,1024]{1,0:T(8,128)(2,1)} collective-permute-done((bf16[128,1024]{1,0:T(8,128)(2,1)}, bf16[128,1024]{1,0:T(8,128)(2,1)}, u32[]{:S(2)}, u32[]{:S(2)}) %collective-permute-start.12) | collective-permute-done | bytes 262176 | tf_op jit(solution)/shard_map/ppermute | solution.py:29
  93.2 5.8 %weight_gradients.1 = (bf16[8,512,128]{2,1,0:T(8,128)(2,1)}, f32[1,1]{1,0:T(1,128)}) custom-call(s32[2]{0:T(128)} %pad_add_fusion.place_ref, bf16[8,528,128]{2,1,0:T(8,128)(2,1)} %copy-done, bf16[128,1024]{1,0:T(8,128)(2,1)} %bitcast.24, bf16[128,1024]{1,0:T(8,128)(2,1)} %copy-done.5, bf16[128,1024]{1,0:T(8,128)(2,1)} %copy-done.4, ...), custom_call_target="tpu_custom_call" | custom-call | flops 1073741824 | bytes 8388608 | tf_op jit(solution)/shard_map/weight_gradients/pallas_call | solution.py:420
  99.0 5.6 %all-to-all-start.2 = ((bf16[8,512,128]{2,1,0:T(8,128)(2,1)}), bf16[8,512,128]{2,1,0:T(8,128)(2,1)S(1)}, u32[]{:S(2)}, u32[]{:S(2)}) async-start(bf16[8,512,128]{2,1,0:T(8,128)(2,1)} %get-tuple-element.35), calls=%async_computation.2 | async-start | bytes 2097152 | tf_op jit(solution)/shard_map/all_to_all | solution.py:566
  106.5 2.3 %collective-permute-done.19 = bf16[112,256]{1,0:T(8,128)(2,1)S(1)} collective-permute-done((bf16[112,256]{1,0:T(8,128)(2,1)S(1)}, bf16[112,256]{1,0:T(8,128)(2,1)S(1)}, u32[]{:S(2)}, u32[]{:S(2)}) %collective-permute-start.19) | collective-permute-done | bytes 57376 | tf_op jit(solution)/shard_map/ppermute | solution.py:29
  110.2 1.6 %collective-permute-start.20 = (bf16[112,256]{1,0:T(8,128)(2,1)S(1)}, bf16[112,256]{1,0:T(8,128)(2,1)S(1)}, u32[]{:S(2)}, u32[]{:S(2)}) collective-permute-start(bf16[112,256]{1,0:T(8,128)(2,1)S(1)} %fusion.2), channel_id=1, source_target_pairs={{0,8},{4,12},{8,0},{12,4},{16,24},{20,28},{24,16},{28,20},{1,9},{5... | collective-permute-start | bytes 172040 | tf_op jit(solution)/shard_map/ppermute | solution.py:29
  111.7 12.1 %collective-permute-done.20 = bf16[112,256]{1,0:T(8,128)(2,1)S(1)} collective-permute-done((bf16[112,256]{1,0:T(8,128)(2,1)S(1)}, bf16[112,256]{1,0:T(8,128)(2,1)S(1)}, u32[]{:S(2)}, u32[]{:S(2)}) %collective-permute-start.20) | collective-permute-done | bytes 57376 | tf_op jit(solution)/shard_map/ppermute | solution.py:29
  123.8 4.0 %collective-permute-start.21 = (bf16[112,256]{1,0:T(8,128)(2,1)S(1)}, bf16[112,256]{1,0:T(8,128)(2,1)S(1)}, u32[]{:S(2)}, u32[]{:S(2)}) collective-permute-start(bf16[112,256]{1,0:T(8,128)(2,1)S(1)} %add_convert_fusion.2), channel_id=1, source_target_pairs={{0,16},{4,20},{8,24},{12,28},{16,0},{20,4},{24,8},{28,12},{1,17},{... | collective-permute-start | bytes 172040 | tf_op jit(solution)/shard_map/ppermute | solution.py:29
  127.9 5.2 %collective-permute-done.21 = bf16[112,256]{1,0:T(8,128)(2,1)S(1)} collective-permute-done((bf16[112,256]{1,0:T(8,128)(2,1)S(1)}, bf16[112,256]{1,0:T(8,128)(2,1)S(1)}, u32[]{:S(2)}, u32[]{:S(2)}) %collective-permute-start.21) | collective-permute-done | bytes 57376 | tf_op jit(solution)/shard_map/ppermute | solution.py:29
  134.6 2.8 %collective-permute-done.22 = bf16[112,256]{1,0:T(8,128)(2,1)S(1)} collective-permute-done((bf16[112,256]{1,0:T(8,128)(2,1)S(1)}, bf16[112,256]{1,0:T(8,128)(2,1)S(1)}, u32[]{:S(2)}, u32[]{:S(2)}) %collective-permute-start.22) | collective-permute-done | bytes 57376 | tf_op jit(solution)/shard_map/ppermute | solution.py:29
  138.0 3.6 %collective-permute-done.24.refs_2_ = bf16[112,256]{1,0:T(8,128)(2,1)S(1)} collective-permute-done((bf16[112,256]{1,0:T(8,128)(2,1)S(1)}, bf16[112,256]{1,0:T(8,128)(2,1)S(1)}, u32[]{:S(2)}, u32[]{:S(2)}) %collective-permute-start.24) | collective-permute-done | bytes 57376 | tf_op jit(solution)/shard_map/ppermute | solution.py:29
  143.5 1.7 %join_columns.1 = f32[100,1024]{1,0:T(8,128)} custom-call(s32[1]{0:T(128)} %bitcast.refs_0_.shard_ref, bf16[112,256]{1,0:T(8,128)(2,1)} %copy-done.17, bf16[112,256]{1,0:T(8,128)(2,1)} %copy-done.20, bf16[112,256]{1,0:T(8,128)(2,1)} %copy-done.19, bf16[112,256]{1,0:T(8,128)(2,1)} %copy-done.21), custom_call_target="tpu_custom_call" | custom-call | tf_op jit(solution)/shard_map/join_columns/pallas_call | solution.py:475
  146.3 2.1 %sum_groups.1 = (f32[128,256]{1,0:T(8,128)}, f32[128,256]{1,0:T(8,128)}, f32[128,256]{1,0:T(8,128)}, f32[128,256]{1,0:T(8,128)}) custom-call(bf16[8,512,128]{2,1,0:T(8,128)(2,1)} %copy-done.1), custom_call_target="tpu_custom_call" | custom-call | tf_op jit(solution)/shard_map/sum_groups/pallas_call | solution.py:453
  (93 shorter events, 20.6 us)
Async XLA Ops:
  0.6 9.6 %collective-permute-start.1 = (bf16[128,1024]{1,0:T(8,128)(2,1)}, bf16[128,1024]{1,0:T(8,128)(2,1)S(1)}, u32[]{:S(2)}, u32[]{:S(2)}) collective-permute-start(bf16[128,1024]{1,0:T(8,128)(2,1)} %bitcast.20), channel_id=1, source_target_pairs={{0,2},{1,3},{2,0},{3,1},{4,6},{5,7},{6,4},{7,5},{8,10},{9,11},{10,... | collective-permute-start | bytes 786440 | tf_op jit(solution)/shard_map/ppermute | solution.py:29
  3.7 10.6 %collective-permute-start = (bf16[128,1024]{1,0:T(8,128)(2,1)}, bf16[128,1024]{1,0:T(8,128)(2,1)S(1)}, u32[]{:S(2)}, u32[]{:S(2)}) collective-permute-start(bf16[128,1024]{1,0:T(8,128)(2,1)} %bitcast.21), channel_id=1, source_target_pairs={{0,1},{1,0},{2,3},{3,2},{4,5},{5,4},{6,7},{7,6},{8,9},{9,8},{10,11... | collective-permute-start | bytes 786440 | tf_op jit(solution)/shard_map/ppermute | solution.py:29
  10.2 4.1 %collective-permute-start.2 = (bf16[128,1024]{1,0:T(8,128)(2,1)S(1)}, bf16[128,1024]{1,0:T(8,128)(2,1)S(1)}, u32[]{:S(2)}, u32[]{:S(2)}) collective-permute-start(bf16[128,1024]{1,0:T(8,128)(2,1)S(1)} %collective-permute-done.1.refs_7_.refs_2_), channel_id=1, source_target_pairs={{0,1},{1,0},{2,3},{3,2},{4,5},{5,4},{6,7},{7,6},{8,9},{9,8},{10,11... | collective-permute-start | bytes 786440 | tf_op jit(solution)/shard_map/ppermute | solution.py:29
  21.7 27.2 %all-to-all-start = ((bf16[8,224,128]{2,1,0:T(8,128)(2,1)}), bf16[8,224,128]{2,1,0:T(8,128)(2,1)S(1)}, u32[]{:S(2)}, u32[]{:S(2)}) async-start(bf16[8,224,128]{2,1,0:T(8,128)(2,1)} %get-tuple-element.24), calls=%async_computation | async-start | bytes 917504 | tf_op jit(solution)/shard_map/all_to_all | solution.py:533
  27.8 19.1 %collective-permute-start.3 = (bf16[256,1024]{1,0:T(8,128)(2,1)S(1)}, bf16[256,1024]{1,0:T(8,128)(2,1)S(1)}, u32[]{:S(2)}, u32[]{:S(2)}) collective-permute-start(bf16[256,1024]{1,0:T(8,128)(2,1)S(1)} %copy-done.22), channel_id=1, source_target_pairs={{0,4},{4,0},{8,12},{12,8},{16,20},{20,16},{24,28},{28,24},{1,5},{5... | collective-permute-start | bytes 1572872 | tf_op jit(solution)/shard_map/ppermute | solution.py:29
  29.8 31.4 %collective-permute-start.15 = (bf16[128,1024]{1,0:T(8,128)(2,1)S(1)}, bf16[128,1024]{1,0:T(8,128)(2,1)S(1)}, u32[]{:S(2)}, u32[]{:S(2)}) collective-permute-start(bf16[128,1024]{1,0:T(8,128)(2,1)S(1)} %bitcast.18), channel_id=1, source_target_pairs={{0,2},{1,3},{2,0},{3,1},{4,6},{5,7},{6,4},{7,5},{8,10},{9,11},{10,... | collective-permute-start | bytes 786440 | tf_op jit(solution)/shard_map/ppermute | solution.py:29
  46.9 35.9 %collective-permute-start.5 = (bf16[256,1024]{1,0:T(8,128)(2,1)S(1)}, bf16[256,1024]{1,0:T(8,128)(2,1)S(1)}, u32[]{:S(2)}, u32[]{:S(2)}) collective-permute-start(bf16[256,1024]{1,0:T(8,128)(2,1)S(1)} %collective-permute-done.3.refs_4_), channel_id=1, source_target_pairs={{0,2},{1,3},{2,0},{3,1},{4,6},{5,7},{6,4},{7,5},{8,10},{9,11},{10,... | collective-permute-start | bytes 1572872 | tf_op jit(solution)/shard_map/ppermute | solution.py:29
  57.1 34.2 %all-to-all-start.1 = ((bf16[8,528,128]{2,1,0:T(8,128)(2,1)}), bf16[8,528,128]{2,1,0:T(8,128)(2,1)S(1)}, u32[]{:S(2)}, u32[]{:S(2)}) async-start(bf16[8,528,128]{2,1,0:T(8,128)(2,1)} %get-tuple-element.30), calls=%async_computation.1 | async-start | bytes 2162688 | tf_op jit(solution)/shard_map/all_to_all | solution.py:553
  61.4 19.9 %collective-permute-start.8 = (bf16[128,1024]{1,0:T(8,128)(2,1)S(1)}, bf16[128,1024]{1,0:T(8,128)(2,1)}, u32[]{:S(2)}, u32[]{:S(2)}) collective-permute-start(bf16[128,1024]{1,0:T(8,128)(2,1)S(1)} %copy-done.11), channel_id=1, source_target_pairs={{0,2},{1,3},{2,0},{3,1},{4,6},{5,7},{6,4},{7,5},{8,10},{9,11},{10,... | collective-permute-start | bytes 786440 | tf_op jit(solution)/shard_map/ppermute | solution.py:29
  63.3 19.6 %collective-permute-start.7 = (bf16[128,1024]{1,0:T(8,128)(2,1)S(1)}, bf16[128,1024]{1,0:T(8,128)(2,1)S(1)}, u32[]{:S(2)}, u32[]{:S(2)}) collective-permute-start(bf16[128,1024]{1,0:T(8,128)(2,1)S(1)} %copy-done.11), channel_id=1, source_target_pairs={{0,1},{1,0},{2,3},{3,2},{4,5},{5,4},{6,7},{7,6},{8,9},{9,8},{10,11... | collective-permute-start | bytes 786440 | tf_op jit(solution)/shard_map/ppermute | solution.py:29
  63.3 20.1 %collective-permute-start.10 = (bf16[128,1024]{1,0:T(8,128)(2,1)S(1)}, bf16[128,1024]{1,0:T(8,128)(2,1)}, u32[]{:S(2)}, u32[]{:S(2)}) collective-permute-start(bf16[128,1024]{1,0:T(8,128)(2,1)S(1)} %copy-done.11), channel_id=1, source_target_pairs={{0,4},{4,0},{8,12},{12,8},{16,20},{20,16},{24,28},{28,24},{1,5},{5... | collective-permute-start | bytes 786440 | tf_op jit(solution)/shard_map/ppermute | solution.py:29
  64.9 25.2 %collective-permute-start.4 = (bf16[256,1024]{1,0:T(8,128)(2,1)S(1)}, bf16[256,1024]{1,0:T(8,128)(2,1)S(1)}, u32[]{:S(2)}, u32[]{:S(2)}) collective-permute-start(bf16[256,1024]{1,0:T(8,128)(2,1)S(1)} %collective-permute-done.3.refs_4_), channel_id=1, source_target_pairs={{0,1},{1,0},{2,3},{3,2},{4,5},{5,4},{6,7},{7,6},{8,9},{9,8},{10,11... | collective-permute-start | bytes 1572872 | tf_op jit(solution)/shard_map/ppermute | solution.py:29
  81.4 8.1 %collective-permute-start.12 = (bf16[128,1024]{1,0:T(8,128)(2,1)}, bf16[128,1024]{1,0:T(8,128)(2,1)}, u32[]{:S(2)}, u32[]{:S(2)}) collective-permute-start(bf16[128,1024]{1,0:T(8,128)(2,1)} %collective-permute-done.8.refs_10_), channel_id=1, source_target_pairs={{0,4},{4,0},{8,12},{12,8},{16,20},{20,16},{24,28},{28,24},{1,5},{5... | collective-permute-start | bytes 786440 | tf_op jit(solution)/shard_map/ppermute | solution.py:29
  82.9 8.5 %collective-permute-start.6 = (bf16[256,1024]{1,0:T(8,128)(2,1)S(1)}, bf16[256,1024]{1,0:T(8,128)(2,1)S(1)}, u32[]{:S(2)}, u32[]{:S(2)}) collective-permute-start(bf16[256,1024]{1,0:T(8,128)(2,1)S(1)} %collective-permute-done.5.refs_6_), channel_id=1, source_target_pairs={{0,1},{1,0},{2,3},{3,2},{4,5},{5,4},{6,7},{7,6},{8,9},{9,8},{10,11... | collective-permute-start | bytes 1572872 | tf_op jit(solution)/shard_map/ppermute | solution.py:29
  83.0 7.1 %collective-permute-start.9 = (bf16[128,1024]{1,0:T(8,128)(2,1)}, bf16[128,1024]{1,0:T(8,128)(2,1)}, u32[]{:S(2)}, u32[]{:S(2)}) collective-permute-start(bf16[128,1024]{1,0:T(8,128)(2,1)} %collective-permute-done.8.refs_10_), channel_id=1, source_target_pairs={{0,1},{1,0},{2,3},{3,2},{4,5},{5,4},{6,7},{7,6},{8,9},{9,8},{10,11... | collective-permute-start | bytes 786440 | tf_op jit(solution)/shard_map/ppermute | solution.py:29
  83.7 6.3 %collective-permute-start.11 = (bf16[128,1024]{1,0:T(8,128)(2,1)}, bf16[128,1024]{1,0:T(8,128)(2,1)S(1)}, u32[]{:S(2)}, u32[]{:S(2)}) collective-permute-start(bf16[128,1024]{1,0:T(8,128)(2,1)} %collective-permute-done.10.refs_12_), channel_id=1, source_target_pairs={{0,1},{1,0},{2,3},{3,2},{4,5},{5,4},{6,7},{7,6},{8,9},{9,8},{10,11... | collective-permute-start | bytes 786440 | tf_op jit(solution)/shard_map/ppermute | solution.py:29
  99.0 46.3 %all-to-all-start.2 = ((bf16[8,512,128]{2,1,0:T(8,128)(2,1)}), bf16[8,512,128]{2,1,0:T(8,128)(2,1)S(1)}, u32[]{:S(2)}, u32[]{:S(2)}) async-start(bf16[8,512,128]{2,1,0:T(8,128)(2,1)} %get-tuple-element.35), calls=%async_computation.2 | async-start | bytes 2097152 | tf_op jit(solution)/shard_map/all_to_all | solution.py:566
  104.6 4.2 %collective-permute-start.19 = (bf16[112,256]{1,0:T(8,128)(2,1)S(1)}, bf16[112,256]{1,0:T(8,128)(2,1)S(1)}, u32[]{:S(2)}, u32[]{:S(2)}) collective-permute-start(bf16[112,256]{1,0:T(8,128)(2,1)S(1)} %get-tuple-element.41), channel_id=1, source_target_pairs={{0,3},{1,2},{2,1},{3,0},{4,7},{5,6},{6,5},{7,4},{8,11},{9,10},{10,... | collective-permute-start | bytes 172040 | tf_op jit(solution)/shard_map/ppermute | solution.py:29
  104.7 5.4 %collective-permute-start.18 = (bf16[112,256]{1,0:T(8,128)(2,1)S(1)}, bf16[112,256]{1,0:T(8,128)(2,1)S(1)}, u32[]{:S(2)}, u32[]{:S(2)}) collective-permute-start(bf16[112,256]{1,0:T(8,128)(2,1)S(1)} %get-tuple-element.42), channel_id=1, source_target_pairs={{0,2},{1,3},{2,0},{3,1},{4,6},{5,7},{6,4},{7,5},{8,10},{9,11},{10,... | collective-permute-start | bytes 172040 | tf_op jit(solution)/shard_map/ppermute | solution.py:29
  106.2 4.0 %collective-permute-start.17 = (bf16[112,256]{1,0:T(8,128)(2,1)S(1)}, bf16[112,256]{1,0:T(8,128)(2,1)S(1)}, u32[]{:S(2)}, u32[]{:S(2)}) collective-permute-start(bf16[112,256]{1,0:T(8,128)(2,1)S(1)} %get-tuple-element.40), channel_id=1, source_target_pairs={{0,1},{1,0},{2,3},{3,2},{4,5},{5,4},{6,7},{7,6},{8,9},{9,8},{10,11... | collective-permute-start | bytes 172040 | tf_op jit(solution)/shard_map/ppermute | solution.py:29
  110.2 13.6 %collective-permute-start.20 = (bf16[112,256]{1,0:T(8,128)(2,1)S(1)}, bf16[112,256]{1,0:T(8,128)(2,1)S(1)}, u32[]{:S(2)}, u32[]{:S(2)}) collective-permute-start(bf16[112,256]{1,0:T(8,128)(2,1)S(1)} %fusion.2), channel_id=1, source_target_pairs={{0,8},{4,12},{8,0},{12,4},{16,24},{20,28},{24,16},{28,20},{1,9},{5... | collective-permute-start | bytes 172040 | tf_op jit(solution)/shard_map/ppermute | solution.py:29
  123.8 9.3 %collective-permute-start.21 = (bf16[112,256]{1,0:T(8,128)(2,1)S(1)}, bf16[112,256]{1,0:T(8,128)(2,1)S(1)}, u32[]{:S(2)}, u32[]{:S(2)}) collective-permute-start(bf16[112,256]{1,0:T(8,128)(2,1)S(1)} %add_convert_fusion.2), channel_id=1, source_target_pairs={{0,16},{4,20},{8,24},{12,28},{16,0},{20,4},{24,8},{28,12},{1,17},{... | collective-permute-start | bytes 172040 | tf_op jit(solution)/shard_map/ppermute | solution.py:29
  133.1 4.2 %collective-permute-start.22 = (bf16[112,256]{1,0:T(8,128)(2,1)S(1)}, bf16[112,256]{1,0:T(8,128)(2,1)S(1)}, u32[]{:S(2)}, u32[]{:S(2)}) collective-permute-start(bf16[112,256]{1,0:T(8,128)(2,1)S(1)} %add_convert_fusion.1), channel_id=1, source_target_pairs={{0,4},{4,0},{8,12},{12,8},{16,20},{20,16},{24,28},{28,24},{1,5},{5... | collective-permute-start | bytes 172040 | tf_op jit(solution)/shard_map/ppermute | solution.py:29
  137.4 4.2 %collective-permute-start.24 = (bf16[112,256]{1,0:T(8,128)(2,1)S(1)}, bf16[112,256]{1,0:T(8,128)(2,1)S(1)}, u32[]{:S(2)}, u32[]{:S(2)}) collective-permute-start(bf16[112,256]{1,0:T(8,128)(2,1)S(1)} %add_convert_fusion.refs_0_), channel_id=1, source_target_pairs={{0,2},{1,3},{2,0},{3,1},{4,6},{5,7},{6,4},{7,5},{8,10},{9,11},{10,... | collective-permute-start | bytes 172040 | tf_op jit(solution)/shard_map/ppermute | solution.py:29
  (28 other events, 165.6 us)

commit v7 on v6

--- a/solution.py
+++ b/solution.py
@@ -12,7 +12,6 @@
 EPS = 1e-06
 SMOOTH = 0.01
 LANES = 128
-MISC = 8
 BF16, F32 = jnp.bfloat16, jnp.float32
 VMEM = pl.BlockSpec(memory_space=pltpu.VMEM)
 SMEM = pl.BlockSpec(memory_space=pltpu.SMEM)
@@ -179,16 +178,43 @@
     )(shard, index, grid_rows, queries, readout, *latents, *weights)
 
 
-def backward_kernel(
+def put(out_ref, kind, column, value):
+    points, width = value.shape[0], out_ref.shape[2]
+    step = min(width, value.shape[1])
+    for c in range(0, value.shape[1], step):
+        block, lane = divmod(column + c, width)
+        out_ref[block, kind * points : (kind + 1) * points, lane : lane + step] = value[
+            :, c : c + step
+        ]
+
+
+def tag_lines(index_ref, nodes, width):
+    index = index_ref[...]
+    points = index.shape[1]
+    step = min(points, width)
+    lines = []
+    for tag in (index // nodes, index % nodes):
+        for c in range(0, points, step):
+            line = tag[:, c : c + step].astype(F32)
+            if step < width:
+                line = jnp.concatenate([line, jnp.zeros((1, width - step), F32)], axis=1)
+            lines.append(line)
+    return lines
+
+
+def stacked(lines, rows):
+    spare = jnp.zeros((rows - len(lines), lines[0].shape[1]), F32)
+    return jnp.concatenate(lines + [spare], axis=0).astype(BF16)
+
+
+def slopes_kernel(
     shards,
     blocks,
     nodes,
     place_ref,
-    packed_ref,
+    fields_ref,
     target_ref,
     index_ref,
-    query_ref,
-    key_ref,
     value_ref,
     soft_ref,
     normed_ref,
@@ -196,18 +222,13 @@
     readout_ref,
     w_hbm,
     out_ref,
-    outer_ref,
-    w_ref,
-    slope_ref,
     d_attended_ref,
-    small_ref,
-    truth_ref,
-    weight_ref,
-    sem,
+    *refs,
 ):
+    outer_refs, (slope_ref, w_ref, truth_ref, weight_ref, sem) = refs[:shards], refs[shards:]
     copy = pltpu.make_async_copy(w_hbm, w_ref, sem)
     copy.start()
-    members = packed_ref.shape[0]
+    members = fields_ref.shape[0]
     points, features = normed_ref.shape
     channels_used = readout_ref.shape[0]
     channels = truth_ref.shape[0]
@@ -224,7 +245,7 @@
         at = pl.ds(pl.multiple_of(c * chunk, chunk), chunk)
         low_at = pl.ds(pl.multiple_of(c * chunk + channels, chunk), chunk)
         fields = [
-            packed_ref[m, at].astype(F32) + packed_ref[m, low_at].astype(F32)
+            fields_ref[m, at].astype(F32) + fields_ref[m, low_at].astype(F32)
             for m in range(members)
         ]
         truth = truth_ref[at]
@@ -254,31 +275,13 @@
 
     loss = lax.fori_loop(0, channels // chunk, crps, jnp.zeros((chunk, points), F32))
     loss = weight * jnp.sum(jnp.sum(loss, axis=0, keepdims=True), axis=1, keepdims=True)
-
-    first = loss.astype(BF16).astype(F32)
-    second = (loss - first).astype(BF16).astype(F32)
-    for i, value in enumerate((first, second, loss - first - second)):
-        small_ref[i : i + 1] = jnp.broadcast_to(value, (1, width))
-    small_ref[3:] = jnp.zeros((small_ref.shape[0] - 3, width), F32)
-    index = index_ref[...]
-    line = 3
-    for tag in (index // nodes, index % nodes):
-        step = min(points, width)
-        for c in range(0, points, step):
-            small_ref[line : line + 1, :step] = tag[:, c : c + step].astype(F32)
-            line = line + 1
-    small = small_ref[...].astype(BF16)
+    high = loss.astype(BF16).astype(F32)
+    low = (loss - high).astype(BF16).astype(F32)
+    lines = [jnp.broadcast_to(value, (1, width)) for value in (high, low, loss - high - low)]
+    lines = lines + tag_lines(index_ref, nodes, width)
+    tags = stacked(lines, out_ref.shape[1] - 2 * points)
     for b in range(blocks):
-        out_ref[b, 4 * points :] = small
-
-    def put(kind, column, value):
-        step = min(width, value.shape[1])
-        for c in range(0, value.shape[1], step):
-            block, lane = divmod(column + c, width)
-            out_ref[block, kind * points : (kind + 1) * points, lane : lane + step] = value[
-                :, c : c + step
-            ]
-
+        out_ref[b, 2 * points :] = tags
     own = slope_ref[place_ref[1]]
     normed = normed_ref[...]
     outer = dot32(own, normed.astype(BF16))
@@ -288,20 +291,57 @@
         part = parts[0]
         for s in range(1, shards):
             part = jnp.where((place_ref[0] ^ k) == s, parts[s], part)
-        outer_ref[k] = part.astype(BF16)
+        outer_refs[k][...] = part.astype(BF16)
     d_normed = dot32(own, weight_ref[...], (0, 0))
     mean = jnp.mean(d_normed * normed, axis=-1, keepdims=True)
     d_hidden = (inverse_ref[...] * (d_normed - normed * mean)).astype(BF16)
-    put(3, 0, d_hidden)
+    put(out_ref, 0, 0, d_hidden)
     copy.wait()
     d_attended_ref[...] = dot32(d_hidden, w_ref[...], (1, 1)).astype(BF16)
-    factor = (features // HEADS) ** (-0.5)
     for pair in range(features // LANES):
         at = slice(pair * LANES, (pair + 1) * LANES)
-        soft = soft_ref[pair]
-        d_out = d_attended_ref[:, at]
-        d_probs = dot32(d_out, halves(value_ref[:, at]), (1, 1))
-        put(2, pair * LANES, joined(dot32(soft.astype(BF16), d_out, (0, 0))).astype(BF16))
+        d_value = joined(dot32(soft_ref[pair].astype(BF16), d_attended_ref[:, at], (0, 0)))
+        put(out_ref, 1, pair * LANES, d_value.astype(BF16))
+
+
+def backward_slopes(place, fields, target, index, saved, readout, w_mix, shards, blocks, nodes):
+    members, points = fields.shape[0], target.shape[1]
+    features = w_mix.shape[0]
+    channels = padded(readout.shape[0])
+    shape = jax.ShapeDtypeStruct
+    return pl.pallas_call(
+        functools.partial(slopes_kernel, shards, blocks, nodes),
+        out_shape=(
+            shape((blocks, 2 * points + 16, features // blocks), BF16),
+            shape((points, features), BF16),
+        )
+        + (shape((channels, features // shards), BF16),) * shards,
+        in_specs=[SMEM] + [VMEM] * 8 + [ANY],
+        out_specs=(VMEM,) * (2 + shards),
+        scratch_shapes=[
+            pltpu.VMEM((members, channels, points), BF16),
+            pltpu.VMEM((features, features), BF16),
+            pltpu.VMEM((channels, points), F32),
+            pltpu.VMEM((channels, features), BF16),
+            pltpu.SemaphoreType.DMA,
+        ],
+        cost_estimate=pl.CostEstimate(
+            flops=2 * points * features * features,
+            bytes_accessed=2 * features * features,
+            transcendentals=0,
+        ),
+        name="backward_slopes",
+    )(place, fields, target, index, *saved, readout, w_mix)
+
+
+def scores_kernel(pair, place_ref, query_ref, key_ref, value_ref, soft_ref, d_attended_ref, *refs):
+    *out_refs, block_ref = refs
+    features = query_ref.shape[1]
+    factor = (features // HEADS) ** (-0.5)
+    for heads in range(features // LANES):
+        at = slice(heads * LANES, (heads + 1) * LANES)
+        soft = soft_ref[heads]
+        d_probs = dot32(d_attended_ref[:, at], halves(value_ref[:, at]), (1, 1))
         product = d_probs * soft
         d_scores = []
         for head in range(2):
@@ -309,131 +349,163 @@
             summed = jnp.sum(product[:, block], axis=-1, keepdims=True)
             d_scores.append(soft[:, block] * (d_probs[:, block] - summed) * factor)
         d_scores = jnp.concatenate(d_scores, axis=1).astype(BF16)
-        put(0, pair * LANES, dot32(d_scores, halves(key_ref[:, at])).astype(BF16))
-        put(1, pair * LANES, joined(dot32(d_scores, query_ref[:, at], (0, 0))).astype(BF16))
-
-
-def backward(place, packed, target, index, saved, readout, w_mix, shards, blocks, nodes):
-    members = packed.shape[0]
-    features = w_mix.shape[0]
-    points = saved[0].shape[0]
-    channels = padded(readout.shape[0])
-    width = features // blocks
-    small = 16
-    return pl.pallas_call(
-        functools.partial(backward_kernel, shards, blocks, nodes),
-        out_shape=(
-            jax.ShapeDtypeStruct((blocks, 4 * points + small, width), BF16),
-            jax.ShapeDtypeStruct((shards, channels, features // shards), BF16),
-        ),
-        in_specs=[SMEM] + [VMEM] * 10 + [ANY],
-        out_specs=(VMEM, VMEM),
-        scratch_shapes=[
-            pltpu.VMEM((features, features), BF16),
-            pltpu.VMEM((members, channels, points), BF16),
-            pltpu.VMEM((points, features), BF16),
-            pltpu.VMEM((small, width), F32),
-            pltpu.VMEM((channels, points), F32),
-            pltpu.VMEM((channels, features), BF16),
-            pltpu.SemaphoreType.DMA,
-        ],
+        put(block_ref, 0, heads * LANES, dot32(d_scores, halves(key_ref[:, at])).astype(BF16))
+        d_key = joined(dot32(d_scores, query_ref[:, at], (0, 0)))
+        put(block_ref, 1, heads * LANES, d_key.astype(BF16))
+    for i, ref in enumerate(out_refs):
+        k, t = divmod(i, pair)
+        ref[...] = block_ref[(place_ref[0] ^ k) * pair + (place_ref[1] ^ t)]
+
+
+def backward_scores(place, saved, d_attended, blocks, pair):
+    points, features = d_attended.shape
+    block = (2 * points, features // blocks)
+    return pl.pallas_call(
+        functools.partial(scores_kernel, pair),
+        out_shape=(jax.ShapeDtypeStruct(block, BF16),) * blocks,
+        in_specs=[SMEM] + [VMEM] * 5,
+        out_specs=(VMEM,) * blocks,
+        scratch_shapes=[pltpu.VMEM((blocks,) + block, BF16)],
         cost_estimate=pl.CostEstimate(
-            flops=4 * points * features * features,
-            bytes_accessed=4 * features * features,
+            flops=12 * points * points * features,
+            bytes_accessed=8 * points * features,
             transcendentals=0,
         ),
-        name="decoder_backward",
-    )(place, packed, target, index, *saved, readout, w_mix)
-
-
-def gradient_kernel(shards, pair, members, nodes, place_ref, blocks_ref, *refs):
-    latent_refs, early_refs, late_refs, other_refs, grid_refs = (
-        refs[i * shards : (i + 1) * shards] for i in range(5)
+        name="backward_scores",
+    )(place, *saved, d_attended)
+
+
+def product_of(lefts, rights):
+    left = jnp.concatenate(lefts, axis=0)
+    return dot32(left, jnp.concatenate(rights, axis=0), (0, 0)).astype(BF16)
+
+
+def node_sums(lefts, chosen, shards):
+    return [
+        dot32(chosen, jnp.concatenate(lefts[t : t + shards], axis=0)).astype(BF16)
+        for t in range(0, len(lefts), shards)
+    ]
+
+
+def first_gradients_kernel(shards, pair, nodes, place_ref, blocks_ref, *refs):
+    latent_refs, early_refs, late_refs, other_refs = (
+        refs[i * shards : (i + 1) * shards] for i in range(4)
     )
-    out_ref, loss_ref = refs[5 * shards :]
+    out_ref, chosen_ref, loss_ref = refs[4 * shards :]
+    members, _, depth = out_ref.shape
     width = blocks_ref.shape[2]
-    features = late_refs[0].shape[1]
     points = late_refs[0].shape[0]
-    depth = features // members
     shard, half = place_ref[0], place_ref[1]
-    start = 4 * points
+    start = 2 * points
     total = blocks_ref[0, start:].astype(F32)
     for s in range(1, shards):
         total = total + blocks_ref[s * pair, start:].astype(F32)
     loss_ref[...] = jnp.sum(total[:3, :1], axis=0, keepdims=True)
 
-    def slots(kind, t):
+    def slots(kind):
         at = slice(kind * points, (kind + 1) * points)
-        return [blocks_ref[(shard ^ k) * pair + (half ^ t), at] for k in range(shards)]
-
-    def put(kind, total):
-        total = total.astype(BF16)
-        at = slice(kind * width, kind * width + total.shape[0])
+        return [
+            blocks_ref[(shard ^ k) * pair + (half ^ t), at]
+            for t in range(pair)
+            for k in range(shards)
+        ]
+
+    def store(kind, total):
         for m in range(members):
-            out_ref[m, at] = total[:, m * depth : (m + 1) * depth]
-
-    def product(kind, parts):
-        left = jnp.concatenate([v for t in range(pair) for v in slots(kind, t)], axis=0)
-        right = jnp.concatenate([v for part in parts for v in part], axis=0)
-        put(kind, dot32(left, right, (0, 0)))
-
-    product(3, [[ref[...] for ref in part] for part in (late_refs, other_refs)[:pair]])
-    chosen = []
+            out_ref[m, kind * width : (kind + 1) * width] = total[:, m * depth : (m + 1) * depth]
+
+    rights = [ref[...] for part in (late_refs, other_refs)[:pair] for ref in part]
+    store(0, product_of(slots(0), rights))
+    lines = max(points // width, 1)
     for k in range(shards):
-        index = blocks_ref[(shard ^ k) * pair, start : start + MISC].astype(jnp.int32)
-        lines = max(points // width, 1)
+        index = blocks_ref[(shard ^ k) * pair, start:].astype(jnp.int32)
         owner, offset = (
             jnp.concatenate([index[3 + b + i : 4 + b + i] for i in range(lines)], axis=1)
             for b in (0, lines)
         )
         position = (owner ^ shard) * nodes + offset
         node = lax.broadcasted_iota(jnp.int32, (nodes * shards, points), 0)
-        chosen.append(jnp.where(node == position, 1.0, 0.0).astype(BF16))
-    chosen = jnp.concatenate(chosen, axis=1)
-    sums = []
-    for t in range(pair):
-        both = [jnp.concatenate(slots(kind, t), axis=0) for kind in (1, 2)]
-        sums.append(dot32(chosen, jnp.concatenate(both, axis=1)).astype(BF16))
-    others = [[ref[...] for ref in latent_refs]]
+        chosen_ref[:, k * points : (k + 1) * points] = jnp.where(node == position, 1.0, 0.0).astype(
+            BF16
+        )
+    rights = [ref[...] for ref in latent_refs]
     if pair > 1:
-        others.append([ref[:nodes] for ref in early_refs])
-    put(
-        1,
-        dot32(
-            jnp.concatenate(sums, axis=0),
-            jnp.concatenate([v for part in others for v in part], axis=0),
-            (0, 0),
-        ),
-    )
-    grids = [[ref[...] for ref in grid_refs]]
-    if pair > 1:
-        grids.append([ref[nodes:] for ref in early_refs])
-    product(0, grids)
-
-
-def gradients(place, blocks, latents, early, late, other, grids, members, pair):
+        rights = rights + [ref[:nodes] for ref in early_refs]
+    store(1, product_of(node_sums(slots(1), chosen_ref[...], shards), rights))
+
+
+def first_gradients(place, blocks, latents, early, late, other, members, pair):
     count, _, width = blocks.shape
     shards = count // pair
-    features = late[0].shape[1]
-    points = late[0].shape[0]
-    depth = features // members
-    return pl.pallas_call(
-        functools.partial(
-            gradient_kernel, shards, pair, members, latents[0].shape[0]
-        ),
+    points, features = late[0].shape
+    nodes = latents[0].shape[0]
+    shape = jax.ShapeDtypeStruct
+    return pl.pallas_call(
+        functools.partial(first_gradients_kernel, shards, pair, nodes),
         out_shape=(
-            jax.ShapeDtypeStruct((members, 4 * width, depth), BF16),
-            jax.ShapeDtypeStruct((1, 1), F32),
-        ),
-        in_specs=[SMEM] + [VMEM] * (1 + 5 * shards),
-        out_specs=(VMEM, VMEM),
+            shape((members, 2 * width, features // members), BF16),
+            shape((nodes * shards, points * shards), BF16),
+            shape((1, 1), F32),
+        ),
+        in_specs=[SMEM] + [VMEM] * (1 + 4 * shards),
+        out_specs=(VMEM,) * 3,
         cost_estimate=pl.CostEstimate(
-            flops=8 * points * count * features * width,
-            bytes_accessed=8 * points * count * features,
+            flops=4 * points * count * features * width,
+            bytes_accessed=4 * points * count * features,
             transcendentals=0,
         ),
-        name="weight_gradients",
-    )(place, blocks, *latents, *early, *late, *other, *grids)
+        name="first_gradients",
+    )(place, blocks, *latents, *early, *late, *other)
+
+
+def last_gradients_kernel(shards, pair, members, nodes, place_ref, chosen_ref, *refs):
+    count = shards * pair
+    left_refs, refs = refs[:count], refs[count:]
+    latent_refs, early_refs, grid_refs = (refs[i * shards : (i + 1) * shards] for i in range(3))
+    *out_refs, block_ref = refs[3 * shards :]
+    points = grid_refs[0].shape[0]
+    width = left_refs[0].shape[1]
+    depth = block_ref.shape[2]
+
+    def slots(kind):
+        at = slice(kind * points, (kind + 1) * points)
+        return [left_refs[k * pair + t][at] for t in range(pair) for k in range(shards)]
+
+    def store(kind, total):
+        for m in range(members):
+            block_ref[m, kind * width : (kind + 1) * width] = total[:, m * depth : (m + 1) * depth]
+
+    rights = [ref[...] for ref in grid_refs]
+    if pair > 1:
+        rights = rights + [ref[nodes:] for ref in early_refs]
+    store(0, product_of(slots(0), rights))
+    rights = [ref[...] for ref in latent_refs]
+    if pair > 1:
+        rights = rights + [ref[:nodes] for ref in early_refs]
+    store(1, product_of(node_sums(slots(1), chosen_ref[...], shards), rights))
+    for k, ref in enumerate(out_refs):
+        ref[...] = block_ref[place_ref[2] ^ k]
+
+
+def last_gradients(place, lefts, chosen, latents, early, grids, members, pair):
+    count, width = len(lefts), lefts[0].shape[1]
+    shards = count // pair
+    points, features = grids[0].shape
+    nodes = latents[0].shape[0]
+    block = (2 * width, features // members)
+    return pl.pallas_call(
+        functools.partial(last_gradients_kernel, shards, pair, members, nodes),
+        out_shape=(jax.ShapeDtypeStruct(block, BF16),) * members,
+        in_specs=[SMEM] + [VMEM] * (1 + count + 3 * shards),
+        out_specs=(VMEM,) * members,
+        scratch_shapes=[pltpu.VMEM((members,) + block, BF16)],
+        cost_estimate=pl.CostEstimate(
+            flops=4 * points * count * features * width,
+            bytes_accessed=4 * points * count * features,
+            transcendentals=0,
+        ),
+        name="last_gradients",
+    )(place, chosen, *lefts, *latents, *early, *grids)
 
 
 def sum_kernel(pair, blocks_ref, *refs):
@@ -452,11 +524,43 @@
     _, rows, depth = blocks.shape
     return pl.pallas_call(
         functools.partial(sum_kernel, pair),
-        out_shape=(jax.ShapeDtypeStruct((depth, pair * rows // 4), F32),) * 4,
+        out_shape=(jax.ShapeDtypeStruct((depth, pair * rows // 2), F32),) * 2,
         in_specs=[VMEM],
-        out_specs=(VMEM,) * 4,
+        out_specs=(VMEM,) * 2,
+        cost_estimate=pl.CostEstimate(
+            flops=blocks.size, bytes_accessed=4 * blocks.size, transcendentals=0
+        ),
         name="sum_groups",
     )(blocks)
+
+
+def sum_slots_kernel(pair, place_ref, *refs):
+    slot_refs, out_refs = refs[:-2], refs[-2:]
+    width = slot_refs[0].shape[0] // 2
+    for i, ref in enumerate(out_refs):
+        at = slice(i * width, (i + 1) * width)
+        totals = []
+        for y in range(pair):
+            total = slot_refs[y][at].astype(F32)
+            for k in range(y + pair, len(slot_refs), pair):
+                total = total + slot_refs[k][at].astype(F32)
+            totals.append(total.T)
+        for y in range(pair):
+            value = totals[y]
+            if pair > 1:
+                value = jnp.where(place_ref[1] == y, totals[0], totals[1])
+            ref[:, y * width : (y + 1) * width] = value
+
+
+def sum_slots(place, parts, pair):
+    rows, depth = parts[0].shape
+    return pl.pallas_call(
+        functools.partial(sum_slots_kernel, pair),
+        out_shape=(jax.ShapeDtypeStruct((depth, pair * rows // 2), F32),) * 2,
+        in_specs=[SMEM] + [VMEM] * len(parts),
+        out_specs=(VMEM,) * 2,
+        name="sum_slots",
+    )(place, *parts)
 
 
 def join_kernel(shard_ref, *refs):
@@ -484,7 +588,7 @@
 def sum_outer(parts):
     total = parts[0].astype(F32)
     received = []
-    for k in range(1, parts.shape[0]):
+    for k in range(1, len(parts)):
         received.append(swap(parts[k], "space", k))
     for value in received:
         total = total + value.astype(F32)
@@ -538,12 +642,13 @@
         for k, part in enumerate(late):
             other.append(swap(other[k - 1], "space", 1) if k % 2 else swap(part, "ens", 1))
     saved = (queries, keyset, valueset, soft, normed, inverse)
-    blocks, outer = backward(
+    place = jnp.stack([shard, half, member])
+    blocks, d_attended, *outer = backward_slopes(
         jnp.stack([shard, member]),
         packed,
         target,
         tile_neighbor_index,
-        saved,
+        (valueset, soft, normed, inverse),
         readout_weight,
         w_mix,
         shards,
@@ -558,15 +663,30 @@
         axis_index_groups=groups,
         tiled=True,
     )
-    place = jnp.stack([shard, half])
+    saved = (queries, keyset, valueset, soft)
+    parts = backward_scores(place, saved, d_attended, count, pair)
+    lefts = [parts[0]]
+    for i in range(1, count):
+        k, t = divmod(i, pair)
+        moves = [
+            (m * shards + s, (m ^ t) * shards + (s ^ k))
+            for m in range(members)
+            for s in range(shards)
+        ]
+        lefts.append(lax.ppermute(parts[i], ("ens", "space"), moves))
     outer = sum_outer(outer)
-    blocks, loss = gradients(
-        place, blocks, latents, early, late, other, grids, members, pair
+    blocks, chosen, loss = first_gradients(
+        place, blocks, latents, early, late, other, members, pair
     )
     blocks = lax.all_to_all(blocks, "ens", split_axis=0, concat_axis=0, tiled=True)
+    parts = last_gradients(place, lefts, chosen, latents, early, grids, members, pair)
+    sums = [parts[0]]
+    for k in range(1, members):
+        sums.append(swap(parts[k], "ens", k))
     grad_out = join_columns(shard[None], outer, channels_used)
-    grads = sum_groups(blocks, pair)
-    return (loss.reshape(()), grad_out, *grads)
+    grad_mix, grad_value = sum_groups(blocks, pair)
+    grad_query, grad_key = sum_slots(place, sums, pair)
+    return (loss.reshape(()), grad_out, grad_query, grad_key, grad_value, grad_mix)
 
 
 def solution(mesh):

time: 149 us -> 144 us (0.966)
  waiting for transfers between devices: 73.5 us -> 45.1 us
  starting transfers between devices: 39.7 us -> 53.5 us
  Pallas kernels: 27.7 us -> 35 us
    ppermute x26 -> x33, waiting for transfers between devices: 73.5 us -> 41.8 us  [swap(): return lax.ppermute(value, axis, [(i, i ^ bits) for i in range(size)])]
    ppermute x26 -> x33, starting transfers between devices: 24.3 us -> 34 us  [swap(): return lax.ppermute(value, axis, [(i, i ^ bits) for i in range(size)])]
    pallas_call x2 -> x5, Pallas kernels: 13.2 us -> 20.8 us  [the longest x1 5.2 us: backward_slopes(): pl.pallas_call(functools.partial(slopes_kernel, shards, blocks, nodes), o...]
    ppermute x0 -> x7, starting transfers between devices: none -> 6.21 us  [body(): lefts.append(lax.ppermute(parts[i], ('ens', 'space'), moves))]
    ppermute x0 -> x7, waiting for transfers between devices: none -> 3.27 us  [body(): lefts.append(lax.ppermute(parts[i], ('ens', 'space'), moves))]
    unnamed x46 -> x72, local copies, waits for them, and re-layouts: 5.36 us -> 6.12 us
  transfers between devices with their start and end apart: 29 -> 43, of which waited for: 12 -> 10; matrix products, arithmetic and copies ran while one was open for 1% -> 2% of each run, Pallas kernels for 9% -> 23%
where the time goes in v7:
time: 144 us; the launch traced here: 143 us
  starting transfers between devices  53.5 us (37%)
  waiting for transfers between devices  45.1 us (31%)
  Pallas kernels  35 us (24%)
  local copies, waits for them, and re-layouts  6.12 us (4%)
  other arithmetic  2.21 us (2%)
    ppermute x33, waiting for transfers between devices, swap(): return lax.ppermute(value, axis, [(i, i ^ bits) for i in range(size)])  41.8 us
    ppermute x33, starting transfers between devices, swap(): return lax.ppermute(value, axis, [(i, i ^ bits) for i in range(size)])  34 us
    pallas_call x1, Pallas kernels, forward(): pl.pallas_call(functools.partial(forward_kernel, len(latents), members),...  6.56 us
    ppermute x7, starting transfers between devices, body(): lefts.append(lax.ppermute(parts[i], ('ens', 'space'), moves))  6.21 us
    unnamed x72, local copies, waits for them, and re-layouts  6.12 us
    pallas_call x1, Pallas kernels, backward_slopes(): pl.pallas_call(functools.partial(slopes_kernel, shards, blocks, nodes), o...  5.2 us
    all_to_all x1, starting transfers between devices, body(): lax.all_to_all(packed, 'ens', split_axis=0, concat_axis=0, tiled=True)  4.89 us
    all_to_all x1, starting transfers between devices, body(): lax.all_to_all(blocks, 'ens', split_axis=0, concat_axis=0, tiled=True)  4.86 us
  transfers between devices with their start and end apart: 43, of which 10 were waited for; matrix products, arithmetic and copies ran while one was open for 2% of the time, Pallas kernels for 23%

profile of v7, /device:TPU:0, one launch (start us, length us, event | category | flops | bytes accessed | tf_op | source)
XLA Modules:
  0.0 142.9 jit_solution(5840799737708589711)
XLA Ops:
  0.6 3.0 %collective-permute-start.1 = (bf16[128,1024]{1,0:T(8,128)(2,1)}, bf16[128,1024]{1,0:T(8,128)(2,1)S(1)}, u32[]{:S(2)}, u32[]{:S(2)}) collective-permute-start(bf16[128,1024]{1,0:T(8,128)(2,1)} %bitcast.6), channel_id=1, source_target_pairs={{0,2},{1,3},{2,0},{3,1},{4,6},{5,7},{6,4},{7,5},{8,10},{9,11},{10,... | collective-permute-start | bytes 786440 | tf_op jit(solution)/shard_map/ppermute | solution.py:28
  3.7 6.5 %collective-permute-done.1.refs_7_.refs_2_.refs_10_ = bf16[128,1024]{1,0:T(8,128)(2,1)S(1)} collective-permute-done((bf16[128,1024]{1,0:T(8,128)(2,1)}, bf16[128,1024]{1,0:T(8,128)(2,1)S(1)}, u32[]{:S(2)}, u32[]{:S(2)}) %collective-permute-start.1) | collective-permute-done | bytes 262176 | tf_op jit(solution)/shard_map/ppermute | solution.py:28
  10.2 4.0 %project_queries.1 = (bf16[128,1024]{1,0:T(8,128)(2,1)}, bf16[256,1024]{1,0:T(8,128)(2,1)}) custom-call(bf16[128,1024]{1,0:T(8,128)(2,1)} %bitcast.8, bf16[128,1024]{1,0:T(8,128)(2,1)} %bitcast.12, bf16[1024,1024]{1,0:T(8,128)(2,1)} %w_hbm.2), custom_call_target="tpu_custom_call" | custom-call | flops 268435456 | bytes 2097152 | tf_op jit(solution)/shard_map/project_queries/pallas_call | solution.py:71
  14.2 1.8 %collective-permute-start.3 = (bf16[256,1024]{1,0:T(8,128)(2,1)}, bf16[256,1024]{1,0:T(8,128)(2,1)S(1)}, u32[]{:S(2)}, u32[]{:S(2)}) collective-permute-start(bf16[256,1024]{1,0:T(8,128)(2,1)} %get-tuple-element.51), channel_id=1, source_target_pairs={{0,4},{4,0},{8,12},{12,8},{16,20},{20,16},{24,28},{28,24},{1,5},{5... | collective-permute-start | bytes 1572872 | tf_op jit(solution)/shard_map/ppermute | solution.py:28
  16.9 6.6 %decoder_forward.1 = (bf16[128,1024]{1,0:T(8,128)(2,1)}, bf16[128,1024]{1,0:T(8,128)(2,1)}, f32[8,128,256]{2,1,0:T(8,128)}, bf16[128,1024]{1,0:T(8,128)(2,1)}, f...) custom-call(s32[1]{0:T(128)} %bitcast.refs_0_.shard_ref, s32[1,128]{1,0:T(1,128)} %index_ref.1, ...), custom_call_target="tpu_custom_call" | custom-call | flops 1073741824 | bytes 6291456 | tf_op jit(solution)/shard_map/decoder_forward/pallas_call | solution.py:157
  23.5 4.9 %all-to-all-start = ((bf16[8,224,128]{2,1,0:T(8,128)(2,1)}), bf16[8,224,128]{2,1,0:T(8,128)(2,1)S(1)}, u32[]{:S(2)}, u32[]{:S(2)}) async-start(bf16[8,224,128]{2,1,0:T(8,128)(2,1)} %get-tuple-element.45), calls=%async_computation | async-start | bytes 917504 | tf_op jit(solution)/shard_map/all_to_all | solution.py:637
  30.8 1.7 %collective-permute-start.10 = (bf16[128,1024]{1,0:T(8,128)(2,1)}, bf16[128,1024]{1,0:T(8,128)(2,1)S(1)}, u32[]{:S(2)}, u32[]{:S(2)}) collective-permute-start(bf16[128,1024]{1,0:T(8,128)(2,1)} %get-tuple-element.52.refs_8_), channel_id=1, source_target_pairs={{0,4},{4,0},{8,12},{12,8},{16,20},{20,16},{24,28},{28,24},{1,5},{5... | collective-permute-start | bytes 786440 | tf_op jit(solution)/shard_map/ppermute | solution.py:28
  32.6 15.3 %collective-permute-done.8.refs_10_ = bf16[128,1024]{1,0:T(8,128)(2,1)S(1)} collective-permute-done((bf16[128,1024]{1,0:T(8,128)(2,1)}, bf16[128,1024]{1,0:T(8,128)(2,1)S(1)}, u32[]{:S(2)}, u32[]{:S(2)}) %collective-permute-start.8) | collective-permute-done | bytes 262176 | tf_op jit(solution)/shard_map/ppermute | solution.py:28
  51.5 5.2 %backward_slopes.1 = (bf16[8,272,128]{2,1,0:T(8,128)(2,1)}, bf16[128,1024]{1,0:T(8,128)(2,1)}, bf16[112,256]{1,0:T(8,128)(2,1)}, bf16[112,256]{1,0:T(8,128)(2,1)...) custom-call(s32[2]{0:T(128)} %pad_add_fusion.1.place_ref, bf16[8,224,128]{2,1,0:T(8,128)(2,1)} %copy-done.10, ...), custom_call_target="tpu_custom_call" | custom-call | flops 268435456 | bytes 2097152 | tf_op jit(solution)/shard_map/backward_slopes/pallas_call | solution.py:312
  56.7 3.5 %all-to-all-start.1 = ((bf16[8,272,128]{2,1,0:T(8,128)(2,1)}), bf16[8,272,128]{2,1,0:T(8,128)(2,1)S(1)}, u32[]{:S(2)}, u32[]{:S(2)}) async-start(bf16[8,272,128]{2,1,0:T(8,128)(2,1)} %get-tuple-element.50), calls=%async_computation.1 | async-start | bytes 1114112 | tf_op jit(solution)/shard_map/all_to_all | solution.py:658
  62.9 8.2 %collective-permute-done.15 = bf16[112,256]{1,0:T(8,128)(2,1)S(1)} collective-permute-done((bf16[112,256]{1,0:T(8,128)(2,1)}, bf16[112,256]{1,0:T(8,128)(2,1)S(1)}, u32[]{:S(2)}, u32[]{:S(2)}) %collective-permute-start.15) | collective-permute-done | bytes 57376 | tf_op jit(solution)/shard_map/ppermute | solution.py:28
  78.0 4.7 %first_gradients.1 = (bf16[8,256,128]{2,1,0:T(8,128)(2,1)}, bf16[512,512]{1,0:T(8,128)(2,1)}, f32[1,1]{1,0:T(1,128)}) custom-call(s32[3]{0:T(128)} %pad_add_fusion.place_ref, bf16[8,272,128]{2,1,0:T(8,128)(2,1)} %copy-done.4, bf16[128,1024]{1,0:T(8,128)(2,1)} %bitcast.10, bf16[128,1024]{1,0:T(8,128)(2,1)} %copy-done.2, bf16[128,1024]{1,0:T(8,128)(2,1)} %copy-done.1, ...), custom_call_target="tpu_custom_call" | custom-call | flops 536870912 | bytes 4194304 | tf_op jit(solution)/shard_map/first_gradients/pallas_call | solution.py:443
  82.7 4.9 %all-to-all-start.2 = ((bf16[8,256,128]{2,1,0:T(8,128)(2,1)}), bf16[8,256,128]{2,1,0:T(8,128)(2,1)S(1)}, u32[]{:S(2)}, u32[]{:S(2)}) async-start(bf16[8,256,128]{2,1,0:T(8,128)(2,1)} %get-tuple-element.79), calls=%async_computation.2 | async-start | bytes 1048576 | tf_op jit(solution)/shard_map/all_to_all | solution.py:681
  87.6 3.0 %collective-permute-start.18 = (bf16[112,256]{1,0:T(8,128)(2,1)S(1)}, bf16[112,256]{1,0:T(8,128)(2,1)S(1)}, u32[]{:S(2)}, u32[]{:S(2)}) collective-permute-start(bf16[112,256]{1,0:T(8,128)(2,1)S(1)} %add_convert_fusion.2), channel_id=1, source_target_pairs={{0,16},{4,20},{8,24},{12,28},{16,0},{20,4},{24,8},{28,12},{1,17},{... | collective-permute-start | bytes 172040 | tf_op jit(solution)/shard_map/ppermute | solution.py:28
  91.0 4.5 %backward_scores.1 = (bf16[256,128]{1,0:T(8,128)(2,1)}, bf16[256,128]{1,0:T(8,128)(2,1)}, bf16[256,128]{1,0:T(8,128)(2,1)}, bf16[256,128]{1,0:T(8,128)(2,1)}, bf...) custom-call(s32[3]{0:T(128)} %pad_add_fusion.place_ref, ...), custom_call_target="tpu_custom_call" | custom-call | flops 201326592 | bytes 1048576 | tf_op jit(solution)/shard_map/backward_scores/pallas_call | solution.py:363
  97.0 7.3 %collective-permute-done.18 = bf16[112,256]{1,0:T(8,128)(2,1)S(1)} collective-permute-done((bf16[112,256]{1,0:T(8,128)(2,1)S(1)}, bf16[112,256]{1,0:T(8,128)(2,1)S(1)}, u32[]{:S(2)}, u32[]{:S(2)}) %collective-permute-start.18) | collective-permute-done | bytes 57376 | tf_op jit(solution)/shard_map/ppermute | solution.py:28
  115.9 4.5 %last_gradients.1 = (bf16[256,128]{1,0:T(8,128)(2,1)}, bf16[256,128]{1,0:T(8,128)(2,1)}, bf16[256,128]{1,0:T(8,128)(2,1)}, bf16[256,128]{1,0:T(8,128)(2,1)}, bf1...) custom-call(s32[3]{0:T(128)} %pad_add_fusion.place_ref, ...), custom_call_target="tpu_custom_call" | custom-call | flops 536870912 | bytes 4194304 | tf_op jit(solution)/shard_map/last_gradients/pallas_call | solution.py:496
  122.5 2.0 %collective-permute-start.35 = (bf16[256,128]{1,0:T(8,128)(2,1)}, bf16[256,128]{1,0:T(8,128)(2,1)S(1)}, u32[]{:S(2)}, u32[]{:S(2)}) collective-permute-start(bf16[256,128]{1,0:T(8,128)(2,1)} %get-tuple-element.72), channel_id=1, source_target_pairs={{0,12},{4,8},{8,4},{12,0},{16,28},{20,24},{24,20},{28,16},{1,13},{... | collective-permute-start | bytes 196616 | tf_op jit(solution)/shard_map/ppermute | solution.py:28
  125.1 3.2 %collective-permute-start.37 = (bf16[256,128]{1,0:T(8,128)(2,1)}, bf16[256,128]{1,0:T(8,128)(2,1)S(1)}, u32[]{:S(2)}, u32[]{:S(2)}) collective-permute-start(bf16[256,128]{1,0:T(8,128)(2,1)} %get-tuple-element.74), channel_id=1, source_target_pairs={{0,20},{4,16},{8,28},{12,24},{16,4},{20,0},{24,12},{28,8},{1,21},{... | collective-permute-start | bytes 196616 | tf_op jit(solution)/shard_map/ppermute | solution.py:28
  129.7 2.5 %collective-permute-start.39 = (bf16[256,128]{1,0:T(8,128)(2,1)}, bf16[256,128]{1,0:T(8,128)(2,1)S(1)}, u32[]{:S(2)}, u32[]{:S(2)}) collective-permute-start(bf16[256,128]{1,0:T(8,128)(2,1)} %get-tuple-element.76), channel_id=1, source_target_pairs={{0,28},{4,24},{8,20},{12,16},{16,12},{20,8},{24,4},{28,0},{1,29},{... | collective-permute-start | bytes 196616 | tf_op jit(solution)/shard_map/ppermute | solution.py:28
  132.2 1.7 %join_columns.1 = f32[100,1024]{1,0:T(8,128)} custom-call(s32[1]{0:T(128)} %bitcast.refs_0_.shard_ref, bf16[112,256]{1,0:T(8,128)(2,1)} %copy-done.17, bf16[112,256]{1,0:T(8,128)(2,1)} %copy-done.33, bf16[112,256]{1,0:T(8,128)(2,1)} %copy-done.32, bf16[112,256]{1,0:T(8,128)(2,1)} %copy-done.34), custom_call_target="tpu_custom_call" | custom-call | tf_op jit(solution)/shard_map/join_columns/pallas_call | solution.py:579
  133.9 3.8 %collective-permute-done.37.refs_5_ = bf16[256,128]{1,0:T(8,128)(2,1)S(1)} collective-permute-done((bf16[256,128]{1,0:T(8,128)(2,1)}, bf16[256,128]{1,0:T(8,128)(2,1)S(1)}, u32[]{:S(2)}, u32[]{:S(2)}) %collective-permute-start.37) | collective-permute-done | bytes 65568 | tf_op jit(solution)/shard_map/ppermute | solution.py:28
  138.4 1.9 %sum_slots.1 = (f32[128,256]{1,0:T(8,128)}, f32[128,256]{1,0:T(8,128)}) custom-call(s32[3]{0:T(128)} %pad_add_fusion.place_ref, bf16[256,128]{1,0:T(8,128)(2,1)} %get-tuple-element.69.refs_0_, bf16[256,128]{1,0:T(8,128)(2,1)} %copy-done.25, bf16[256,128]{1,0:T(8,128)(2,1)} %copy-done.26, bf16[256,128]{1,0:T(8,128)(2,1)} %copy-done.27, ...), custom_call_target="tpu_custom_call" | custom-call | tf_op jit(solution)/shard_map/sum_slots/pallas_call | solution.py:557
  141.1 1.8 %sum_groups.1 = (f32[128,256]{1,0:T(8,128)}, f32[128,256]{1,0:T(8,128)}) custom-call(bf16[8,256,128]{2,1,0:T(8,128)(2,1)} %copy-done.5), custom_call_target="tpu_custom_call" | custom-call | flops 262144 | bytes 1048576 | tf_op jit(solution)/shard_map/sum_groups/pallas_call | solution.py:525
  (149 shorter events, 35.2 us)
Async XLA Ops:
  3.7 12.4 %collective-permute-start = (bf16[128,1024]{1,0:T(8,128)(2,1)}, bf16[128,1024]{1,0:T(8,128)(2,1)S(1)}, u32[]{:S(2)}, u32[]{:S(2)}) collective-permute-start(bf16[128,1024]{1,0:T(8,128)(2,1)} %bitcast.7), channel_id=1, source_target_pairs={{0,1},{1,0},{2,3},{3,2},{4,5},{5,4},{6,7},{7,6},{8,9},{9,8},{10,11... | collective-permute-start | bytes 786440 | tf_op jit(solution)/shard_map/ppermute | solution.py:28
  14.2 14.5 %collective-permute-start.3 = (bf16[256,1024]{1,0:T(8,128)(2,1)}, bf16[256,1024]{1,0:T(8,128)(2,1)S(1)}, u32[]{:S(2)}, u32[]{:S(2)}) collective-permute-start(bf16[256,1024]{1,0:T(8,128)(2,1)} %get-tuple-element.51), channel_id=1, source_target_pairs={{0,4},{4,0},{8,12},{12,8},{16,20},{20,16},{24,28},{28,24},{1,5},{5... | collective-permute-start | bytes 1572872 | tf_op jit(solution)/shard_map/ppermute | solution.py:28
  23.5 27.2 %all-to-all-start = ((bf16[8,224,128]{2,1,0:T(8,128)(2,1)}), bf16[8,224,128]{2,1,0:T(8,128)(2,1)S(1)}, u32[]{:S(2)}, u32[]{:S(2)}) async-start(bf16[8,224,128]{2,1,0:T(8,128)(2,1)} %get-tuple-element.45), calls=%async_computation | async-start | bytes 917504 | tf_op jit(solution)/shard_map/all_to_all | solution.py:637
  28.8 20.8 %collective-permute-start.5 = (bf16[256,1024]{1,0:T(8,128)(2,1)S(1)}, bf16[256,1024]{1,0:T(8,128)(2,1)S(1)}, u32[]{:S(2)}, u32[]{:S(2)}) collective-permute-start(bf16[256,1024]{1,0:T(8,128)(2,1)S(1)} %collective-permute-done.3.refs_4_.refs_12_), channel_id=1, source_target_pairs={{0,2},{1,3},{2,0},{3,1},{4,6},{5,7},{6,4},{7,5},{8,10},{9,11},{10,... | collective-permute-start | bytes 1572872 | tf_op jit(solution)/shard_map/ppermute | solution.py:28
  30.5 17.3 %collective-permute-start.8 = (bf16[128,1024]{1,0:T(8,128)(2,1)}, bf16[128,1024]{1,0:T(8,128)(2,1)S(1)}, u32[]{:S(2)}, u32[]{:S(2)}) collective-permute-start(bf16[128,1024]{1,0:T(8,128)(2,1)} %get-tuple-element.52.refs_8_), channel_id=1, source_target_pairs={{0,2},{1,3},{2,0},{3,1},{4,6},{5,7},{6,4},{7,5},{8,10},{9,11},{10,... | collective-permute-start | bytes 786440 | tf_op jit(solution)/shard_map/ppermute | solution.py:28
  30.8 29.4 %collective-permute-start.10 = (bf16[128,1024]{1,0:T(8,128)(2,1)}, bf16[128,1024]{1,0:T(8,128)(2,1)S(1)}, u32[]{:S(2)}, u32[]{:S(2)}) collective-permute-start(bf16[128,1024]{1,0:T(8,128)(2,1)} %get-tuple-element.52.refs_8_), channel_id=1, source_target_pairs={{0,4},{4,0},{8,12},{12,8},{16,20},{20,16},{24,28},{28,24},{1,5},{5... | collective-permute-start | bytes 786440 | tf_op jit(solution)/shard_map/ppermute | solution.py:28
  32.6 28.2 %collective-permute-start.7 = (bf16[128,1024]{1,0:T(8,128)(2,1)}, bf16[128,1024]{1,0:T(8,128)(2,1)}, u32[]{:S(2)}, u32[]{:S(2)}) collective-permute-start(bf16[128,1024]{1,0:T(8,128)(2,1)} %get-tuple-element.52.refs_8_), channel_id=1, source_target_pairs={{0,1},{1,0},{2,3},{3,2},{4,5},{5,4},{6,7},{7,6},{8,9},{9,8},{10,11... | collective-permute-start | bytes 786440 | tf_op jit(solution)/shard_map/ppermute | solution.py:28
  47.8 14.6 %collective-permute-start.12 = (bf16[128,1024]{1,0:T(8,128)(2,1)S(1)}, bf16[128,1024]{1,0:T(8,128)(2,1)}, u32[]{:S(2)}, u32[]{:S(2)}) collective-permute-start(bf16[128,1024]{1,0:T(8,128)(2,1)S(1)} %collective-permute-done.8.refs_10_), channel_id=1, source_target_pairs={{0,4},{4,0},{8,12},{12,8},{16,20},{20,16},{24,28},{28,24},{1,5},{5... | collective-permute-start | bytes 786440 | tf_op jit(solution)/shard_map/ppermute | solution.py:28
  49.5 25.9 %collective-permute-start.4 = (bf16[256,1024]{1,0:T(8,128)(2,1)S(1)}, bf16[256,1024]{1,0:T(8,128)(2,1)S(1)}, u32[]{:S(2)}, u32[]{:S(2)}) collective-permute-start(bf16[256,1024]{1,0:T(8,128)(2,1)S(1)} %collective-permute-done.3.refs_4_.refs_12_), channel_id=1, source_target_pairs={{0,1},{1,0},{2,3},{3,2},{4,5},{5,4},{6,7},{7,6},{8,9},{9,8},{10,11... | collective-permute-start | bytes 1572872 | tf_op jit(solution)/shard_map/ppermute | solution.py:28
  49.5 26.8 %collective-permute-start.6 = (bf16[256,1024]{1,0:T(8,128)(2,1)S(1)}, bf16[256,1024]{1,0:T(8,128)(2,1)S(1)}, u32[]{:S(2)}, u32[]{:S(2)}) collective-permute-start(bf16[256,1024]{1,0:T(8,128)(2,1)S(1)} %collective-permute-done.5.refs_6_.refs_14_), channel_id=1, source_target_pairs={{0,1},{1,0},{2,3},{3,2},{4,5},{5,4},{6,7},{7,6},{8,9},{9,8},{10,11... | collective-permute-start | bytes 1572872 | tf_op jit(solution)/shard_map/ppermute | solution.py:28
  56.7 19.7 %all-to-all-start.1 = ((bf16[8,272,128]{2,1,0:T(8,128)(2,1)}), bf16[8,272,128]{2,1,0:T(8,128)(2,1)S(1)}, u32[]{:S(2)}, u32[]{:S(2)}) async-start(bf16[8,272,128]{2,1,0:T(8,128)(2,1)} %get-tuple-element.50), calls=%async_computation.1 | async-start | bytes 1114112 | tf_op jit(solution)/shard_map/all_to_all | solution.py:658
  60.7 10.4 %collective-permute-start.15 = (bf16[112,256]{1,0:T(8,128)(2,1)}, bf16[112,256]{1,0:T(8,128)(2,1)S(1)}, u32[]{:S(2)}, u32[]{:S(2)}) collective-permute-start(bf16[112,256]{1,0:T(8,128)(2,1)} %get-tuple-element.56), channel_id=1, source_target_pairs={{0,2},{1,3},{2,0},{3,1},{4,6},{5,7},{6,4},{7,5},{8,10},{9,11},{10,... | collective-permute-start | bytes 172040 | tf_op jit(solution)/shard_map/ppermute | solution.py:28
  62.5 10.2 %collective-permute-start.9 = (bf16[128,1024]{1,0:T(8,128)(2,1)S(1)}, bf16[128,1024]{1,0:T(8,128)(2,1)}, u32[]{:S(2)}, u32[]{:S(2)}) collective-permute-start(bf16[128,1024]{1,0:T(8,128)(2,1)S(1)} %collective-permute-done.8.refs_10_), channel_id=1, source_target_pairs={{0,1},{1,0},{2,3},{3,2},{4,5},{5,4},{6,7},{7,6},{8,9},{9,8},{10,11... | collective-permute-start | bytes 786440 | tf_op jit(solution)/shard_map/ppermute | solution.py:28
  72.7 14.9 %collective-permute-start.17 = (bf16[112,256]{1,0:T(8,128)(2,1)S(1)}, bf16[112,256]{1,0:T(8,128)(2,1)S(1)}, u32[]{:S(2)}, u32[]{:S(2)}) collective-permute-start(bf16[112,256]{1,0:T(8,128)(2,1)S(1)} %add_convert_fusion.3), channel_id=1, source_target_pairs={{0,8},{4,12},{8,0},{12,4},{16,24},{20,28},{24,16},{28,20},{1,9},{5... | collective-permute-start | bytes 172040 | tf_op jit(solution)/shard_map/ppermute | solution.py:28
  75.0 15.6 %collective-permute-start.31 = (bf16[128,1024]{1,0:T(8,128)(2,1)S(1)}, bf16[128,1024]{1,0:T(8,128)(2,1)}, u32[]{:S(2)}, u32[]{:S(2)}) collective-permute-start(bf16[128,1024]{1,0:T(8,128)(2,1)S(1)} %bitcast.15), channel_id=1, source_target_pairs={{0,2},{1,3},{2,0},{3,1},{4,6},{5,7},{6,4},{7,5},{8,10},{9,11},{10,... | collective-permute-start | bytes 786440 | tf_op jit(solution)/shard_map/ppermute | solution.py:28
  82.7 57.6 %all-to-all-start.2 = ((bf16[8,256,128]{2,1,0:T(8,128)(2,1)}), bf16[8,256,128]{2,1,0:T(8,128)(2,1)S(1)}, u32[]{:S(2)}, u32[]{:S(2)}) async-start(bf16[8,256,128]{2,1,0:T(8,128)(2,1)} %get-tuple-element.79), calls=%async_computation.2 | async-start | bytes 1048576 | tf_op jit(solution)/shard_map/all_to_all | solution.py:681
  87.6 16.8 %collective-permute-start.18 = (bf16[112,256]{1,0:T(8,128)(2,1)S(1)}, bf16[112,256]{1,0:T(8,128)(2,1)S(1)}, u32[]{:S(2)}, u32[]{:S(2)}) collective-permute-start(bf16[112,256]{1,0:T(8,128)(2,1)S(1)} %add_convert_fusion.2), channel_id=1, source_target_pairs={{0,16},{4,20},{8,24},{12,28},{16,0},{20,4},{24,8},{28,12},{1,17},{... | collective-permute-start | bytes 172040 | tf_op jit(solution)/shard_map/ppermute | solution.py:28
  90.5 15.4 %collective-permute-start.30 = (bf16[128,1024]{1,0:T(8,128)(2,1)S(1)}, bf16[128,1024]{1,0:T(8,128)(2,1)S(1)}, u32[]{:S(2)}, u32[]{:S(2)}) collective-permute-start(bf16[128,1024]{1,0:T(8,128)(2,1)S(1)} %bitcast.16), channel_id=1, source_target_pairs={{0,1},{1,0},{2,3},{3,2},{4,5},{5,4},{6,7},{7,6},{8,9},{9,8},{10,11... | collective-permute-start | bytes 786440 | tf_op jit(solution)/shard_map/ppermute | solution.py:28
  90.5 15.4 %collective-permute-start.32 = (bf16[128,1024]{1,0:T(8,128)(2,1)}, bf16[128,1024]{1,0:T(8,128)(2,1)S(1)}, u32[]{:S(2)}, u32[]{:S(2)}) collective-permute-start(bf16[128,1024]{1,0:T(8,128)(2,1)} %collective-permute-done.31.refs_18_), channel_id=1, source_target_pairs={{0,1},{1,0},{2,3},{3,2},{4,5},{5,4},{6,7},{7,6},{8,9},{9,8},{10,11... | collective-permute-start | bytes 786440 | tf_op jit(solution)/shard_map/ppermute | solution.py:28
  95.6 11.6 %collective-permute-start.23 = (bf16[256,128]{1,0:T(8,128)(2,1)}, bf16[256,128]{1,0:T(8,128)(2,1)S(1)}, u32[]{:S(2)}, u32[]{:S(2)}) collective-permute-start(bf16[256,128]{1,0:T(8,128)(2,1)} %get-tuple-element.62), channel_id=1, source_target_pairs={{0,4},{1,5},{2,6},{3,7},{4,0},{5,1},{6,2},{7,3},{8,12},{9,13},{10,... | collective-permute-start | bytes 196616 | tf_op jit(solution)/shard_map/ppermute | solution.py:676
  97.0 11.0 %collective-permute-start.24 = (bf16[256,128]{1,0:T(8,128)(2,1)}, bf16[256,128]{1,0:T(8,128)(2,1)S(1)}, u32[]{:S(2)}, u32[]{:S(2)}) collective-permute-start(bf16[256,128]{1,0:T(8,128)(2,1)} %get-tuple-element.63), channel_id=1, source_target_pairs={{0,1},{1,0},{2,3},{3,2},{4,5},{5,4},{6,7},{7,6},{8,9},{9,8},{10,11... | collective-permute-start | bytes 196616 | tf_op jit(solution)/shard_map/ppermute | solution.py:676
  110.7 11.2 %collective-permute-start.21 = (bf16[112,256]{1,0:T(8,128)(2,1)S(1)}, bf16[112,256]{1,0:T(8,128)(2,1)S(1)}, u32[]{:S(2)}, u32[]{:S(2)}) collective-permute-start(bf16[112,256]{1,0:T(8,128)(2,1)S(1)} %add_convert_fusion.refs_0_), channel_id=1, source_target_pairs={{0,2},{1,3},{2,0},{3,1},{4,6},{5,7},{6,4},{7,5},{8,10},{9,11},{10,... | collective-permute-start | bytes 172040 | tf_op jit(solution)/shard_map/ppermute | solution.py:28
  122.5 11.4 %collective-permute-start.35 = (bf16[256,128]{1,0:T(8,128)(2,1)}, bf16[256,128]{1,0:T(8,128)(2,1)S(1)}, u32[]{:S(2)}, u32[]{:S(2)}) collective-permute-start(bf16[256,128]{1,0:T(8,128)(2,1)} %get-tuple-element.72), channel_id=1, source_target_pairs={{0,12},{4,8},{8,4},{12,0},{16,28},{20,24},{24,20},{28,16},{1,13},{... | collective-permute-start | bytes 196616 | tf_op jit(solution)/shard_map/ppermute | solution.py:28
  125.1 12.6 %collective-permute-start.37 = (bf16[256,128]{1,0:T(8,128)(2,1)}, bf16[256,128]{1,0:T(8,128)(2,1)S(1)}, u32[]{:S(2)}, u32[]{:S(2)}) collective-permute-start(bf16[256,128]{1,0:T(8,128)(2,1)} %get-tuple-element.74), channel_id=1, source_target_pairs={{0,20},{4,16},{8,28},{12,24},{16,4},{20,0},{24,12},{28,8},{1,21},{... | collective-permute-start | bytes 196616 | tf_op jit(solution)/shard_map/ppermute | solution.py:28
  (55 other events, 342.4 us)

commit v8 on v6

--- a/solution.py
+++ b/solution.py
@@ -17,6 +17,7 @@
 VMEM = pl.BlockSpec(memory_space=pltpu.VMEM)
 SMEM = pl.BlockSpec(memory_space=pltpu.SMEM)
 ANY = pl.BlockSpec(memory_space=pl.ANY)
+HBM = pl.BlockSpec(memory_space=pltpu.HBM)
 
 
 def dot32(left, right, contract=(1, 0)):
@@ -84,7 +85,7 @@
         cost_estimate=pl.CostEstimate(
             flops=2 * rows.size * features, bytes_accessed=2 * weight.size, transcendentals=0
         ),
-        name="project_queries",
+        name="proj",
     )(latent, rows, weight)
 
 
@@ -175,7 +176,7 @@
             bytes_accessed=6 * features * features,
             transcendentals=points * LANES * HEADS,
         ),
-        name="decoder_forward",
+        name="fwd",
     )(shard, index, grid_rows, queries, readout, *latents, *weights)
 
 
@@ -196,15 +197,10 @@
     readout_ref,
     w_hbm,
     out_ref,
-    outer_ref,
-    w_ref,
-    slope_ref,
-    d_attended_ref,
-    small_ref,
-    truth_ref,
-    weight_ref,
-    sem,
+    *refs,
 ):
+    outer_refs = refs[:shards]
+    slope_ref, d_attended_ref, small_ref, truth_ref, weight_ref, w_ref, sem = refs[shards:]
     copy = pltpu.make_async_copy(w_hbm, w_ref, sem)
     copy.start()
     members = packed_ref.shape[0]
@@ -288,7 +284,7 @@
         part = parts[0]
         for s in range(1, shards):
             part = jnp.where((place_ref[0] ^ k) == s, parts[s], part)
-        outer_ref[k] = part.astype(BF16)
+        outer_refs[k][...] = part.astype(BF16)
     d_normed = dot32(own, weight_ref[...], (0, 0))
     mean = jnp.mean(d_normed * normed, axis=-1, keepdims=True)
     d_hidden = (inverse_ref[...] * (d_normed - normed * mean)).astype(BF16)
@@ -324,17 +320,17 @@
         functools.partial(backward_kernel, shards, blocks, nodes),
         out_shape=(
             jax.ShapeDtypeStruct((blocks, 4 * points + small, width), BF16),
-            jax.ShapeDtypeStruct((shards, channels, features // shards), BF16),
-        ),
+        )
+        + (jax.ShapeDtypeStruct((channels, features // shards), BF16),) * shards,
         in_specs=[SMEM] + [VMEM] * 10 + [ANY],
-        out_specs=(VMEM, VMEM),
+        out_specs=(VMEM,) * (1 + shards),
         scratch_shapes=[
-            pltpu.VMEM((features, features), BF16),
             pltpu.VMEM((members, channels, points), BF16),
             pltpu.VMEM((points, features), BF16),
             pltpu.VMEM((small, width), F32),
             pltpu.VMEM((channels, points), F32),
             pltpu.VMEM((channels, features), BF16),
+            pltpu.VMEM((features, features), BF16),
             pltpu.SemaphoreType.DMA,
         ],
         cost_estimate=pl.CostEstimate(
@@ -342,18 +338,39 @@
             bytes_accessed=4 * features * features,
             transcendentals=0,
         ),
-        name="decoder_backward",
+        name="bwd",
     )(place, packed, target, index, *saved, readout, w_mix)
 
 
-def gradient_kernel(shards, pair, members, nodes, place_ref, blocks_ref, *refs):
+def gradient_kernel(shards, pair, members, nodes, place_ref, blocks_hbm, *refs):
     latent_refs, early_refs, late_refs, other_refs, grid_refs = (
         refs[i * shards : (i + 1) * shards] for i in range(5)
     )
-    out_ref, loss_ref = refs[5 * shards :]
+    out_ref, loss_ref, blocks_ref, late_ref, node_ref, grid_ref, sems = refs[5 * shards :]
+    sources = [late_refs, latent_refs, grid_refs]
+    if pair > 1:
+        sources = [
+            late_refs + other_refs,
+            latent_refs + tuple(ref.at[:nodes] for ref in early_refs),
+            grid_refs + tuple(ref.at[nodes:] for ref in early_refs),
+        ]
+    first = pltpu.make_async_copy(blocks_hbm, blocks_ref, sems.at[0, 0])
+    first.start()
+    copies = []
+    for i, (parts, full) in enumerate(zip(sources, (late_ref, node_ref, grid_ref))):
+        step = full.shape[0] // len(parts)
+        copies.append(
+            [
+                pltpu.make_async_copy(part, full.at[pl.ds(k * step, step)], sems.at[i + 1, k])
+                for k, part in enumerate(parts)
+            ]
+        )
+        for copy in copies[-1]:
+            copy.start()
+    first.wait()
     width = blocks_ref.shape[2]
-    features = late_refs[0].shape[1]
-    points = late_refs[0].shape[0]
+    features = late_ref.shape[1]
+    points = grid_ref.shape[0] // (shards * pair)
     depth = features // members
     shard, half = place_ref[0], place_ref[1]
     start = 4 * points
@@ -372,12 +389,13 @@
         for m in range(members):
             out_ref[m, at] = total[:, m * depth : (m + 1) * depth]
 
-    def product(kind, parts):
+    def product(kind, full, group):
         left = jnp.concatenate([v for t in range(pair) for v in slots(kind, t)], axis=0)
-        right = jnp.concatenate([v for part in parts for v in part], axis=0)
-        put(kind, dot32(left, right, (0, 0)))
-
-    product(3, [[ref[...] for ref in part] for part in (late_refs, other_refs)[:pair]])
+        for copy in copies[group]:
+            copy.wait()
+        put(kind, dot32(left, full[...], (0, 0)))
+
+    product(3, late_ref, 0)
     chosen = []
     for k in range(shards):
         index = blocks_ref[(shard ^ k) * pair, start : start + MISC].astype(jnp.int32)
@@ -394,21 +412,10 @@
     for t in range(pair):
         both = [jnp.concatenate(slots(kind, t), axis=0) for kind in (1, 2)]
         sums.append(dot32(chosen, jnp.concatenate(both, axis=1)).astype(BF16))
-    others = [[ref[...] for ref in latent_refs]]
-    if pair > 1:
-        others.append([ref[:nodes] for ref in early_refs])
-    put(
-        1,
-        dot32(
-            jnp.concatenate(sums, axis=0),
-            jnp.concatenate([v for part in others for v in part], axis=0),
-            (0, 0),
-        ),
-    )
-    grids = [[ref[...] for ref in grid_refs]]
-    if pair > 1:
-        grids.append([ref[nodes:] for ref in early_refs])
-    product(0, grids)
+    for copy in copies[1]:
+        copy.wait()
+    put(1, dot32(jnp.concatenate(sums, axis=0), node_ref[...], (0, 0)))
+    product(0, grid_ref, 2)
 
 
 def gradients(place, blocks, latents, early, late, other, grids, members, pair):
@@ -425,21 +432,35 @@
             jax.ShapeDtypeStruct((members, 4 * width, depth), BF16),
             jax.ShapeDtypeStruct((1, 1), F32),
         ),
-        in_specs=[SMEM] + [VMEM] * (1 + 5 * shards),
+        in_specs=[SMEM] + [HBM] * (1 + 5 * shards),
         out_specs=(VMEM, VMEM),
+        scratch_shapes=[pltpu.VMEM(blocks.shape, BF16)]
+        + [
+            pltpu.VMEM((count * rows, features), BF16)
+            for rows in (points, latents[0].shape[0], points)
+        ]
+        + [pltpu.SemaphoreType.DMA((4, count))],
         cost_estimate=pl.CostEstimate(
             flops=8 * points * count * features * width,
             bytes_accessed=8 * points * count * features,
             transcendentals=0,
         ),
-        name="weight_gradients",
+        name="wgrad",
     )(place, blocks, *latents, *early, *late, *other, *grids)
 
 
-def sum_kernel(pair, blocks_ref, *refs):
+def sum_kernel(pair, blocks_hbm, *refs):
+    *refs, blocks_ref, sem = refs
     members, rows, _ = blocks_ref.shape
     width = rows // len(refs)
+    copies = [
+        pltpu.make_async_copy(blocks_hbm.at[:, pl.ds(i * width, width)], blocks_ref.at[:, pl.ds(i * width, width)], sem.at[i])
+        for i in range(len(refs))
+    ]
+    for copy in copies:
+        copy.start()
     for i, ref in enumerate(refs):
+        copies[i].wait()
         at = slice(i * width, (i + 1) * width)
         for y in range(pair):
             total = blocks_ref[y, at].astype(F32)
@@ -453,9 +474,10 @@
     return pl.pallas_call(
         functools.partial(sum_kernel, pair),
         out_shape=(jax.ShapeDtypeStruct((depth, pair * rows // 4), F32),) * 4,
-        in_specs=[VMEM],
+        in_specs=[HBM],
         out_specs=(VMEM,) * 4,
-        name="sum_groups",
+        scratch_shapes=[pltpu.VMEM(blocks.shape, BF16), pltpu.SemaphoreType.DMA((4,))],
+        name="sums",
     )(blocks)
 
 
@@ -477,14 +499,14 @@
         out_shape=jax.ShapeDtypeStruct((channels_used, columns), F32),
         in_specs=[SMEM] + [VMEM] * len(parts),
         out_specs=VMEM,
-        name="join_columns",
+        name="join",
     )(shard, *parts)
 
 
 def sum_outer(parts):
     total = parts[0].astype(F32)
     received = []
-    for k in range(1, parts.shape[0]):
+    for k in range(1, len(parts)):
         received.append(swap(parts[k], "space", k))
     for value in received:
         total = total + value.astype(F32)
@@ -538,7 +560,7 @@
         for k, part in enumerate(late):
             other.append(swap(other[k - 1], "space", 1) if k % 2 else swap(part, "ens", 1))
     saved = (queries, keyset, valueset, soft, normed, inverse)
-    blocks, outer = backward(
+    blocks, *outer = backward(
         jnp.stack([shard, member]),
         packed,
         target,

time: 149 us -> 149 us (level)
    unnamed x46 -> x52, local copies, waits for them, and re-layouts: 5.36 us -> 5.38 us
where the time goes in v8:
time: 149 us; the launch traced here: 148 us
  waiting for transfers between devices  73.5 us (49%)
  starting transfers between devices  39.6 us (27%)
  Pallas kernels  27.7 us (19%)
  local copies, waits for them, and re-layouts  5.38 us (4%)
    ppermute x26, waiting for transfers between devices, swap(): return lax.ppermute(value, axis, [(i, i ^ bits) for i in range(size)])  73.5 us
    ppermute x26, starting transfers between devices, swap(): return lax.ppermute(value, axis, [(i, i ^ bits) for i in range(size)])  24.3 us
    pallas_call x1, Pallas kernels, backward(): pl.pallas_call(functools.partial(backward_kernel, shards, blocks, nodes),...  7.38 us
    pallas_call x1, Pallas kernels, forward(): pl.pallas_call(functools.partial(forward_kernel, len(latents), members),...  6.63 us
    all_to_all x1, starting transfers between devices, body(): lax.all_to_all(packed, 'ens', split_axis=0, concat_axis=0, tiled=True)  6.09 us
    pallas_call x1, Pallas kernels, gradients(): pl.pallas_call(functools.partial(gradient_kernel, shards, pair, members,...  5.78 us
    all_to_all x1, starting transfers between devices, body(): lax.all_to_all(blocks, 'ens', split_axis=0, concat_axis=0, tiled=True)  5.58 us
    unnamed x52, local copies, waits for them, and re-layouts  5.38 us
  transfers between devices with their start and end apart: 29, of which 12 were waited for; matrix products, arithmetic and copies ran while one was open for 1% of the time, Pallas kernels for 9%

profile of v8, /device:TPU:0, one launch (start us, length us, event | category | flops | bytes accessed | tf_op | source)
XLA Modules:
  0.0 148.5 jit_solution(11524915500592606892)
XLA Ops:
  0.6 3.0 %collective-permute-start.1 = (bf16[128,1024]{1,0:T(8,128)(2,1)}, bf16[128,1024]{1,0:T(8,128)(2,1)S(1)}, u32[]{:S(2)}, u32[]{:S(2)}) collective-permute-start(bf16[128,1024]{1,0:T(8,128)(2,1)} %bitcast.11), channel_id=1, source_target_pairs={{0,2},{1,3},{2,0},{3,1},{4,6},{5,7},{6,4},{7,5},{8,10},{9,11},{10,... | collective-permute-start | bytes 786440 | tf_op jit(solution)/shard_map/ppermute | solution.py:30
  3.7 6.5 %collective-permute-done.1.refs_7_.refs_2_ = bf16[128,1024]{1,0:T(8,128)(2,1)S(1)} collective-permute-done((bf16[128,1024]{1,0:T(8,128)(2,1)}, bf16[128,1024]{1,0:T(8,128)(2,1)S(1)}, u32[]{:S(2)}, u32[]{:S(2)}) %collective-permute-start.1) | collective-permute-done | bytes 262176 | tf_op jit(solution)/shard_map/ppermute | solution.py:30
  10.2 4.0 %proj.1 = (bf16[128,1024]{1,0:T(8,128)(2,1)}, bf16[256,1024]{1,0:T(8,128)(2,1)}) custom-call(bf16[128,1024]{1,0:T(8,128)(2,1)} %bitcast.13, bf16[128,1024]{1,0:T(8,128)(2,1)} %bitcast.6, bf16[1024,1024]{1,0:T(8,128)(2,1)} %w_hbm.2), custom_call_target="tpu_custom_call" | custom-call | flops 268435456 | bytes 2097152 | tf_op jit(solution)/shard_map/proj/pallas_call | solution.py:73
  15.1 6.6 %fwd.1 = (bf16[128,1024]{1,0:T(8,128)(2,1)}, bf16[128,1024]{1,0:T(8,128)(2,1)}, f32[8,128,256]{2,1,0:T(8,128)}, bf16[128,1024]{1,0:T(8,128)(2,1)}, f32[128,1024]...) custom-call(s32[1]{0:T(128)} %bitcast.refs_0_.shard_ref, s32[1,128]{1,0:T(1,128)} %index_ref.1, ...), custom_call_target="tpu_custom_call" | custom-call | flops 1073741824 | bytes 6291456 | tf_op jit(solution)/shard_map/fwd/pallas_call | solution.py:159
  21.7 6.1 %all-to-all-start = ((bf16[8,224,128]{2,1,0:T(8,128)(2,1)}), bf16[8,224,128]{2,1,0:T(8,128)(2,1)S(1)}, u32[]{:S(2)}, u32[]{:S(2)}) async-start(bf16[8,224,128]{2,1,0:T(8,128)(2,1)} %get-tuple-element.27), calls=%async_computation | async-start | bytes 917504 | tf_op jit(solution)/shard_map/all_to_all | solution.py:555
  27.8 2.0 %collective-permute-start.3 = (bf16[256,1024]{1,0:T(8,128)(2,1)S(1)}, bf16[256,1024]{1,0:T(8,128)(2,1)S(1)}, u32[]{:S(2)}, u32[]{:S(2)}) collective-permute-start(bf16[256,1024]{1,0:T(8,128)(2,1)S(1)} %copy-done.22), channel_id=1, source_target_pairs={{0,4},{4,0},{8,12},{12,8},{16,20},{20,16},{24,28},{28,24},{1,5},{5... | collective-permute-start | bytes 1572872 | tf_op jit(solution)/shard_map/ppermute | solution.py:30
  31.3 15.6 %collective-permute-done.3.refs_4_ = bf16[256,1024]{1,0:T(8,128)(2,1)S(1)} collective-permute-done((bf16[256,1024]{1,0:T(8,128)(2,1)S(1)}, bf16[256,1024]{1,0:T(8,128)(2,1)S(1)}, u32[]{:S(2)}, u32[]{:S(2)}) %collective-permute-start.3) | collective-permute-done | bytes 524320 | tf_op jit(solution)/shard_map/ppermute | solution.py:30
  49.8 7.4 %bwd.1 = (bf16[8,528,128]{2,1,0:T(8,128)(2,1)}, bf16[112,256]{1,0:T(8,128)(2,1)}, bf16[112,256]{1,0:T(8,128)(2,1)}, bf16[112,256]{1,0:T(8,128)(2,1)}, bf16[112,256]{1,0:T(8,128)(2,1)}) custom-call(s32[2]{0:T(128)} %pad_add_fusion.1.place_ref, bf16[8,224,128]{2,1,0:T(8,128)(2,1)} %copy-done.3, f32[100,128]{1,0:T(8,128)} %target_ref.1, s32[1,128]{1,0:T(1,128)} %index_ref.1, ...), custom_call_target="tpu_custom_call" | custom-call | flops 536870912 | bytes 4194304 | tf_op jit(solution)/shard_map/bwd/pallas_call | solution.py:319
  57.2 3.7 %all-to-all-start.1 = ((bf16[8,528,128]{2,1,0:T(8,128)(2,1)}), bf16[8,528,128]{2,1,0:T(8,128)(2,1)S(1)}, u32[]{:S(2)}, u32[]{:S(2)}) async-start(bf16[8,528,128]{2,1,0:T(8,128)(2,1)} %get-tuple-element.33), calls=%async_computation.1 | async-start | bytes 2162688 | tf_op jit(solution)/shard_map/all_to_all | solution.py:575
  61.5 1.9 %collective-permute-start.8 = (bf16[128,1024]{1,0:T(8,128)(2,1)S(1)}, bf16[128,1024]{1,0:T(8,128)(2,1)}, u32[]{:S(2)}, u32[]{:S(2)}) collective-permute-start(bf16[128,1024]{1,0:T(8,128)(2,1)S(1)} %copy-done.11), channel_id=1, source_target_pairs={{0,2},{1,3},{2,0},{3,1},{4,6},{5,7},{6,4},{7,5},{8,10},{9,11},{10,... | collective-permute-start | bytes 786440 | tf_op jit(solution)/shard_map/ppermute | solution.py:30
  63.4 1.5 %collective-permute-start.10 = (bf16[128,1024]{1,0:T(8,128)(2,1)S(1)}, bf16[128,1024]{1,0:T(8,128)(2,1)}, u32[]{:S(2)}, u32[]{:S(2)}) collective-permute-start(bf16[128,1024]{1,0:T(8,128)(2,1)S(1)} %copy-done.11), channel_id=1, source_target_pairs={{0,4},{4,0},{8,12},{12,8},{16,20},{20,16},{24,28},{28,24},{1,5},{5... | collective-permute-start | bytes 786440 | tf_op jit(solution)/shard_map/ppermute | solution.py:30
  65.2 16.3 %collective-permute-done.8.refs_10_ = bf16[128,1024]{1,0:T(8,128)(2,1)} collective-permute-done((bf16[128,1024]{1,0:T(8,128)(2,1)S(1)}, bf16[128,1024]{1,0:T(8,128)(2,1)}, u32[]{:S(2)}, u32[]{:S(2)}) %collective-permute-start.8) | collective-permute-done | bytes 262176 | tf_op jit(solution)/shard_map/ppermute | solution.py:30
  84.2 5.3 %collective-permute-done.12.refs_14_ = bf16[128,1024]{1,0:T(8,128)(2,1)} collective-permute-done((bf16[128,1024]{1,0:T(8,128)(2,1)}, bf16[128,1024]{1,0:T(8,128)(2,1)}, u32[]{:S(2)}, u32[]{:S(2)}) %collective-permute-start.12) | collective-permute-done | bytes 262176 | tf_op jit(solution)/shard_map/ppermute | solution.py:30
  93.3 5.8 %wgrad.1 = (bf16[8,512,128]{2,1,0:T(8,128)(2,1)}, f32[1,1]{1,0:T(1,128)}) custom-call(s32[2]{0:T(128)} %pad_add_fusion.place_ref, bf16[8,528,128]{2,1,0:T(8,128)(2,1)} %copy-done, bf16[128,1024]{1,0:T(8,128)(2,1)} %bitcast.15, bf16[128,1024]{1,0:T(8,128)(2,1)} %copy-done.5, bf16[128,1024]{1,0:T(8,128)(2,1)} %copy-done.4, bf16[128,1024]{1,0:T(8,128)(2,1)} %copy-done.6, ...), custom_call_target="tpu_custom_call" | custom-call | flops 1073741824 | bytes 8388608 | tf_op jit(solution)/shard_map/wgrad/pallas_call | solution.py:427
  99.1 5.6 %all-to-all-start.2 = ((bf16[8,512,128]{2,1,0:T(8,128)(2,1)}), bf16[8,512,128]{2,1,0:T(8,128)(2,1)S(1)}, u32[]{:S(2)}, u32[]{:S(2)}) async-start(bf16[8,512,128]{2,1,0:T(8,128)(2,1)} %get-tuple-element.41), calls=%async_computation.2 | async-start | bytes 2097152 | tf_op jit(solution)/shard_map/all_to_all | solution.py:588
  106.6 2.3 %collective-permute-done.19 = bf16[112,256]{1,0:T(8,128)(2,1)S(1)} collective-permute-done((bf16[112,256]{1,0:T(8,128)(2,1)S(1)}, bf16[112,256]{1,0:T(8,128)(2,1)S(1)}, u32[]{:S(2)}, u32[]{:S(2)}) %collective-permute-start.19) | collective-permute-done | bytes 57376 | tf_op jit(solution)/shard_map/ppermute | solution.py:30
  110.2 1.5 %collective-permute-start.20 = (bf16[112,256]{1,0:T(8,128)(2,1)S(1)}, bf16[112,256]{1,0:T(8,128)(2,1)S(1)}, u32[]{:S(2)}, u32[]{:S(2)}) collective-permute-start(bf16[112,256]{1,0:T(8,128)(2,1)S(1)} %add_convert_fusion.3), channel_id=1, source_target_pairs={{0,8},{4,12},{8,0},{12,4},{16,24},{20,28},{24,16},{28,20},{1,9},{5... | collective-permute-start | bytes 172040 | tf_op jit(solution)/shard_map/ppermute | solution.py:30
  111.8 12.1 %collective-permute-done.20 = bf16[112,256]{1,0:T(8,128)(2,1)S(1)} collective-permute-done((bf16[112,256]{1,0:T(8,128)(2,1)S(1)}, bf16[112,256]{1,0:T(8,128)(2,1)S(1)}, u32[]{:S(2)}, u32[]{:S(2)}) %collective-permute-start.20) | collective-permute-done | bytes 57376 | tf_op jit(solution)/shard_map/ppermute | solution.py:30
  123.9 4.0 %collective-permute-start.21 = (bf16[112,256]{1,0:T(8,128)(2,1)S(1)}, bf16[112,256]{1,0:T(8,128)(2,1)S(1)}, u32[]{:S(2)}, u32[]{:S(2)}) collective-permute-start(bf16[112,256]{1,0:T(8,128)(2,1)S(1)} %add_convert_fusion.2), channel_id=1, source_target_pairs={{0,16},{4,20},{8,24},{12,28},{16,0},{20,4},{24,8},{28,12},{1,17},{... | collective-permute-start | bytes 172040 | tf_op jit(solution)/shard_map/ppermute | solution.py:30
  128.0 5.2 %collective-permute-done.21 = bf16[112,256]{1,0:T(8,128)(2,1)S(1)} collective-permute-done((bf16[112,256]{1,0:T(8,128)(2,1)S(1)}, bf16[112,256]{1,0:T(8,128)(2,1)S(1)}, u32[]{:S(2)}, u32[]{:S(2)}) %collective-permute-start.21) | collective-permute-done | bytes 57376 | tf_op jit(solution)/shard_map/ppermute | solution.py:30
  134.7 2.8 %collective-permute-done.22 = bf16[112,256]{1,0:T(8,128)(2,1)S(1)} collective-permute-done((bf16[112,256]{1,0:T(8,128)(2,1)S(1)}, bf16[112,256]{1,0:T(8,128)(2,1)S(1)}, u32[]{:S(2)}, u32[]{:S(2)}) %collective-permute-start.22) | collective-permute-done | bytes 57376 | tf_op jit(solution)/shard_map/ppermute | solution.py:30
  138.1 3.6 %collective-permute-done.24.refs_2_ = bf16[112,256]{1,0:T(8,128)(2,1)S(1)} collective-permute-done((bf16[112,256]{1,0:T(8,128)(2,1)S(1)}, bf16[112,256]{1,0:T(8,128)(2,1)S(1)}, u32[]{:S(2)}, u32[]{:S(2)}) %collective-permute-start.24) | collective-permute-done | bytes 57376 | tf_op jit(solution)/shard_map/ppermute | solution.py:30
  143.6 1.7 %join.1 = f32[100,1024]{1,0:T(8,128)} custom-call(s32[1]{0:T(128)} %bitcast.refs_0_.shard_ref, bf16[112,256]{1,0:T(8,128)(2,1)} %copy-done.17, bf16[112,256]{1,0:T(8,128)(2,1)} %copy-done.19, bf16[112,256]{1,0:T(8,128)(2,1)} %copy-done.18, bf16[112,256]{1,0:T(8,128)(2,1)} %copy-done.20), custom_call_target="tpu_custom_call" | custom-call | tf_op jit(solution)/shard_map/join/pallas_call | solution.py:497
  146.4 2.1 %sums.1 = (f32[128,256]{1,0:T(8,128)}, f32[128,256]{1,0:T(8,128)}, f32[128,256]{1,0:T(8,128)}, f32[128,256]{1,0:T(8,128)}) custom-call(bf16[8,512,128]{2,1,0:T(8,128)(2,1)} %copy-done.1), custom_call_target="tpu_custom_call" | custom-call | tf_op jit(solution)/shard_map/sums/pallas_call | solution.py:474
  (98 shorter events, 20.7 us)
Async XLA Ops:
  0.6 9.6 %collective-permute-start.1 = (bf16[128,1024]{1,0:T(8,128)(2,1)}, bf16[128,1024]{1,0:T(8,128)(2,1)S(1)}, u32[]{:S(2)}, u32[]{:S(2)}) collective-permute-start(bf16[128,1024]{1,0:T(8,128)(2,1)} %bitcast.11), channel_id=1, source_target_pairs={{0,2},{1,3},{2,0},{3,1},{4,6},{5,7},{6,4},{7,5},{8,10},{9,11},{10,... | collective-permute-start | bytes 786440 | tf_op jit(solution)/shard_map/ppermute | solution.py:30
  3.7 10.6 %collective-permute-start = (bf16[128,1024]{1,0:T(8,128)(2,1)}, bf16[128,1024]{1,0:T(8,128)(2,1)S(1)}, u32[]{:S(2)}, u32[]{:S(2)}) collective-permute-start(bf16[128,1024]{1,0:T(8,128)(2,1)} %bitcast.12), channel_id=1, source_target_pairs={{0,1},{1,0},{2,3},{3,2},{4,5},{5,4},{6,7},{7,6},{8,9},{9,8},{10,11... | collective-permute-start | bytes 786440 | tf_op jit(solution)/shard_map/ppermute | solution.py:30
  10.2 4.1 %collective-permute-start.2 = (bf16[128,1024]{1,0:T(8,128)(2,1)S(1)}, bf16[128,1024]{1,0:T(8,128)(2,1)S(1)}, u32[]{:S(2)}, u32[]{:S(2)}) collective-permute-start(bf16[128,1024]{1,0:T(8,128)(2,1)S(1)} %collective-permute-done.1.refs_7_.refs_2_), channel_id=1, source_target_pairs={{0,1},{1,0},{2,3},{3,2},{4,5},{5,4},{6,7},{7,6},{8,9},{9,8},{10,11... | collective-permute-start | bytes 786440 | tf_op jit(solution)/shard_map/ppermute | solution.py:30
  21.7 27.3 %all-to-all-start = ((bf16[8,224,128]{2,1,0:T(8,128)(2,1)}), bf16[8,224,128]{2,1,0:T(8,128)(2,1)S(1)}, u32[]{:S(2)}, u32[]{:S(2)}) async-start(bf16[8,224,128]{2,1,0:T(8,128)(2,1)} %get-tuple-element.27), calls=%async_computation | async-start | bytes 917504 | tf_op jit(solution)/shard_map/all_to_all | solution.py:555
  27.8 19.1 %collective-permute-start.3 = (bf16[256,1024]{1,0:T(8,128)(2,1)S(1)}, bf16[256,1024]{1,0:T(8,128)(2,1)S(1)}, u32[]{:S(2)}, u32[]{:S(2)}) collective-permute-start(bf16[256,1024]{1,0:T(8,128)(2,1)S(1)} %copy-done.22), channel_id=1, source_target_pairs={{0,4},{4,0},{8,12},{12,8},{16,20},{20,16},{24,28},{28,24},{1,5},{5... | collective-permute-start | bytes 1572872 | tf_op jit(solution)/shard_map/ppermute | solution.py:30
  29.8 31.5 %collective-permute-start.15 = (bf16[128,1024]{1,0:T(8,128)(2,1)S(1)}, bf16[128,1024]{1,0:T(8,128)(2,1)S(1)}, u32[]{:S(2)}, u32[]{:S(2)}) collective-permute-start(bf16[128,1024]{1,0:T(8,128)(2,1)S(1)} %bitcast.9), channel_id=1, source_target_pairs={{0,2},{1,3},{2,0},{3,1},{4,6},{5,7},{6,4},{7,5},{8,10},{9,11},{10,... | collective-permute-start | bytes 786440 | tf_op jit(solution)/shard_map/ppermute | solution.py:30
  46.9 36.0 %collective-permute-start.5 = (bf16[256,1024]{1,0:T(8,128)(2,1)S(1)}, bf16[256,1024]{1,0:T(8,128)(2,1)S(1)}, u32[]{:S(2)}, u32[]{:S(2)}) collective-permute-start(bf16[256,1024]{1,0:T(8,128)(2,1)S(1)} %collective-permute-done.3.refs_4_), channel_id=1, source_target_pairs={{0,2},{1,3},{2,0},{3,1},{4,6},{5,7},{6,4},{7,5},{8,10},{9,11},{10,... | collective-permute-start | bytes 1572872 | tf_op jit(solution)/shard_map/ppermute | solution.py:30
  57.2 34.2 %all-to-all-start.1 = ((bf16[8,528,128]{2,1,0:T(8,128)(2,1)}), bf16[8,528,128]{2,1,0:T(8,128)(2,1)S(1)}, u32[]{:S(2)}, u32[]{:S(2)}) async-start(bf16[8,528,128]{2,1,0:T(8,128)(2,1)} %get-tuple-element.33), calls=%async_computation.1 | async-start | bytes 2162688 | tf_op jit(solution)/shard_map/all_to_all | solution.py:575
  61.5 19.9 %collective-permute-start.8 = (bf16[128,1024]{1,0:T(8,128)(2,1)S(1)}, bf16[128,1024]{1,0:T(8,128)(2,1)}, u32[]{:S(2)}, u32[]{:S(2)}) collective-permute-start(bf16[128,1024]{1,0:T(8,128)(2,1)S(1)} %copy-done.11), channel_id=1, source_target_pairs={{0,2},{1,3},{2,0},{3,1},{4,6},{5,7},{6,4},{7,5},{8,10},{9,11},{10,... | collective-permute-start | bytes 786440 | tf_op jit(solution)/shard_map/ppermute | solution.py:30
  63.4 19.6 %collective-permute-start.7 = (bf16[128,1024]{1,0:T(8,128)(2,1)S(1)}, bf16[128,1024]{1,0:T(8,128)(2,1)S(1)}, u32[]{:S(2)}, u32[]{:S(2)}) collective-permute-start(bf16[128,1024]{1,0:T(8,128)(2,1)S(1)} %copy-done.11), channel_id=1, source_target_pairs={{0,1},{1,0},{2,3},{3,2},{4,5},{5,4},{6,7},{7,6},{8,9},{9,8},{10,11... | collective-permute-start | bytes 786440 | tf_op jit(solution)/shard_map/ppermute | solution.py:30
  63.4 20.1 %collective-permute-start.10 = (bf16[128,1024]{1,0:T(8,128)(2,1)S(1)}, bf16[128,1024]{1,0:T(8,128)(2,1)}, u32[]{:S(2)}, u32[]{:S(2)}) collective-permute-start(bf16[128,1024]{1,0:T(8,128)(2,1)S(1)} %copy-done.11), channel_id=1, source_target_pairs={{0,4},{4,0},{8,12},{12,8},{16,20},{20,16},{24,28},{28,24},{1,5},{5... | collective-permute-start | bytes 786440 | tf_op jit(solution)/shard_map/ppermute | solution.py:30
  64.9 25.2 %collective-permute-start.4 = (bf16[256,1024]{1,0:T(8,128)(2,1)S(1)}, bf16[256,1024]{1,0:T(8,128)(2,1)S(1)}, u32[]{:S(2)}, u32[]{:S(2)}) collective-permute-start(bf16[256,1024]{1,0:T(8,128)(2,1)S(1)} %collective-permute-done.3.refs_4_), channel_id=1, source_target_pairs={{0,1},{1,0},{2,3},{3,2},{4,5},{5,4},{6,7},{7,6},{8,9},{9,8},{10,11... | collective-permute-start | bytes 1572872 | tf_op jit(solution)/shard_map/ppermute | solution.py:30
  81.4 8.1 %collective-permute-start.12 = (bf16[128,1024]{1,0:T(8,128)(2,1)}, bf16[128,1024]{1,0:T(8,128)(2,1)}, u32[]{:S(2)}, u32[]{:S(2)}) collective-permute-start(bf16[128,1024]{1,0:T(8,128)(2,1)} %collective-permute-done.8.refs_10_), channel_id=1, source_target_pairs={{0,4},{4,0},{8,12},{12,8},{16,20},{20,16},{24,28},{28,24},{1,5},{5... | collective-permute-start | bytes 786440 | tf_op jit(solution)/shard_map/ppermute | solution.py:30
  82.9 8.5 %collective-permute-start.6 = (bf16[256,1024]{1,0:T(8,128)(2,1)S(1)}, bf16[256,1024]{1,0:T(8,128)(2,1)S(1)}, u32[]{:S(2)}, u32[]{:S(2)}) collective-permute-start(bf16[256,1024]{1,0:T(8,128)(2,1)S(1)} %collective-permute-done.5.refs_6_), channel_id=1, source_target_pairs={{0,1},{1,0},{2,3},{3,2},{4,5},{5,4},{6,7},{7,6},{8,9},{9,8},{10,11... | collective-permute-start | bytes 1572872 | tf_op jit(solution)/shard_map/ppermute | solution.py:30
  83.0 7.1 %collective-permute-start.9 = (bf16[128,1024]{1,0:T(8,128)(2,1)}, bf16[128,1024]{1,0:T(8,128)(2,1)}, u32[]{:S(2)}, u32[]{:S(2)}) collective-permute-start(bf16[128,1024]{1,0:T(8,128)(2,1)} %collective-permute-done.8.refs_10_), channel_id=1, source_target_pairs={{0,1},{1,0},{2,3},{3,2},{4,5},{5,4},{6,7},{7,6},{8,9},{9,8},{10,11... | collective-permute-start | bytes 786440 | tf_op jit(solution)/shard_map/ppermute | solution.py:30
  83.8 6.3 %collective-permute-start.11 = (bf16[128,1024]{1,0:T(8,128)(2,1)}, bf16[128,1024]{1,0:T(8,128)(2,1)S(1)}, u32[]{:S(2)}, u32[]{:S(2)}) collective-permute-start(bf16[128,1024]{1,0:T(8,128)(2,1)} %collective-permute-done.10.refs_12_), channel_id=1, source_target_pairs={{0,1},{1,0},{2,3},{3,2},{4,5},{5,4},{6,7},{7,6},{8,9},{9,8},{10,11... | collective-permute-start | bytes 786440 | tf_op jit(solution)/shard_map/ppermute | solution.py:30
  99.1 46.3 %all-to-all-start.2 = ((bf16[8,512,128]{2,1,0:T(8,128)(2,1)}), bf16[8,512,128]{2,1,0:T(8,128)(2,1)S(1)}, u32[]{:S(2)}, u32[]{:S(2)}) async-start(bf16[8,512,128]{2,1,0:T(8,128)(2,1)} %get-tuple-element.41), calls=%async_computation.2 | async-start | bytes 2097152 | tf_op jit(solution)/shard_map/all_to_all | solution.py:588
  104.7 4.2 %collective-permute-start.19 = (bf16[112,256]{1,0:T(8,128)(2,1)S(1)}, bf16[112,256]{1,0:T(8,128)(2,1)S(1)}, u32[]{:S(2)}, u32[]{:S(2)}) collective-permute-start(bf16[112,256]{1,0:T(8,128)(2,1)S(1)} %copy-done.25), channel_id=1, source_target_pairs={{0,3},{1,2},{2,1},{3,0},{4,7},{5,6},{6,5},{7,4},{8,11},{9,10},{10,... | collective-permute-start | bytes 172040 | tf_op jit(solution)/shard_map/ppermute | solution.py:30
  104.8 5.4 %collective-permute-start.18 = (bf16[112,256]{1,0:T(8,128)(2,1)S(1)}, bf16[112,256]{1,0:T(8,128)(2,1)S(1)}, u32[]{:S(2)}, u32[]{:S(2)}) collective-permute-start(bf16[112,256]{1,0:T(8,128)(2,1)S(1)} %copy-done.24), channel_id=1, source_target_pairs={{0,2},{1,3},{2,0},{3,1},{4,6},{5,7},{6,4},{7,5},{8,10},{9,11},{10,... | collective-permute-start | bytes 172040 | tf_op jit(solution)/shard_map/ppermute | solution.py:30
  106.2 4.0 %collective-permute-start.17 = (bf16[112,256]{1,0:T(8,128)(2,1)S(1)}, bf16[112,256]{1,0:T(8,128)(2,1)S(1)}, u32[]{:S(2)}, u32[]{:S(2)}) collective-permute-start(bf16[112,256]{1,0:T(8,128)(2,1)S(1)} %copy-done.23), channel_id=1, source_target_pairs={{0,1},{1,0},{2,3},{3,2},{4,5},{5,4},{6,7},{7,6},{8,9},{9,8},{10,11... | collective-permute-start | bytes 172040 | tf_op jit(solution)/shard_map/ppermute | solution.py:30
  110.2 13.7 %collective-permute-start.20 = (bf16[112,256]{1,0:T(8,128)(2,1)S(1)}, bf16[112,256]{1,0:T(8,128)(2,1)S(1)}, u32[]{:S(2)}, u32[]{:S(2)}) collective-permute-start(bf16[112,256]{1,0:T(8,128)(2,1)S(1)} %add_convert_fusion.3), channel_id=1, source_target_pairs={{0,8},{4,12},{8,0},{12,4},{16,24},{20,28},{24,16},{28,20},{1,9},{5... | collective-permute-start | bytes 172040 | tf_op jit(solution)/shard_map/ppermute | solution.py:30
  123.9 9.3 %collective-permute-start.21 = (bf16[112,256]{1,0:T(8,128)(2,1)S(1)}, bf16[112,256]{1,0:T(8,128)(2,1)S(1)}, u32[]{:S(2)}, u32[]{:S(2)}) collective-permute-start(bf16[112,256]{1,0:T(8,128)(2,1)S(1)} %add_convert_fusion.2), channel_id=1, source_target_pairs={{0,16},{4,20},{8,24},{12,28},{16,0},{20,4},{24,8},{28,12},{1,17},{... | collective-permute-start | bytes 172040 | tf_op jit(solution)/shard_map/ppermute | solution.py:30
  133.2 4.2 %collective-permute-start.22 = (bf16[112,256]{1,0:T(8,128)(2,1)S(1)}, bf16[112,256]{1,0:T(8,128)(2,1)S(1)}, u32[]{:S(2)}, u32[]{:S(2)}) collective-permute-start(bf16[112,256]{1,0:T(8,128)(2,1)S(1)} %add_convert_fusion.1), channel_id=1, source_target_pairs={{0,4},{4,0},{8,12},{12,8},{16,20},{20,16},{24,28},{28,24},{1,5},{5... | collective-permute-start | bytes 172040 | tf_op jit(solution)/shard_map/ppermute | solution.py:30
  137.5 4.2 %collective-permute-start.24 = (bf16[112,256]{1,0:T(8,128)(2,1)S(1)}, bf16[112,256]{1,0:T(8,128)(2,1)S(1)}, u32[]{:S(2)}, u32[]{:S(2)}) collective-permute-start(bf16[112,256]{1,0:T(8,128)(2,1)S(1)} %add_convert_fusion.refs_0_), channel_id=1, source_target_pairs={{0,2},{1,3},{2,0},{3,1},{4,6},{5,7},{6,4},{7,5},{8,10},{9,11},{10,... | collective-permute-start | bytes 172040 | tf_op jit(solution)/shard_map/ppermute | solution.py:30
  (31 other events, 189.7 us)

commit v9 on v8

--- a/solution.py
+++ b/solution.py
@@ -94,19 +94,34 @@
     latent_refs = refs[5 : 5 + shards]
     weights_hbm = refs[5 + shards : 8 + shards]
     (
+        key_hbm,
+        value_hbm,
+        soft_hbm,
+        attended_ref,
+        normed_hbm,
+        inverse_ref,
+        packed_ref,
         key_ref,
         value_ref,
         soft_ref,
-        attended_ref,
         normed_ref,
-        inverse_ref,
-        packed_ref,
         *w_refs,
         sem,
+        out_sem,
     ) = refs[8 + shards :]
     copies = [pltpu.make_async_copy(s, d, sem.at[i]) for i, (s, d) in enumerate(zip(weights_hbm, w_refs))]
     for copy in copies:
         copy.start()
+    key_copy, value_copy, normed_copy = (
+        pltpu.make_async_copy(full, out, out_sem.at[i])
+        for i, (full, out) in enumerate(
+            ((key_ref, key_hbm), (value_ref, value_hbm), (normed_ref, normed_hbm))
+        )
+    )
+    soft_copies = [
+        pltpu.make_async_copy(soft_ref.at[i], soft_hbm.at[i], out_sem.at[3 + i])
+        for i in range(soft_ref.shape[0])
+    ]
     points, features = grid_ref.shape
     latents = jnp.concatenate([ref[...] for ref in latent_refs], axis=0)
     each = latent_refs[0].shape[0]
@@ -117,8 +132,10 @@
     nodes = dot32(chosen, latents, (0, 0)).astype(BF16)
     copies[0].wait()
     key_ref[...] = dot32(nodes, w_refs[0][...]).astype(BF16)
+    key_copy.start()
     copies[1].wait()
     value_ref[...] = dot32(nodes, w_refs[1][...]).astype(BF16)
+    value_copy.start()
     factor = (features // HEADS) ** (-0.5)
     for pair in range(features // LANES):
         at = slice(pair * LANES, (pair + 1) * LANES)
@@ -130,12 +147,14 @@
             soft.append(raised / jnp.sum(raised, axis=-1, keepdims=True))
         soft = jnp.concatenate(soft, axis=1)
         soft_ref[pair] = soft
+        soft_copies[pair].start()
         attended_ref[:, at] = dot32(soft.astype(BF16), halves(value_ref[:, at])).astype(BF16)
     copies[2].wait()
     hidden = grid_ref[...].astype(F32) + dot32(attended_ref[...], w_refs[2][...])
     inverse = lax.rsqrt(jnp.mean(hidden * hidden, axis=-1, keepdims=True) + EPS)
     normed = hidden * inverse
     normed_ref[...] = normed
+    normed_copy.start()
     inverse_ref[...] = inverse
     normed_b = normed.astype(BF16)
     forecast = dot32(readout_ref[...], normed_b, (1, 1))
@@ -146,6 +165,8 @@
     fields = jnp.concatenate([high, spare, low, spare], axis=0)
     for m in range(members):
         packed_ref[m] = fields
+    for copy in (key_copy, value_copy, normed_copy, *soft_copies):
+        copy.wait()
 
 
 def padded(channels):
@@ -168,9 +189,18 @@
             shape((members, 2 * channels, points), BF16),
         ),
         in_specs=[SMEM] + [VMEM] * (4 + len(latents)) + [ANY] * 3,
-        out_specs=(VMEM,) * 7,
-        scratch_shapes=[pltpu.VMEM((features, features), BF16)] * 3
-        + [pltpu.SemaphoreType.DMA((3,))],
+        out_specs=(HBM, HBM, HBM, VMEM, HBM, VMEM, VMEM),
+        scratch_shapes=[
+            pltpu.VMEM((points, features), BF16),
+            pltpu.VMEM((points, features), BF16),
+            pltpu.VMEM((features // LANES, points, 2 * LANES), F32),
+            pltpu.VMEM((points, features), F32),
+        ]
+        + [pltpu.VMEM((features, features), BF16)] * 3
+        + [
+            pltpu.SemaphoreType.DMA((3,)),
+            pltpu.SemaphoreType.DMA((3 + features // LANES,)),
+        ],
         cost_estimate=pl.CostEstimate(
             flops=8 * points * features * features,
             bytes_accessed=6 * features * features,
@@ -188,21 +218,27 @@
     packed_ref,
     target_ref,
     index_ref,
-    query_ref,
-    key_ref,
-    value_ref,
-    soft_ref,
-    normed_ref,
+    query_hbm,
+    key_hbm,
+    value_hbm,
+    soft_hbm,
+    normed_hbm,
     inverse_ref,
     readout_ref,
     w_hbm,
     out_ref,
     *refs,
 ):
-    outer_refs = refs[:shards]
-    slope_ref, d_attended_ref, small_ref, truth_ref, weight_ref, w_ref, sem = refs[shards:]
-    copy = pltpu.make_async_copy(w_hbm, w_ref, sem)
-    copy.start()
+    outer_refs, refs = refs[:shards], refs[shards:]
+    slope_ref, d_attended_ref, small_ref, truth_ref, weight_ref, *full_refs, sem = refs
+    sources = (normed_hbm, w_hbm, value_hbm, soft_hbm, key_hbm, query_hbm)
+    copies = [
+        pltpu.make_async_copy(part, full, sem.at[i])
+        for i, (part, full) in enumerate(zip(sources, full_refs))
+    ]
+    for copy in copies:
+        copy.start()
+    normed_ref, w_ref, value_ref, soft_ref, key_ref, query_ref = full_refs
     members = packed_ref.shape[0]
     points, features = normed_ref.shape
     channels_used = readout_ref.shape[0]
@@ -276,6 +312,7 @@
             ]
 
     own = slope_ref[place_ref[1]]
+    copies[0].wait()
     normed = normed_ref[...]
     outer = dot32(own, normed.astype(BF16))
     columns = features // shards
@@ -289,9 +326,11 @@
     mean = jnp.mean(d_normed * normed, axis=-1, keepdims=True)
     d_hidden = (inverse_ref[...] * (d_normed - normed * mean)).astype(BF16)
     put(3, 0, d_hidden)
-    copy.wait()
+    copies[1].wait()
     d_attended_ref[...] = dot32(d_hidden, w_ref[...], (1, 1)).astype(BF16)
     factor = (features // HEADS) ** (-0.5)
+    for copy in copies[2:]:
+        copy.wait()
     for pair in range(features // LANES):
         at = slice(pair * LANES, (pair + 1) * LANES)
         soft = soft_ref[pair]
@@ -322,7 +361,7 @@
             jax.ShapeDtypeStruct((blocks, 4 * points + small, width), BF16),
         )
         + (jax.ShapeDtypeStruct((channels, features // shards), BF16),) * shards,
-        in_specs=[SMEM] + [VMEM] * 10 + [ANY],
+        in_specs=[SMEM] + [VMEM] * 3 + [HBM] * 5 + [VMEM] * 2 + [HBM],
         out_specs=(VMEM,) * (1 + shards),
         scratch_shapes=[
             pltpu.VMEM((members, channels, points), BF16),
@@ -330,8 +369,13 @@
             pltpu.VMEM((small, width), F32),
             pltpu.VMEM((channels, points), F32),
             pltpu.VMEM((channels, features), BF16),
+            pltpu.VMEM((points, features), F32),
             pltpu.VMEM((features, features), BF16),
-            pltpu.SemaphoreType.DMA,
+            pltpu.VMEM((points, features), BF16),
+            pltpu.VMEM((features // LANES, points, 2 * LANES), F32),
+            pltpu.VMEM((points, features), BF16),
+            pltpu.VMEM((points, features), BF16),
+            pltpu.SemaphoreType.DMA((6,)),
         ],
         cost_estimate=pl.CostEstimate(
             flops=4 * points * features * features,
@@ -432,7 +476,7 @@
             jax.ShapeDtypeStruct((members, 4 * width, depth), BF16),
             jax.ShapeDtypeStruct((1, 1), F32),
         ),
-        in_specs=[SMEM] + [HBM] * (1 + 5 * shards),
+        in_specs=[SMEM, ANY] + [HBM] * (5 * shards),
         out_specs=(VMEM, VMEM),
         scratch_shapes=[pltpu.VMEM(blocks.shape, BF16)]
         + [
@@ -474,9 +518,10 @@
     return pl.pallas_call(
         functools.partial(sum_kernel, pair),
         out_shape=(jax.ShapeDtypeStruct((depth, pair * rows // 4), F32),) * 4,
-        in_specs=[HBM],
+        in_specs=[ANY],
         out_specs=(VMEM,) * 4,
         scratch_shapes=[pltpu.VMEM(blocks.shape, BF16), pltpu.SemaphoreType.DMA((4,))],
+        compiler_params=pltpu.CompilerParams(vmem_limit_bytes=8 << 20),
         name="sums",
     )(blocks)
 

time: 149 us -> 148 us (level)
    unnamed x52 -> x50, local copies, waits for them, and re-layouts: 5.38 us -> 4.36 us
where the time goes in v9:
time: 148 us; the launch traced here: 147 us
  waiting for transfers between devices  73.5 us (50%)
  starting transfers between devices  39.6 us (27%)
  Pallas kernels  27.2 us (18%)
  local copies, waits for them, and re-layouts  4.36 us (3%)
    ppermute x26, waiting for transfers between devices, swap(): return lax.ppermute(value, axis, [(i, i ^ bits) for i in range(size)])  73.5 us
    ppermute x26, starting transfers between devices, swap(): return lax.ppermute(value, axis, [(i, i ^ bits) for i in range(size)])  24.2 us
    pallas_call x1, Pallas kernels, forward(): pl.pallas_call(functools.partial(forward_kernel, len(latents), members),...  7.4 us
    pallas_call x1, Pallas kernels, backward(): pl.pallas_call(functools.partial(backward_kernel, shards, blocks, nodes),...  7.06 us
    all_to_all x1, starting transfers between devices, body(): lax.all_to_all(packed, 'ens', split_axis=0, concat_axis=0, tiled=True)  6.09 us
    pallas_call x1, Pallas kernels, gradients(): pl.pallas_call(functools.partial(gradient_kernel, shards, pair, members,...  5.77 us
    all_to_all x1, starting transfers between devices, body(): lax.all_to_all(blocks, 'ens', split_axis=0, concat_axis=0, tiled=True)  5.59 us
    unnamed x50, local copies, waits for them, and re-layouts  4.36 us
  transfers between devices with their start and end apart: 29, of which 12 were waited for; matrix products, arithmetic and copies ran while one was open for 1% of the time, Pallas kernels for 9%

profile of v9, /device:TPU:0, one launch (start us, length us, event | category | flops | bytes accessed | tf_op | source)
XLA Modules:
  0.0 147.0 jit_solution(10097619086565561430)
XLA Ops:
  0.6 3.0 %collective-permute-start.1 = (bf16[128,1024]{1,0:T(8,128)(2,1)}, bf16[128,1024]{1,0:T(8,128)(2,1)S(1)}, u32[]{:S(2)}, u32[]{:S(2)}) collective-permute-start(bf16[128,1024]{1,0:T(8,128)(2,1)} %bitcast.11), channel_id=1, source_target_pairs={{0,2},{1,3},{2,0},{3,1},{4,6},{5,7},{6,4},{7,5},{8,10},{9,11},{10,... | collective-permute-start | bytes 786440 | tf_op jit(solution)/shard_map/ppermute | solution.py:30
  3.7 6.5 %collective-permute-done.1.refs_7_.refs_2_ = bf16[128,1024]{1,0:T(8,128)(2,1)S(1)} collective-permute-done((bf16[128,1024]{1,0:T(8,128)(2,1)}, bf16[128,1024]{1,0:T(8,128)(2,1)S(1)}, u32[]{:S(2)}, u32[]{:S(2)}) %collective-permute-start.1) | collective-permute-done | bytes 262176 | tf_op jit(solution)/shard_map/ppermute | solution.py:30
  10.2 4.0 %proj.1 = (bf16[128,1024]{1,0:T(8,128)(2,1)}, bf16[256,1024]{1,0:T(8,128)(2,1)}) custom-call(bf16[128,1024]{1,0:T(8,128)(2,1)} %bitcast.13, bf16[128,1024]{1,0:T(8,128)(2,1)} %bitcast.6, bf16[1024,1024]{1,0:T(8,128)(2,1)} %w_hbm.2), custom_call_target="tpu_custom_call" | custom-call | flops 268435456 | bytes 2097152 | tf_op jit(solution)/shard_map/proj/pallas_call | solution.py:73
  15.1 7.4 %fwd.1 = (bf16[128,1024]{1,0:T(8,128)(2,1)}, bf16[128,1024]{1,0:T(8,128)(2,1)}, f32[8,128,256]{2,1,0:T(8,128)}, bf16[128,1024]{1,0:T(8,128)(2,1)}, f32[128,1024]...) custom-call(s32[1]{0:T(128)} %bitcast.refs_0_.shard_ref, s32[1,128]{1,0:T(1,128)} %index_ref.1, ...), custom_call_target="tpu_custom_call" | custom-call | flops 1073741824 | bytes 6291456 | tf_op jit(solution)/shard_map/fwd/pallas_call | solution.py:180
  22.5 6.1 %all-to-all-start = ((bf16[8,224,128]{2,1,0:T(8,128)(2,1)}), bf16[8,224,128]{2,1,0:T(8,128)(2,1)S(1)}, u32[]{:S(2)}, u32[]{:S(2)}) async-start(bf16[8,224,128]{2,1,0:T(8,128)(2,1)} %get-tuple-element.27), calls=%async_computation | async-start | bytes 917504 | tf_op jit(solution)/shard_map/all_to_all | solution.py:600
  28.6 2.0 %collective-permute-start.3 = (bf16[256,1024]{1,0:T(8,128)(2,1)S(1)}, bf16[256,1024]{1,0:T(8,128)(2,1)S(1)}, u32[]{:S(2)}, u32[]{:S(2)}) collective-permute-start(bf16[256,1024]{1,0:T(8,128)(2,1)S(1)} %copy-done.21), channel_id=1, source_target_pairs={{0,4},{4,0},{8,12},{12,8},{16,20},{20,16},{24,28},{28,24},{1,5},{5... | collective-permute-start | bytes 1572872 | tf_op jit(solution)/shard_map/ppermute | solution.py:30
  32.1 15.6 %collective-permute-done.3.refs_4_ = bf16[256,1024]{1,0:T(8,128)(2,1)S(1)} collective-permute-done((bf16[256,1024]{1,0:T(8,128)(2,1)S(1)}, bf16[256,1024]{1,0:T(8,128)(2,1)S(1)}, u32[]{:S(2)}, u32[]{:S(2)}) %collective-permute-start.3) | collective-permute-done | bytes 524320 | tf_op jit(solution)/shard_map/ppermute | solution.py:30
  47.7 1.5 %collective-permute-start.5 = (bf16[256,1024]{1,0:T(8,128)(2,1)S(1)}, bf16[256,1024]{1,0:T(8,128)(2,1)S(1)}, u32[]{:S(2)}, u32[]{:S(2)}) collective-permute-start(bf16[256,1024]{1,0:T(8,128)(2,1)S(1)} %collective-permute-done.3.refs_4_), channel_id=1, source_target_pairs={{0,2},{1,3},{2,0},{3,1},{4,6},{5,7},{6,4},{7,5},{8,10},{9,11},{10,... | collective-permute-start | bytes 1572872 | tf_op jit(solution)/shard_map/ppermute | solution.py:30
  50.5 7.1 %bwd.1 = (bf16[8,528,128]{2,1,0:T(8,128)(2,1)}, bf16[112,256]{1,0:T(8,128)(2,1)}, bf16[112,256]{1,0:T(8,128)(2,1)}, bf16[112,256]{1,0:T(8,128)(2,1)}, bf16[112,256]{1,0:T(8,128)(2,1)}) custom-call(s32[2]{0:T(128)} %pad_add_fusion.1.place_ref, bf16[8,224,128]{2,1,0:T(8,128)(2,1)} %copy-done.2, f32[100,128]{1,0:T(8,128)} %target_ref.1, s32[1,128]{1,0:T(1,128)} %index_ref.1, ...), custom_call_target="tpu_custom_call" | custom-call | flops 536870912 | bytes 4194304 | tf_op jit(solution)/shard_map/bwd/pallas_call | solution.py:358
  57.6 3.7 %all-to-all-start.1 = ((bf16[8,528,128]{2,1,0:T(8,128)(2,1)}), bf16[8,528,128]{2,1,0:T(8,128)(2,1)S(1)}, u32[]{:S(2)}, u32[]{:S(2)}) async-start(bf16[8,528,128]{2,1,0:T(8,128)(2,1)} %get-tuple-element.33), calls=%async_computation.1 | async-start | bytes 2162688 | tf_op jit(solution)/shard_map/all_to_all | solution.py:620
  61.9 1.9 %collective-permute-start.8 = (bf16[128,1024]{1,0:T(8,128)(2,1)S(1)}, bf16[128,1024]{1,0:T(8,128)(2,1)}, u32[]{:S(2)}, u32[]{:S(2)}) collective-permute-start(bf16[128,1024]{1,0:T(8,128)(2,1)S(1)} %copy-done.10), channel_id=1, source_target_pairs={{0,2},{1,3},{2,0},{3,1},{4,6},{5,7},{6,4},{7,5},{8,10},{9,11},{10,... | collective-permute-start | bytes 786440 | tf_op jit(solution)/shard_map/ppermute | solution.py:30
  63.8 1.5 %collective-permute-start.10 = (bf16[128,1024]{1,0:T(8,128)(2,1)S(1)}, bf16[128,1024]{1,0:T(8,128)(2,1)}, u32[]{:S(2)}, u32[]{:S(2)}) collective-permute-start(bf16[128,1024]{1,0:T(8,128)(2,1)S(1)} %copy-done.10), channel_id=1, source_target_pairs={{0,4},{4,0},{8,12},{12,8},{16,20},{20,16},{24,28},{28,24},{1,5},{5... | collective-permute-start | bytes 786440 | tf_op jit(solution)/shard_map/ppermute | solution.py:30
  65.6 16.3 %collective-permute-done.8.refs_10_ = bf16[128,1024]{1,0:T(8,128)(2,1)} collective-permute-done((bf16[128,1024]{1,0:T(8,128)(2,1)S(1)}, bf16[128,1024]{1,0:T(8,128)(2,1)}, u32[]{:S(2)}, u32[]{:S(2)}) %collective-permute-start.8) | collective-permute-done | bytes 262176 | tf_op jit(solution)/shard_map/ppermute | solution.py:30
  84.6 5.3 %collective-permute-done.12.refs_14_ = bf16[128,1024]{1,0:T(8,128)(2,1)} collective-permute-done((bf16[128,1024]{1,0:T(8,128)(2,1)}, bf16[128,1024]{1,0:T(8,128)(2,1)}, u32[]{:S(2)}, u32[]{:S(2)}) %collective-permute-start.12) | collective-permute-done | bytes 262176 | tf_op jit(solution)/shard_map/ppermute | solution.py:30
  93.7 5.8 %wgrad.1 = (bf16[8,512,128]{2,1,0:T(8,128)(2,1)}, f32[1,1]{1,0:T(1,128)}) custom-call(s32[2]{0:T(128)} %pad_add_fusion.place_ref, bf16[8,528,128]{2,1,0:T(8,128)(2,1)} %copy-done, bf16[128,1024]{1,0:T(8,128)(2,1)} %bitcast.15, bf16[128,1024]{1,0:T(8,128)(2,1)} %copy-done.4, bf16[128,1024]{1,0:T(8,128)(2,1)} %copy-done.3, bf16[128,1024]{1,0:T(8,128)(2,1)} %copy-done.5, ...), custom_call_target="tpu_custom_call" | custom-call | flops 1073741824 | bytes 8388608 | tf_op jit(solution)/shard_map/wgrad/pallas_call | solution.py:471
  99.5 5.6 %all-to-all-start.2 = ((bf16[8,512,128]{2,1,0:T(8,128)(2,1)}), bf16[8,512,128]{2,1,0:T(8,128)(2,1)S(1)}, u32[]{:S(2)}, u32[]{:S(2)}) async-start(bf16[8,512,128]{2,1,0:T(8,128)(2,1)} %get-tuple-element.41), calls=%async_computation.2 | async-start | bytes 2097152 | tf_op jit(solution)/shard_map/all_to_all | solution.py:633
  107.0 2.3 %collective-permute-done.19 = bf16[112,256]{1,0:T(8,128)(2,1)S(1)} collective-permute-done((bf16[112,256]{1,0:T(8,128)(2,1)S(1)}, bf16[112,256]{1,0:T(8,128)(2,1)S(1)}, u32[]{:S(2)}, u32[]{:S(2)}) %collective-permute-start.19) | collective-permute-done | bytes 57376 | tf_op jit(solution)/shard_map/ppermute | solution.py:30
  110.7 1.5 %collective-permute-start.20 = (bf16[112,256]{1,0:T(8,128)(2,1)S(1)}, bf16[112,256]{1,0:T(8,128)(2,1)S(1)}, u32[]{:S(2)}, u32[]{:S(2)}) collective-permute-start(bf16[112,256]{1,0:T(8,128)(2,1)S(1)} %add_convert_fusion.3), channel_id=1, source_target_pairs={{0,8},{4,12},{8,0},{12,4},{16,24},{20,28},{24,16},{28,20},{1,9},{5... | collective-permute-start | bytes 172040 | tf_op jit(solution)/shard_map/ppermute | solution.py:30
  112.2 12.1 %collective-permute-done.20 = bf16[112,256]{1,0:T(8,128)(2,1)S(1)} collective-permute-done((bf16[112,256]{1,0:T(8,128)(2,1)S(1)}, bf16[112,256]{1,0:T(8,128)(2,1)S(1)}, u32[]{:S(2)}, u32[]{:S(2)}) %collective-permute-start.20) | collective-permute-done | bytes 57376 | tf_op jit(solution)/shard_map/ppermute | solution.py:30
  124.3 4.0 %collective-permute-start.21 = (bf16[112,256]{1,0:T(8,128)(2,1)S(1)}, bf16[112,256]{1,0:T(8,128)(2,1)S(1)}, u32[]{:S(2)}, u32[]{:S(2)}) collective-permute-start(bf16[112,256]{1,0:T(8,128)(2,1)S(1)} %add_convert_fusion.2), channel_id=1, source_target_pairs={{0,16},{4,20},{8,24},{12,28},{16,0},{20,4},{24,8},{28,12},{1,17},{... | collective-permute-start | bytes 172040 | tf_op jit(solution)/shard_map/ppermute | solution.py:30
  128.4 5.2 %collective-permute-done.21 = bf16[112,256]{1,0:T(8,128)(2,1)S(1)} collective-permute-done((bf16[112,256]{1,0:T(8,128)(2,1)S(1)}, bf16[112,256]{1,0:T(8,128)(2,1)S(1)}, u32[]{:S(2)}, u32[]{:S(2)}) %collective-permute-start.21) | collective-permute-done | bytes 57376 | tf_op jit(solution)/shard_map/ppermute | solution.py:30
  135.1 2.8 %collective-permute-done.22 = bf16[112,256]{1,0:T(8,128)(2,1)S(1)} collective-permute-done((bf16[112,256]{1,0:T(8,128)(2,1)S(1)}, bf16[112,256]{1,0:T(8,128)(2,1)S(1)}, u32[]{:S(2)}, u32[]{:S(2)}) %collective-permute-start.22) | collective-permute-done | bytes 57376 | tf_op jit(solution)/shard_map/ppermute | solution.py:30
  138.5 3.6 %collective-permute-done.24.refs_2_ = bf16[112,256]{1,0:T(8,128)(2,1)S(1)} collective-permute-done((bf16[112,256]{1,0:T(8,128)(2,1)S(1)}, bf16[112,256]{1,0:T(8,128)(2,1)S(1)}, u32[]{:S(2)}, u32[]{:S(2)}) %collective-permute-start.24) | collective-permute-done | bytes 57376 | tf_op jit(solution)/shard_map/ppermute | solution.py:30
  144.0 1.7 %join.1 = f32[100,1024]{1,0:T(8,128)} custom-call(s32[1]{0:T(128)} %bitcast.refs_0_.shard_ref, bf16[112,256]{1,0:T(8,128)(2,1)} %copy-done.16, bf16[112,256]{1,0:T(8,128)(2,1)} %copy-done.18, bf16[112,256]{1,0:T(8,128)(2,1)} %copy-done.17, bf16[112,256]{1,0:T(8,128)(2,1)} %copy-done.19), custom_call_target="tpu_custom_call" | custom-call | tf_op jit(solution)/shard_map/join/pallas_call | solution.py:542
  (96 shorter events, 19.4 us)
Async XLA Ops:
  0.6 9.6 %collective-permute-start.1 = (bf16[128,1024]{1,0:T(8,128)(2,1)}, bf16[128,1024]{1,0:T(8,128)(2,1)S(1)}, u32[]{:S(2)}, u32[]{:S(2)}) collective-permute-start(bf16[128,1024]{1,0:T(8,128)(2,1)} %bitcast.11), channel_id=1, source_target_pairs={{0,2},{1,3},{2,0},{3,1},{4,6},{5,7},{6,4},{7,5},{8,10},{9,11},{10,... | collective-permute-start | bytes 786440 | tf_op jit(solution)/shard_map/ppermute | solution.py:30
  3.7 10.6 %collective-permute-start = (bf16[128,1024]{1,0:T(8,128)(2,1)}, bf16[128,1024]{1,0:T(8,128)(2,1)S(1)}, u32[]{:S(2)}, u32[]{:S(2)}) collective-permute-start(bf16[128,1024]{1,0:T(8,128)(2,1)} %bitcast.12), channel_id=1, source_target_pairs={{0,1},{1,0},{2,3},{3,2},{4,5},{5,4},{6,7},{7,6},{8,9},{9,8},{10,11... | collective-permute-start | bytes 786440 | tf_op jit(solution)/shard_map/ppermute | solution.py:30
  10.2 4.1 %collective-permute-start.2 = (bf16[128,1024]{1,0:T(8,128)(2,1)S(1)}, bf16[128,1024]{1,0:T(8,128)(2,1)S(1)}, u32[]{:S(2)}, u32[]{:S(2)}) collective-permute-start(bf16[128,1024]{1,0:T(8,128)(2,1)S(1)} %collective-permute-done.1.refs_7_.refs_2_), channel_id=1, source_target_pairs={{0,1},{1,0},{2,3},{3,2},{4,5},{5,4},{6,7},{7,6},{8,9},{9,8},{10,11... | collective-permute-start | bytes 786440 | tf_op jit(solution)/shard_map/ppermute | solution.py:30
  22.5 27.3 %all-to-all-start = ((bf16[8,224,128]{2,1,0:T(8,128)(2,1)}), bf16[8,224,128]{2,1,0:T(8,128)(2,1)S(1)}, u32[]{:S(2)}, u32[]{:S(2)}) async-start(bf16[8,224,128]{2,1,0:T(8,128)(2,1)} %get-tuple-element.27), calls=%async_computation | async-start | bytes 917504 | tf_op jit(solution)/shard_map/all_to_all | solution.py:600
  28.6 19.1 %collective-permute-start.3 = (bf16[256,1024]{1,0:T(8,128)(2,1)S(1)}, bf16[256,1024]{1,0:T(8,128)(2,1)S(1)}, u32[]{:S(2)}, u32[]{:S(2)}) collective-permute-start(bf16[256,1024]{1,0:T(8,128)(2,1)S(1)} %copy-done.21), channel_id=1, source_target_pairs={{0,4},{4,0},{8,12},{12,8},{16,20},{20,16},{24,28},{28,24},{1,5},{5... | collective-permute-start | bytes 1572872 | tf_op jit(solution)/shard_map/ppermute | solution.py:30
  30.6 31.1 %collective-permute-start.15 = (bf16[128,1024]{1,0:T(8,128)(2,1)S(1)}, bf16[128,1024]{1,0:T(8,128)(2,1)S(1)}, u32[]{:S(2)}, u32[]{:S(2)}) collective-permute-start(bf16[128,1024]{1,0:T(8,128)(2,1)S(1)} %bitcast.9), channel_id=1, source_target_pairs={{0,2},{1,3},{2,0},{3,1},{4,6},{5,7},{6,4},{7,5},{8,10},{9,11},{10,... | collective-permute-start | bytes 786440 | tf_op jit(solution)/shard_map/ppermute | solution.py:30
  47.7 35.7 %collective-permute-start.5 = (bf16[256,1024]{1,0:T(8,128)(2,1)S(1)}, bf16[256,1024]{1,0:T(8,128)(2,1)S(1)}, u32[]{:S(2)}, u32[]{:S(2)}) collective-permute-start(bf16[256,1024]{1,0:T(8,128)(2,1)S(1)} %collective-permute-done.3.refs_4_), channel_id=1, source_target_pairs={{0,2},{1,3},{2,0},{3,1},{4,6},{5,7},{6,4},{7,5},{8,10},{9,11},{10,... | collective-permute-start | bytes 1572872 | tf_op jit(solution)/shard_map/ppermute | solution.py:30
  57.6 34.2 %all-to-all-start.1 = ((bf16[8,528,128]{2,1,0:T(8,128)(2,1)}), bf16[8,528,128]{2,1,0:T(8,128)(2,1)S(1)}, u32[]{:S(2)}, u32[]{:S(2)}) async-start(bf16[8,528,128]{2,1,0:T(8,128)(2,1)} %get-tuple-element.33), calls=%async_computation.1 | async-start | bytes 2162688 | tf_op jit(solution)/shard_map/all_to_all | solution.py:620
  61.9 19.9 %collective-permute-start.8 = (bf16[128,1024]{1,0:T(8,128)(2,1)S(1)}, bf16[128,1024]{1,0:T(8,128)(2,1)}, u32[]{:S(2)}, u32[]{:S(2)}) collective-permute-start(bf16[128,1024]{1,0:T(8,128)(2,1)S(1)} %copy-done.10), channel_id=1, source_target_pairs={{0,2},{1,3},{2,0},{3,1},{4,6},{5,7},{6,4},{7,5},{8,10},{9,11},{10,... | collective-permute-start | bytes 786440 | tf_op jit(solution)/shard_map/ppermute | solution.py:30
  63.8 19.6 %collective-permute-start.7 = (bf16[128,1024]{1,0:T(8,128)(2,1)S(1)}, bf16[128,1024]{1,0:T(8,128)(2,1)S(1)}, u32[]{:S(2)}, u32[]{:S(2)}) collective-permute-start(bf16[128,1024]{1,0:T(8,128)(2,1)S(1)} %copy-done.10), channel_id=1, source_target_pairs={{0,1},{1,0},{2,3},{3,2},{4,5},{5,4},{6,7},{7,6},{8,9},{9,8},{10,11... | collective-permute-start | bytes 786440 | tf_op jit(solution)/shard_map/ppermute | solution.py:30
  63.8 20.1 %collective-permute-start.10 = (bf16[128,1024]{1,0:T(8,128)(2,1)S(1)}, bf16[128,1024]{1,0:T(8,128)(2,1)}, u32[]{:S(2)}, u32[]{:S(2)}) collective-permute-start(bf16[128,1024]{1,0:T(8,128)(2,1)S(1)} %copy-done.10), channel_id=1, source_target_pairs={{0,4},{4,0},{8,12},{12,8},{16,20},{20,16},{24,28},{28,24},{1,5},{5... | collective-permute-start | bytes 786440 | tf_op jit(solution)/shard_map/ppermute | solution.py:30
  65.3 25.2 %collective-permute-start.4 = (bf16[256,1024]{1,0:T(8,128)(2,1)S(1)}, bf16[256,1024]{1,0:T(8,128)(2,1)S(1)}, u32[]{:S(2)}, u32[]{:S(2)}) collective-permute-start(bf16[256,1024]{1,0:T(8,128)(2,1)S(1)} %collective-permute-done.3.refs_4_), channel_id=1, source_target_pairs={{0,1},{1,0},{2,3},{3,2},{4,5},{5,4},{6,7},{7,6},{8,9},{9,8},{10,11... | collective-permute-start | bytes 1572872 | tf_op jit(solution)/shard_map/ppermute | solution.py:30
  81.9 8.1 %collective-permute-start.12 = (bf16[128,1024]{1,0:T(8,128)(2,1)}, bf16[128,1024]{1,0:T(8,128)(2,1)}, u32[]{:S(2)}, u32[]{:S(2)}) collective-permute-start(bf16[128,1024]{1,0:T(8,128)(2,1)} %collective-permute-done.8.refs_10_), channel_id=1, source_target_pairs={{0,4},{4,0},{8,12},{12,8},{16,20},{20,16},{24,28},{28,24},{1,5},{5... | collective-permute-start | bytes 786440 | tf_op jit(solution)/shard_map/ppermute | solution.py:30
  83.3 8.5 %collective-permute-start.6 = (bf16[256,1024]{1,0:T(8,128)(2,1)S(1)}, bf16[256,1024]{1,0:T(8,128)(2,1)S(1)}, u32[]{:S(2)}, u32[]{:S(2)}) collective-permute-start(bf16[256,1024]{1,0:T(8,128)(2,1)S(1)} %collective-permute-done.5.refs_6_), channel_id=1, source_target_pairs={{0,1},{1,0},{2,3},{3,2},{4,5},{5,4},{6,7},{7,6},{8,9},{9,8},{10,11... | collective-permute-start | bytes 1572872 | tf_op jit(solution)/shard_map/ppermute | solution.py:30
  83.4 7.1 %collective-permute-start.9 = (bf16[128,1024]{1,0:T(8,128)(2,1)}, bf16[128,1024]{1,0:T(8,128)(2,1)}, u32[]{:S(2)}, u32[]{:S(2)}) collective-permute-start(bf16[128,1024]{1,0:T(8,128)(2,1)} %collective-permute-done.8.refs_10_), channel_id=1, source_target_pairs={{0,1},{1,0},{2,3},{3,2},{4,5},{5,4},{6,7},{7,6},{8,9},{9,8},{10,11... | collective-permute-start | bytes 786440 | tf_op jit(solution)/shard_map/ppermute | solution.py:30
  84.2 6.3 %collective-permute-start.11 = (bf16[128,1024]{1,0:T(8,128)(2,1)}, bf16[128,1024]{1,0:T(8,128)(2,1)S(1)}, u32[]{:S(2)}, u32[]{:S(2)}) collective-permute-start(bf16[128,1024]{1,0:T(8,128)(2,1)} %collective-permute-done.10.refs_12_), channel_id=1, source_target_pairs={{0,1},{1,0},{2,3},{3,2},{4,5},{5,4},{6,7},{7,6},{8,9},{9,8},{10,11... | collective-permute-start | bytes 786440 | tf_op jit(solution)/shard_map/ppermute | solution.py:30
  99.5 46.3 %all-to-all-start.2 = ((bf16[8,512,128]{2,1,0:T(8,128)(2,1)}), bf16[8,512,128]{2,1,0:T(8,128)(2,1)S(1)}, u32[]{:S(2)}, u32[]{:S(2)}) async-start(bf16[8,512,128]{2,1,0:T(8,128)(2,1)} %get-tuple-element.41), calls=%async_computation.2 | async-start | bytes 2097152 | tf_op jit(solution)/shard_map/all_to_all | solution.py:633
  105.1 4.2 %collective-permute-start.19 = (bf16[112,256]{1,0:T(8,128)(2,1)S(1)}, bf16[112,256]{1,0:T(8,128)(2,1)S(1)}, u32[]{:S(2)}, u32[]{:S(2)}) collective-permute-start(bf16[112,256]{1,0:T(8,128)(2,1)S(1)} %copy-done.24), channel_id=1, source_target_pairs={{0,3},{1,2},{2,1},{3,0},{4,7},{5,6},{6,5},{7,4},{8,11},{9,10},{10,... | collective-permute-start | bytes 172040 | tf_op jit(solution)/shard_map/ppermute | solution.py:30
  105.2 5.4 %collective-permute-start.18 = (bf16[112,256]{1,0:T(8,128)(2,1)S(1)}, bf16[112,256]{1,0:T(8,128)(2,1)S(1)}, u32[]{:S(2)}, u32[]{:S(2)}) collective-permute-start(bf16[112,256]{1,0:T(8,128)(2,1)S(1)} %copy-done.23), channel_id=1, source_target_pairs={{0,2},{1,3},{2,0},{3,1},{4,6},{5,7},{6,4},{7,5},{8,10},{9,11},{10,... | collective-permute-start | bytes 172040 | tf_op jit(solution)/shard_map/ppermute | solution.py:30
  106.7 4.0 %collective-permute-start.17 = (bf16[112,256]{1,0:T(8,128)(2,1)S(1)}, bf16[112,256]{1,0:T(8,128)(2,1)S(1)}, u32[]{:S(2)}, u32[]{:S(2)}) collective-permute-start(bf16[112,256]{1,0:T(8,128)(2,1)S(1)} %copy-done.22), channel_id=1, source_target_pairs={{0,1},{1,0},{2,3},{3,2},{4,5},{5,4},{6,7},{7,6},{8,9},{9,8},{10,11... | collective-permute-start | bytes 172040 | tf_op jit(solution)/shard_map/ppermute | solution.py:30
  110.7 13.7 %collective-permute-start.20 = (bf16[112,256]{1,0:T(8,128)(2,1)S(1)}, bf16[112,256]{1,0:T(8,128)(2,1)S(1)}, u32[]{:S(2)}, u32[]{:S(2)}) collective-permute-start(bf16[112,256]{1,0:T(8,128)(2,1)S(1)} %add_convert_fusion.3), channel_id=1, source_target_pairs={{0,8},{4,12},{8,0},{12,4},{16,24},{20,28},{24,16},{28,20},{1,9},{5... | collective-permute-start | bytes 172040 | tf_op jit(solution)/shard_map/ppermute | solution.py:30
  124.3 9.3 %collective-permute-start.21 = (bf16[112,256]{1,0:T(8,128)(2,1)S(1)}, bf16[112,256]{1,0:T(8,128)(2,1)S(1)}, u32[]{:S(2)}, u32[]{:S(2)}) collective-permute-start(bf16[112,256]{1,0:T(8,128)(2,1)S(1)} %add_convert_fusion.2), channel_id=1, source_target_pairs={{0,16},{4,20},{8,24},{12,28},{16,0},{20,4},{24,8},{28,12},{1,17},{... | collective-permute-start | bytes 172040 | tf_op jit(solution)/shard_map/ppermute | solution.py:30
  133.6 4.2 %collective-permute-start.22 = (bf16[112,256]{1,0:T(8,128)(2,1)S(1)}, bf16[112,256]{1,0:T(8,128)(2,1)S(1)}, u32[]{:S(2)}, u32[]{:S(2)}) collective-permute-start(bf16[112,256]{1,0:T(8,128)(2,1)S(1)} %add_convert_fusion.1), channel_id=1, source_target_pairs={{0,4},{4,0},{8,12},{12,8},{16,20},{20,16},{24,28},{28,24},{1,5},{5... | collective-permute-start | bytes 172040 | tf_op jit(solution)/shard_map/ppermute | solution.py:30
  137.9 4.2 %collective-permute-start.24 = (bf16[112,256]{1,0:T(8,128)(2,1)S(1)}, bf16[112,256]{1,0:T(8,128)(2,1)S(1)}, u32[]{:S(2)}, u32[]{:S(2)}) collective-permute-start(bf16[112,256]{1,0:T(8,128)(2,1)S(1)} %add_convert_fusion.refs_0_), channel_id=1, source_target_pairs={{0,2},{1,3},{2,0},{3,1},{4,6},{5,7},{6,4},{7,5},{8,10},{9,11},{10,... | collective-permute-start | bytes 172040 | tf_op jit(solution)/shard_map/ppermute | solution.py:30
  (30 other events, 189.9 us)

commit v10 on v8

--- a/solution.py
+++ b/solution.py
@@ -149,7 +149,7 @@
 
 
 def padded(channels):
-    return channels + -channels % 16
+    return channels + -channels % 8
 
 
 def forward(shard, index, grid_rows, queries, readout, latents, weights, members):
@@ -188,21 +188,27 @@
     packed_ref,
     target_ref,
     index_ref,
-    query_ref,
-    key_ref,
-    value_ref,
-    soft_ref,
-    normed_ref,
+    query_hbm,
+    key_hbm,
+    value_hbm,
+    soft_hbm,
+    normed_hbm,
     inverse_ref,
     readout_ref,
     w_hbm,
     out_ref,
     *refs,
 ):
-    outer_refs = refs[:shards]
-    slope_ref, d_attended_ref, small_ref, truth_ref, weight_ref, w_ref, sem = refs[shards:]
-    copy = pltpu.make_async_copy(w_hbm, w_ref, sem)
-    copy.start()
+    outer_refs, refs = refs[:shards], refs[shards:]
+    slope_ref, d_attended_ref, small_ref, truth_ref, weight_ref, *full_refs, sem = refs
+    sources = (normed_hbm, w_hbm, value_hbm, soft_hbm, key_hbm, query_hbm)
+    copies = [
+        pltpu.make_async_copy(part, full, sem.at[i])
+        for i, (part, full) in enumerate(zip(sources, full_refs))
+    ]
+    for copy in copies:
+        copy.start()
+    normed_ref, w_ref, value_ref, soft_ref, key_ref, query_ref = full_refs
     members = packed_ref.shape[0]
     points, features = normed_ref.shape
     channels_used = readout_ref.shape[0]
@@ -214,7 +220,7 @@
     width = features // blocks
     weight = (channels_used * points * shards) ** (-0.5)
     pair_weight = 1.0 / (members * (members - 1))
-    chunk = 16
+    chunk = 8
 
     def crps(c, loss):
         at = pl.ds(pl.multiple_of(c * chunk, chunk), chunk)
@@ -276,6 +282,7 @@
             ]
 
     own = slope_ref[place_ref[1]]
+    copies[0].wait()
     normed = normed_ref[...]
     outer = dot32(own, normed.astype(BF16))
     columns = features // shards
@@ -289,9 +296,11 @@
     mean = jnp.mean(d_normed * normed, axis=-1, keepdims=True)
     d_hidden = (inverse_ref[...] * (d_normed - normed * mean)).astype(BF16)
     put(3, 0, d_hidden)
-    copy.wait()
+    copies[1].wait()
     d_attended_ref[...] = dot32(d_hidden, w_ref[...], (1, 1)).astype(BF16)
     factor = (features // HEADS) ** (-0.5)
+    for copy in copies[2:]:
+        copy.wait()
     for pair in range(features // LANES):
         at = slice(pair * LANES, (pair + 1) * LANES)
         soft = soft_ref[pair]
@@ -322,7 +331,7 @@
             jax.ShapeDtypeStruct((blocks, 4 * points + small, width), BF16),
         )
         + (jax.ShapeDtypeStruct((channels, features // shards), BF16),) * shards,
-        in_specs=[SMEM] + [VMEM] * 10 + [ANY],
+        in_specs=[SMEM] + [VMEM] * 3 + [HBM] * 5 + [VMEM] * 2 + [HBM],
         out_specs=(VMEM,) * (1 + shards),
         scratch_shapes=[
             pltpu.VMEM((members, channels, points), BF16),
@@ -330,8 +339,13 @@
             pltpu.VMEM((small, width), F32),
             pltpu.VMEM((channels, points), F32),
             pltpu.VMEM((channels, features), BF16),
+            pltpu.VMEM((points, features), F32),
             pltpu.VMEM((features, features), BF16),
-            pltpu.SemaphoreType.DMA,
+            pltpu.VMEM((points, features), BF16),
+            pltpu.VMEM((features // LANES, points, 2 * LANES), F32),
+            pltpu.VMEM((points, features), BF16),
+            pltpu.VMEM((points, features), BF16),
+            pltpu.SemaphoreType.DMA((6,)),
         ],
         cost_estimate=pl.CostEstimate(
             flops=4 * points * features * features,
@@ -342,111 +356,176 @@
     )(place, packed, target, index, *saved, readout, w_mix)
 
 
-def gradient_kernel(shards, pair, members, nodes, place_ref, blocks_hbm, *refs):
-    latent_refs, early_refs, late_refs, other_refs, grid_refs = (
-        refs[i * shards : (i + 1) * shards] for i in range(5)
-    )
-    out_ref, loss_ref, blocks_ref, late_ref, node_ref, grid_ref, sems = refs[5 * shards :]
-    sources = [late_refs, latent_refs, grid_refs]
-    if pair > 1:
-        sources = [
-            late_refs + other_refs,
-            latent_refs + tuple(ref.at[:nodes] for ref in early_refs),
-            grid_refs + tuple(ref.at[nodes:] for ref in early_refs),
-        ]
-    first = pltpu.make_async_copy(blocks_hbm, blocks_ref, sems.at[0, 0])
-    first.start()
-    copies = []
-    for i, (parts, full) in enumerate(zip(sources, (late_ref, node_ref, grid_ref))):
-        step = full.shape[0] // len(parts)
-        copies.append(
-            [
-                pltpu.make_async_copy(part, full.at[pl.ds(k * step, step)], sems.at[i + 1, k])
-                for k, part in enumerate(parts)
-            ]
-        )
-        for copy in copies[-1]:
-            copy.start()
-    first.wait()
-    width = blocks_ref.shape[2]
-    features = late_ref.shape[1]
-    points = grid_ref.shape[0] // (shards * pair)
-    depth = features // members
-    shard, half = place_ref[0], place_ref[1]
-    start = 4 * points
-    total = blocks_ref[0, start:].astype(F32)
-    for s in range(1, shards):
-        total = total + blocks_ref[s * pair, start:].astype(F32)
-    loss_ref[...] = jnp.sum(total[:3, :1], axis=0, keepdims=True)
-
-    def slots(kind, t):
-        at = slice(kind * points, (kind + 1) * points)
-        return [blocks_ref[(shard ^ k) * pair + (half ^ t), at] for k in range(shards)]
-
-    def put(kind, total):
-        total = total.astype(BF16)
-        at = slice(kind * width, kind * width + total.shape[0])
-        for m in range(members):
-            out_ref[m, at] = total[:, m * depth : (m + 1) * depth]
-
-    def product(kind, full, group):
-        left = jnp.concatenate([v for t in range(pair) for v in slots(kind, t)], axis=0)
-        for copy in copies[group]:
-            copy.wait()
-        put(kind, dot32(left, full[...], (0, 0)))
-
-    product(3, late_ref, 0)
+def fetch(parts, full_ref, sems):
+    step = full_ref.shape[0] // len(parts)
+    copies = [
+        pltpu.make_async_copy(part, full_ref.at[pl.ds(k * step, step)], sems.at[k])
+        for k, part in enumerate(parts)
+    ]
+    for copy in copies:
+        copy.start()
+    return copies
+
+
+def in_slots(blocks_ref, place_ref, pair, kind, points):
+    at = slice(kind * points, (kind + 1) * points)
+    return [
+        blocks_ref[(place_ref[0] ^ k) * pair + (place_ref[1] ^ t), at]
+        for t in range(pair)
+        for k in range(blocks_ref.shape[0] // pair)
+    ]
+
+
+def chosen_nodes(tags_ref, place_ref, pair, start, nodes, points):
+    shards = tags_ref.shape[0] // pair
+    lines = max(points // tags_ref.shape[2], 1)
     chosen = []
     for k in range(shards):
-        index = blocks_ref[(shard ^ k) * pair, start : start + MISC].astype(jnp.int32)
-        lines = max(points // width, 1)
+        at = slice(start, start + MISC)
+        index = tags_ref[(place_ref[0] ^ k) * pair, at].astype(jnp.int32)
         owner, offset = (
             jnp.concatenate([index[3 + b + i : 4 + b + i] for i in range(lines)], axis=1)
             for b in (0, lines)
         )
-        position = (owner ^ shard) * nodes + offset
+        position = (owner ^ place_ref[0]) * nodes + offset
         node = lax.broadcasted_iota(jnp.int32, (nodes * shards, points), 0)
         chosen.append(jnp.where(node == position, 1.0, 0.0).astype(BF16))
-    chosen = jnp.concatenate(chosen, axis=1)
-    sums = []
-    for t in range(pair):
-        both = [jnp.concatenate(slots(kind, t), axis=0) for kind in (1, 2)]
-        sums.append(dot32(chosen, jnp.concatenate(both, axis=1)).astype(BF16))
-    for copy in copies[1]:
+    return jnp.concatenate(chosen, axis=1)
+
+
+def node_sums(lefts, chosen, shards):
+    sums = [
+        dot32(chosen, jnp.concatenate(lefts[t : t + shards], axis=0)).astype(BF16)
+        for t in range(0, len(lefts), shards)
+    ]
+    return jnp.concatenate(sums, axis=0)
+
+
+def put_members(out_ref, kind, total):
+    width, depth = total.shape[0], out_ref.shape[2]
+    total = total.astype(BF16)
+    for m in range(out_ref.shape[0]):
+        out_ref[m, kind * width : (kind + 1) * width] = total[:, m * depth : (m + 1) * depth]
+
+
+def first_kernel(shards, pair, nodes, points, place_ref, blocks_hbm, *refs):
+    latent_refs, early_refs, late_refs, other_refs = (
+        refs[i * shards : (i + 1) * shards] for i in range(4)
+    )
+    out_ref, loss_ref, blocks_ref, late_ref, node_ref, sems = refs[4 * shards :]
+    head = 2 * points
+    used = pl.ds(head, blocks_hbm.shape[1] - head)
+    first = pltpu.make_async_copy(blocks_hbm.at[:, used], blocks_ref, sems.at[0, 0])
+    first.start()
+    late_parts, node_parts = late_refs, latent_refs
+    if pair > 1:
+        late_parts = late_refs + other_refs
+        node_parts = latent_refs + tuple(ref.at[:nodes] for ref in early_refs)
+    late_copies = fetch(late_parts, late_ref, sems.at[1])
+    node_copies = fetch(node_parts, node_ref, sems.at[2])
+    first.wait()
+    total = blocks_ref[0, head:].astype(F32)
+    for s in range(1, shards):
+        total = total + blocks_ref[s * pair, head:].astype(F32)
+    loss_ref[...] = jnp.sum(total[:3, :1], axis=0, keepdims=True)
+    left = jnp.concatenate(in_slots(blocks_ref, place_ref, pair, 1, points), axis=0)
+    for copy in late_copies:
         copy.wait()
-    put(1, dot32(jnp.concatenate(sums, axis=0), node_ref[...], (0, 0)))
-    product(0, grid_ref, 2)
-
-
-def gradients(place, blocks, latents, early, late, other, grids, members, pair):
-    count, _, width = blocks.shape
+    put_members(out_ref, 0, dot32(left, late_ref[...], (0, 0)))
+    chosen = chosen_nodes(blocks_ref, place_ref, pair, head, nodes, points)
+    left = node_sums(in_slots(blocks_ref, place_ref, pair, 0, points), chosen, shards)
+    for copy in node_copies:
+        copy.wait()
+    put_members(out_ref, 1, dot32(left, node_ref[...], (0, 0)))
+
+
+def first_gradients(place, blocks, latents, early, late, other, members, pair):
+    count, rows, width = blocks.shape
     shards = count // pair
-    features = late[0].shape[1]
-    points = late[0].shape[0]
-    depth = features // members
+    points, features = late[0].shape
+    nodes = latents[0].shape[0]
     return pl.pallas_call(
-        functools.partial(
-            gradient_kernel, shards, pair, members, latents[0].shape[0]
-        ),
+        functools.partial(first_kernel, shards, pair, nodes, points),
         out_shape=(
-            jax.ShapeDtypeStruct((members, 4 * width, depth), BF16),
+            jax.ShapeDtypeStruct((members, 2 * width, features // members), BF16),
             jax.ShapeDtypeStruct((1, 1), F32),
         ),
-        in_specs=[SMEM] + [HBM] * (1 + 5 * shards),
+        in_specs=[SMEM] + [HBM] * (1 + 4 * shards),
         out_specs=(VMEM, VMEM),
-        scratch_shapes=[pltpu.VMEM(blocks.shape, BF16)]
-        + [
-            pltpu.VMEM((count * rows, features), BF16)
-            for rows in (points, latents[0].shape[0], points)
-        ]
-        + [pltpu.SemaphoreType.DMA((4, count))],
+        scratch_shapes=[
+            pltpu.VMEM((count, rows - 2 * points, width), BF16),
+            pltpu.VMEM((count * points, features), BF16),
+            pltpu.VMEM((count * nodes, features), BF16),
+            pltpu.SemaphoreType.DMA((3, count)),
+        ],
         cost_estimate=pl.CostEstimate(
-            flops=8 * points * count * features * width,
-            bytes_accessed=8 * points * count * features,
+            flops=4 * points * count * features * width,
+            bytes_accessed=4 * points * count * features,
             transcendentals=0,
         ),
-        name="wgrad",
-    )(place, blocks, *latents, *early, *late, *other, *grids)
+        name="wga",
+    )(place, blocks, *latents, *early, *late, *other)
+
+
+def last_kernel(shards, pair, nodes, points, place_ref, blocks_hbm, *refs):
+    latent_refs, early_refs, grid_refs = (refs[i * shards : (i + 1) * shards] for i in range(3))
+    *out_refs, total_ref, blocks_ref, tags_ref, node_ref, grid_ref, sems = refs[3 * shards :]
+    start = 4 * points
+    copies = [
+        pltpu.make_async_copy(blocks_hbm.at[:, pl.ds(at, rows)], full, sems.at[0, i])
+        for i, (full, at, rows) in enumerate(
+            ((blocks_ref, 0, 2 * points), (tags_ref, start, tags_ref.shape[1]))
+        )
+    ]
+    for copy in copies:
+        copy.start()
+    node_parts, grid_parts = latent_refs, grid_refs
+    if pair > 1:
+        node_parts = latent_refs + tuple(ref.at[:nodes] for ref in early_refs)
+        grid_parts = grid_refs + tuple(ref.at[nodes:] for ref in early_refs)
+    grid_copies = fetch(grid_parts, grid_ref, sems.at[1])
+    node_copies = fetch(node_parts, node_ref, sems.at[2])
+    for copy in copies:
+        copy.wait()
+    left = jnp.concatenate(in_slots(blocks_ref, place_ref, pair, 0, points), axis=0)
+    for copy in grid_copies:
+        copy.wait()
+    put_members(total_ref, 0, dot32(left, grid_ref[...], (0, 0)))
+    chosen = chosen_nodes(tags_ref, place_ref, pair, 0, nodes, points)
+    left = node_sums(in_slots(blocks_ref, place_ref, pair, 1, points), chosen, shards)
+    for copy in node_copies:
+        copy.wait()
+    put_members(total_ref, 1, dot32(left, node_ref[...], (0, 0)))
+    for k, ref in enumerate(out_refs):
+        ref[...] = total_ref[place_ref[2] ^ k]
+
+
+def last_gradients(place, blocks, latents, early, grids, members, pair):
+    count, rows, width = blocks.shape
+    shards = count // pair
+    points, features = grids[0].shape
+    nodes = latents[0].shape[0]
+    block = (2 * width, features // members)
+    return pl.pallas_call(
+        functools.partial(last_kernel, shards, pair, nodes, points),
+        out_shape=(jax.ShapeDtypeStruct(block, BF16),) * members,
+        in_specs=[SMEM] + [HBM] * (1 + 3 * shards),
+        out_specs=(VMEM,) * members,
+        scratch_shapes=[
+            pltpu.VMEM((members,) + block, BF16),
+            pltpu.VMEM((count, 2 * points, width), BF16),
+            pltpu.VMEM((count, rows - 4 * points, width), BF16),
+            pltpu.VMEM((count * nodes, features), BF16),
+            pltpu.VMEM((count * points, features), BF16),
+            pltpu.SemaphoreType.DMA((3, count)),
+        ],
+        cost_estimate=pl.CostEstimate(
+            flops=4 * points * count * features * width,
+            bytes_accessed=4 * points * count * features,
+            transcendentals=0,
+        ),
+        name="wgb",
+    )(place, blocks, *latents, *early, *grids)
 
 
 def sum_kernel(pair, blocks_hbm, *refs):
@@ -473,12 +552,43 @@
     _, rows, depth = blocks.shape
     return pl.pallas_call(
         functools.partial(sum_kernel, pair),
-        out_shape=(jax.ShapeDtypeStruct((depth, pair * rows // 4), F32),) * 4,
-        in_specs=[HBM],
-        out_specs=(VMEM,) * 4,
-        scratch_shapes=[pltpu.VMEM(blocks.shape, BF16), pltpu.SemaphoreType.DMA((4,))],
+        out_shape=(jax.ShapeDtypeStruct((depth, pair * rows // 2), F32),) * 2,
+        in_specs=[ANY],
+        out_specs=(VMEM,) * 2,
+        scratch_shapes=[pltpu.VMEM(blocks.shape, BF16), pltpu.SemaphoreType.DMA((2,))],
+        compiler_params=pltpu.CompilerParams(vmem_limit_bytes=8 << 20),
         name="sums",
     )(blocks)
+
+
+def sum_slots_kernel(pair, place_ref, *refs):
+    slot_refs, out_refs = refs[:-2], refs[-2:]
+    width = slot_refs[0].shape[0] // 2
+    for i, ref in enumerate(out_refs):
+        at = slice(i * width, (i + 1) * width)
+        totals = []
+        for y in range(pair):
+            total = slot_refs[y][at].astype(F32)
+            for k in range(y + pair, len(slot_refs), pair):
+                total = total + slot_refs[k][at].astype(F32)
+            totals.append(total.T)
+        for y in range(pair):
+            value = totals[y]
+            if pair > 1:
+                value = jnp.where(place_ref[1] == y, totals[0], totals[1])
+            ref[:, y * width : (y + 1) * width] = value
+
+
+def sum_slots(place, parts, pair):
+    rows, depth = parts[0].shape
+    return pl.pallas_call(
+        functools.partial(sum_slots_kernel, pair),
+        out_shape=(jax.ShapeDtypeStruct((depth, pair * rows // 2), F32),) * 2,
+        in_specs=[SMEM] + [VMEM] * len(parts),
+        out_specs=(VMEM,) * 2,
+        compiler_params=pltpu.CompilerParams(vmem_limit_bytes=8 << 20),
+        name="sumb",
+    )(place, *parts)
 
 
 def join_kernel(shard_ref, *refs):
@@ -499,6 +609,7 @@
         out_shape=jax.ShapeDtypeStruct((channels_used, columns), F32),
         in_specs=[SMEM] + [VMEM] * len(parts),
         out_specs=VMEM,
+        compiler_params=pltpu.CompilerParams(vmem_limit_bytes=6 << 20),
         name="join",
     )(shard, *parts)
 
@@ -580,15 +691,18 @@
         axis_index_groups=groups,
         tiled=True,
     )
-    place = jnp.stack([shard, half])
+    place = jnp.stack([shard, half, member])
     outer = sum_outer(outer)
-    blocks, loss = gradients(
-        place, blocks, latents, early, late, other, grids, members, pair
-    )
-    blocks = lax.all_to_all(blocks, "ens", split_axis=0, concat_axis=0, tiled=True)
+    first, loss = first_gradients(place, blocks, latents, early, late, other, members, pair)
+    first = lax.all_to_all(first, "ens", split_axis=0, concat_axis=0, tiled=True)
+    parts = last_gradients(place, blocks, latents, early, grids, members, pair)
+    last = [parts[0]]
+    for k in range(1, members):
+        last.append(swap(parts[k], "ens", k))
     grad_out = join_columns(shard[None], outer, channels_used)
-    grads = sum_groups(blocks, pair)
-    return (loss.reshape(()), grad_out, *grads)
+    grad_mix, grad_value = sum_groups(first, pair)
+    grad_query, grad_key = sum_slots(place, last, pair)
+    return (loss.reshape(()), grad_out, grad_query, grad_key, grad_value, grad_mix)
 
 
 def solution(mesh):

time: 149 us -> 155 us (1.040)
  starting transfers between devices: 39.6 us -> 48.2 us
  waiting for transfers between devices: 73.5 us -> 65.6 us
  local copies, waits for them, and re-layouts: 5.38 us -> 7.71 us
  Pallas kernels: 27.7 us -> 29.9 us
    ppermute x26 -> x33, starting transfers between devices: 24.3 us -> 33.8 us  [swap(): return lax.ppermute(value, axis, [(i, i ^ bits) for i in range(size)])]
    ppermute x26 -> x33, waiting for transfers between devices: 73.5 us -> 65.6 us  [swap(): return lax.ppermute(value, axis, [(i, i ^ bits) for i in range(size)])]
    pallas_call x1 -> x3, Pallas kernels: 5.78 us -> 10.5 us  [the longest x1 4.57 us: first_gradients(): pl.pallas_call(functools.partial(first_kernel, shards, pair, nodes, point...]
    unnamed x52, local copies, waits for them, and re-layouts: 5.38 us -> 7.71 us
  transfers between devices with their start and end apart: 29 -> 36, of which waited for: 12 -> 9; matrix products, arithmetic and copies ran while one was open for 1% -> 1% of each run, Pallas kernels for 9% -> 14%
where the time goes in v10:
time: 155 us; the launch traced here: 154 us
  waiting for transfers between devices  65.6 us (42%)
  starting transfers between devices  48.2 us (31%)
  Pallas kernels  29.9 us (19%)
  local copies, waits for them, and re-layouts  7.71 us (5%)
  other arithmetic  2.11 us (1%)
    ppermute x33, waiting for transfers between devices, swap(): return lax.ppermute(value, axis, [(i, i ^ bits) for i in range(size)])  65.6 us
    ppermute x33, starting transfers between devices, swap(): return lax.ppermute(value, axis, [(i, i ^ bits) for i in range(size)])  33.8 us
    unnamed x52, local copies, waits for them, and re-layouts  7.71 us
    pallas_call x1, Pallas kernels, backward(): pl.pallas_call(functools.partial(backward_kernel, shards, blocks, nodes),...  7.04 us
    pallas_call x1, Pallas kernels, forward(): pl.pallas_call(functools.partial(forward_kernel, len(latents), members),...  6.58 us
    all_to_all x1, starting transfers between devices, body(): lax.all_to_all(packed, 'ens', split_axis=0, concat_axis=0, tiled=True)  6.09 us
    pallas_call x1, Pallas kernels, first_gradients(): pl.pallas_call(functools.partial(first_kernel, shards, pair, nodes, point...  4.57 us
    all_to_all x1, starting transfers between devices, body(): lax.all_to_all(first, 'ens', split_axis=0, concat_axis=0, tiled=True)  4.56 us
  transfers between devices with their start and end apart: 36, of which 9 were waited for; matrix products, arithmetic and copies ran while one was open for 1% of the time, Pallas kernels for 14%

profile of v10, /device:TPU:0, one launch (start us, length us, event | category | flops | bytes accessed | tf_op | source)
XLA Modules:
  0.0 154.4 jit_solution(15191165895198299837)
XLA Ops:
  0.6 3.0 %collective-permute-start.1 = (bf16[128,1024]{1,0:T(8,128)(2,1)}, bf16[128,1024]{1,0:T(8,128)(2,1)S(1)}, u32[]{:S(2)}, u32[]{:S(2)}) collective-permute-start(bf16[128,1024]{1,0:T(8,128)(2,1)} %bitcast.6), channel_id=1, source_target_pairs={{0,2},{1,3},{2,0},{3,1},{4,6},{5,7},{6,4},{7,5},{8,10},{9,11},{10,... | collective-permute-start | bytes 786440 | tf_op jit(solution)/shard_map/ppermute | solution.py:30
  3.7 6.5 %collective-permute-done.1.refs_7_.refs_2_ = bf16[128,1024]{1,0:T(8,128)(2,1)S(1)} collective-permute-done((bf16[128,1024]{1,0:T(8,128)(2,1)}, bf16[128,1024]{1,0:T(8,128)(2,1)S(1)}, u32[]{:S(2)}, u32[]{:S(2)}) %collective-permute-start.1) | collective-permute-done | bytes 262176 | tf_op jit(solution)/shard_map/ppermute | solution.py:30
  10.2 4.0 %proj.1 = (bf16[128,1024]{1,0:T(8,128)(2,1)}, bf16[256,1024]{1,0:T(8,128)(2,1)}) custom-call(bf16[128,1024]{1,0:T(8,128)(2,1)} %bitcast.8, bf16[128,1024]{1,0:T(8,128)(2,1)} %bitcast.12, bf16[1024,1024]{1,0:T(8,128)(2,1)} %w_hbm.2), custom_call_target="tpu_custom_call" | custom-call | flops 268435456 | bytes 2097152 | tf_op jit(solution)/shard_map/proj/pallas_call | solution.py:73
  15.1 6.6 %fwd.1 = (bf16[128,1024]{1,0:T(8,128)(2,1)}, bf16[128,1024]{1,0:T(8,128)(2,1)}, f32[8,128,256]{2,1,0:T(8,128)}, bf16[128,1024]{1,0:T(8,128)(2,1)}, f32[128,1024]...) custom-call(s32[1]{0:T(128)} %bitcast.refs_0_.shard_ref, s32[1,128]{1,0:T(1,128)} %index_ref.1, ...), custom_call_target="tpu_custom_call" | custom-call | flops 1073741824 | bytes 6291456 | tf_op jit(solution)/shard_map/fwd/pallas_call | solution.py:159
  21.6 6.1 %all-to-all-start = ((bf16[8,208,128]{2,1,0:T(8,128)(2,1)}), bf16[8,208,128]{2,1,0:T(8,128)(2,1)S(1)}, u32[]{:S(2)}, u32[]{:S(2)}) async-start(bf16[8,208,128]{2,1,0:T(8,128)(2,1)} %get-tuple-element.35), calls=%async_computation | async-start | bytes 851968 | tf_op jit(solution)/shard_map/all_to_all | solution.py:666
  27.7 2.0 %collective-permute-start.3 = (bf16[256,1024]{1,0:T(8,128)(2,1)S(1)}, bf16[256,1024]{1,0:T(8,128)(2,1)S(1)}, u32[]{:S(2)}, u32[]{:S(2)}) collective-permute-start(bf16[256,1024]{1,0:T(8,128)(2,1)S(1)} %copy-done.25), channel_id=1, source_target_pairs={{0,4},{4,0},{8,12},{12,8},{16,20},{20,16},{24,28},{28,24},{1,5},{5... | collective-permute-start | bytes 1572872 | tf_op jit(solution)/shard_map/ppermute | solution.py:30
  29.8 16.7 %collective-permute-done.3.refs_4_ = bf16[256,1024]{1,0:T(8,128)(2,1)S(1)} collective-permute-done((bf16[256,1024]{1,0:T(8,128)(2,1)S(1)}, bf16[256,1024]{1,0:T(8,128)(2,1)S(1)}, u32[]{:S(2)}, u32[]{:S(2)}) %collective-permute-start.3) | collective-permute-done | bytes 524320 | tf_op jit(solution)/shard_map/ppermute | solution.py:30
  49.3 7.0 %bwd.1 = (bf16[8,528,128]{2,1,0:T(8,128)(2,1)}, bf16[104,256]{1,0:T(8,128)(2,1)}, bf16[104,256]{1,0:T(8,128)(2,1)}, bf16[104,256]{1,0:T(8,128)(2,1)}, bf16[104,256]{1,0:T(8,128)(2,1)}) custom-call(s32[2]{0:T(128)} %pad_add_fusion.1.place_ref, bf16[8,208,128]{2,1,0:T(8,128)(2,1)} %copy-done.11, f32[100,128]{1,0:T(8,128)} %target_ref.1, s32[1,128]{1,0:T(1,128)} %index_ref.1, ...), custom_call_target="tpu_custom_call" | custom-call | flops 536870912 | bytes 4194304 | tf_op jit(solution)/shard_map/bwd/pallas_call | solution.py:328
  56.3 3.7 %all-to-all-start.1 = ((bf16[8,528,128]{2,1,0:T(8,128)(2,1)}), bf16[8,528,128]{2,1,0:T(8,128)(2,1)S(1)}, u32[]{:S(2)}, u32[]{:S(2)}) async-start(bf16[8,528,128]{2,1,0:T(8,128)(2,1)} %get-tuple-element.41), calls=%async_computation.1 | async-start | bytes 2162688 | tf_op jit(solution)/shard_map/all_to_all | solution.py:686
  60.1 1.9 %collective-permute-start.8 = (bf16[128,1024]{1,0:T(8,128)(2,1)S(1)}, bf16[128,1024]{1,0:T(8,128)(2,1)S(1)}, u32[]{:S(2)}, u32[]{:S(2)}) collective-permute-start(bf16[128,1024]{1,0:T(8,128)(2,1)S(1)} %copy-done.12), channel_id=1, source_target_pairs={{0,2},{1,3},{2,0},{3,1},{4,6},{5,7},{6,4},{7,5},{8,10},{9,11},{10,... | collective-permute-start | bytes 786440 | tf_op jit(solution)/shard_map/ppermute | solution.py:30
  63.5 17.0 %collective-permute-done.8.refs_10_ = bf16[128,1024]{1,0:T(8,128)(2,1)S(1)} collective-permute-done((bf16[128,1024]{1,0:T(8,128)(2,1)S(1)}, bf16[128,1024]{1,0:T(8,128)(2,1)S(1)}, u32[]{:S(2)}, u32[]{:S(2)}) %collective-permute-start.8) | collective-permute-done | bytes 262176 | tf_op jit(solution)/shard_map/ppermute | solution.py:30
  82.7 1.6 %collective-permute-start.15 = (bf16[104,256]{1,0:T(8,128)(2,1)}, bf16[104,256]{1,0:T(8,128)(2,1)}, u32[]{:S(2)}, u32[]{:S(2)}) collective-permute-start(bf16[104,256]{1,0:T(8,128)(2,1)} %get-tuple-element.47), channel_id=1, source_target_pairs={{0,2},{1,3},{2,0},{3,1},{4,6},{5,7},{6,4},{7,5},{8,10},{9,11},{10,... | collective-permute-start | bytes 159752 | tf_op jit(solution)/shard_map/ppermute | solution.py:30
  84.3 4.0 %collective-permute-done.12.refs_14_ = bf16[128,1024]{1,0:T(8,128)(2,1)S(1)} collective-permute-done((bf16[128,1024]{1,0:T(8,128)(2,1)S(1)}, bf16[128,1024]{1,0:T(8,128)(2,1)S(1)}, u32[]{:S(2)}, u32[]{:S(2)}) %collective-permute-start.12) | collective-permute-done | bytes 262176 | tf_op jit(solution)/shard_map/ppermute | solution.py:30
  97.0 4.6 %wga.1 = (bf16[8,256,128]{2,1,0:T(8,128)(2,1)}, f32[1,1]{1,0:T(1,128)}) custom-call(s32[3]{0:T(128)} %pad_add_fusion.place_ref, bf16[8,528,128]{2,1,0:T(8,128)(2,1)} %copy-done.2, bf16[128,1024]{1,0:T(8,128)(2,1)} %bitcast.10, bf16[128,1024]{1,0:T(8,128)(2,1)} %copy-done.5, bf16[128,1024]{1,0:T(8,128)(2,1)} %copy-done.4, bf16[128,1024]{1,0:T(8,128)(2,1)} %copy-done.6, ...), custom_call_target="tpu_custom_call" | custom-call | flops 536870912 | bytes 4194304 | tf_op jit(solution)/shard_map/wga/pallas_call | solution.py:447
  101.6 4.6 %all-to-all-start.2 = ((bf16[8,256,128]{2,1,0:T(8,128)(2,1)}), bf16[8,256,128]{2,1,0:T(8,128)(2,1)S(1)}, u32[]{:S(2)}, u32[]{:S(2)}) async-start(bf16[8,256,128]{2,1,0:T(8,128)(2,1)} %get-tuple-element.59), calls=%async_computation.2 | async-start | bytes 1048576 | tf_op jit(solution)/shard_map/all_to_all | solution.py:697
  106.2 3.0 %collective-permute-start.18 = (bf16[104,256]{1,0:T(8,128)(2,1)S(1)}, bf16[104,256]{1,0:T(8,128)(2,1)S(1)}, u32[]{:S(2)}, u32[]{:S(2)}) collective-permute-start(bf16[104,256]{1,0:T(8,128)(2,1)S(1)} %add_convert_fusion.2), channel_id=1, source_target_pairs={{0,16},{4,20},{8,24},{12,28},{16,0},{20,4},{24,8},{28,12},{1,17},{... | collective-permute-start | bytes 159752 | tf_op jit(solution)/shard_map/ppermute | solution.py:30
  109.7 13.5 %collective-permute-done.18 = bf16[104,256]{1,0:T(8,128)(2,1)S(1)} collective-permute-done((bf16[104,256]{1,0:T(8,128)(2,1)S(1)}, bf16[104,256]{1,0:T(8,128)(2,1)S(1)}, u32[]{:S(2)}, u32[]{:S(2)}) %collective-permute-start.18) | collective-permute-done | bytes 53280 | tf_op jit(solution)/shard_map/ppermute | solution.py:30
  125.2 2.2 %collective-permute-done.19 = bf16[104,256]{1,0:T(8,128)(2,1)S(1)} collective-permute-done((bf16[104,256]{1,0:T(8,128)(2,1)S(1)}, bf16[104,256]{1,0:T(8,128)(2,1)S(1)}, u32[]{:S(2)}, u32[]{:S(2)}) %collective-permute-start.19) | collective-permute-done | bytes 53280 | tf_op jit(solution)/shard_map/ppermute | solution.py:30
  129.4 4.5 %wgb.1 = (bf16[256,128]{1,0:T(8,128)(2,1)}, bf16[256,128]{1,0:T(8,128)(2,1)}, bf16[256,128]{1,0:T(8,128)(2,1)}, bf16[256,128]{1,0:T(8,128)(2,1)}, bf16[256,128]{...) custom-call(s32[3]{0:T(128)} %pad_add_fusion.place_ref, ...), custom_call_target="tpu_custom_call" | custom-call | flops 536870912 | bytes 4194304 | tf_op jit(solution)/shard_map/wgb/pallas_call | solution.py:509
  136.0 2.0 %collective-permute-start.28 = (bf16[256,128]{1,0:T(8,128)(2,1)}, bf16[256,128]{1,0:T(8,128)(2,1)S(1)}, u32[]{:S(2)}, u32[]{:S(2)}) collective-permute-start(bf16[256,128]{1,0:T(8,128)(2,1)} %get-tuple-element.52), channel_id=1, source_target_pairs={{0,12},{4,8},{8,4},{12,0},{16,28},{20,24},{24,20},{28,16},{1,13},{... | collective-permute-start | bytes 196616 | tf_op jit(solution)/shard_map/ppermute | solution.py:30
  138.8 3.1 %collective-permute-start.30 = (bf16[256,128]{1,0:T(8,128)(2,1)}, bf16[256,128]{1,0:T(8,128)(2,1)S(1)}, u32[]{:S(2)}, u32[]{:S(2)}) collective-permute-start(bf16[256,128]{1,0:T(8,128)(2,1)} %get-tuple-element.54), channel_id=1, source_target_pairs={{0,20},{4,16},{8,28},{12,24},{16,4},{20,0},{24,12},{28,8},{1,21},{... | collective-permute-start | bytes 196616 | tf_op jit(solution)/shard_map/ppermute | solution.py:30
  143.4 2.4 %collective-permute-start.32 = (bf16[256,128]{1,0:T(8,128)(2,1)}, bf16[256,128]{1,0:T(8,128)(2,1)S(1)}, u32[]{:S(2)}, u32[]{:S(2)}) collective-permute-start(bf16[256,128]{1,0:T(8,128)(2,1)} %get-tuple-element.56), channel_id=1, source_target_pairs={{0,28},{4,24},{8,20},{12,16},{16,12},{20,8},{24,4},{28,0},{1,29},{... | collective-permute-start | bytes 196616 | tf_op jit(solution)/shard_map/ppermute | solution.py:30
  146.6 1.9 %collective-permute-done.29.refs_4_ = bf16[256,128]{1,0:T(8,128)(2,1)S(1)} collective-permute-done((bf16[256,128]{1,0:T(8,128)(2,1)}, bf16[256,128]{1,0:T(8,128)(2,1)S(1)}, u32[]{:S(2)}, u32[]{:S(2)}) %collective-permute-start.29) | collective-permute-done | bytes 65568 | tf_op jit(solution)/shard_map/ppermute | solution.py:30
  148.5 2.8 %collective-permute-done.30.refs_5_ = bf16[256,128]{1,0:T(8,128)(2,1)S(1)} collective-permute-done((bf16[256,128]{1,0:T(8,128)(2,1)}, bf16[256,128]{1,0:T(8,128)(2,1)S(1)}, u32[]{:S(2)}, u32[]{:S(2)}) %collective-permute-start.30) | collective-permute-done | bytes 65568 | tf_op jit(solution)/shard_map/ppermute | solution.py:30
  (114 shorter events, 28.8 us)
Async XLA Ops:
  0.6 9.6 %collective-permute-start.1 = (bf16[128,1024]{1,0:T(8,128)(2,1)}, bf16[128,1024]{1,0:T(8,128)(2,1)S(1)}, u32[]{:S(2)}, u32[]{:S(2)}) collective-permute-start(bf16[128,1024]{1,0:T(8,128)(2,1)} %bitcast.6), channel_id=1, source_target_pairs={{0,2},{1,3},{2,0},{3,1},{4,6},{5,7},{6,4},{7,5},{8,10},{9,11},{10,... | collective-permute-start | bytes 786440 | tf_op jit(solution)/shard_map/ppermute | solution.py:30
  3.7 10.6 %collective-permute-start = (bf16[128,1024]{1,0:T(8,128)(2,1)}, bf16[128,1024]{1,0:T(8,128)(2,1)S(1)}, u32[]{:S(2)}, u32[]{:S(2)}) collective-permute-start(bf16[128,1024]{1,0:T(8,128)(2,1)} %bitcast.7), channel_id=1, source_target_pairs={{0,1},{1,0},{2,3},{3,2},{4,5},{5,4},{6,7},{7,6},{8,9},{9,8},{10,11... | collective-permute-start | bytes 786440 | tf_op jit(solution)/shard_map/ppermute | solution.py:30
  21.6 26.9 %all-to-all-start = ((bf16[8,208,128]{2,1,0:T(8,128)(2,1)}), bf16[8,208,128]{2,1,0:T(8,128)(2,1)S(1)}, u32[]{:S(2)}, u32[]{:S(2)}) async-start(bf16[8,208,128]{2,1,0:T(8,128)(2,1)} %get-tuple-element.35), calls=%async_computation | async-start | bytes 851968 | tf_op jit(solution)/shard_map/all_to_all | solution.py:666
  27.7 18.7 %collective-permute-start.3 = (bf16[256,1024]{1,0:T(8,128)(2,1)S(1)}, bf16[256,1024]{1,0:T(8,128)(2,1)S(1)}, u32[]{:S(2)}, u32[]{:S(2)}) collective-permute-start(bf16[256,1024]{1,0:T(8,128)(2,1)S(1)} %copy-done.25), channel_id=1, source_target_pairs={{0,4},{4,0},{8,12},{12,8},{16,20},{20,16},{24,28},{28,24},{1,5},{5... | collective-permute-start | bytes 1572872 | tf_op jit(solution)/shard_map/ppermute | solution.py:30
  46.5 35.5 %collective-permute-start.5 = (bf16[256,1024]{1,0:T(8,128)(2,1)S(1)}, bf16[256,1024]{1,0:T(8,128)(2,1)S(1)}, u32[]{:S(2)}, u32[]{:S(2)}) collective-permute-start(bf16[256,1024]{1,0:T(8,128)(2,1)S(1)} %collective-permute-done.3.refs_4_), channel_id=1, source_target_pairs={{0,2},{1,3},{2,0},{3,1},{4,6},{5,7},{6,4},{7,5},{8,10},{9,11},{10,... | collective-permute-start | bytes 1572872 | tf_op jit(solution)/shard_map/ppermute | solution.py:30
  56.3 38.8 %all-to-all-start.1 = ((bf16[8,528,128]{2,1,0:T(8,128)(2,1)}), bf16[8,528,128]{2,1,0:T(8,128)(2,1)S(1)}, u32[]{:S(2)}, u32[]{:S(2)}) async-start(bf16[8,528,128]{2,1,0:T(8,128)(2,1)} %get-tuple-element.41), calls=%async_computation.1 | async-start | bytes 2162688 | tf_op jit(solution)/shard_map/all_to_all | solution.py:686
  60.1 20.4 %collective-permute-start.8 = (bf16[128,1024]{1,0:T(8,128)(2,1)S(1)}, bf16[128,1024]{1,0:T(8,128)(2,1)S(1)}, u32[]{:S(2)}, u32[]{:S(2)}) collective-permute-start(bf16[128,1024]{1,0:T(8,128)(2,1)S(1)} %copy-done.12), channel_id=1, source_target_pairs={{0,2},{1,3},{2,0},{3,1},{4,6},{5,7},{6,4},{7,5},{8,10},{9,11},{10,... | collective-permute-start | bytes 786440 | tf_op jit(solution)/shard_map/ppermute | solution.py:30
  62.0 20.5 %collective-permute-start.7 = (bf16[128,1024]{1,0:T(8,128)(2,1)S(1)}, bf16[128,1024]{1,0:T(8,128)(2,1)S(1)}, u32[]{:S(2)}, u32[]{:S(2)}) collective-permute-start(bf16[128,1024]{1,0:T(8,128)(2,1)S(1)} %copy-done.12), channel_id=1, source_target_pairs={{0,1},{1,0},{2,3},{3,2},{4,5},{5,4},{6,7},{7,6},{8,9},{9,8},{10,11... | collective-permute-start | bytes 786440 | tf_op jit(solution)/shard_map/ppermute | solution.py:30
  62.0 20.7 %collective-permute-start.10 = (bf16[128,1024]{1,0:T(8,128)(2,1)S(1)}, bf16[128,1024]{1,0:T(8,128)(2,1)S(1)}, u32[]{:S(2)}, u32[]{:S(2)}) collective-permute-start(bf16[128,1024]{1,0:T(8,128)(2,1)S(1)} %copy-done.12), channel_id=1, source_target_pairs={{0,4},{4,0},{8,12},{12,8},{16,20},{20,16},{24,28},{28,24},{1,5},{5... | collective-permute-start | bytes 786440 | tf_op jit(solution)/shard_map/ppermute | solution.py:30
  80.5 7.8 %collective-permute-start.12 = (bf16[128,1024]{1,0:T(8,128)(2,1)S(1)}, bf16[128,1024]{1,0:T(8,128)(2,1)S(1)}, u32[]{:S(2)}, u32[]{:S(2)}) collective-permute-start(bf16[128,1024]{1,0:T(8,128)(2,1)S(1)} %collective-permute-done.8.refs_10_), channel_id=1, source_target_pairs={{0,4},{4,0},{8,12},{12,8},{16,20},{20,16},{24,28},{28,24},{1,5},{5... | collective-permute-start | bytes 786440 | tf_op jit(solution)/shard_map/ppermute | solution.py:30
  81.9 9.6 %collective-permute-start.4 = (bf16[256,1024]{1,0:T(8,128)(2,1)S(1)}, bf16[256,1024]{1,0:T(8,128)(2,1)S(1)}, u32[]{:S(2)}, u32[]{:S(2)}) collective-permute-start(bf16[256,1024]{1,0:T(8,128)(2,1)S(1)} %collective-permute-done.3.refs_4_), channel_id=1, source_target_pairs={{0,1},{1,0},{2,3},{3,2},{4,5},{5,4},{6,7},{7,6},{8,9},{9,8},{10,11... | collective-permute-start | bytes 1572872 | tf_op jit(solution)/shard_map/ppermute | solution.py:30
  82.0 13.2 %collective-permute-start.6 = (bf16[256,1024]{1,0:T(8,128)(2,1)S(1)}, bf16[256,1024]{1,0:T(8,128)(2,1)S(1)}, u32[]{:S(2)}, u32[]{:S(2)}) collective-permute-start(bf16[256,1024]{1,0:T(8,128)(2,1)S(1)} %collective-permute-done.5.refs_6_), channel_id=1, source_target_pairs={{0,1},{1,0},{2,3},{3,2},{4,5},{5,4},{6,7},{7,6},{8,9},{9,8},{10,11... | collective-permute-start | bytes 1572872 | tf_op jit(solution)/shard_map/ppermute | solution.py:30
  91.6 14.6 %collective-permute-start.17 = (bf16[104,256]{1,0:T(8,128)(2,1)S(1)}, bf16[104,256]{1,0:T(8,128)(2,1)S(1)}, u32[]{:S(2)}, u32[]{:S(2)}) collective-permute-start(bf16[104,256]{1,0:T(8,128)(2,1)S(1)} %add_convert_fusion.3), channel_id=1, source_target_pairs={{0,8},{4,12},{8,0},{12,4},{16,24},{20,28},{24,16},{28,20},{1,9},{5... | collective-permute-start | bytes 159752 | tf_op jit(solution)/shard_map/ppermute | solution.py:30
  101.6 51.9 %all-to-all-start.2 = ((bf16[8,256,128]{2,1,0:T(8,128)(2,1)}), bf16[8,256,128]{2,1,0:T(8,128)(2,1)S(1)}, u32[]{:S(2)}, u32[]{:S(2)}) async-start(bf16[8,256,128]{2,1,0:T(8,128)(2,1)} %get-tuple-element.59), calls=%async_computation.2 | async-start | bytes 1048576 | tf_op jit(solution)/shard_map/all_to_all | solution.py:697
  106.2 17.0 %collective-permute-start.18 = (bf16[104,256]{1,0:T(8,128)(2,1)S(1)}, bf16[104,256]{1,0:T(8,128)(2,1)S(1)}, u32[]{:S(2)}, u32[]{:S(2)}) collective-permute-start(bf16[104,256]{1,0:T(8,128)(2,1)S(1)} %add_convert_fusion.2), channel_id=1, source_target_pairs={{0,16},{4,20},{8,24},{12,28},{16,0},{20,4},{24,8},{28,12},{1,17},{... | collective-permute-start | bytes 159752 | tf_op jit(solution)/shard_map/ppermute | solution.py:30
  109.2 15.5 %collective-permute-start.24 = (bf16[128,1024]{1,0:T(8,128)(2,1)S(1)}, bf16[128,1024]{1,0:T(8,128)(2,1)S(1)}, u32[]{:S(2)}, u32[]{:S(2)}) collective-permute-start(bf16[128,1024]{1,0:T(8,128)(2,1)S(1)} %bitcast.15), channel_id=1, source_target_pairs={{0,2},{1,3},{2,0},{3,1},{4,6},{5,7},{6,4},{7,5},{8,10},{9,11},{10,... | collective-permute-start | bytes 786440 | tf_op jit(solution)/shard_map/ppermute | solution.py:30
  127.4 8.1 %collective-permute-start.21 = (bf16[104,256]{1,0:T(8,128)(2,1)S(1)}, bf16[104,256]{1,0:T(8,128)(2,1)S(1)}, u32[]{:S(2)}, u32[]{:S(2)}) collective-permute-start(bf16[104,256]{1,0:T(8,128)(2,1)S(1)} %add_convert_fusion.refs_0_), channel_id=1, source_target_pairs={{0,2},{1,3},{2,0},{3,1},{4,6},{5,7},{6,4},{7,5},{8,10},{9,11},{10,... | collective-permute-start | bytes 159752 | tf_op jit(solution)/shard_map/ppermute | solution.py:30
  134.0 7.9 %collective-permute-start.26 = (bf16[256,128]{1,0:T(8,128)(2,1)}, bf16[256,128]{1,0:T(8,128)(2,1)S(1)}, u32[]{:S(2)}, u32[]{:S(2)}) collective-permute-start(bf16[256,128]{1,0:T(8,128)(2,1)} %get-tuple-element.50), channel_id=1, source_target_pairs={{0,4},{4,0},{8,12},{12,8},{16,20},{20,16},{24,28},{28,24},{1,5},{5... | collective-permute-start | bytes 196616 | tf_op jit(solution)/shard_map/ppermute | solution.py:30
  135.5 7.8 %collective-permute-start.27 = (bf16[256,128]{1,0:T(8,128)(2,1)}, bf16[256,128]{1,0:T(8,128)(2,1)S(1)}, u32[]{:S(2)}, u32[]{:S(2)}) collective-permute-start(bf16[256,128]{1,0:T(8,128)(2,1)} %get-tuple-element.51), channel_id=1, source_target_pairs={{0,8},{4,12},{8,0},{12,4},{16,24},{20,28},{24,16},{28,20},{1,9},{5... | collective-permute-start | bytes 196616 | tf_op jit(solution)/shard_map/ppermute | solution.py:30
  136.0 10.5 %collective-permute-start.28 = (bf16[256,128]{1,0:T(8,128)(2,1)}, bf16[256,128]{1,0:T(8,128)(2,1)S(1)}, u32[]{:S(2)}, u32[]{:S(2)}) collective-permute-start(bf16[256,128]{1,0:T(8,128)(2,1)} %get-tuple-element.52), channel_id=1, source_target_pairs={{0,12},{4,8},{8,4},{12,0},{16,28},{20,24},{24,20},{28,16},{1,13},{... | collective-permute-start | bytes 196616 | tf_op jit(solution)/shard_map/ppermute | solution.py:30
  138.1 10.4 %collective-permute-start.29 = (bf16[256,128]{1,0:T(8,128)(2,1)}, bf16[256,128]{1,0:T(8,128)(2,1)S(1)}, u32[]{:S(2)}, u32[]{:S(2)}) collective-permute-start(bf16[256,128]{1,0:T(8,128)(2,1)} %get-tuple-element.53), channel_id=1, source_target_pairs={{0,16},{4,20},{8,24},{12,28},{16,0},{20,4},{24,8},{28,12},{1,17},{... | collective-permute-start | bytes 196616 | tf_op jit(solution)/shard_map/ppermute | solution.py:30
  138.8 12.5 %collective-permute-start.30 = (bf16[256,128]{1,0:T(8,128)(2,1)}, bf16[256,128]{1,0:T(8,128)(2,1)S(1)}, u32[]{:S(2)}, u32[]{:S(2)}) collective-permute-start(bf16[256,128]{1,0:T(8,128)(2,1)} %get-tuple-element.54), channel_id=1, source_target_pairs={{0,20},{4,16},{8,28},{12,24},{16,4},{20,0},{24,12},{28,8},{1,21},{... | collective-permute-start | bytes 196616 | tf_op jit(solution)/shard_map/ppermute | solution.py:30
  141.9 9.4 %collective-permute-start.31 = (bf16[256,128]{1,0:T(8,128)(2,1)}, bf16[256,128]{1,0:T(8,128)(2,1)S(1)}, u32[]{:S(2)}, u32[]{:S(2)}) collective-permute-start(bf16[256,128]{1,0:T(8,128)(2,1)} %get-tuple-element.55), channel_id=1, source_target_pairs={{0,24},{4,28},{8,16},{12,20},{16,8},{20,12},{24,0},{28,4},{1,25},{... | collective-permute-start | bytes 196616 | tf_op jit(solution)/shard_map/ppermute | solution.py:30
  143.4 7.9 %collective-permute-start.32 = (bf16[256,128]{1,0:T(8,128)(2,1)}, bf16[256,128]{1,0:T(8,128)(2,1)S(1)}, u32[]{:S(2)}, u32[]{:S(2)}) collective-permute-start(bf16[256,128]{1,0:T(8,128)(2,1)} %get-tuple-element.56), channel_id=1, source_target_pairs={{0,28},{4,24},{8,20},{12,16},{16,12},{20,8},{24,4},{28,0},{1,29},{... | collective-permute-start | bytes 196616 | tf_op jit(solution)/shard_map/ppermute | solution.py:30
  (38 other events, 222.8 us)

commit v11 on v9

--- a/solution.py
+++ b/solution.py
@@ -94,34 +94,19 @@
     latent_refs = refs[5 : 5 + shards]
     weights_hbm = refs[5 + shards : 8 + shards]
     (
-        key_hbm,
-        value_hbm,
-        soft_hbm,
-        attended_ref,
-        normed_hbm,
-        inverse_ref,
-        packed_ref,
         key_ref,
         value_ref,
         soft_ref,
+        attended_ref,
         normed_ref,
+        inverse_ref,
+        packed_ref,
         *w_refs,
         sem,
-        out_sem,
     ) = refs[8 + shards :]
     copies = [pltpu.make_async_copy(s, d, sem.at[i]) for i, (s, d) in enumerate(zip(weights_hbm, w_refs))]
     for copy in copies:
         copy.start()
-    key_copy, value_copy, normed_copy = (
-        pltpu.make_async_copy(full, out, out_sem.at[i])
-        for i, (full, out) in enumerate(
-            ((key_ref, key_hbm), (value_ref, value_hbm), (normed_ref, normed_hbm))
-        )
-    )
-    soft_copies = [
-        pltpu.make_async_copy(soft_ref.at[i], soft_hbm.at[i], out_sem.at[3 + i])
-        for i in range(soft_ref.shape[0])
-    ]
     points, features = grid_ref.shape
     latents = jnp.concatenate([ref[...] for ref in latent_refs], axis=0)
     each = latent_refs[0].shape[0]
@@ -132,10 +117,8 @@
     nodes = dot32(chosen, latents, (0, 0)).astype(BF16)
     copies[0].wait()
     key_ref[...] = dot32(nodes, w_refs[0][...]).astype(BF16)
-    key_copy.start()
     copies[1].wait()
     value_ref[...] = dot32(nodes, w_refs[1][...]).astype(BF16)
-    value_copy.start()
     factor = (features // HEADS) ** (-0.5)
     for pair in range(features // LANES):
         at = slice(pair * LANES, (pair + 1) * LANES)
@@ -147,14 +130,12 @@
             soft.append(raised / jnp.sum(raised, axis=-1, keepdims=True))
         soft = jnp.concatenate(soft, axis=1)
         soft_ref[pair] = soft
-        soft_copies[pair].start()
         attended_ref[:, at] = dot32(soft.astype(BF16), halves(value_ref[:, at])).astype(BF16)
     copies[2].wait()
     hidden = grid_ref[...].astype(F32) + dot32(attended_ref[...], w_refs[2][...])
     inverse = lax.rsqrt(jnp.mean(hidden * hidden, axis=-1, keepdims=True) + EPS)
     normed = hidden * inverse
     normed_ref[...] = normed
-    normed_copy.start()
     inverse_ref[...] = inverse
     normed_b = normed.astype(BF16)
     forecast = dot32(readout_ref[...], normed_b, (1, 1))
@@ -165,12 +146,10 @@
     fields = jnp.concatenate([high, spare, low, spare], axis=0)
     for m in range(members):
         packed_ref[m] = fields
-    for copy in (key_copy, value_copy, normed_copy, *soft_copies):
-        copy.wait()
 
 
 def padded(channels):
-    return channels + -channels % 16
+    return channels + -channels % 8
 
 
 def forward(shard, index, grid_rows, queries, readout, latents, weights, members):
@@ -189,18 +168,9 @@
             shape((members, 2 * channels, points), BF16),
         ),
         in_specs=[SMEM] + [VMEM] * (4 + len(latents)) + [ANY] * 3,
-        out_specs=(HBM, HBM, HBM, VMEM, HBM, VMEM, VMEM),
-        scratch_shapes=[
-            pltpu.VMEM((points, features), BF16),
-            pltpu.VMEM((points, features), BF16),
-            pltpu.VMEM((features // LANES, points, 2 * LANES), F32),
-            pltpu.VMEM((points, features), F32),
-        ]
-        + [pltpu.VMEM((features, features), BF16)] * 3
-        + [
-            pltpu.SemaphoreType.DMA((3,)),
-            pltpu.SemaphoreType.DMA((3 + features // LANES,)),
-        ],
+        out_specs=(VMEM,) * 7,
+        scratch_shapes=[pltpu.VMEM((features, features), BF16)] * 3
+        + [pltpu.SemaphoreType.DMA((3,))],
         cost_estimate=pl.CostEstimate(
             flops=8 * points * features * features,
             bytes_accessed=6 * features * features,
@@ -250,7 +220,7 @@
     width = features // blocks
     weight = (channels_used * points * shards) ** (-0.5)
     pair_weight = 1.0 / (members * (members - 1))
-    chunk = 16
+    chunk = 8
 
     def crps(c, loss):
         at = pl.ds(pl.multiple_of(c * chunk, chunk), chunk)
@@ -284,7 +254,9 @@
         term = skill * (1.0 / members) - spread * pair_weight
         return loss + jnp.where(channel < channels_used, term, 0.0)
 
-    loss = lax.fori_loop(0, channels // chunk, crps, jnp.zeros((chunk, points), F32))
+    loss = lax.fori_loop(
+        0, channels // chunk, crps, jnp.zeros((chunk, points), F32), unroll=members <= 8
+    )
     loss = weight * jnp.sum(jnp.sum(loss, axis=0, keepdims=True), axis=1, keepdims=True)
 
     first = loss.astype(BF16).astype(F32)
@@ -354,7 +326,7 @@
     points = saved[0].shape[0]
     channels = padded(readout.shape[0])
     width = features // blocks
-    small = 16
+    small = MISC
     return pl.pallas_call(
         functools.partial(backward_kernel, shards, blocks, nodes),
         out_shape=(
@@ -489,6 +461,7 @@
             bytes_accessed=8 * points * count * features,
             transcendentals=0,
         ),
+        compiler_params=pltpu.CompilerParams(vmem_limit_bytes=51 << 20),
         name="wgrad",
     )(place, blocks, *latents, *early, *late, *other, *grids)
 
@@ -544,6 +517,7 @@
         out_shape=jax.ShapeDtypeStruct((channels_used, columns), F32),
         in_specs=[SMEM] + [VMEM] * len(parts),
         out_specs=VMEM,
+        compiler_params=pltpu.CompilerParams(vmem_limit_bytes=6 << 20),
         name="join",
     )(shard, *parts)
 

time: 148 us -> 142 us (0.959)
  local copies, waits for them, and re-layouts: 4.36 us -> 1.61 us
  Pallas kernels: 27.2 us -> 24.9 us
    unnamed x50 -> x38, local copies, waits for them, and re-layouts: 4.36 us -> 1.61 us
  transfers between devices with their start and end apart: 29 -> 29, of which waited for: 12 -> 12; matrix products, arithmetic and copies ran while one was open for 1% -> 1% of each run, Pallas kernels for 9% -> 8%
where the time goes in v11:
time: 142 us; the launch traced here: 141 us
  waiting for transfers between devices  73.4 us (52%)
  starting transfers between devices  39.8 us (28%)
  Pallas kernels  24.9 us (18%)
  local copies, waits for them, and re-layouts  1.61 us (1%)
    ppermute x26, waiting for transfers between devices, swap(): return lax.ppermute(value, axis, [(i, i ^ bits) for i in range(size)])  73.4 us
    ppermute x26, starting transfers between devices, swap(): return lax.ppermute(value, axis, [(i, i ^ bits) for i in range(size)])  23.8 us
    pallas_call x1, Pallas kernels, backward(): pl.pallas_call(functools.partial(backward_kernel, shards, blocks, nodes),...  7.02 us
    pallas_call x1, Pallas kernels, forward(): pl.pallas_call(functools.partial(forward_kernel, len(latents), members),...  6.6 us
    all_to_all x1, starting transfers between devices, body(): lax.all_to_all(packed, 'ens', split_axis=0, concat_axis=0, tiled=True)  6.09 us
    all_to_all x1, starting transfers between devices, body(): lax.all_to_all(blocks, 'ens', split_axis=0, concat_axis=0, tiled=True)  5.58 us
    pallas_call x1, Pallas kernels, gradients(): pl.pallas_call(functools.partial(gradient_kernel, shards, pair, members,...  5.16 us
    all_to_all x1, starting transfers between devices, body(): lax.all_to_all(blocks, ('ens', 'space'), split_axis=0, concat_axis=0, axi...  4.39 us
  transfers between devices with their start and end apart: 29, of which 12 were waited for; matrix products, arithmetic and copies ran while one was open for 1% of the time, Pallas kernels for 8%

profile of v11, /device:TPU:0, one launch (start us, length us, event | category | flops | bytes accessed | tf_op | source)
XLA Modules:
  0.0 141.4 jit_solution(16835819709945298767)
XLA Ops:
  0.6 3.0 %collective-permute-start.1 = (bf16[128,1024]{1,0:T(8,128)(2,1)}, bf16[128,1024]{1,0:T(8,128)(2,1)S(1)}, u32[]{:S(2)}, u32[]{:S(2)}) collective-permute-start(bf16[128,1024]{1,0:T(8,128)(2,1)} %bitcast.6), channel_id=1, source_target_pairs={{0,2},{1,3},{2,0},{3,1},{4,6},{5,7},{6,4},{7,5},{8,10},{9,11},{10,... | collective-permute-start | bytes 786440 | tf_op jit(solution)/shard_map/ppermute | solution.py:30
  3.7 6.5 %collective-permute-done.1.refs_7_.refs_2_ = bf16[128,1024]{1,0:T(8,128)(2,1)S(1)} collective-permute-done((bf16[128,1024]{1,0:T(8,128)(2,1)}, bf16[128,1024]{1,0:T(8,128)(2,1)S(1)}, u32[]{:S(2)}, u32[]{:S(2)}) %collective-permute-start.1) | collective-permute-done | bytes 262176 | tf_op jit(solution)/shard_map/ppermute | solution.py:30
  10.2 4.1 %proj.1 = (bf16[128,1024]{1,0:T(8,128)(2,1)}, bf16[256,1024]{1,0:T(8,128)(2,1)}) custom-call(bf16[128,1024]{1,0:T(8,128)(2,1)} %bitcast.8, bf16[128,1024]{1,0:T(8,128)(2,1)} %bitcast.11, bf16[1024,1024]{1,0:T(8,128)(2,1)} %w_hbm.2), custom_call_target="tpu_custom_call" | custom-call | flops 268435456 | bytes 2097152 | tf_op jit(solution)/shard_map/proj/pallas_call | solution.py:73
  15.1 6.6 %fwd.1 = (bf16[128,1024]{1,0:T(8,128)(2,1)}, bf16[128,1024]{1,0:T(8,128)(2,1)}, f32[8,128,256]{2,1,0:T(8,128)}, bf16[128,1024]{1,0:T(8,128)(2,1)}, f32[128,1024]...) custom-call(s32[1]{0:T(128)} %bitcast.refs_0_.shard_ref, s32[1,128]{1,0:T(1,128)} %index_ref.1, ...), custom_call_target="tpu_custom_call" | custom-call | flops 1073741824 | bytes 6291456 | tf_op jit(solution)/shard_map/fwd/pallas_call | solution.py:159
  21.7 6.1 %all-to-all-start = ((bf16[8,208,128]{2,1,0:T(8,128)(2,1)}), bf16[8,208,128]{2,1,0:T(8,128)(2,1)S(1)}, u32[]{:S(2)}, u32[]{:S(2)}) async-start(bf16[8,208,128]{2,1,0:T(8,128)(2,1)} %get-tuple-element.27), calls=%async_computation | async-start | bytes 851968 | tf_op jit(solution)/shard_map/all_to_all | solution.py:574
  27.8 2.0 %collective-permute-start.3 = (bf16[256,1024]{1,0:T(8,128)(2,1)S(1)}, bf16[256,1024]{1,0:T(8,128)(2,1)S(1)}, u32[]{:S(2)}, u32[]{:S(2)}) collective-permute-start(bf16[256,1024]{1,0:T(8,128)(2,1)S(1)} %copy-done.15), channel_id=1, source_target_pairs={{0,4},{4,0},{8,12},{12,8},{16,20},{20,16},{24,28},{28,24},{1,5},{5... | collective-permute-start | bytes 1572872 | tf_op jit(solution)/shard_map/ppermute | solution.py:30
  29.8 1.5 %collective-permute-start.15 = (bf16[128,1024]{1,0:T(8,128)(2,1)S(1)}, bf16[128,1024]{1,0:T(8,128)(2,1)S(1)}, u32[]{:S(2)}, u32[]{:S(2)}) collective-permute-start(bf16[128,1024]{1,0:T(8,128)(2,1)S(1)} %bitcast.14), channel_id=1, source_target_pairs={{0,2},{1,3},{2,0},{3,1},{4,6},{5,7},{6,4},{7,5},{8,10},{9,11},{10,... | collective-permute-start | bytes 786440 | tf_op jit(solution)/shard_map/ppermute | solution.py:30
  31.3 15.2 %collective-permute-done.3.refs_4_ = bf16[256,1024]{1,0:T(8,128)(2,1)S(1)} collective-permute-done((bf16[256,1024]{1,0:T(8,128)(2,1)S(1)}, bf16[256,1024]{1,0:T(8,128)(2,1)S(1)}, u32[]{:S(2)}, u32[]{:S(2)}) %collective-permute-start.3) | collective-permute-done | bytes 524320 | tf_op jit(solution)/shard_map/ppermute | solution.py:30
  49.4 7.0 %bwd.1 = (bf16[8,520,128]{2,1,0:T(8,128)(2,1)}, bf16[104,256]{1,0:T(8,128)(2,1)}, bf16[104,256]{1,0:T(8,128)(2,1)}, bf16[104,256]{1,0:T(8,128)(2,1)}, bf16[104,256]{1,0:T(8,128)(2,1)}) custom-call(s32[2]{0:T(128)} %pad_add_fusion.1.place_ref, bf16[8,208,128]{2,1,0:T(8,128)(2,1)} %copy-done.9, f32[100,128]{1,0:T(8,128)} %target_ref.1, s32[1,128]{1,0:T(1,128)} %index_ref.1, ...), custom_call_target="tpu_custom_call" | custom-call | flops 536870912 | bytes 4194304 | tf_op jit(solution)/shard_map/bwd/pallas_call | solution.py:330
  56.4 4.4 %all-to-all-start.1 = ((bf16[8,520,128]{2,1,0:T(8,128)(2,1)}), bf16[8,520,128]{2,1,0:T(8,128)(2,1)}, u32[]{:S(2)}, u32[]{:S(2)}) async-start(bf16[8,520,128]{2,1,0:T(8,128)(2,1)} %get-tuple-element.33), calls=%async_computation.1 | async-start | bytes 2129920 | tf_op jit(solution)/shard_map/all_to_all | solution.py:594
  61.4 1.9 %collective-permute-start.8 = (bf16[128,1024]{1,0:T(8,128)(2,1)S(1)}, bf16[128,1024]{1,0:T(8,128)(2,1)S(1)}, u32[]{:S(2)}, u32[]{:S(2)}) collective-permute-start(bf16[128,1024]{1,0:T(8,128)(2,1)S(1)} %copy-done.7), channel_id=1, source_target_pairs={{0,2},{1,3},{2,0},{3,1},{4,6},{5,7},{6,4},{7,5},{8,10},{9,11},{10,... | collective-permute-start | bytes 786440 | tf_op jit(solution)/shard_map/ppermute | solution.py:30
  63.3 1.5 %collective-permute-start.10 = (bf16[128,1024]{1,0:T(8,128)(2,1)S(1)}, bf16[128,1024]{1,0:T(8,128)(2,1)S(1)}, u32[]{:S(2)}, u32[]{:S(2)}) collective-permute-start(bf16[128,1024]{1,0:T(8,128)(2,1)S(1)} %copy-done.7), channel_id=1, source_target_pairs={{0,4},{4,0},{8,12},{12,8},{16,20},{20,16},{24,28},{28,24},{1,5},{5... | collective-permute-start | bytes 786440 | tf_op jit(solution)/shard_map/ppermute | solution.py:30
  65.0 16.1 %collective-permute-done.8.refs_10_ = bf16[128,1024]{1,0:T(8,128)(2,1)S(1)} collective-permute-done((bf16[128,1024]{1,0:T(8,128)(2,1)S(1)}, bf16[128,1024]{1,0:T(8,128)(2,1)S(1)}, u32[]{:S(2)}, u32[]{:S(2)}) %collective-permute-start.8) | collective-permute-done | bytes 262176 | tf_op jit(solution)/shard_map/ppermute | solution.py:30
  83.1 5.7 %collective-permute-done.12.refs_14_ = bf16[128,1024]{1,0:T(8,128)(2,1)S(1)} collective-permute-done((bf16[128,1024]{1,0:T(8,128)(2,1)S(1)}, bf16[128,1024]{1,0:T(8,128)(2,1)S(1)}, u32[]{:S(2)}, u32[]{:S(2)}) %collective-permute-start.12) | collective-permute-done | bytes 262176 | tf_op jit(solution)/shard_map/ppermute | solution.py:30
  88.9 1.6 %collective-permute-done.13.refs_15_ = bf16[128,1024]{1,0:T(8,128)(2,1)} collective-permute-done((bf16[128,1024]{1,0:T(8,128)(2,1)S(1)}, bf16[128,1024]{1,0:T(8,128)(2,1)}, u32[]{:S(2)}, u32[]{:S(2)}) %collective-permute-start.13) | collective-permute-done | bytes 262176 | tf_op jit(solution)/shard_map/ppermute | solution.py:30
  90.5 5.2 %wgrad.1 = (bf16[8,512,128]{2,1,0:T(8,128)(2,1)}, f32[1,1]{1,0:T(1,128)}) custom-call(s32[2]{0:T(128)S(1)} %pad_add_fusion.place_ref, bf16[8,520,128]{2,1,0:T(8,128)(2,1)} %all-to-all-done.1.blocks_hbm, bf16[128,1024]{1,0:T(8,128)(2,1)S(1)} %bitcast.10, bf16[128,1024]{1,0:T(8,128)(2,1)S(1)} %copy-done.4, bf16[128,1024]{1,0:T(8,128)(2,1)S(1)} %copy-done.2, ...), custom_call_target="tpu_custom_call" | custom-call | flops 1073741824 | bytes 8388608 | tf_op jit(solution)/shard_map/wgrad/pallas_call | solution.py:443
  95.7 5.6 %all-to-all-start.2 = ((bf16[8,512,128]{2,1,0:T(8,128)(2,1)}), bf16[8,512,128]{2,1,0:T(8,128)(2,1)S(1)}, u32[]{:S(2)}, u32[]{:S(2)}) async-start(bf16[8,512,128]{2,1,0:T(8,128)(2,1)} %get-tuple-element.41), calls=%async_computation.2 | async-start | bytes 2097152 | tf_op jit(solution)/shard_map/all_to_all | solution.py:607
  103.3 2.2 %collective-permute-done.19 = bf16[104,256]{1,0:T(8,128)(2,1)S(1)} collective-permute-done((bf16[104,256]{1,0:T(8,128)(2,1)S(1)}, bf16[104,256]{1,0:T(8,128)(2,1)S(1)}, u32[]{:S(2)}, u32[]{:S(2)}) %collective-permute-start.19) | collective-permute-done | bytes 53280 | tf_op jit(solution)/shard_map/ppermute | solution.py:30
  106.7 1.5 %collective-permute-start.20 = (bf16[104,256]{1,0:T(8,128)(2,1)S(1)}, bf16[104,256]{1,0:T(8,128)(2,1)S(1)}, u32[]{:S(2)}, u32[]{:S(2)}) collective-permute-start(bf16[104,256]{1,0:T(8,128)(2,1)S(1)} %add_convert_fusion.3), channel_id=1, source_target_pairs={{0,8},{4,12},{8,0},{12,4},{16,24},{20,28},{24,16},{28,20},{1,9},{5... | collective-permute-start | bytes 159752 | tf_op jit(solution)/shard_map/ppermute | solution.py:30
  108.3 12.2 %collective-permute-done.20 = bf16[104,256]{1,0:T(8,128)(2,1)S(1)} collective-permute-done((bf16[104,256]{1,0:T(8,128)(2,1)S(1)}, bf16[104,256]{1,0:T(8,128)(2,1)S(1)}, u32[]{:S(2)}, u32[]{:S(2)}) %collective-permute-start.20) | collective-permute-done | bytes 53280 | tf_op jit(solution)/shard_map/ppermute | solution.py:30
  120.5 4.0 %collective-permute-start.21 = (bf16[104,256]{1,0:T(8,128)(2,1)S(1)}, bf16[104,256]{1,0:T(8,128)(2,1)S(1)}, u32[]{:S(2)}, u32[]{:S(2)}) collective-permute-start(bf16[104,256]{1,0:T(8,128)(2,1)S(1)} %add_convert_fusion.2), channel_id=1, source_target_pairs={{0,16},{4,20},{8,24},{12,28},{16,0},{20,4},{24,8},{28,12},{1,17},{... | collective-permute-start | bytes 159752 | tf_op jit(solution)/shard_map/ppermute | solution.py:30
  124.5 5.2 %collective-permute-done.21 = bf16[104,256]{1,0:T(8,128)(2,1)S(1)} collective-permute-done((bf16[104,256]{1,0:T(8,128)(2,1)S(1)}, bf16[104,256]{1,0:T(8,128)(2,1)S(1)}, u32[]{:S(2)}, u32[]{:S(2)}) %collective-permute-start.21) | collective-permute-done | bytes 53280 | tf_op jit(solution)/shard_map/ppermute | solution.py:30
  131.2 2.7 %collective-permute-done.22 = bf16[104,256]{1,0:T(8,128)(2,1)S(1)} collective-permute-done((bf16[104,256]{1,0:T(8,128)(2,1)S(1)}, bf16[104,256]{1,0:T(8,128)(2,1)S(1)}, u32[]{:S(2)}, u32[]{:S(2)}) %collective-permute-start.22) | collective-permute-done | bytes 53280 | tf_op jit(solution)/shard_map/ppermute | solution.py:30
  134.5 3.6 %collective-permute-done.24.refs_2_ = bf16[104,256]{1,0:T(8,128)(2,1)S(1)} collective-permute-done((bf16[104,256]{1,0:T(8,128)(2,1)S(1)}, bf16[104,256]{1,0:T(8,128)(2,1)S(1)}, u32[]{:S(2)}, u32[]{:S(2)}) %collective-permute-start.24) | collective-permute-done | bytes 53280 | tf_op jit(solution)/shard_map/ppermute | solution.py:30
  (84 shorter events, 15.1 us)
Async XLA Ops:
  0.6 9.6 %collective-permute-start.1 = (bf16[128,1024]{1,0:T(8,128)(2,1)}, bf16[128,1024]{1,0:T(8,128)(2,1)S(1)}, u32[]{:S(2)}, u32[]{:S(2)}) collective-permute-start(bf16[128,1024]{1,0:T(8,128)(2,1)} %bitcast.6), channel_id=1, source_target_pairs={{0,2},{1,3},{2,0},{3,1},{4,6},{5,7},{6,4},{7,5},{8,10},{9,11},{10,... | collective-permute-start | bytes 786440 | tf_op jit(solution)/shard_map/ppermute | solution.py:30
  3.7 10.6 %collective-permute-start = (bf16[128,1024]{1,0:T(8,128)(2,1)}, bf16[128,1024]{1,0:T(8,128)(2,1)S(1)}, u32[]{:S(2)}, u32[]{:S(2)}) collective-permute-start(bf16[128,1024]{1,0:T(8,128)(2,1)} %bitcast.7), channel_id=1, source_target_pairs={{0,1},{1,0},{2,3},{3,2},{4,5},{5,4},{6,7},{7,6},{8,9},{9,8},{10,11... | collective-permute-start | bytes 786440 | tf_op jit(solution)/shard_map/ppermute | solution.py:30
  10.2 4.1 %collective-permute-start.2 = (bf16[128,1024]{1,0:T(8,128)(2,1)S(1)}, bf16[128,1024]{1,0:T(8,128)(2,1)S(1)}, u32[]{:S(2)}, u32[]{:S(2)}) collective-permute-start(bf16[128,1024]{1,0:T(8,128)(2,1)S(1)} %collective-permute-done.1.refs_7_.refs_2_), channel_id=1, source_target_pairs={{0,1},{1,0},{2,3},{3,2},{4,5},{5,4},{6,7},{7,6},{8,9},{9,8},{10,11... | collective-permute-start | bytes 786440 | tf_op jit(solution)/shard_map/ppermute | solution.py:30
  21.7 26.9 %all-to-all-start = ((bf16[8,208,128]{2,1,0:T(8,128)(2,1)}), bf16[8,208,128]{2,1,0:T(8,128)(2,1)S(1)}, u32[]{:S(2)}, u32[]{:S(2)}) async-start(bf16[8,208,128]{2,1,0:T(8,128)(2,1)} %get-tuple-element.27), calls=%async_computation | async-start | bytes 851968 | tf_op jit(solution)/shard_map/all_to_all | solution.py:574
  27.8 18.7 %collective-permute-start.3 = (bf16[256,1024]{1,0:T(8,128)(2,1)S(1)}, bf16[256,1024]{1,0:T(8,128)(2,1)S(1)}, u32[]{:S(2)}, u32[]{:S(2)}) collective-permute-start(bf16[256,1024]{1,0:T(8,128)(2,1)S(1)} %copy-done.15), channel_id=1, source_target_pairs={{0,4},{4,0},{8,12},{12,8},{16,20},{20,16},{24,28},{28,24},{1,5},{5... | collective-permute-start | bytes 1572872 | tf_op jit(solution)/shard_map/ppermute | solution.py:30
  29.8 31.4 %collective-permute-start.15 = (bf16[128,1024]{1,0:T(8,128)(2,1)S(1)}, bf16[128,1024]{1,0:T(8,128)(2,1)S(1)}, u32[]{:S(2)}, u32[]{:S(2)}) collective-permute-start(bf16[128,1024]{1,0:T(8,128)(2,1)S(1)} %bitcast.14), channel_id=1, source_target_pairs={{0,2},{1,3},{2,0},{3,1},{4,6},{5,7},{6,4},{7,5},{8,10},{9,11},{10,... | collective-permute-start | bytes 786440 | tf_op jit(solution)/shard_map/ppermute | solution.py:30
  46.5 36.0 %collective-permute-start.5 = (bf16[256,1024]{1,0:T(8,128)(2,1)S(1)}, bf16[256,1024]{1,0:T(8,128)(2,1)}, u32[]{:S(2)}, u32[]{:S(2)}) collective-permute-start(bf16[256,1024]{1,0:T(8,128)(2,1)S(1)} %collective-permute-done.3.refs_4_), channel_id=1, source_target_pairs={{0,2},{1,3},{2,0},{3,1},{4,6},{5,7},{6,4},{7,5},{8,10},{9,11},{10,... | collective-permute-start | bytes 1572872 | tf_op jit(solution)/shard_map/ppermute | solution.py:30
  56.4 34.1 %all-to-all-start.1 = ((bf16[8,520,128]{2,1,0:T(8,128)(2,1)}), bf16[8,520,128]{2,1,0:T(8,128)(2,1)}, u32[]{:S(2)}, u32[]{:S(2)}) async-start(bf16[8,520,128]{2,1,0:T(8,128)(2,1)} %get-tuple-element.33), calls=%async_computation.1 | async-start | bytes 2129920 | tf_op jit(solution)/shard_map/all_to_all | solution.py:594
  61.4 19.6 %collective-permute-start.8 = (bf16[128,1024]{1,0:T(8,128)(2,1)S(1)}, bf16[128,1024]{1,0:T(8,128)(2,1)S(1)}, u32[]{:S(2)}, u32[]{:S(2)}) collective-permute-start(bf16[128,1024]{1,0:T(8,128)(2,1)S(1)} %copy-done.7), channel_id=1, source_target_pairs={{0,2},{1,3},{2,0},{3,1},{4,6},{5,7},{6,4},{7,5},{8,10},{9,11},{10,... | collective-permute-start | bytes 786440 | tf_op jit(solution)/shard_map/ppermute | solution.py:30
  63.3 19.3 %collective-permute-start.7 = (bf16[128,1024]{1,0:T(8,128)(2,1)S(1)}, bf16[128,1024]{1,0:T(8,128)(2,1)S(1)}, u32[]{:S(2)}, u32[]{:S(2)}) collective-permute-start(bf16[128,1024]{1,0:T(8,128)(2,1)S(1)} %copy-done.7), channel_id=1, source_target_pairs={{0,1},{1,0},{2,3},{3,2},{4,5},{5,4},{6,7},{7,6},{8,9},{9,8},{10,11... | collective-permute-start | bytes 786440 | tf_op jit(solution)/shard_map/ppermute | solution.py:30
  63.3 19.8 %collective-permute-start.10 = (bf16[128,1024]{1,0:T(8,128)(2,1)S(1)}, bf16[128,1024]{1,0:T(8,128)(2,1)S(1)}, u32[]{:S(2)}, u32[]{:S(2)}) collective-permute-start(bf16[128,1024]{1,0:T(8,128)(2,1)S(1)} %copy-done.7), channel_id=1, source_target_pairs={{0,4},{4,0},{8,12},{12,8},{16,20},{20,16},{24,28},{28,24},{1,5},{5... | collective-permute-start | bytes 786440 | tf_op jit(solution)/shard_map/ppermute | solution.py:30
  64.8 24.1 %collective-permute-start.4 = (bf16[256,1024]{1,0:T(8,128)(2,1)S(1)}, bf16[256,1024]{1,0:T(8,128)(2,1)}, u32[]{:S(2)}, u32[]{:S(2)}) collective-permute-start(bf16[256,1024]{1,0:T(8,128)(2,1)S(1)} %collective-permute-done.3.refs_4_), channel_id=1, source_target_pairs={{0,1},{1,0},{2,3},{3,2},{4,5},{5,4},{6,7},{7,6},{8,9},{9,8},{10,11... | collective-permute-start | bytes 1572872 | tf_op jit(solution)/shard_map/ppermute | solution.py:30
  81.0 7.8 %collective-permute-start.12 = (bf16[128,1024]{1,0:T(8,128)(2,1)S(1)}, bf16[128,1024]{1,0:T(8,128)(2,1)S(1)}, u32[]{:S(2)}, u32[]{:S(2)}) collective-permute-start(bf16[128,1024]{1,0:T(8,128)(2,1)S(1)} %collective-permute-done.8.refs_10_), channel_id=1, source_target_pairs={{0,4},{4,0},{8,12},{12,8},{16,20},{20,16},{24,28},{28,24},{1,5},{5... | collective-permute-start | bytes 786440 | tf_op jit(solution)/shard_map/ppermute | solution.py:30
  82.5 8.0 %collective-permute-start.6 = (bf16[256,1024]{1,0:T(8,128)(2,1)}, bf16[256,1024]{1,0:T(8,128)(2,1)}, u32[]{:S(2)}, u32[]{:S(2)}) collective-permute-start(bf16[256,1024]{1,0:T(8,128)(2,1)} %collective-permute-done.5.refs_6_), channel_id=1, source_target_pairs={{0,1},{1,0},{2,3},{3,2},{4,5},{5,4},{6,7},{7,6},{8,9},{9,8},{10,11... | collective-permute-start | bytes 1572872 | tf_op jit(solution)/shard_map/ppermute | solution.py:30
  82.5 6.4 %collective-permute-start.9 = (bf16[128,1024]{1,0:T(8,128)(2,1)S(1)}, bf16[128,1024]{1,0:T(8,128)(2,1)S(1)}, u32[]{:S(2)}, u32[]{:S(2)}) collective-permute-start(bf16[128,1024]{1,0:T(8,128)(2,1)S(1)} %collective-permute-done.8.refs_10_), channel_id=1, source_target_pairs={{0,1},{1,0},{2,3},{3,2},{4,5},{5,4},{6,7},{7,6},{8,9},{9,8},{10,11... | collective-permute-start | bytes 786440 | tf_op jit(solution)/shard_map/ppermute | solution.py:30
  83.0 5.9 %collective-permute-start.11 = (bf16[128,1024]{1,0:T(8,128)(2,1)S(1)}, bf16[128,1024]{1,0:T(8,128)(2,1)S(1)}, u32[]{:S(2)}, u32[]{:S(2)}) collective-permute-start(bf16[128,1024]{1,0:T(8,128)(2,1)S(1)} %collective-permute-done.10.refs_12_), channel_id=1, source_target_pairs={{0,1},{1,0},{2,3},{3,2},{4,5},{5,4},{6,7},{7,6},{8,9},{9,8},{10,11... | collective-permute-start | bytes 786440 | tf_op jit(solution)/shard_map/ppermute | solution.py:30
  95.7 44.5 %all-to-all-start.2 = ((bf16[8,512,128]{2,1,0:T(8,128)(2,1)}), bf16[8,512,128]{2,1,0:T(8,128)(2,1)S(1)}, u32[]{:S(2)}, u32[]{:S(2)}) async-start(bf16[8,512,128]{2,1,0:T(8,128)(2,1)} %get-tuple-element.41), calls=%async_computation.2 | async-start | bytes 2097152 | tf_op jit(solution)/shard_map/all_to_all | solution.py:607
  101.3 4.2 %collective-permute-start.19 = (bf16[104,256]{1,0:T(8,128)(2,1)S(1)}, bf16[104,256]{1,0:T(8,128)(2,1)S(1)}, u32[]{:S(2)}, u32[]{:S(2)}) collective-permute-start(bf16[104,256]{1,0:T(8,128)(2,1)S(1)} %copy-done.18), channel_id=1, source_target_pairs={{0,3},{1,2},{2,1},{3,0},{4,7},{5,6},{6,5},{7,4},{8,11},{9,10},{10,... | collective-permute-start | bytes 159752 | tf_op jit(solution)/shard_map/ppermute | solution.py:30
  101.4 5.2 %collective-permute-start.18 = (bf16[104,256]{1,0:T(8,128)(2,1)S(1)}, bf16[104,256]{1,0:T(8,128)(2,1)S(1)}, u32[]{:S(2)}, u32[]{:S(2)}) collective-permute-start(bf16[104,256]{1,0:T(8,128)(2,1)S(1)} %copy-done.17), channel_id=1, source_target_pairs={{0,2},{1,3},{2,0},{3,1},{4,6},{5,7},{6,4},{7,5},{8,10},{9,11},{10,... | collective-permute-start | bytes 159752 | tf_op jit(solution)/shard_map/ppermute | solution.py:30
  102.9 3.8 %collective-permute-start.17 = (bf16[104,256]{1,0:T(8,128)(2,1)S(1)}, bf16[104,256]{1,0:T(8,128)(2,1)S(1)}, u32[]{:S(2)}, u32[]{:S(2)}) collective-permute-start(bf16[104,256]{1,0:T(8,128)(2,1)S(1)} %copy-done.16), channel_id=1, source_target_pairs={{0,1},{1,0},{2,3},{3,2},{4,5},{5,4},{6,7},{7,6},{8,9},{9,8},{10,11... | collective-permute-start | bytes 159752 | tf_op jit(solution)/shard_map/ppermute | solution.py:30
  106.7 13.8 %collective-permute-start.20 = (bf16[104,256]{1,0:T(8,128)(2,1)S(1)}, bf16[104,256]{1,0:T(8,128)(2,1)S(1)}, u32[]{:S(2)}, u32[]{:S(2)}) collective-permute-start(bf16[104,256]{1,0:T(8,128)(2,1)S(1)} %add_convert_fusion.3), channel_id=1, source_target_pairs={{0,8},{4,12},{8,0},{12,4},{16,24},{20,28},{24,16},{28,20},{1,9},{5... | collective-permute-start | bytes 159752 | tf_op jit(solution)/shard_map/ppermute | solution.py:30
  120.5 9.2 %collective-permute-start.21 = (bf16[104,256]{1,0:T(8,128)(2,1)S(1)}, bf16[104,256]{1,0:T(8,128)(2,1)S(1)}, u32[]{:S(2)}, u32[]{:S(2)}) collective-permute-start(bf16[104,256]{1,0:T(8,128)(2,1)S(1)} %add_convert_fusion.2), channel_id=1, source_target_pairs={{0,16},{4,20},{8,24},{12,28},{16,0},{20,4},{24,8},{28,12},{1,17},{... | collective-permute-start | bytes 159752 | tf_op jit(solution)/shard_map/ppermute | solution.py:30
  129.7 4.2 %collective-permute-start.22 = (bf16[104,256]{1,0:T(8,128)(2,1)S(1)}, bf16[104,256]{1,0:T(8,128)(2,1)S(1)}, u32[]{:S(2)}, u32[]{:S(2)}) collective-permute-start(bf16[104,256]{1,0:T(8,128)(2,1)S(1)} %add_convert_fusion.1), channel_id=1, source_target_pairs={{0,4},{4,0},{8,12},{12,8},{16,20},{20,16},{24,28},{28,24},{1,5},{5... | collective-permute-start | bytes 159752 | tf_op jit(solution)/shard_map/ppermute | solution.py:30
  133.9 4.2 %collective-permute-start.24 = (bf16[104,256]{1,0:T(8,128)(2,1)S(1)}, bf16[104,256]{1,0:T(8,128)(2,1)S(1)}, u32[]{:S(2)}, u32[]{:S(2)}) collective-permute-start(bf16[104,256]{1,0:T(8,128)(2,1)S(1)} %add_convert_fusion.refs_0_), channel_id=1, source_target_pairs={{0,2},{1,3},{2,0},{3,1},{4,6},{5,7},{6,4},{7,5},{8,10},{9,11},{10,... | collective-permute-start | bytes 159752 | tf_op jit(solution)/shard_map/ppermute | solution.py:30
  (24 other events, 314.6 us)
